TPU v7x, 256 devices: a whole 4x4x8 slice. The times are simulated.
256 devices in a mesh: row: 2 (over core), span: 32 (over z_lo, y, x), pitch: 4 (over z_hi).
Axes of the slice: x: 4, y: 4, z: 8 (z_hi: 4, z_lo: 2; z = z_hi * 2 + z_lo), core: 2. Of those that a mesh axis runs over, the one named last changes fastest.
Arguments:
- adjoint: float32 [2, 6, 128, 32, 128], P('row', None, 'span', 'pitch'), may hold values from -6 to 6
- source: float32 [2, 6, 128, 32, 128], P('row', None, 'span', 'pitch'), may hold values from -6 to 6
- pseudo_step: float32 [2, 128, 32, 128], P('row', 'span', 'pitch'), may hold values from 0.05 to 0.12
- jac_blocks: bfloat16 [2, 7, 6, 6, 128, 32, 128], P('row', None, None, None, 'span', 'pitch'), as said below
- band_map: int32 [2, 128], replicated, may hold values from 0 to 31, never falling along the last dimension, each value on 1 to 8 neighbouring positions
- face_cell: int32 [2, 32, 4, 128], P('row', 'span', 'pitch'), may hold values from 0 to 4095
- face_owner: int32 [2, 32, 4, 128], P('row', 'span', 'pitch'), may hold values from 0 to 16383
- face_weight: float32 [2, 32, 4, 18, 128], P('row', 'span', 'pitch'), may hold values from -6 to 6
Outputs:
- adjoint_out: float32 [2, 6, 128, 32, 128], P('row', None, 'span', 'pitch')
- sensitivity: float32 [2, 3, 16384], P('row', None, ('span', 'pitch'))
Inputs may be any that keep to these rules, and one draw needn't show every extreme that they name: `band_map`: in each row the span bands never fall with span and every band 0 to 31 holds 1 to 8 span cells. `jac_blocks`: the centre block of each cell is diagonally dominant.
All inputs are finite; a program needn't handle non-finite values.
Results may differ from a plain program's by a relative error of at most 0.0003.
Values sent between devices are 32-bit elements; how exact they have to be, the bound alone decides.
No kernel may reach another device: no remote copies, remote signals or barrier semaphores. Data moves between devices by JAX's collectives and lax.ppermute only.
A program may use at most 64 MiB of HBM per device.

v0:
```python
import jax
import jax.numpy as jnp
from jax import lax
from jax.sharding import PartitionSpec as P

ITERS = 2
NODE_DEV = 128


def padded(value, sides, width, wrap):
    for axis, dim in sides:
        devices, length = (lax.axis_size(axis), value.shape[dim])
        up = [(i, (i + 1) % devices) for i in range(devices if wrap else devices - 1)]
        down = [(j, i) for i, j in up]
        last = lax.slice_in_dim(value, length - width, length, axis=dim)
        first = lax.slice_in_dim(value, 0, width, axis=dim)
        before = lax.ppermute(last, axis, up)
        after = lax.ppermute(first, axis, down)
        value = jnp.concatenate([before, value, after], axis=dim)
    return value


def shifted(value, axis, by):
    devices = lax.axis_size(axis)
    return lax.ppermute(value, axis, [(i, (i + by) % devices) for i in range(devices)])


def neighbours(field, cycle_lower, cycle_upper):
    span_padded = padded(field, (("span", 1),), 1, False)
    pitch_padded = padded(field, (("pitch", 2),), 1, True)
    axial_lower = jnp.concatenate([cycle_lower[..., None], field[..., :-1]], axis=3)
    axial_upper = jnp.concatenate([field[..., 1:], cycle_upper[..., None]], axis=3)
    return [
        field,
        span_padded[:, :-2],
        span_padded[:, 2:],
        pitch_padded[:, :, :-2],
        pitch_padded[:, :, 2:],
        axial_lower,
        axial_upper,
    ]


def apply_blocks(blocks, fields):
    summed = jnp.zeros_like(fields[0])
    for stencil in range(7):
        summed = summed + jnp.einsum(
            "cdjpa,djpa->cjpa",
            blocks[stencil].astype(jnp.float32),
            fields[stencil],
            precision=lax.Precision.HIGHEST,
        )
    return summed


def mixing_cycles(fields, row_ids, own_locals, other_locals, other_counts):
    outlet = jnp.stack([jnp.where(row_ids[0] == 0, fields[0][..., -1], fields[0][..., 0])], axis=0)
    received = shifted(outlet, "row", 1)[::-1]
    partial_totals = jnp.stack(
        [jnp.einsum("cjp,jb->cb", received[0], other_locals[0], precision=lax.Precision.HIGHEST)],
        axis=0,
    )
    other_totals = lax.psum(partial_totals, ("span", "pitch"))
    other_list = other_totals[0]
    band_means = other_list / other_counts[0][None, :]
    cycle_values = jnp.dot(band_means, own_locals[0].T, precision=lax.Precision.HIGHEST)
    cycle_full = jnp.broadcast_to(cycle_values[:, :, None], outlet[0].shape)
    zero_cycle = jnp.zeros_like(cycle_full)
    cycles = [
        (
            jnp.where(row_ids[0] == 1, cycle_full, zero_cycle),
            jnp.where(row_ids[0] == 0, cycle_full, zero_cycle),
        )
    ]
    return cycles


def on_device(
    adjoint, source, pseudo_step, jac_blocks, band_map, face_cell, face_owner, face_weight
):
    local_rows = adjoint.shape[0]
    first_row = lax.axis_index("row") * local_rows
    row_ids = [first_row + 0]
    span_cells = adjoint.shape[2]
    pitch_cells = adjoint.shape[3]
    band_count = band_map.shape[1] // 4
    band_ids = jnp.arange(band_count, dtype=jnp.int32)
    span_start = lax.axis_index("span") * span_cells
    k = 0
    own_map = lax.dynamic_index_in_dim(band_map, row_ids[k], 0, keepdims=False)
    other_map = lax.dynamic_index_in_dim(band_map, 1 - row_ids[k], 0, keepdims=False)
    own_members = (own_map[:, None] == band_ids[None, :]).astype(jnp.float32)
    other_members = (other_map[:, None] == band_ids[None, :]).astype(jnp.float32)
    own_locals = [lax.dynamic_slice_in_dim(own_members, span_start, span_cells, 0)]
    other_locals = [lax.dynamic_slice_in_dim(other_members, span_start, span_cells, 0)]
    other_counts = [jnp.sum(other_members, axis=0) * (pitch_cells * lax.axis_size("pitch"))]
    fields = [adjoint[0]]
    for sweep in range(ITERS):
        cycles = mixing_cycles(fields, row_ids, own_locals, other_locals, other_counts)
        k = 0
        image = apply_blocks(jac_blocks[k], neighbours(fields[k], cycles[k][0], cycles[k][1]))
        updated = [fields[k] + pseudo_step[k][None] * (source[k] - image)]
        fields = updated
    k = 0
    flat_field = fields[k].reshape(fields[k].shape[0], -1)
    cells = face_cell[k, 0, 0]
    face_values = jnp.take(flat_field, cells, axis=1)
    weights = face_weight[k, 0, 0].reshape(3, fields[k].shape[0], cells.shape[0])
    face_list = jnp.sum(weights * face_values[None], axis=1)
    owner_list = face_owner[k, 0, 0]
    node_total = NODE_DEV * lax.axis_size("span") * lax.axis_size("pitch")
    dense_terms = jnp.stack(
        [jnp.zeros((3, node_total), jnp.float32).at[:, owner_list].add(face_list)], axis=0
    )
    node_values = lax.psum_scatter(dense_terms, ("span", "pitch"), scatter_dimension=2, tiled=True)
    return (jnp.stack(fields, axis=0), node_values)


def solution(mesh):
    in_specs = (
        P("row", None, "span", "pitch", None),
        P("row", None, "span", "pitch", None),
        P("row", "span", "pitch", None),
        P("row", None, None, None, "span", "pitch", None),
        P(),
        P("row", "span", "pitch", None),
        P("row", "span", "pitch", None),
        P("row", "span", "pitch", None, None),
    )
    out_specs = (P("row", None, "span", "pitch", None), P("row", None, ("span", "pitch")))
    return jax.shard_map(
        on_device, mesh=mesh, in_specs=in_specs, out_specs=out_specs, check_vma=False
    )
```

profile of v0, /device:TPU:32, one launch (start us, length us, event | category | flops | bytes accessed | tf_op | source)
XLA Modules:
  0.0 1694.4 jit_solution(16444251439627728813)
XLA Ops:
  7.3 1.3 fusion.21
  8.6 1.0 fusion.53
  9.6 3.3 collective-permute-start.2
  13.0 2.2 collective-permute-start.3
  15.2 0.8 fusion.52
  15.9 7.5 collective-permute-start.1
  23.5 1.9 collective-permute-start
  25.4 0.8 fusion.45
  26.3 1.1 fusion.51
  27.4 0.7 compare_and_fusion
  28.1 0.7 fusion.46
  28.7 0.7 reduce.18
  29.8 408.2 %psum.14 = f32[6,32]{1,0:T(8,128)S(1)} all-reduce(f32[6,32]{1,0:T(8,128)S(1)} %fusion.32), channel_id=1, replica_groups=mesh['row'=2,'span'=32,'pitch'=4] {'span','pitch'}, use_global_device_ids=true, to_apply=%region_1.2 | all-reduce | flops 192 | bytes 1536 | tf_op jit(solution)/shard_map/psum | solution.py:63
  438.8 1.1 fusion.24
  440.0 2.1 fusion.4
  442.1 1.0 fusion.29
  443.7 2.9 collective-permute-start.7
  446.6 1.9 collective-permute-start.6
  448.5 3.9 collective-permute-start.5
  452.7 404.9 %psum.15 = f32[6,32]{1,0:T(8,128)S(1)} all-reduce(f32[6,32]{1,0:T(8,128)S(1)} %fusion.30), channel_id=1, replica_groups=mesh['row'=2,'span'=32,'pitch'=4] {'span','pitch'}, use_global_device_ids=true, to_apply=%region_4.5 | all-reduce | flops 192 | bytes 1536 | tf_op jit(solution)/shard_map/psum | solution.py:63
  859.2 0.7 copy.36
  860.8 4.7 scatter_custom_fusion
  865.5 820.5 %reduce-scatter.2.cloned.1.call-done = f32[1,3,128]{1,2,0:T(8,128)} async-done(((f32[1,3,16384]{1,2,0:T(8,128)}), f32[1,3,128]{1,2,0:T(8,128)}) %reduce-scatter.2.cloned.1.call-update) | async-done | bytes 1552 | tf_op jit(solution)/shard_map/reduce_scatter | solution.py:115
  1686.1 1.5 copy.39
  (58 shorter events, 4.4 us)
Async XLA Ops:
  7.2 851.4 %copy-start = (bf16[1,7,6,6,4,8,128]{6,5,4,3,2,1,0:T(8,128)(2,1)S(1)}, bf16[1,7,6,6,4,8,128]{6,5,4,3,2,1,0:T(8,128)(2,1)}, u32[]{:S(2)}) copy-start(bf16[1,7,6,6,4,8,128]{6,5,4,3,2,1,0:T(8,128)(2,1)} %param.11) | copy-start | bytes 6193156
  7.2 851.9 %copy-start.2 = (f32[1,6,4,8,128]{4,3,2,1,0:T(8,128)S(1)}, f32[1,6,4,8,128]{4,3,2,1,0:T(8,128)}, u32[]{:S(2)}) copy-start(f32[1,6,4,8,128]{4,3,2,1,0:T(8,128)} %param.9) | copy-start | bytes 294916
  7.2 851.9 %copy-start.3 = (f32[1,4,8,128]{3,2,1,0:T(8,128)S(1)}, f32[1,4,8,128]{3,2,1,0:T(8,128)}, u32[]{:S(2)}) copy-start(f32[1,4,8,128]{3,2,1,0:T(8,128)} %param.10) | copy-start | bytes 49156
  7.2 1678.9 %reduce-scatter.2.cloned.1.call-start = ((), (), s32[]{:S(2)}) async-start(), calls=%async_computation.1 | async-start | bytes 8454144 | tf_op jit(solution)/shard_map/reduce_scatter | solution.py:115
  8.5 21.0 %collective-permute-start.4 = (f32[1,6,4,8]{3,2,1,0:T(4,128)S(1)}, f32[1,6,4,8]{3,2,1,0:T(4,128)S(1)}, u32[]{:S(2)}, u32[]{:S(2)}) collective-permute-start(f32[1,6,4,8]{3,2,1,0:T(4,128)S(1)} %bitcast.130), channel_id=1, source_target_pairs={{0,128},{128,0},{1,129},{129,1},{2,130},{130,2},{3,131},{131,3},{4... | collective-permute-start | bytes 2312 | tf_op jit(solution)/shard_map/ppermute | solution.py:25
  9.6 429.2 %collective-permute-start.2 = (f32[6,4,1,128]{3,2,1,0:T(1,128)S(1)}, f32[6,4,1,128]{3,2,1,0:T(1,128)S(1)}, u32[]{:S(2)}, u32[]{:S(2)}) collective-permute-start(f32[6,4,1,128]{3,2,1,0:T(1,128)S(1)} %get-tuple-element.42), channel_id=1, source_target_pairs={{0,1},{1,2},{2,3},{3,0},{4,5},{5,6},{6,7},{7,4},{8,9},{9,10},{10,1... | collective-permute-start | bytes 36872 | tf_op jit(solution)/shard_map/ppermute | solution.py:17
  13.0 425.8 %collective-permute-start.3 = (f32[6,4,1,128]{3,2,1,0:T(1,128)S(1)}, f32[6,4,1,128]{3,2,1,0:T(1,128)S(1)}, u32[]{:S(2)}, u32[]{:S(2)}) collective-permute-start(f32[6,4,1,128]{3,2,1,0:T(1,128)S(1)} %get-tuple-element.43), channel_id=1, source_target_pairs={{1,0},{2,1},{3,2},{0,3},{5,4},{6,5},{7,6},{4,7},{9,8},{10,9},{11,1... | collective-permute-start | bytes 36872 | tf_op jit(solution)/shard_map/ppermute | solution.py:18
  15.9 422.9 %collective-permute-start.1 = (f32[6,1,8,128]{3,2,1,0:T(8,128)S(1)}, f32[6,1,8,128]{3,2,1,0:T(8,128)S(1)}, u32[]{:S(2)}, u32[]{:S(2)}) collective-permute-start(f32[6,1,8,128]{3,2,1,0:T(8,128)S(1)} %get-tuple-element.40), channel_id=1, source_target_pairs={{4,0},{8,4},{12,8},{16,12},{20,16},{24,20},{28,24},{32,28},{36,32}... | collective-permute-start | bytes 73736 | tf_op jit(solution)/shard_map/ppermute | solution.py:18
  23.5 415.3 %collective-permute-start = (f32[6,1,8,128]{3,2,1,0:T(8,128)S(1)}, f32[6,1,8,128]{3,2,1,0:T(8,128)S(1)}, u32[]{:S(2)}, u32[]{:S(2)}) collective-permute-start(f32[6,1,8,128]{3,2,1,0:T(8,128)S(1)} %get-tuple-element.41), channel_id=1, source_target_pairs={{0,4},{4,8},{8,12},{12,16},{16,20},{20,24},{24,28},{28,32},{32,36}... | collective-permute-start | bytes 73736 | tf_op jit(solution)/shard_map/ppermute | solution.py:17
  443.5 9.0 collective-permute-start.9
  443.6 414.9 %collective-permute-start.8 = (f32[6,4,1,128]{3,2,1,0:T(1,128)S(1)}, f32[6,4,1,128]{3,2,1,0:T(1,128)S(1)}, u32[]{:S(2)}, u32[]{:S(2)}) collective-permute-start(f32[6,4,1,128]{3,2,1,0:T(1,128)S(1)} %get-tuple-element.30), channel_id=1, source_target_pairs={{1,0},{2,1},{3,2},{0,3},{5,4},{6,5},{7,6},{4,7},{9,8},{10,9},{11,1... | collective-permute-start | bytes 36872 | tf_op jit(solution)/shard_map/ppermute | solution.py:18
  443.7 414.8 %collective-permute-start.7 = (f32[6,4,1,128]{3,2,1,0:T(1,128)S(1)}, f32[6,4,1,128]{3,2,1,0:T(1,128)S(1)}, u32[]{:S(2)}, u32[]{:S(2)}) collective-permute-start(f32[6,4,1,128]{3,2,1,0:T(1,128)S(1)} %get-tuple-element.31), channel_id=1, source_target_pairs={{0,1},{1,2},{2,3},{3,0},{4,5},{5,6},{6,7},{7,4},{8,9},{9,10},{10,1... | collective-permute-start | bytes 36872 | tf_op jit(solution)/shard_map/ppermute | solution.py:17
  446.6 411.9 %collective-permute-start.6 = (f32[6,1,8,128]{3,2,1,0:T(8,128)S(1)}, f32[6,1,8,128]{3,2,1,0:T(8,128)S(1)}, u32[]{:S(2)}, u32[]{:S(2)}) collective-permute-start(f32[6,1,8,128]{3,2,1,0:T(8,128)S(1)} %get-tuple-element.32), channel_id=1, source_target_pairs={{4,0},{8,4},{12,8},{16,12},{20,16},{24,20},{28,24},{32,28},{36,32}... | collective-permute-start | bytes 73736 | tf_op jit(solution)/shard_map/ppermute | solution.py:18
  448.5 410.0 %collective-permute-start.5 = (f32[6,1,8,128]{3,2,1,0:T(8,128)S(1)}, f32[6,1,8,128]{3,2,1,0:T(8,128)S(1)}, u32[]{:S(2)}, u32[]{:S(2)}) collective-permute-start(f32[6,1,8,128]{3,2,1,0:T(8,128)S(1)} %get-tuple-element.33), channel_id=1, source_target_pairs={{0,4},{4,8},{8,12},{12,16},{16,20},{20,24},{24,28},{28,32},{32,36}... | collective-permute-start | bytes 73736 | tf_op jit(solution)/shard_map/ppermute | solution.py:17
  859.1 6.4 copy-start.1
Sparse Core Ops, SparseCore 0:
  865.7 820.3 reduce-scatter.1
where the time goes:
time: 1690 us
  waiting for transfers between devices  821 us (49%)
  blocking collectives  813 us (48%)
  starting transfers between devices  24.1 us (1%)
    reduce_scatter x1, waiting for transfers between devices, on_device(): lax.psum_scatter(dense_terms, ('span', 'pitch'), scatter_dimension=2, til...  821 us
    psum x2, blocking collectives, mixing_cycles(): other_totals = lax.psum(partial_totals, ('span', 'pitch'))  813 us
  transfers between devices with their start and end apart: 11, of which 1 were waited for; matrix products, arithmetic and copies ran while one was open for 0% of the time, Pallas kernels for 0%

commit v1 on v0

--- a/solution.py
+++ b/solution.py
@@ -53,6 +53,13 @@
     return summed
 
 
+def summed_over_row(value):
+    devices = lax.axis_size("span") * lax.axis_size("pitch")
+    copies = jnp.broadcast_to(value.reshape(1, 1, -1), (devices, 1, value.size))
+    received = lax.all_to_all(copies, ("span", "pitch"), 0, 0)
+    return jnp.sum(received, axis=(0, 1)).reshape(value.shape)
+
+
 def mixing_cycles(fields, row_ids, own_locals, other_locals, other_counts):
     outlet = jnp.stack([jnp.where(row_ids[0] == 0, fields[0][..., -1], fields[0][..., 0])], axis=0)
     received = shifted(outlet, "row", 1)[::-1]
@@ -60,8 +67,7 @@
         [jnp.einsum("cjp,jb->cb", received[0], other_locals[0], precision=lax.Precision.HIGHEST)],
         axis=0,
     )
-    other_totals = lax.psum(partial_totals, ("span", "pitch"))
-    other_list = other_totals[0]
+    other_list = summed_over_row(partial_totals[0])
     band_means = other_list / other_counts[0][None, :]
     cycle_values = jnp.dot(band_means, own_locals[0].T, precision=lax.Precision.HIGHEST)
     cycle_full = jnp.broadcast_to(cycle_values[:, :, None], outlet[0].shape)
@@ -108,11 +114,14 @@
     weights = face_weight[k, 0, 0].reshape(3, fields[k].shape[0], cells.shape[0])
     face_list = jnp.sum(weights * face_values[None], axis=1)
     owner_list = face_owner[k, 0, 0]
-    node_total = NODE_DEV * lax.axis_size("span") * lax.axis_size("pitch")
-    dense_terms = jnp.stack(
-        [jnp.zeros((3, node_total), jnp.float32).at[:, owner_list].add(face_list)], axis=0
+    devices = lax.axis_size("span") * lax.axis_size("pitch")
+    dense_terms = (
+        jnp.zeros((devices, 3, NODE_DEV), jnp.float32)
+        .at[owner_list // NODE_DEV, :, owner_list % NODE_DEV]
+        .add(face_list.T)
     )
-    node_values = lax.psum_scatter(dense_terms, ("span", "pitch"), scatter_dimension=2, tiled=True)
+    received = lax.all_to_all(dense_terms, ("span", "pitch"), 0, 0)
+    node_values = jnp.sum(received, axis=0)[None]
     return (jnp.stack(fields, axis=0), node_values)
 
 

time: 1690 us -> 131 us (0.08)
  waiting for transfers between devices: 821 us -> 20.2 us
  blocking collectives: 813 us -> 19.1 us
  starting transfers between devices: 24.1 us -> 50 us
    reduce_scatter x1 -> x0, waiting for transfers between devices: 821 us -> none  [on_device(): lax.psum_scatter(dense_terms, ('span', 'pitch'), scatter_dimension=2, til...]
    psum x2 -> x0, blocking collectives: 813 us -> none  [mixing_cycles(): other_totals = lax.psum(partial_totals, ('span', 'pitch'))]
    all_to_all x0 -> x2, starting transfers between devices: none -> 25.8 us  [summed_over_row(): received = lax.all_to_all(copies, ('span', 'pitch'), 0, 0)]
    all_to_all x0 -> x2, waiting for transfers between devices: none -> 20.1 us  [summed_over_row(): received = lax.all_to_all(copies, ('span', 'pitch'), 0, 0)]
    all_to_all x0 -> x1, blocking collectives: none -> 19.1 us  [on_device(): received = lax.all_to_all(dense_terms, ('span', 'pitch'), 0, 0)]
  transfers between devices with their start and end apart: 11 -> 12, of which waited for: 1 -> 2; matrix products, arithmetic and copies ran while one was open for 0% -> 7% of each run, Pallas kernels for 0% -> 0%
where the time goes in v1:
time: 131 us; the launch traced here: 130 us
  starting transfers between devices  50 us (38%)
  other arithmetic  20.6 us (16%)
  waiting for transfers between devices  20.2 us (15%)
  blocking collectives  19.1 us (15%)
  local copies, waits for them, and re-layouts  18.5 us (14%)
    all_to_all x2, starting transfers between devices, summed_over_row(): received = lax.all_to_all(copies, ('span', 'pitch'), 0, 0)  25.8 us
    all_to_all x2, waiting for transfers between devices, summed_over_row(): received = lax.all_to_all(copies, ('span', 'pitch'), 0, 0)  20.1 us
    all_to_all x1, blocking collectives, on_device(): received = lax.all_to_all(dense_terms, ('span', 'pitch'), 0, 0)  19.1 us
    ppermute x4, starting transfers between devices, padded(): after = lax.ppermute(first, axis, down)  15.5 us
    scatter-add x1, other arithmetic, on_device(): dense_terms = jnp.zeros((devices, 3, NODE_DEV), jnp.float32).at[owner_lis...  13.6 us
    ppermute x4, starting transfers between devices, padded(): before = lax.ppermute(last, axis, up)  8.44 us
    scatter-add x1, local copies, waits for them, and re-layouts, on_device(): dense_terms = jnp.zeros((devices, 3, NODE_DEV), jnp.float32).at[owner_lis...  5.49 us
    broadcast_in_dim x1, local copies, waits for them, and re-layouts, on_device(): jnp.zeros((devices, 3, NODE_DEV), jnp.float32)  4.28 us
  transfers between devices with their start and end apart: 12, of which 2 were waited for; matrix products, arithmetic and copies ran while one was open for 7% of the time, Pallas kernels for 0%

profile of v1, /device:TPU:32, one launch (start us, length us, event | category | flops | bytes accessed | tf_op | source)
XLA Modules:
  0.0 130.1 jit_solution(10083411536899795659)
XLA Ops:
  0.7 1.3 fusion.19
  2.0 1.0 fusion.52
  3.0 3.3 %collective-permute-start.2 = (f32[6,4,1,128]{3,2,1,0:T(1,128)S(1)}, f32[6,4,1,128]{3,2,1,0:T(1,128)S(1)}, u32[]{:S(2)}, u32[]{:S(2)}) collective-permute-start(f32[6,4,1,128]{3,2,1,0:T(1,128)S(1)} %get-tuple-element.40), channel_id=1, source_target_pairs={{0,1},{1,2},{2,3},{3,0},{4,5},{5,6},{6,7},{7,4},{8,9},{9,10},{10,1... | collective-permute-start | bytes 36872 | tf_op jit(solution)/shard_map/ppermute | solution.py:17
  6.4 2.2 %collective-permute-start.3 = (f32[6,4,1,128]{3,2,1,0:T(1,128)S(1)}, f32[6,4,1,128]{3,2,1,0:T(1,128)S(1)}, u32[]{:S(2)}, u32[]{:S(2)}) collective-permute-start(f32[6,4,1,128]{3,2,1,0:T(1,128)S(1)} %get-tuple-element.41), channel_id=1, source_target_pairs={{1,0},{2,1},{3,2},{0,3},{5,4},{6,5},{7,6},{4,7},{9,8},{10,9},{11,1... | collective-permute-start | bytes 36872 | tf_op jit(solution)/shard_map/ppermute | solution.py:18
  8.6 0.8 fusion.51
  9.4 7.5 %collective-permute-start.1 = (f32[6,1,8,128]{3,2,1,0:T(8,128)S(1)}, f32[6,1,8,128]{3,2,1,0:T(8,128)S(1)}, u32[]{:S(2)}, u32[]{:S(2)}) collective-permute-start(f32[6,1,8,128]{3,2,1,0:T(8,128)S(1)} %get-tuple-element.38), channel_id=1, source_target_pairs={{4,0},{8,4},{12,8},{16,12},{20,16},{24,20},{28,24},{32,28},{36,32}... | collective-permute-start | bytes 73736 | tf_op jit(solution)/shard_map/ppermute | solution.py:18
  16.9 1.9 %collective-permute-start = (f32[6,1,8,128]{3,2,1,0:T(8,128)S(1)}, f32[6,1,8,128]{3,2,1,0:T(8,128)S(1)}, u32[]{:S(2)}, u32[]{:S(2)}) collective-permute-start(f32[6,1,8,128]{3,2,1,0:T(8,128)S(1)} %get-tuple-element.39), channel_id=1, source_target_pairs={{0,4},{4,8},{8,12},{12,16},{16,20},{20,24},{24,28},{28,32},{32,36}... | collective-permute-start | bytes 73736 | tf_op jit(solution)/shard_map/ppermute | solution.py:17
  18.9 0.8 fusion.44
  19.7 1.1 fusion.50
  22.5 0.7 broadcast_in_dim.31
  23.3 14.1 %all-to-all-start = ((f32[128,1,192]{2,1,0:T(1,128)}), f32[128,1,192]{2,1,0:T(1,128)S(1)}, u32[]{:S(2)}, u32[]{:S(2)}) async-start(f32[128,1,192]{2,1,0:T(1,128)} %broadcast_in_dim.31), calls=%async_computation | async-start | bytes 262144 | tf_op jit(solution)/shard_map/all_to_all | solution.py:59
  38.3 1.1 fusion.22
  39.4 9.1 %all-to-all-done = f32[128,1,192]{2,1,0:T(1,128)S(1)} async-done(((f32[128,1,192]{2,1,0:T(1,128)}), f32[128,1,192]{2,1,0:T(1,128)S(1)}, u32[]{:S(2)}, u32[]{:S(2)}) %all-to-all-start) | async-done | bytes 98336 | tf_op jit(solution)/shard_map/all_to_all | solution.py:59
  50.6 1.8 %collective-permute-start.8 = (f32[6,4,1,128]{3,2,1,0:T(1,128)S(1)}, f32[6,4,1,128]{3,2,1,0:T(1,128)S(1)}, u32[]{:S(2)}, u32[]{:S(2)}) collective-permute-start(f32[6,4,1,128]{3,2,1,0:T(1,128)S(1)} %get-tuple-element.28), channel_id=1, source_target_pairs={{1,0},{2,1},{3,2},{0,3},{5,4},{6,5},{7,6},{4,7},{9,8},{10,9},{11,1... | collective-permute-start | bytes 36872 | tf_op jit(solution)/shard_map/ppermute | solution.py:18
  52.3 1.3 collective-permute-start.7
  53.6 4.0 %collective-permute-start.6 = (f32[6,1,8,128]{3,2,1,0:T(8,128)S(1)}, f32[6,1,8,128]{3,2,1,0:T(8,128)S(1)}, u32[]{:S(2)}, u32[]{:S(2)}) collective-permute-start(f32[6,1,8,128]{3,2,1,0:T(8,128)S(1)} %get-tuple-element.30), channel_id=1, source_target_pairs={{4,0},{8,4},{12,8},{16,12},{20,16},{24,20},{28,24},{32,28},{36,32}... | collective-permute-start | bytes 73736 | tf_op jit(solution)/shard_map/ppermute | solution.py:18
  57.6 1.9 %collective-permute-start.5 = (f32[6,1,8,128]{3,2,1,0:T(8,128)S(1)}, f32[6,1,8,128]{3,2,1,0:T(8,128)S(1)}, u32[]{:S(2)}, u32[]{:S(2)}) collective-permute-start(f32[6,1,8,128]{3,2,1,0:T(8,128)S(1)} %get-tuple-element.31), channel_id=1, source_target_pairs={{0,4},{4,8},{8,12},{12,16},{16,20},{20,24},{24,28},{28,32},{32,36}... | collective-permute-start | bytes 73736 | tf_op jit(solution)/shard_map/ppermute | solution.py:17
  59.9 0.7 broadcast_in_dim.64
  60.6 11.7 %all-to-all-start.1 = ((f32[128,1,192]{2,1,0:T(1,128)}), f32[128,1,192]{2,1,0:T(1,128)S(1)}, u32[]{:S(2)}, u32[]{:S(2)}) async-start(f32[128,1,192]{2,1,0:T(1,128)} %broadcast_in_dim.64), calls=%async_computation.1 | async-start | bytes 262144 | tf_op jit(solution)/shard_map/all_to_all | solution.py:59
  72.6 11.0 %all-to-all-done.1 = f32[128,1,192]{2,1,0:T(1,128)S(1)} async-done(((f32[128,1,192]{2,1,0:T(1,128)}), f32[128,1,192]{2,1,0:T(1,128)S(1)}, u32[]{:S(2)}, u32[]{:S(2)}) %all-to-all-start.1) | async-done | bytes 98336 | tf_op jit(solution)/shard_map/all_to_all | solution.py:59
  86.8 4.3 %broadcast_in_dim.67 = f32[128,3,128]{1,2,0:T(8,128)} broadcast(f32[]{:T(128)} %constant.62.clone.1), dimensions={} | broadcast | bytes 196612 | tf_op jit(solution)/shard_map/broadcast_in_dim | solution.py:119
  91.1 13.6 %scatter_fusion = f32[128,3,128]{1,2,0:T(8,128)} fusion(f32[128,3,128]{1,2,0:T(8,128)} %broadcast_in_dim.67, s32[128]{0:T(128)S(1)} %get-tuple-element.49, f32[128,3]{1,0:T(8,128)S(1)} %copy.50), kind=kCustom, calls=%fused_computation.1 | custom fusion | flops 384 | bytes 5632 | tf_op jit(solution)/shard_map/scatter-add | solution.py:121
  104.6 5.5 %copy.51 = f32[128,3,128]{2,1,0:T(4,128)S(1)} copy(f32[128,3,128]{1,2,0:T(8,128)} %scatter_fusion) | data formatting | bytes 393216 | tf_op jit(solution)/shard_map/scatter-add | solution.py:121
  110.1 19.1 %all_to_all.15 = f32[128,3,128]{2,1,0:T(4,128)S(1)} all-to-all(f32[128,3,128]{2,1,0:T(4,128)S(1)} %copy.51), channel_id=1, replica_groups=mesh['row'=2,'span'=32,'pitch'=4] {'span','pitch'}, dimensions={0} | all-to-all | bytes 393216 | tf_op jit(solution)/shard_map/all_to_all | solution.py:123
  (72 shorter events, 9.2 us)
Async XLA Ops:
  0.6 48.9 %copy-start.1 = (f32[1,6,4,8,128]{4,3,2,1,0:T(8,128)S(1)}, f32[1,6,4,8,128]{4,3,2,1,0:T(8,128)}, u32[]{:S(2)}) copy-start(f32[1,6,4,8,128]{4,3,2,1,0:T(8,128)} %param.8) | copy-start | bytes 294916
  0.6 48.9 %copy-start = (bf16[1,7,6,6,4,8,128]{6,5,4,3,2,1,0:T(8,128)(2,1)S(1)}, bf16[1,7,6,6,4,8,128]{6,5,4,3,2,1,0:T(8,128)(2,1)}, u32[]{:S(2)}) copy-start(bf16[1,7,6,6,4,8,128]{6,5,4,3,2,1,0:T(8,128)(2,1)} %param.11) | copy-start | bytes 6193156
  1.9 20.2 %collective-permute-start.4 = (f32[1,6,4,8]{3,2,1,0:T(4,128)S(1)}, f32[1,6,4,8]{3,2,1,0:T(4,128)S(1)}, u32[]{:S(2)}, u32[]{:S(2)}) collective-permute-start(f32[1,6,4,8]{3,2,1,0:T(4,128)S(1)} %bitcast.143), channel_id=1, source_target_pairs={{0,128},{128,0},{1,129},{129,1},{2,130},{130,2},{3,131},{131,3},{4... | collective-permute-start | bytes 2312 | tf_op jit(solution)/shard_map/ppermute | solution.py:25
  3.0 35.2 %collective-permute-start.2 = (f32[6,4,1,128]{3,2,1,0:T(1,128)S(1)}, f32[6,4,1,128]{3,2,1,0:T(1,128)S(1)}, u32[]{:S(2)}, u32[]{:S(2)}) collective-permute-start(f32[6,4,1,128]{3,2,1,0:T(1,128)S(1)} %get-tuple-element.40), channel_id=1, source_target_pairs={{0,1},{1,2},{2,3},{3,0},{4,5},{5,6},{6,7},{7,4},{8,9},{9,10},{10,1... | collective-permute-start | bytes 36872 | tf_op jit(solution)/shard_map/ppermute | solution.py:17
  6.4 31.8 %collective-permute-start.3 = (f32[6,4,1,128]{3,2,1,0:T(1,128)S(1)}, f32[6,4,1,128]{3,2,1,0:T(1,128)S(1)}, u32[]{:S(2)}, u32[]{:S(2)}) collective-permute-start(f32[6,4,1,128]{3,2,1,0:T(1,128)S(1)} %get-tuple-element.41), channel_id=1, source_target_pairs={{1,0},{2,1},{3,2},{0,3},{5,4},{6,5},{7,6},{4,7},{9,8},{10,9},{11,1... | collective-permute-start | bytes 36872 | tf_op jit(solution)/shard_map/ppermute | solution.py:18
  9.4 28.9 %collective-permute-start.1 = (f32[6,1,8,128]{3,2,1,0:T(8,128)S(1)}, f32[6,1,8,128]{3,2,1,0:T(8,128)S(1)}, u32[]{:S(2)}, u32[]{:S(2)}) collective-permute-start(f32[6,1,8,128]{3,2,1,0:T(8,128)S(1)} %get-tuple-element.38), channel_id=1, source_target_pairs={{4,0},{8,4},{12,8},{16,12},{20,16},{24,20},{28,24},{32,28},{36,32}... | collective-permute-start | bytes 73736 | tf_op jit(solution)/shard_map/ppermute | solution.py:18
  16.9 21.3 %collective-permute-start = (f32[6,1,8,128]{3,2,1,0:T(8,128)S(1)}, f32[6,1,8,128]{3,2,1,0:T(8,128)S(1)}, u32[]{:S(2)}, u32[]{:S(2)}) collective-permute-start(f32[6,1,8,128]{3,2,1,0:T(8,128)S(1)} %get-tuple-element.39), channel_id=1, source_target_pairs={{0,4},{4,8},{8,12},{12,16},{16,20},{20,24},{24,28},{28,32},{32,36}... | collective-permute-start | bytes 73736 | tf_op jit(solution)/shard_map/ppermute | solution.py:17
  23.3 25.3 %all-to-all-start = ((f32[128,1,192]{2,1,0:T(1,128)}), f32[128,1,192]{2,1,0:T(1,128)S(1)}, u32[]{:S(2)}, u32[]{:S(2)}) async-start(f32[128,1,192]{2,1,0:T(1,128)} %broadcast_in_dim.31), calls=%async_computation | async-start | bytes 262144 | tf_op jit(solution)/shard_map/all_to_all | solution.py:59
  49.3 0.9 copy-start.3
  49.3 0.9 copy-start.4
  50.5 9.1 %collective-permute-start.9 = (f32[1,6,4,8]{3,2,1,0:T(4,128)S(1)}, f32[1,6,4,8]{3,2,1,0:T(4,128)S(1)}, u32[]{:S(2)}, u32[]{:S(2)}) collective-permute-start(f32[1,6,4,8]{3,2,1,0:T(4,128)S(1)} %bitcast.144), channel_id=1, source_target_pairs={{0,128},{128,0},{1,129},{129,1},{2,130},{130,2},{3,131},{131,3},{4... | collective-permute-start | bytes 2312 | tf_op jit(solution)/shard_map/ppermute | solution.py:25
  50.6 21.9 %collective-permute-start.8 = (f32[6,4,1,128]{3,2,1,0:T(1,128)S(1)}, f32[6,4,1,128]{3,2,1,0:T(1,128)S(1)}, u32[]{:S(2)}, u32[]{:S(2)}) collective-permute-start(f32[6,4,1,128]{3,2,1,0:T(1,128)S(1)} %get-tuple-element.28), channel_id=1, source_target_pairs={{1,0},{2,1},{3,2},{0,3},{5,4},{6,5},{7,6},{4,7},{9,8},{10,9},{11,1... | collective-permute-start | bytes 36872 | tf_op jit(solution)/shard_map/ppermute | solution.py:18
  52.3 20.2 %collective-permute-start.7 = (f32[6,4,1,128]{3,2,1,0:T(1,128)S(1)}, f32[6,4,1,128]{3,2,1,0:T(1,128)S(1)}, u32[]{:S(2)}, u32[]{:S(2)}) collective-permute-start(f32[6,4,1,128]{3,2,1,0:T(1,128)S(1)} %get-tuple-element.29), channel_id=1, source_target_pairs={{0,1},{1,2},{2,3},{3,0},{4,5},{5,6},{6,7},{7,4},{8,9},{9,10},{10,1... | collective-permute-start | bytes 36872 | tf_op jit(solution)/shard_map/ppermute | solution.py:17
  53.6 18.9 %collective-permute-start.6 = (f32[6,1,8,128]{3,2,1,0:T(8,128)S(1)}, f32[6,1,8,128]{3,2,1,0:T(8,128)S(1)}, u32[]{:S(2)}, u32[]{:S(2)}) collective-permute-start(f32[6,1,8,128]{3,2,1,0:T(8,128)S(1)} %get-tuple-element.30), channel_id=1, source_target_pairs={{4,0},{8,4},{12,8},{16,12},{20,16},{24,20},{28,24},{32,28},{36,32}... | collective-permute-start | bytes 73736 | tf_op jit(solution)/shard_map/ppermute | solution.py:18
  57.6 14.9 %collective-permute-start.5 = (f32[6,1,8,128]{3,2,1,0:T(8,128)S(1)}, f32[6,1,8,128]{3,2,1,0:T(8,128)S(1)}, u32[]{:S(2)}, u32[]{:S(2)}) collective-permute-start(f32[6,1,8,128]{3,2,1,0:T(8,128)S(1)} %get-tuple-element.31), channel_id=1, source_target_pairs={{0,4},{4,8},{8,12},{12,16},{16,20},{20,24},{24,28},{28,32},{32,36}... | collective-permute-start | bytes 73736 | tf_op jit(solution)/shard_map/ppermute | solution.py:17
  60.6 22.9 %all-to-all-start.1 = ((f32[128,1,192]{2,1,0:T(1,128)}), f32[128,1,192]{2,1,0:T(1,128)S(1)}, u32[]{:S(2)}, u32[]{:S(2)}) async-start(f32[128,1,192]{2,1,0:T(1,128)} %broadcast_in_dim.64), calls=%async_computation.1 | async-start | bytes 262144 | tf_op jit(solution)/shard_map/all_to_all | solution.py:59
  85.1 5.9 %copy-start.2 = (f32[6,4,8,128]{3,2,1,0:T(8,128)}, f32[6,4,8,128]{3,2,1,0:T(8,128)S(1)}, u32[]{:S(2)}) copy-start(f32[6,4,8,128]{3,2,1,0:T(8,128)S(1)} %fusion.25) | copy-start | bytes 294916

commit v2 on v0

v2 whole, which is shorter than its diff:
```python
import jax
import jax.numpy as jnp
from jax import lax
from jax.experimental import pallas as pl
from jax.experimental.pallas import tpu as pltpu
from jax.sharding import PartitionSpec as P

NVAR = 6
CS = 4
CP = 8
LANES = 128
F32 = jnp.float32
BF16 = jnp.bfloat16
FIRST_AT = 8
WEIGHT_AT = 16
COUNT_AT = 6


def lane_ids(shape):
    return lax.broadcasted_iota(jnp.int32, shape, len(shape) - 1)


def row_ids(shape):
    return lax.broadcasted_iota(jnp.int32, shape, len(shape) - 2)


def split3(x):
    hi = x.astype(BF16)
    rest = x - hi.astype(F32)
    mid = rest.astype(BF16)
    low = (rest - mid.astype(F32)).astype(BF16)
    return hi, mid, low


def dot3(x, onehot, dims):
    parts = [
        lax.dot_general(part, onehot, (dims, ((), ())), preferred_element_type=F32)
        for part in split3(x)
    ]
    return parts[0] + (parts[1] + parts[2])


def fill_stencil(vs, field, up, down, left, right, lower, upper):
    tile = (CP, LANES)
    lane, sub = lane_ids(tile), row_ids(tile)
    for d in range(NVAR):
        for j in range(CS):
            x = field(d, j)
            vs[d, j] = x
            vs[6 + d, j] = field(d, j - 1) if j > 0 else up(d)
            vs[12 + d, j] = field(d, j + 1) if j < CS - 1 else down(d)
            vs[18 + d, j] = jnp.where(
                sub == 0, jnp.broadcast_to(left(d, j), tile), pltpu.roll(x, 1, 0)
            )
            vs[24 + d, j] = jnp.where(
                sub == CP - 1, jnp.broadcast_to(right(d, j), tile), pltpu.roll(x, CP - 1, 0)
            )
            vs[30 + d, j] = jnp.where(lane == 0, lower(d, j), pltpu.roll(x, 1, 1))
            vs[36 + d, j] = jnp.where(lane == LANES - 1, upper(d, j), pltpu.roll(x, LANES - 1, 1))


def image_of(jac_ref, vs, c):
    acc = jnp.zeros((CS, CP, LANES), F32)
    for s in range(7):
        for d in range(NVAR):
            acc = acc + jac_ref[0, s, c, d].astype(F32) * vs[6 * s + d]
    return acc


def first_kernel(
    adj_ref, src_ref, tau_ref, jac_ref, up_ref, down_ref, left_ref, right_ref,
    f1_ref, msg_ref, to_up_ref, to_down_ref, to_left_ref, to_right_ref, vs, rec,
):
    row = lax.axis_index("row")
    outlet = (1 - row) * (LANES - 1)
    ghost = 6 - row
    tile = (CP, LANES)
    zero = jnp.zeros(tile, F32)
    fill_stencil(
        vs,
        lambda d, j: adj_ref[0, d, j],
        lambda d: up_ref[d],
        lambda d: down_ref[d],
        lambda d, j: left_ref[d, j : j + 1],
        lambda d, j: right_ref[d, j : j + 1],
        lambda d, j: zero,
        lambda d, j: zero,
    )
    lane = lane_ids(tile)

    def body(c, carry):
        weights, sums = carry
        f0 = adj_ref[0, c]
        new = f0 + tau_ref[0] * (src_ref[0, c] - image_of(jac_ref, vs, c))
        f1_ref[c] = new
        weights, sums = list(weights), list(sums)
        for j in range(CS):
            for d in range(NVAR):
                at = WEIGHT_AT + 8 * d + c
                moved = pltpu.roll(jac_ref[0, ghost, c, d, j].astype(F32), at + 1 - row, 1)
                weights[j] = jnp.where(lane == at, moved, weights[j])
            sums[j] = jnp.where(lane == c, pltpu.roll(f0[j], c + 1 - row, 1), sums[j])
            at = FIRST_AT + c
            sums[j] = jnp.where(lane == at, pltpu.roll(new[j], at + 1 - row, 1), sums[j])
        return tuple(weights), tuple(sums)

    ones = jnp.where(lane == COUNT_AT, 1.0, 0.0).astype(F32)
    weights, sums = lax.fori_loop(0, NVAR, body, ((zero,) * CS, (ones,) * CS))
    rows = []
    for j in range(CS):
        tau_out = jnp.sum(jnp.where(lane == outlet, tau_ref[0, j], 0.0), axis=1, keepdims=True)
        record = sums[j] + weights[j] * tau_out
        rec[j] = record
        rows.append(jnp.sum(record, axis=0, keepdims=True))
    halves = [
        jnp.broadcast_to(rows[2 * h] + pltpu.roll(rows[2 * h + 1], 64, 1), tile) for h in range(2)
    ]
    packed = jnp.where(row_ids(tile) % 2 == 0, halves[0], halves[1])
    for i in range(msg_ref.shape[0] // CP):
        msg_ref[CP * i : CP * (i + 1)] = packed
    to_up_ref[0:NVAR] = f1_ref[:, 0]
    to_up_ref[NVAR] = rec[0]
    to_down_ref[0:NVAR] = f1_ref[:, CS - 1]
    to_down_ref[NVAR] = rec[CS - 1]
    for c in range(NVAR):
        to_left_ref[c] = f1_ref[c, :, 0, :]
        to_right_ref[c] = f1_ref[c, :, CP - 1, :]
    to_left_ref[NVAR] = rec[:, 0, :]
    to_right_ref[NVAR] = rec[:, CP - 1, :]


def weight_sum(x):
    for by in (32, 16, 8):
        x = x + pltpu.roll(x, LANES - by, 1)
    return x


def spread(values):
    lane = lane_ids(values.shape)
    out = jnp.zeros(values.shape, F32)
    for d in range(NVAR):
        out = jnp.where(
            lane // 8 == d + WEIGHT_AT // 8,
            jnp.broadcast_to(values[:, d : d + 1], values.shape),
            out,
        )
    return out


def second_kernel(
    bands_ref, f1_ref, src_ref, tau_ref, jac_ref, all_ref, ids_ref, up_ref, down_ref, left_ref,
    right_ref, cell_ref, owner_ref, weight_ref, out_ref, dense_ref, vs, field, cycle, edge, side,
):
    row = lax.axis_index("row")
    span = lax.axis_index("span")
    outlet = (1 - row) * (LANES - 1)
    ghost = 6 - row
    tile = (CP, LANES)
    lane = lane_ids(tile)
    last_cell = bands_ref.shape[1] - 1
    wanted = [
        bands_ref[row, jnp.clip(span * CS - 1 + t, 0, last_cell)] for t in range(CS + 2)
    ]
    half = all_ref.shape[0] // 2
    zero = jnp.zeros(tile, F32)

    def gather_bands(base):
        def body(i, sums):
            at = pl.multiple_of(base + i * CP, CP)
            ids, values = ids_ref[pl.ds(at, CP), :], all_ref[pl.ds(at, CP), :]
            return tuple(
                total + jnp.where(ids == band, values, 0.0) for total, band in zip(sums, wanted)
            )

        sums = lax.fori_loop(0, half // CP, body, (zero,) * (CS + 2), unroll=4)
        rows = [jnp.sum(x, axis=0, keepdims=True) for x in sums]
        rows = rows + [rows[-1]] * (CP - len(rows))
        folded = jnp.concatenate(rows, axis=0)
        folded = folded + pltpu.roll(folded, 64, 1)
        return folded, jnp.broadcast_to(folded[:, COUNT_AT : COUNT_AT + 1], tile)

    other, other_count = gather_bands(pl.multiple_of((1 - row) * half, CP))
    mine, my_count = gather_bands(pl.multiple_of(row * half, CP))
    cycle0 = other / other_count
    spread0 = spread(cycle0)
    lost = weight_sum(other * spread(mine / my_count))
    cycle1 = (other - pltpu.roll(lost, LANES - (WEIGHT_AT - FIRST_AT), 1)) / other_count
    at_outlet = lane == outlet

    for j in range(CS):
        for d in range(NVAR):
            cycle[d, j] = jnp.broadcast_to(cycle0[j + 1 : j + 2, d : d + 1], tile)

    def correct(c, carry):
        acc = jnp.zeros((CS, CP, LANES), F32)
        for d in range(NVAR):
            acc = acc + jac_ref[0, ghost, c, d].astype(F32) * cycle[d]
        field[c] = f1_ref[c] - jnp.where(at_outlet[None], tau_ref[0] * acc, 0.0)
        return carry

    lax.fori_loop(0, NVAR, correct, 0)
    for n, (ref, at) in enumerate(((up_ref, 0), (down_ref, CS + 1))):
        moved = weight_sum(ref[NVAR] * spread0[at : at + 1])
        for c in range(NVAR):
            part = jnp.broadcast_to(moved[:, WEIGHT_AT + c : WEIGHT_AT + c + 1], tile)
            edge[n, c] = ref[c] - jnp.where(at_outlet, part, 0.0)
    low = (CS, LANES)
    low_outlet = lane_ids(low) == outlet
    for n, ref in enumerate((left_ref, right_ref)):
        moved = weight_sum(ref[NVAR] * spread0[1 : 1 + CS])
        for c in range(NVAR):
            part = jnp.broadcast_to(moved[:, WEIGHT_AT + c : WEIGHT_AT + c + 1], low)
            side[n, c] = ref[c] - jnp.where(low_outlet, part, 0.0)
    is_upper = jnp.where(row == 0, 1.0, 0.0).astype(F32)

    def cycled(d, j):
        at = FIRST_AT + d
        return jnp.broadcast_to(cycle1[j + 1 : j + 2, at : at + 1], tile)

    fill_stencil(
        vs,
        lambda d, j: field[d, j],
        lambda d: edge[0, d],
        lambda d: edge[1, d],
        lambda d, j: side[0, d, j : j + 1],
        lambda d, j: side[1, d, j : j + 1],
        lambda d, j: cycled(d, j) * (1.0 - is_upper),
        lambda d, j: cycled(d, j) * is_upper,
    )

    def advance(c, carry):
        new = field[c] + tau_ref[0] * (src_ref[0, c] - image_of(jac_ref, vs, c))
        out_ref[0, c] = new
        return carry

    lax.fori_loop(0, NVAR, advance, 0)

    cells = cell_ref[0, 0]
    square = (LANES, LANES)
    axial_pick = (row_ids(square) == cells % LANES).astype(F32).astype(BF16)
    flat = out_ref[0].reshape(NVAR * CS * CP, LANES)
    picked = dot3(flat, axial_pick, ((1,), (0,)))
    here = row_ids((CS * CP, LANES)) == cells // LANES
    terms = [jnp.zeros((1, LANES), F32)] * 3
    for c in range(NVAR):
        block = picked[c * CS * CP : (c + 1) * CS * CP]
        value = jnp.sum(jnp.where(here, block, 0.0), axis=0, keepdims=True)
        for k in range(3):
            at = NVAR * k + c
            terms[k] = terms[k] + weight_ref[0, 0, 0, at : at + 1] * value
    owners = owner_ref[0, 0]
    shape = dense_ref.shape
    line = row_ids(shape)
    device = (line * 43691) >> 17
    coord = line - 3 * device
    value = jnp.where(
        coord == 0,
        jnp.broadcast_to(terms[0], shape),
        jnp.where(coord == 1, jnp.broadcast_to(terms[1], shape), jnp.broadcast_to(terms[2], shape)),
    )
    placed = jnp.where(device == owners // LANES, value, 0.0)
    node_pick = (row_ids(square) == owners % LANES).astype(F32).astype(BF16)
    dense_ref[...] = dot3(placed, node_pick, ((1,), (1,)))


def third_kernel(parts_ref, out_ref):
    folded = jnp.sum(parts_ref[...].reshape(-1, 24, LANES), axis=0)
    coord = row_ids(folded.shape) % 3
    for k in range(3):
        out_ref[0, k : k + 1] = jnp.sum(jnp.where(coord == k, folded, 0.0), axis=0, keepdims=True)


VM = pl.BlockSpec(memory_space=pltpu.VMEM)
SM = pl.BlockSpec(memory_space=pltpu.SMEM)
PARAMS = pltpu.CompilerParams(vmem_limit_bytes=32 * 1024 * 1024)


def exchange(to_up, to_down, to_left, to_right):
    spans, pitches = lax.axis_size("span"), lax.axis_size("pitch")
    rising = [(i, i + 1) for i in range(spans - 1)]
    falling = [(i + 1, i) for i in range(spans - 1)]
    onward = [(i, (i + 1) % pitches) for i in range(pitches)]
    back = [((i + 1) % pitches, i) for i in range(pitches)]
    return (
        lax.ppermute(to_down, "span", rising),
        lax.ppermute(to_up, "span", falling),
        lax.ppermute(to_right, "pitch", onward),
        lax.ppermute(to_left, "pitch", back),
    )


def on_device(
    adjoint, source, pseudo_step, jac_blocks, band_map, face_cell, face_owner, face_weight
):
    rows, spans, pitches = (lax.axis_size(name) for name in ("row", "span", "pitch"))
    devices = rows * spans * pitches
    peers = spans * pitches
    halo = exchange(adjoint[0, :, 0], adjoint[0, :, CS - 1], adjoint[0, :, :, 0], adjoint[0, :, :, CP - 1])
    edge_shape = jax.ShapeDtypeStruct((NVAR + 1, CP, LANES), F32)
    side_shape = jax.ShapeDtypeStruct((NVAR + 1, CS, LANES), F32)
    block = (NVAR, CS, CP, LANES)
    first, record, *sends = pl.pallas_call(
        first_kernel,
        out_shape=(
            jax.ShapeDtypeStruct(block, F32),
            jax.ShapeDtypeStruct((2 * devices, LANES), F32),
            edge_shape, edge_shape, side_shape, side_shape,
        ),
        in_specs=[VM] * 8,
        out_specs=(VM,) * 6,
        scratch_shapes=[
            pltpu.VMEM((7 * NVAR, CS, CP, LANES), F32),
            pltpu.VMEM((CS, CP, LANES), F32),
        ],
        compiler_params=PARAMS,
        name="first_iteration",
    )(adjoint, source, pseudo_step, jac_blocks, *halo)
    records = lax.all_to_all(
        record.reshape(devices, 1, 2 * LANES), ("row", "span", "pitch"), 0, 0
    ).reshape(2 * devices, LANES)
    halo = exchange(*sends)
    ids = jnp.broadcast_to(
        band_map.reshape(rows, spans, 1, CS // 2, 2, 1),
        (rows, spans, pitches, CS // 2, 2, LANES // 2),
    ).reshape(2 * devices, LANES)
    field, dense = pl.pallas_call(
        second_kernel,
        out_shape=(
            jax.ShapeDtypeStruct((1,) + block, F32),
            jax.ShapeDtypeStruct((3 * peers, LANES), F32),
        ),
        in_specs=[SM] + [VM] * 13,
        out_specs=(VM,) * 2,
        scratch_shapes=[
            pltpu.VMEM((7 * NVAR, CS, CP, LANES), F32),
            pltpu.VMEM(block, F32),
            pltpu.VMEM(block, F32),
            pltpu.VMEM((2, NVAR, CP, LANES), F32),
            pltpu.VMEM((2, NVAR, CS, LANES), F32),
        ],
        compiler_params=PARAMS,
        name="second_iteration",
    )(
        band_map, first, source, pseudo_step, jac_blocks, records, ids, *halo,
        face_cell, face_owner, face_weight,
    )
    parts = lax.all_to_all(dense.reshape(peers, 1, 3 * LANES), ("span", "pitch"), 0, 0)
    nodes = pl.pallas_call(
        third_kernel,
        out_shape=jax.ShapeDtypeStruct((1, 3, LANES), F32),
        in_specs=[VM],
        out_specs=VM,
        compiler_params=PARAMS,
        name="node_sums",
    )(parts.reshape(3 * peers, LANES))
    return field, nodes


def solution(mesh):
    in_specs = (
        P("row", None, "span", "pitch", None),
        P("row", None, "span", "pitch", None),
        P("row", "span", "pitch", None),
        P("row", None, None, None, "span", "pitch", None),
        P(),
        P("row", "span", "pitch", None),
        P("row", "span", "pitch", None),
        P("row", "span", "pitch", None, None),
    )
    out_specs = (P("row", None, "span", "pitch", None), P("row", None, ("span", "pitch")))
    return jax.shard_map(
        on_device, mesh=mesh, in_specs=in_specs, out_specs=out_specs, check_vma=False
    )
```

time: 1690 us -> 78.9 us (0.05)
  waiting for transfers between devices: 821 us -> 5.74 us
  blocking collectives: 813 us -> 20.8 us
    reduce_scatter x1 -> x0, waiting for transfers between devices: 821 us -> none  [on_device(): lax.psum_scatter(dense_terms, ('span', 'pitch'), scatter_dimension=2, til...]
    psum x2 -> x0, blocking collectives: 813 us -> none  [mixing_cycles(): other_totals = lax.psum(partial_totals, ('span', 'pitch'))]
    all_to_all x0 -> x1, blocking collectives: none -> 20.8 us  [on_device(): lax.all_to_all(dense.reshape(peers, 1, 3 * LANES), ('span', 'pitch'), 0, 0)]
  transfers between devices with their start and end apart: 11 -> 9, of which waited for: 1 -> 4; matrix products, arithmetic and copies ran while one was open for 0% -> 2% of each run, Pallas kernels for 0% -> 0%
where the time goes in v2:
time: 78.9 us; the launch traced here: 78.4 us
  starting transfers between devices  38.6 us (49%)
  blocking collectives  20.8 us (26%)
  local copies, waits for them, and re-layouts  7.09 us (9%)
  waiting for transfers between devices  5.74 us (7%)
  Pallas kernels  5.34 us (7%)
  between operations  0.79 us (1%)
    all_to_all x1, blocking collectives, on_device(): lax.all_to_all(dense.reshape(peers, 1, 3 * LANES), ('span', 'pitch'), 0, 0)  20.8 us
    ppermute x2, starting transfers between devices, exchange(): lax.ppermute(to_up, 'span', falling)  13.3 us
    all_to_all x1, starting transfers between devices, on_device(): lax.all_to_all(record.reshape(devices, 1, 2 * LANES), ('row', 'span', 'pi...  8.46 us
    ppermute x2, starting transfers between devices, exchange(): lax.ppermute(to_down, 'span', rising)  6.78 us
    ppermute x2, starting transfers between devices, exchange(): lax.ppermute(to_right, 'pitch', onward)  6.33 us
    unnamed x24, local copies, waits for them, and re-layouts  4.67 us
    ppermute x2, starting transfers between devices, exchange(): lax.ppermute(to_left, 'pitch', back)  3.72 us
    pallas_call x1, Pallas kernels, on_device(): pl.pallas_call(second_kernel, out_shape=(jax.ShapeDtypeStruct((1,) + bloc...  3.34 us
  transfers between devices with their start and end apart: 9, of which 4 were waited for; matrix products, arithmetic and copies ran while one was open for 2% of the time, Pallas kernels for 0%

profile of v2, /device:TPU:32, one launch (start us, length us, event | category | flops | bytes accessed | tf_op | source)
XLA Modules:
  0.0 78.4 jit_solution(17075565243398459660)
XLA Ops:
  0.6 0.8 slice_bitcast_fusion
  1.4 3.4 %collective-permute-start = (f32[6,8,128]{2,1,0:T(8,128)S(1)}, f32[6,8,128]{2,1,0:T(8,128)S(1)}, u32[]{:S(2)}, u32[]{:S(2)}) collective-permute-start(f32[6,8,128]{2,1,0:T(8,128)S(1)} %get-tuple-element.27), channel_id=1, source_target_pairs={{0,4},{4,8},{8,12},{12,16},{16,20},{20,24},{24,28},{28,32},{32,36}... | collective-permute-start | bytes 73736 | tf_op jit(solution)/shard_map/ppermute | solution.py:285
  4.8 6.7 %collective-permute-start.1 = (f32[6,8,128]{2,1,0:T(8,128)S(1)}, f32[6,8,128]{2,1,0:T(8,128)S(1)}, u32[]{:S(2)}, u32[]{:S(2)}) collective-permute-start(f32[6,8,128]{2,1,0:T(8,128)S(1)} %get-tuple-element.26), channel_id=1, source_target_pairs={{4,0},{8,4},{12,8},{16,12},{20,16},{24,20},{28,24},{32,28},{36,32}... | collective-permute-start | bytes 73736 | tf_op jit(solution)/shard_map/ppermute | solution.py:286
  11.5 1.0 %fusion = (f32[1,6,4,1,128]{4,3,2,1,0:T(1,128)S(1)}, f32[1,6,4,1,128]{4,3,2,1,0:T(1,128)S(1)}) fusion(f32[1,6,4,8,128]{4,3,2,1,0:T(8,128)} %adj_ref.1), kind=kLoop, calls=%fused_computation.2 | loop fusion | bytes 49152 | tf_op jit(solution)/shard_map/slice | solution.py:298
  12.5 3.3 %collective-permute-start.2 = (f32[6,4,128]{2,1,0:T(4,128)S(1)}, f32[6,4,128]{2,1,0:T(4,128)S(1)}, u32[]{:S(2)}, u32[]{:S(2)}) collective-permute-start(f32[6,4,128]{2,1,0:T(4,128)S(1)} %bitcast.22), channel_id=1, source_target_pairs={{0,1},{1,2},{2,3},{3,0},{4,5},{5,6},{6,7},{7,4},{8,9},{9,10},{10,1... | collective-permute-start | bytes 36872 | tf_op jit(solution)/shard_map/ppermute | solution.py:287
  15.8 2.2 %collective-permute-start.3 = (f32[6,4,128]{2,1,0:T(4,128)S(1)}, f32[6,4,128]{2,1,0:T(4,128)S(1)}, u32[]{:S(2)}, u32[]{:S(2)}) collective-permute-start(f32[6,4,128]{2,1,0:T(4,128)S(1)} %bitcast.21), channel_id=1, source_target_pairs={{1,0},{2,1},{3,2},{0,3},{5,4},{6,5},{7,6},{4,7},{9,8},{10,9},{11,1... | collective-permute-start | bytes 36872 | tf_op jit(solution)/shard_map/ppermute | solution.py:288
  18.1 1.6 %collective-permute-done.2.left_ref = f32[6,4,128]{2,1,0:T(4,128)S(1)} collective-permute-done((f32[6,4,128]{2,1,0:T(4,128)S(1)}, f32[6,4,128]{2,1,0:T(4,128)S(1)}, u32[]{:S(2)}, u32[]{:S(2)}) %collective-permute-start.2) | collective-permute-done | bytes 12320 | tf_op jit(solution)/shard_map/ppermute | solution.py:287
  19.6 1.5 %collective-permute-done.3.right_ref = f32[6,4,128]{2,1,0:T(4,128)S(1)} collective-permute-done((f32[6,4,128]{2,1,0:T(4,128)S(1)}, f32[6,4,128]{2,1,0:T(4,128)S(1)}, u32[]{:S(2)}, u32[]{:S(2)}) %collective-permute-start.3) | collective-permute-done | bytes 12320 | tf_op jit(solution)/shard_map/ppermute | solution.py:288
  21.1 1.6 %copy-done = bf16[1,7,6,6,4,8,128]{6,5,4,3,2,1,0:T(8,128)(2,1)S(1)} copy-done((bf16[1,7,6,6,4,8,128]{6,5,4,3,2,1,0:T(8,128)(2,1)S(1)}, bf16[1,7,6,6,4,8,128]{6,5,4,3,2,1,0:T(8,128)(2,1)}, u32[]{:S(2)}) %copy-start) | copy-done | bytes 2064408
  22.7 0.9 %copy-done.2 = f32[1,6,4,8,128]{4,3,2,1,0:T(8,128)S(1)} copy-done((f32[1,6,4,8,128]{4,3,2,1,0:T(8,128)S(1)}, f32[1,6,4,8,128]{4,3,2,1,0:T(8,128)}, u32[]{:S(2)}) %copy-start.2) | copy-done | bytes 98328
  23.6 0.9 %copy-done.4 = f32[1,6,4,8,128]{4,3,2,1,0:T(8,128)S(1)} copy-done((f32[1,6,4,8,128]{4,3,2,1,0:T(8,128)S(1)}, f32[1,6,4,8,128]{4,3,2,1,0:T(8,128)}, u32[]{:S(2)}) %copy-start.4) | copy-done | bytes 98328
  24.4 0.7 copy-done.5
  25.2 2.0 %first_iteration.1 = (f32[6,4,8,128]{3,2,1,0:T(8,128)S(1)}, f32[512,128]{1,0:T(8,128)}, f32[7,8,128]{2,1,0:T(8,128)S(1)}, f32[7,8,128]{2,1,0:T(8,128)S(1)}, f32[...) custom-call(f32[1,6,4,8,128]{4,3,2,1,0:T(8,128)S(1)} %copy-done.4, f32[1,6,4,8,128]{4,3,2,1,0:T(8,128)S(1)} %copy-done.2, ...), custom_call_target="tpu_custom_call" | custom-call | tf_op jit(solution)/shard_map/first_iteration/pallas_call | solution.py:302
  27.1 8.5 %all-to-all-start = ((f32[256,1,256]{2,1,0:T(1,128)}), f32[256,1,256]{2,1,0:T(1,128)S(1)}, u32[]{:S(2)}, u32[]{:S(2)}) async-start(f32[256,1,256]{2,1,0:T(1,128)} %bitcast.4), calls=%async_computation | async-start | bytes 524288 | tf_op jit(solution)/shard_map/all_to_all | solution.py:318
  35.6 3.4 %collective-permute-start.4 = (f32[7,8,128]{2,1,0:T(8,128)S(1)}, f32[7,8,128]{2,1,0:T(8,128)S(1)}, u32[]{:S(2)}, u32[]{:S(2)}) collective-permute-start(f32[7,8,128]{2,1,0:T(8,128)S(1)} %get-tuple-element.12), channel_id=1, source_target_pairs={{0,4},{4,8},{8,12},{12,16},{16,20},{20,24},{24,28},{28,32},{32,36}... | collective-permute-start | bytes 86024 | tf_op jit(solution)/shard_map/ppermute | solution.py:285
  39.0 6.7 %collective-permute-start.5 = (f32[7,8,128]{2,1,0:T(8,128)S(1)}, f32[7,8,128]{2,1,0:T(8,128)S(1)}, u32[]{:S(2)}, u32[]{:S(2)}) collective-permute-start(f32[7,8,128]{2,1,0:T(8,128)S(1)} %get-tuple-element.13), channel_id=1, source_target_pairs={{4,0},{8,4},{12,8},{16,12},{20,16},{24,20},{28,24},{32,28},{36,32}... | collective-permute-start | bytes 86024 | tf_op jit(solution)/shard_map/ppermute | solution.py:286
  45.7 3.0 %collective-permute-start.6 = (f32[7,4,128]{2,1,0:T(4,128)S(1)}, f32[7,4,128]{2,1,0:T(4,128)S(1)}, u32[]{:S(2)}, u32[]{:S(2)}) collective-permute-start(f32[7,4,128]{2,1,0:T(4,128)S(1)} %get-tuple-element.14), channel_id=1, source_target_pairs={{0,1},{1,2},{2,3},{3,0},{4,5},{5,6},{6,7},{7,4},{8,9},{9,10},{10,1... | collective-permute-start | bytes 43016 | tf_op jit(solution)/shard_map/ppermute | solution.py:287
  48.7 1.5 %collective-permute-start.7 = (f32[7,4,128]{2,1,0:T(4,128)S(1)}, f32[7,4,128]{2,1,0:T(4,128)S(1)}, u32[]{:S(2)}, u32[]{:S(2)}) collective-permute-start(f32[7,4,128]{2,1,0:T(4,128)S(1)} %get-tuple-element.15), channel_id=1, source_target_pairs={{1,0},{2,1},{3,2},{0,3},{5,4},{6,5},{7,6},{4,7},{9,8},{10,9},{11,1... | collective-permute-start | bytes 43016 | tf_op jit(solution)/shard_map/ppermute | solution.py:288
  50.5 0.3 reshape.23.ids_ref
  50.9 0.9 %collective-permute-done.6.left_ref = f32[7,4,128]{2,1,0:T(4,128)S(1)} collective-permute-done((f32[7,4,128]{2,1,0:T(4,128)S(1)}, f32[7,4,128]{2,1,0:T(4,128)S(1)}, u32[]{:S(2)}, u32[]{:S(2)}) %collective-permute-start.6) | collective-permute-done | bytes 14368 | tf_op jit(solution)/shard_map/ppermute | solution.py:287
  51.8 1.8 %collective-permute-done.7.right_ref = f32[7,4,128]{2,1,0:T(4,128)S(1)} collective-permute-done((f32[7,4,128]{2,1,0:T(4,128)S(1)}, f32[7,4,128]{2,1,0:T(4,128)S(1)}, u32[]{:S(2)}, u32[]{:S(2)}) %collective-permute-start.7) | collective-permute-done | bytes 14368 | tf_op jit(solution)/shard_map/ppermute | solution.py:288
  53.6 3.3 %second_iteration.1 = (f32[1,6,4,8,128]{4,3,2,1,0:T(8,128)}, f32[384,128]{1,0:T(8,128)S(1)}) custom-call(s32[2,128]{1,0:T(2,128)S(1)} %copy-done.7, f32[6,4,8,128]{3,2,1,0:T(8,128)S(1)} %get-tuple-element.10.f1_ref, f32[1,6,4,8,128]{4,3,2,1,0:T(8,128)S(1)} %copy-done.3, f32[1,4,8,128]{3,2,1,0:T(8,128)S(1)} %copy-done.6, ...), custom_call_target="tpu_custom_call" | custom-call | tf_op jit(solution)/shard_map/second_iteration/pallas_call | solution.py:326
  57.0 20.8 %all_to_all.10 = f32[128,1,384]{2,1,0:T(1,128)S(1)} all-to-all(f32[128,1,384]{2,1,0:T(1,128)S(1)} %bitcast.20), channel_id=1, replica_groups=mesh['row'=2,'span'=32,'pitch'=4] {'span','pitch'}, dimensions={0} | all-to-all | bytes 393216 | tf_op jit(solution)/shard_map/all_to_all | solution.py:347
  77.9 0.6 copy.29
  (27 shorter events, 0.4 us)
Async XLA Ops:
  0.6 49.5 %copy-start.7 = (s32[2,128]{1,0:T(2,128)S(1)}, s32[2,128]{1,0:T(2,128)}, u32[]{:S(2)}) copy-start(s32[2,128]{1,0:T(2,128)} %bands_ref.1) | copy-start | bytes 3076
  1.4 19.7 %collective-permute-start = (f32[6,8,128]{2,1,0:T(8,128)S(1)}, f32[6,8,128]{2,1,0:T(8,128)S(1)}, u32[]{:S(2)}, u32[]{:S(2)}) collective-permute-start(f32[6,8,128]{2,1,0:T(8,128)S(1)} %get-tuple-element.27), channel_id=1, source_target_pairs={{0,4},{4,8},{8,12},{12,16},{16,20},{20,24},{24,28},{28,32},{32,36}... | collective-permute-start | bytes 73736 | tf_op jit(solution)/shard_map/ppermute | solution.py:285
  4.8 16.3 %collective-permute-start.1 = (f32[6,8,128]{2,1,0:T(8,128)S(1)}, f32[6,8,128]{2,1,0:T(8,128)S(1)}, u32[]{:S(2)}, u32[]{:S(2)}) collective-permute-start(f32[6,8,128]{2,1,0:T(8,128)S(1)} %get-tuple-element.26), channel_id=1, source_target_pairs={{4,0},{8,4},{12,8},{16,12},{20,16},{24,20},{28,24},{32,28},{36,32}... | collective-permute-start | bytes 73736 | tf_op jit(solution)/shard_map/ppermute | solution.py:286
  12.5 7.2 %collective-permute-start.2 = (f32[6,4,128]{2,1,0:T(4,128)S(1)}, f32[6,4,128]{2,1,0:T(4,128)S(1)}, u32[]{:S(2)}, u32[]{:S(2)}) collective-permute-start(f32[6,4,128]{2,1,0:T(4,128)S(1)} %bitcast.22), channel_id=1, source_target_pairs={{0,1},{1,2},{2,3},{3,0},{4,5},{5,6},{6,7},{7,4},{8,9},{9,10},{10,1... | collective-permute-start | bytes 36872 | tf_op jit(solution)/shard_map/ppermute | solution.py:287
  15.8 37.8 %copy-start.8 = (s32[1,1,1,128]{3,2,1,0:T(1,128)S(1)}, s32[1,1,1,128]{3,2,1,0:T(1,128)}, u32[]{:S(2)}) copy-start(s32[1,1,1,128]{3,2,1,0:T(1,128)} %cell_ref.1) | copy-start | bytes 1540
  15.8 37.8 %copy-start.9 = (s32[1,1,1,128]{3,2,1,0:T(1,128)S(1)}, s32[1,1,1,128]{3,2,1,0:T(1,128)}, u32[]{:S(2)}) copy-start(s32[1,1,1,128]{3,2,1,0:T(1,128)} %owner_ref.1) | copy-start | bytes 1540
  15.8 5.3 %collective-permute-start.3 = (f32[6,4,128]{2,1,0:T(4,128)S(1)}, f32[6,4,128]{2,1,0:T(4,128)S(1)}, u32[]{:S(2)}, u32[]{:S(2)}) collective-permute-start(f32[6,4,128]{2,1,0:T(4,128)S(1)} %bitcast.21), channel_id=1, source_target_pairs={{1,0},{2,1},{3,2},{0,3},{5,4},{6,5},{7,6},{4,7},{9,8},{10,9},{11,1... | collective-permute-start | bytes 36872 | tf_op jit(solution)/shard_map/ppermute | solution.py:288
  21.1 1.6 %copy-start = (bf16[1,7,6,6,4,8,128]{6,5,4,3,2,1,0:T(8,128)(2,1)S(1)}, bf16[1,7,6,6,4,8,128]{6,5,4,3,2,1,0:T(8,128)(2,1)}, u32[]{:S(2)}) copy-start(bf16[1,7,6,6,4,8,128]{6,5,4,3,2,1,0:T(8,128)(2,1)} %jac_ref.3) | copy-start | bytes 6193156
  22.7 0.9 %copy-start.2 = (f32[1,6,4,8,128]{4,3,2,1,0:T(8,128)S(1)}, f32[1,6,4,8,128]{4,3,2,1,0:T(8,128)}, u32[]{:S(2)}) copy-start(f32[1,6,4,8,128]{4,3,2,1,0:T(8,128)} %src_ref.3) | copy-start | bytes 294916
  23.6 0.9 %copy-start.4 = (f32[1,6,4,8,128]{4,3,2,1,0:T(8,128)S(1)}, f32[1,6,4,8,128]{4,3,2,1,0:T(8,128)}, u32[]{:S(2)}) copy-start(f32[1,6,4,8,128]{4,3,2,1,0:T(8,128)} %adj_ref.1) | copy-start | bytes 294916
  24.4 0.7 copy-start.5
  25.2 25.7 %copy-start.10 = (f32[1,1,1,18,128]{4,2,3,1,0:T(1,128)S(1)}, f32[1,1,1,18,128]{4,2,3,1,0:T(1,128)}, u32[]{:S(2)}) copy-start(f32[1,1,1,18,128]{4,2,3,1,0:T(1,128)} %param.15) | copy-start | bytes 27652
  25.2 28.4 %copy-start.1 = (bf16[1,7,6,6,4,8,128]{6,5,4,3,2,1,0:T(8,128)(2,1)S(1)}, bf16[1,7,6,6,4,8,128]{6,5,4,3,2,1,0:T(8,128)(2,1)}, u32[]{:S(2)}) copy-start(bf16[1,7,6,6,4,8,128]{6,5,4,3,2,1,0:T(8,128)(2,1)} %jac_ref.3) | copy-start | bytes 6193156
  25.2 28.5 %copy-start.3 = (f32[1,6,4,8,128]{4,3,2,1,0:T(8,128)S(1)}, f32[1,6,4,8,128]{4,3,2,1,0:T(8,128)}, u32[]{:S(2)}) copy-start(f32[1,6,4,8,128]{4,3,2,1,0:T(8,128)} %src_ref.3) | copy-start | bytes 294916
  25.2 28.5 %copy-start.6 = (f32[1,4,8,128]{3,2,1,0:T(8,128)S(1)}, f32[1,4,8,128]{3,2,1,0:T(8,128)}, u32[]{:S(2)}) copy-start(f32[1,4,8,128]{3,2,1,0:T(8,128)} %tau_ref.3) | copy-start | bytes 49156
  27.1 26.4 %all-to-all-start = ((f32[256,1,256]{2,1,0:T(1,128)}), f32[256,1,256]{2,1,0:T(1,128)S(1)}, u32[]{:S(2)}, u32[]{:S(2)}) async-start(f32[256,1,256]{2,1,0:T(1,128)} %bitcast.4), calls=%async_computation | async-start | bytes 524288 | tf_op jit(solution)/shard_map/all_to_all | solution.py:318
  35.6 18.0 %collective-permute-start.4 = (f32[7,8,128]{2,1,0:T(8,128)S(1)}, f32[7,8,128]{2,1,0:T(8,128)S(1)}, u32[]{:S(2)}, u32[]{:S(2)}) collective-permute-start(f32[7,8,128]{2,1,0:T(8,128)S(1)} %get-tuple-element.12), channel_id=1, source_target_pairs={{0,4},{4,8},{8,12},{12,16},{16,20},{20,24},{24,28},{28,32},{32,36}... | collective-permute-start | bytes 86024 | tf_op jit(solution)/shard_map/ppermute | solution.py:285
  39.0 14.6 %collective-permute-start.5 = (f32[7,8,128]{2,1,0:T(8,128)S(1)}, f32[7,8,128]{2,1,0:T(8,128)S(1)}, u32[]{:S(2)}, u32[]{:S(2)}) collective-permute-start(f32[7,8,128]{2,1,0:T(8,128)S(1)} %get-tuple-element.13), channel_id=1, source_target_pairs={{4,0},{8,4},{12,8},{16,12},{20,16},{24,20},{28,24},{32,28},{36,32}... | collective-permute-start | bytes 86024 | tf_op jit(solution)/shard_map/ppermute | solution.py:286
  45.7 6.1 %collective-permute-start.6 = (f32[7,4,128]{2,1,0:T(4,128)S(1)}, f32[7,4,128]{2,1,0:T(4,128)S(1)}, u32[]{:S(2)}, u32[]{:S(2)}) collective-permute-start(f32[7,4,128]{2,1,0:T(4,128)S(1)} %get-tuple-element.14), channel_id=1, source_target_pairs={{0,1},{1,2},{2,3},{3,0},{4,5},{5,6},{6,7},{7,4},{8,9},{9,10},{10,1... | collective-permute-start | bytes 43016 | tf_op jit(solution)/shard_map/ppermute | solution.py:287
  48.7 4.9 %collective-permute-start.7 = (f32[7,4,128]{2,1,0:T(4,128)S(1)}, f32[7,4,128]{2,1,0:T(4,128)S(1)}, u32[]{:S(2)}, u32[]{:S(2)}) collective-permute-start(f32[7,4,128]{2,1,0:T(4,128)S(1)} %get-tuple-element.15), channel_id=1, source_target_pairs={{1,0},{2,1},{3,2},{0,3},{5,4},{6,5},{7,6},{4,7},{9,8},{10,9},{11,1... | collective-permute-start | bytes 43016 | tf_op jit(solution)/shard_map/ppermute | solution.py:288

commit v3 on v2

--- a/solution.py
+++ b/solution.py
@@ -63,59 +63,133 @@
     acc = jnp.zeros((CS, CP, LANES), F32)
     for s in range(7):
         for d in range(NVAR):
-            acc = acc + jac_ref[0, s, c, d].astype(F32) * vs[6 * s + d]
+            acc = acc + jac_ref[s, c, d].astype(F32) * vs[6 * s + d]
     return acc
 
 
-def first_kernel(
-    adj_ref, src_ref, tau_ref, jac_ref, up_ref, down_ref, left_ref, right_ref,
-    f1_ref, msg_ref, to_up_ref, to_down_ref, to_left_ref, to_right_ref, vs, rec,
+def edges_kernel(adj_ref, up_ref, down_ref, left_ref, right_ref, sems):
+    adj = adj_ref.at[0]
+    copies = [
+        pltpu.make_async_copy(adj.at[:, 0], up_ref, sems.at[0]),
+        pltpu.make_async_copy(adj.at[:, CS - 1], down_ref, sems.at[1]),
+        pltpu.make_async_copy(adj.at[:, :, 0], left_ref, sems.at[2]),
+        pltpu.make_async_copy(adj.at[:, :, CP - 1], right_ref, sems.at[3]),
+    ]
+    for copy in copies:
+        copy.start()
+    for copy in copies:
+        copy.wait()
+
+
+def interior_kernel(
+    adj_hbm, src_hbm, tau_hbm, jac_hbm, part_ref, rec_ref, jac_ref, src_ref, tau_ref, adj_ref, vs,
+    image, sems,
 ):
     row = lax.axis_index("row")
     outlet = (1 - row) * (LANES - 1)
     ghost = 6 - row
     tile = (CP, LANES)
     zero = jnp.zeros(tile, F32)
+    lane = lane_ids(tile)
+    load_adj = pltpu.make_async_copy(adj_hbm.at[0], adj_ref, sems.at[0])
+    load_jac = [
+        pltpu.make_async_copy(jac_hbm.at[0, s], jac_ref.at[s], sems.at[1 + s]) for s in range(7)
+    ]
+    load_tau = pltpu.make_async_copy(tau_hbm.at[0], tau_ref, sems.at[8])
+    load_src = pltpu.make_async_copy(src_hbm.at[0], src_ref, sems.at[9])
+    for copy in [load_adj] + load_jac + [load_tau, load_src]:
+        copy.start()
+    load_adj.wait()
     fill_stencil(
         vs,
-        lambda d, j: adj_ref[0, d, j],
-        lambda d: up_ref[d],
-        lambda d: down_ref[d],
-        lambda d, j: left_ref[d, j : j + 1],
-        lambda d, j: right_ref[d, j : j + 1],
+        lambda d, j: adj_ref[d, j],
+        lambda d: zero,
+        lambda d: zero,
         lambda d, j: zero,
         lambda d, j: zero,
-    )
-    lane = lane_ids(tile)
-
-    def body(c, carry):
-        weights, sums = carry
-        f0 = adj_ref[0, c]
-        new = f0 + tau_ref[0] * (src_ref[0, c] - image_of(jac_ref, vs, c))
-        f1_ref[c] = new
-        weights, sums = list(weights), list(sums)
+        lambda d, j: zero,
+        lambda d, j: zero,
+    )
+    for s in range(7):
+        load_jac[s].wait()
+
+        def apply(c, carry):
+            acc = jnp.zeros((CS, CP, LANES), F32) if s == 0 else image[c]
+            for d in range(NVAR):
+                acc = acc + jac_ref[s, c, d].astype(F32) * vs[6 * s + d]
+            image[c] = acc
+            return carry
+
+        lax.fori_loop(0, NVAR, apply, 0)
+    load_tau.wait()
+    load_src.wait()
+
+    def finish(c, carry):
+        weights, sums = (list(x) for x in carry)
+        f0 = adj_ref[c]
+        part_ref[c] = f0 + tau_ref[...] * (src_ref[c] - image[c])
         for j in range(CS):
             for d in range(NVAR):
                 at = WEIGHT_AT + 8 * d + c
-                moved = pltpu.roll(jac_ref[0, ghost, c, d, j].astype(F32), at + 1 - row, 1)
+                moved = pltpu.roll(jac_ref[ghost, c, d, j].astype(F32), at + 1 - row, 1)
                 weights[j] = jnp.where(lane == at, moved, weights[j])
             sums[j] = jnp.where(lane == c, pltpu.roll(f0[j], c + 1 - row, 1), sums[j])
-            at = FIRST_AT + c
-            sums[j] = jnp.where(lane == at, pltpu.roll(new[j], at + 1 - row, 1), sums[j])
         return tuple(weights), tuple(sums)
 
     ones = jnp.where(lane == COUNT_AT, 1.0, 0.0).astype(F32)
-    weights, sums = lax.fori_loop(0, NVAR, body, ((zero,) * CS, (ones,) * CS))
+    weights, sums = lax.fori_loop(0, NVAR, finish, ((zero,) * CS, (ones,) * CS))
+    for j in range(CS):
+        tau_out = jnp.sum(jnp.where(lane == outlet, tau_ref[j], 0.0), axis=1, keepdims=True)
+        rec_ref[j] = sums[j] + weights[j] * tau_out
+
+
+def edge_kernel(
+    part_ref, rec_in, jac_ref, tau_ref, up_ref, down_ref, left_ref, right_ref,
+    f1_ref, msg_ref, to_up_ref, to_down_ref, to_left_ref, to_right_ref, sides, rec,
+):
+    row = lax.axis_index("row")
+    tile = (CP, LANES)
+    lane, sub = lane_ids(tile), row_ids(tile)
+    for d in range(NVAR):
+        for j in range(CS):
+            sides[d, j] = jnp.where(
+                sub == 0, jnp.broadcast_to(left_ref[d, j : j + 1], tile), 0.0
+            )
+            sides[NVAR + d, j] = jnp.where(
+                sub == CP - 1, jnp.broadcast_to(right_ref[d, j : j + 1], tile), 0.0
+            )
+
+    def body(c, sums):
+        sums = list(sums)
+        acc = jnp.zeros((CS, CP, LANES), F32)
+        first = jnp.zeros(tile, F32)
+        last = jnp.zeros(tile, F32)
+        for d in range(NVAR):
+            acc = acc + jac_ref[3, c, d].astype(F32) * sides[d]
+            acc = acc + jac_ref[4, c, d].astype(F32) * sides[NVAR + d]
+            first = first + jac_ref[1, c, d, 0].astype(F32) * up_ref[d]
+            last = last + jac_ref[2, c, d, CS - 1].astype(F32) * down_ref[d]
+        at = FIRST_AT + c
+        for j in range(CS):
+            lost = acc[j]
+            if j == 0:
+                lost = lost + first
+            if j == CS - 1:
+                lost = lost + last
+            new = part_ref[c, j] - tau_ref[j] * lost
+            f1_ref[c, j] = new
+            sums[j] = jnp.where(lane == at, pltpu.roll(new, at + 1 - row, 1), sums[j])
+        return tuple(sums)
+
+    sums = lax.fori_loop(0, NVAR, body, tuple(rec_in[j] for j in range(CS)))
     rows = []
     for j in range(CS):
-        tau_out = jnp.sum(jnp.where(lane == outlet, tau_ref[0, j], 0.0), axis=1, keepdims=True)
-        record = sums[j] + weights[j] * tau_out
-        rec[j] = record
-        rows.append(jnp.sum(record, axis=0, keepdims=True))
+        rec[j] = sums[j]
+        rows.append(jnp.sum(sums[j], axis=0, keepdims=True))
     halves = [
         jnp.broadcast_to(rows[2 * h] + pltpu.roll(rows[2 * h + 1], 64, 1), tile) for h in range(2)
     ]
-    packed = jnp.where(row_ids(tile) % 2 == 0, halves[0], halves[1])
+    packed = jnp.where(sub % 2 == 0, halves[0], halves[1])
     for i in range(msg_ref.shape[0] // CP):
         msg_ref[CP * i : CP * (i + 1)] = packed
     to_up_ref[0:NVAR] = f1_ref[:, 0]
@@ -148,8 +222,8 @@
 
 
 def second_kernel(
-    bands_ref, f1_ref, src_ref, tau_ref, jac_ref, all_ref, ids_ref, up_ref, down_ref, left_ref,
-    right_ref, cell_ref, owner_ref, weight_ref, out_ref, dense_ref, vs, field, cycle, edge, side,
+    bands_ref, f1_ref, src_ref, tau_ref, jac_ref, all_ref, up_ref, down_ref, left_ref, right_ref,
+    cell_ref, owner_ref, weight_ref, out_ref, dense_ref, vs, field, cycle, edge, side,
 ):
     row = lax.axis_index("row")
     span = lax.axis_index("span")
@@ -164,10 +238,20 @@
     half = all_ref.shape[0] // 2
     zero = jnp.zeros(tile, F32)
 
-    def gather_bands(base):
+    second_half = lane >= LANES // 2
+    odd = row_ids(tile) % 2 == 1
+
+    def gather_bands(of_row):
+        base = of_row * half
+
         def body(i, sums):
-            at = pl.multiple_of(base + i * CP, CP)
-            ids, values = ids_ref[pl.ds(at, CP), :], all_ref[pl.ds(at, CP), :]
+            values = all_ref[pl.ds(pl.multiple_of(base + i * CP, CP), CP), :]
+            cells = [bands_ref[of_row, i * CS + j] for j in range(CS)]
+            ids = jnp.where(
+                odd,
+                jnp.where(second_half, cells[3], cells[2]),
+                jnp.where(second_half, cells[1], cells[0]),
+            )
             return tuple(
                 total + jnp.where(ids == band, values, 0.0) for total, band in zip(sums, wanted)
             )
@@ -179,8 +263,8 @@
         folded = folded + pltpu.roll(folded, 64, 1)
         return folded, jnp.broadcast_to(folded[:, COUNT_AT : COUNT_AT + 1], tile)
 
-    other, other_count = gather_bands(pl.multiple_of((1 - row) * half, CP))
-    mine, my_count = gather_bands(pl.multiple_of(row * half, CP))
+    other, other_count = gather_bands(1 - row)
+    mine, my_count = gather_bands(row)
     cycle0 = other / other_count
     spread0 = spread(cycle0)
     lost = weight_sum(other * spread(mine / my_count))
@@ -194,8 +278,8 @@
     def correct(c, carry):
         acc = jnp.zeros((CS, CP, LANES), F32)
         for d in range(NVAR):
-            acc = acc + jac_ref[0, ghost, c, d].astype(F32) * cycle[d]
-        field[c] = f1_ref[c] - jnp.where(at_outlet[None], tau_ref[0] * acc, 0.0)
+            acc = acc + jac_ref[ghost, c, d].astype(F32) * cycle[d]
+        field[c] = f1_ref[c] - jnp.where(at_outlet[None], tau_ref[...] * acc, 0.0)
         return carry
 
     lax.fori_loop(0, NVAR, correct, 0)
@@ -229,7 +313,7 @@
     )
 
     def advance(c, carry):
-        new = field[c] + tau_ref[0] * (src_ref[0, c] - image_of(jac_ref, vs, c))
+        new = field[c] + tau_ref[...] * (src_ref[c] - image_of(jac_ref, vs, c))
         out_ref[0, c] = new
         return carry
 
@@ -267,12 +351,29 @@
     folded = jnp.sum(parts_ref[...].reshape(-1, 24, LANES), axis=0)
     coord = row_ids(folded.shape) % 3
     for k in range(3):
-        out_ref[0, k : k + 1] = jnp.sum(jnp.where(coord == k, folded, 0.0), axis=0, keepdims=True)
+        out_ref[k] = jnp.sum(jnp.where(coord == k, folded, 0.0), axis=0, keepdims=True)
 
 
 VM = pl.BlockSpec(memory_space=pltpu.VMEM)
 SM = pl.BlockSpec(memory_space=pltpu.SMEM)
 PARAMS = pltpu.CompilerParams(vmem_limit_bytes=32 * 1024 * 1024)
+
+
+HBM = pl.BlockSpec(memory_space=pltpu.HBM)
+
+
+def call(kernel, name, outs, in_specs, scratch=(), cost=None):
+    outs = [out if isinstance(out[0], tuple) else (out, F32) for out in outs]
+    return pl.pallas_call(
+        kernel,
+        out_shape=tuple(jax.ShapeDtypeStruct(shape, dtype) for shape, dtype in outs),
+        in_specs=in_specs,
+        out_specs=(VM,) * len(outs),
+        scratch_shapes=list(scratch),
+        compiler_params=PARAMS,
+        cost_estimate=cost,
+        name=name,
+    )
 
 
 def exchange(to_up, to_down, to_left, to_right):
@@ -295,65 +396,66 @@
     rows, spans, pitches = (lax.axis_size(name) for name in ("row", "span", "pitch"))
     devices = rows * spans * pitches
     peers = spans * pitches
-    halo = exchange(adjoint[0, :, 0], adjoint[0, :, CS - 1], adjoint[0, :, :, 0], adjoint[0, :, :, CP - 1])
-    edge_shape = jax.ShapeDtypeStruct((NVAR + 1, CP, LANES), F32)
-    side_shape = jax.ShapeDtypeStruct((NVAR + 1, CS, LANES), F32)
     block = (NVAR, CS, CP, LANES)
-    first, record, *sends = pl.pallas_call(
-        first_kernel,
-        out_shape=(
-            jax.ShapeDtypeStruct(block, F32),
-            jax.ShapeDtypeStruct((2 * devices, LANES), F32),
-            edge_shape, edge_shape, side_shape, side_shape,
-        ),
+    edge = (NVAR, CP, LANES)
+    side = (NVAR, CS, LANES)
+    edges = call(
+        edges_kernel,
+        "edges",
+        [edge, edge, side, side],
+        in_specs=[HBM],
+        scratch=[pltpu.SemaphoreType.DMA((4,))],
+    )(adjoint)
+    halo = exchange(*edges)
+    part, record, jac, src, tau = call(
+        interior_kernel,
+        "interior",
+        [block, (CS, CP, LANES), ((7, NVAR) + block, BF16), block, (CS, CP, LANES)],
+        in_specs=[HBM] * 4,
+        scratch=[
+            pltpu.VMEM(block, F32),
+            pltpu.VMEM((7 * NVAR, CS, CP, LANES), F32),
+            pltpu.VMEM(block, F32),
+            pltpu.SemaphoreType.DMA((10,)),
+        ],
+        cost=pl.CostEstimate(flops=9_000_000, bytes_accessed=3_000_000, transcendentals=0),
+    )(adjoint, source, pseudo_step, jac_blocks)
+    edge = (NVAR + 1, CP, LANES)
+    side = (NVAR + 1, CS, LANES)
+    first, message, *sends = call(
+        edge_kernel,
+        "edge_update",
+        [block, (2 * devices, LANES), edge, edge, side, side],
         in_specs=[VM] * 8,
-        out_specs=(VM,) * 6,
-        scratch_shapes=[
-            pltpu.VMEM((7 * NVAR, CS, CP, LANES), F32),
+        scratch=[
+            pltpu.VMEM((2 * NVAR, CS, CP, LANES), F32),
             pltpu.VMEM((CS, CP, LANES), F32),
         ],
-        compiler_params=PARAMS,
-        name="first_iteration",
-    )(adjoint, source, pseudo_step, jac_blocks, *halo)
+    )(part, record, jac, tau, *halo)
     records = lax.all_to_all(
-        record.reshape(devices, 1, 2 * LANES), ("row", "span", "pitch"), 0, 0
+        message.reshape(devices, 1, 2 * LANES), ("row", "span", "pitch"), 0, 0
     ).reshape(2 * devices, LANES)
     halo = exchange(*sends)
-    ids = jnp.broadcast_to(
-        band_map.reshape(rows, spans, 1, CS // 2, 2, 1),
-        (rows, spans, pitches, CS // 2, 2, LANES // 2),
-    ).reshape(2 * devices, LANES)
-    field, dense = pl.pallas_call(
+    field, dense = call(
         second_kernel,
-        out_shape=(
-            jax.ShapeDtypeStruct((1,) + block, F32),
-            jax.ShapeDtypeStruct((3 * peers, LANES), F32),
-        ),
-        in_specs=[SM] + [VM] * 13,
-        out_specs=(VM,) * 2,
-        scratch_shapes=[
+        "second_iteration",
+        [(1,) + block, (3 * peers, LANES)],
+        in_specs=[SM] + [VM] * 12,
+        scratch=[
             pltpu.VMEM((7 * NVAR, CS, CP, LANES), F32),
             pltpu.VMEM(block, F32),
             pltpu.VMEM(block, F32),
             pltpu.VMEM((2, NVAR, CP, LANES), F32),
             pltpu.VMEM((2, NVAR, CS, LANES), F32),
         ],
-        compiler_params=PARAMS,
-        name="second_iteration",
     )(
-        band_map, first, source, pseudo_step, jac_blocks, records, ids, *halo,
-        face_cell, face_owner, face_weight,
+        band_map, first, src, tau, jac, records, *halo, face_cell, face_owner, face_weight,
     )
     parts = lax.all_to_all(dense.reshape(peers, 1, 3 * LANES), ("span", "pitch"), 0, 0)
-    nodes = pl.pallas_call(
-        third_kernel,
-        out_shape=jax.ShapeDtypeStruct((1, 3, LANES), F32),
-        in_specs=[VM],
-        out_specs=VM,
-        compiler_params=PARAMS,
-        name="node_sums",
-    )(parts.reshape(3 * peers, LANES))
-    return field, nodes
+    (nodes,) = call(third_kernel, "node_sums", [(3, 1, LANES)], in_specs=[VM])(
+        parts.reshape(3 * peers, LANES)
+    )
+    return field, nodes.transpose(1, 0, 2)
 
 
 def solution(mesh):

time: 78.9 us -> 76.6 us (0.971)
  local copies, waits for them, and re-layouts: 7.09 us -> 4.09 us
  Pallas kernels: 5.34 us -> 8.11 us
  waiting for transfers between devices: 5.74 us -> 3.44 us
    pallas_call x3 -> x5, Pallas kernels: 5.34 us -> 8.11 us  [the longest x1 3.79 us: on_device(): call(second_kernel, 'second_iteration', [(1,) + block, (3 * peers, LANES)...]
    ppermute x2, waiting for transfers between devices: 3.27 us -> 1.82 us  [exchange(): lax.ppermute(to_left, 'pitch', back)]
    slice x1 -> x0, local copies, waits for them, and re-layouts: 0.99 us -> none  [on_device(): adjoint[0, :, :, 0]]
    ppermute x2, waiting for transfers between devices: 2.46 us -> 1.6 us  [exchange(): lax.ppermute(to_right, 'pitch', onward)]
    unnamed x24 -> x17, local copies, waits for them, and re-layouts: 4.67 us -> 4.09 us
  transfers between devices with their start and end apart: 9 -> 9, of which waited for: 4 -> 2; matrix products, arithmetic and copies ran while one was open for 2% -> 0% of each run, Pallas kernels for 0% -> 3%
where the time goes in v3:
time: 76.6 us; the launch traced here: 76.2 us
  starting transfers between devices  39 us (51%)
  blocking collectives  20.8 us (27%)
  Pallas kernels  8.11 us (11%)
  local copies, waits for them, and re-layouts  4.09 us (5%)
  waiting for transfers between devices  3.44 us (4%)
  between operations  0.77 us (1%)
    all_to_all x1, blocking collectives, on_device(): lax.all_to_all(dense.reshape(peers, 1, 3 * LANES), ('span', 'pitch'), 0, 0)  20.8 us
    ppermute x2, starting transfers between devices, exchange(): lax.ppermute(to_up, 'span', falling)  13.3 us
    all_to_all x1, starting transfers between devices, on_device(): lax.all_to_all(message.reshape(devices, 1, 2 * LANES), ('row', 'span', 'p...  8.81 us
    ppermute x2, starting transfers between devices, exchange(): lax.ppermute(to_down, 'span', rising)  6.79 us
    ppermute x2, starting transfers between devices, exchange(): lax.ppermute(to_right, 'pitch', onward)  6.33 us
    unnamed x17, local copies, waits for them, and re-layouts  4.09 us
    pallas_call x1, Pallas kernels, on_device(): call(second_kernel, 'second_iteration', [(1,) + block, (3 * peers, LANES)...  3.79 us
    ppermute x2, starting transfers between devices, exchange(): lax.ppermute(to_left, 'pitch', back)  3.7 us
  transfers between devices with their start and end apart: 9, of which 2 were waited for; matrix products, arithmetic and copies ran while one was open for 0% of the time, Pallas kernels for 3%

profile of v3, /device:TPU:32, one launch (start us, length us, event | category | flops | bytes accessed | tf_op | source)
XLA Modules:
  0.0 76.2 jit_solution(6166624311175746889)
XLA Ops:
  0.6 0.9 %copy-done.1 = f32[1,6,4,8,128]{4,3,2,1,0:T(8,128)S(1)} copy-done((f32[1,6,4,8,128]{4,3,2,1,0:T(8,128)S(1)}, f32[1,6,4,8,128]{4,3,2,1,0:T(8,128)}, u32[]{:S(2)}) %copy-start.1) | copy-done | bytes 98328
  1.5 0.1 edges.1
  1.6 3.4 %collective-permute-start = (f32[6,8,128]{2,1,0:T(8,128)S(1)}, f32[6,8,128]{2,1,0:T(8,128)S(1)}, u32[]{:S(2)}, u32[]{:S(2)}) collective-permute-start(f32[6,8,128]{2,1,0:T(8,128)S(1)} %get-tuple-element.23), channel_id=1, source_target_pairs={{0,4},{4,8},{8,12},{12,16},{16,20},{20,24},{24,28},{28,32},{32,36}... | collective-permute-start | bytes 73736 | tf_op jit(solution)/shard_map/ppermute | solution.py:386
  5.0 6.7 %collective-permute-start.1 = (f32[6,8,128]{2,1,0:T(8,128)S(1)}, f32[6,8,128]{2,1,0:T(8,128)S(1)}, u32[]{:S(2)}, u32[]{:S(2)}) collective-permute-start(f32[6,8,128]{2,1,0:T(8,128)S(1)} %get-tuple-element.24), channel_id=1, source_target_pairs={{4,0},{8,4},{12,8},{16,12},{20,16},{24,20},{28,24},{32,28},{36,32}... | collective-permute-start | bytes 73736 | tf_op jit(solution)/shard_map/ppermute | solution.py:387
  11.7 3.3 %collective-permute-start.2 = (f32[6,4,128]{2,1,0:T(4,128)S(1)}, f32[6,4,128]{2,1,0:T(4,128)S(1)}, u32[]{:S(2)}, u32[]{:S(2)}) collective-permute-start(f32[6,4,128]{2,1,0:T(4,128)S(1)} %get-tuple-element.25), channel_id=1, source_target_pairs={{0,1},{1,2},{2,3},{3,0},{4,5},{5,6},{6,7},{7,4},{8,9},{9,10},{10,1... | collective-permute-start | bytes 36872 | tf_op jit(solution)/shard_map/ppermute | solution.py:388
  15.0 2.2 %collective-permute-start.3 = (f32[6,4,128]{2,1,0:T(4,128)S(1)}, f32[6,4,128]{2,1,0:T(4,128)S(1)}, u32[]{:S(2)}, u32[]{:S(2)}) collective-permute-start(f32[6,4,128]{2,1,0:T(4,128)S(1)} %get-tuple-element.26), channel_id=1, source_target_pairs={{1,0},{2,1},{3,2},{0,3},{5,4},{6,5},{7,6},{4,7},{9,8},{10,9},{11,1... | collective-permute-start | bytes 36872 | tf_op jit(solution)/shard_map/ppermute | solution.py:389
  17.2 1.6 %copy-done = bf16[1,7,6,6,4,8,128]{6,5,4,3,2,1,0:T(8,128)(2,1)S(1)} copy-done((bf16[1,7,6,6,4,8,128]{6,5,4,3,2,1,0:T(8,128)(2,1)S(1)}, bf16[1,7,6,6,4,8,128]{6,5,4,3,2,1,0:T(8,128)(2,1)}, u32[]{:S(2)}) %copy-start) | copy-done | bytes 2064408
  18.8 0.9 %copy-done.2 = f32[1,6,4,8,128]{4,3,2,1,0:T(8,128)S(1)} copy-done((f32[1,6,4,8,128]{4,3,2,1,0:T(8,128)S(1)}, f32[1,6,4,8,128]{4,3,2,1,0:T(8,128)}, u32[]{:S(2)}) %copy-start.2) | copy-done | bytes 98328
  19.7 0.7 copy-done.3
  20.4 2.2 %interior.1 = (f32[6,4,8,128]{3,2,1,0:T(8,128)S(1)}, f32[4,8,128]{2,1,0:T(8,128)S(1)}, bf16[7,6,6,4,8,128]{5,4,3,2,1,0:T(8,128)(2,1)S(1)}, f32[6,4,8,128]{3,2,1,0:T(8,128)S(1)}, f32[4,8,128]{2,1,0:T(8,128)S(1)}) custom-call(f32[1,6,4,8,128]{4,3,2,1,0:T(8,128)S(1)} %copy-done.1, f32[1,6,4,8,128]{4,3,2,1,0:T(8,128)S(1)} %copy-done.2, ...), custom_call_target="tpu_custom_call" | custom-call | flops 9000000 | bytes 3000000 | tf_op jit(solution)/shard_map/interior/pallas_call | solution.py:410
  22.7 0.0 collective-permute-done.3.right_ref
  22.7 0.0 collective-permute-done.up_ref
  22.7 1.5 %edge_update.1 = (f32[6,4,8,128]{3,2,1,0:T(8,128)S(1)}, f32[512,128]{1,0:T(8,128)}, f32[7,8,128]{2,1,0:T(8,128)S(1)}, f32[7,8,128]{2,1,0:T(8,128)S(1)}, f32[7,4,...) custom-call(f32[6,4,8,128]{3,2,1,0:T(8,128)S(1)} %get-tuple-element.19.part_ref, f32[4,8,128]{2,1,0:T(8,128)S(1)} %get-tuple-element.20.rec_in, ...), custom_call_target="tpu_custom_call" | custom-call | tf_op jit(solution)/shard_map/edge_update/pallas_call | solution.py:425
  24.2 8.8 %all-to-all-start = ((f32[256,1,256]{2,1,0:T(1,128)}), f32[256,1,256]{2,1,0:T(1,128)S(1)}, u32[]{:S(2)}, u32[]{:S(2)}) async-start(f32[256,1,256]{2,1,0:T(1,128)} %bitcast), calls=%async_computation | async-start | bytes 524288 | tf_op jit(solution)/shard_map/all_to_all | solution.py:435
  33.0 3.4 %collective-permute-start.4 = (f32[7,8,128]{2,1,0:T(8,128)S(1)}, f32[7,8,128]{2,1,0:T(8,128)S(1)}, u32[]{:S(2)}, u32[]{:S(2)}) collective-permute-start(f32[7,8,128]{2,1,0:T(8,128)S(1)} %get-tuple-element.30), channel_id=1, source_target_pairs={{0,4},{4,8},{8,12},{12,16},{16,20},{20,24},{24,28},{28,32},{32,36}... | collective-permute-start | bytes 86024 | tf_op jit(solution)/shard_map/ppermute | solution.py:386
  36.4 6.7 %collective-permute-start.5 = (f32[7,8,128]{2,1,0:T(8,128)S(1)}, f32[7,8,128]{2,1,0:T(8,128)S(1)}, u32[]{:S(2)}, u32[]{:S(2)}) collective-permute-start(f32[7,8,128]{2,1,0:T(8,128)S(1)} %get-tuple-element.31), channel_id=1, source_target_pairs={{4,0},{8,4},{12,8},{16,12},{20,16},{24,20},{28,24},{32,28},{36,32}... | collective-permute-start | bytes 86024 | tf_op jit(solution)/shard_map/ppermute | solution.py:387
  43.1 3.0 %collective-permute-start.6 = (f32[7,4,128]{2,1,0:T(4,128)S(1)}, f32[7,4,128]{2,1,0:T(4,128)S(1)}, u32[]{:S(2)}, u32[]{:S(2)}) collective-permute-start(f32[7,4,128]{2,1,0:T(4,128)S(1)} %get-tuple-element.32), channel_id=1, source_target_pairs={{0,1},{1,2},{2,3},{3,0},{4,5},{5,6},{6,7},{7,4},{8,9},{9,10},{10,1... | collective-permute-start | bytes 43016 | tf_op jit(solution)/shard_map/ppermute | solution.py:388
  46.0 1.5 %collective-permute-start.7 = (f32[7,4,128]{2,1,0:T(4,128)S(1)}, f32[7,4,128]{2,1,0:T(4,128)S(1)}, u32[]{:S(2)}, u32[]{:S(2)}) collective-permute-start(f32[7,4,128]{2,1,0:T(4,128)S(1)} %get-tuple-element.33), channel_id=1, source_target_pairs={{1,0},{2,1},{3,2},{0,3},{5,4},{6,5},{7,6},{4,7},{9,8},{10,9},{11,1... | collective-permute-start | bytes 43016 | tf_op jit(solution)/shard_map/ppermute | solution.py:389
  47.5 1.6 %collective-permute-done.6.left_ref = f32[7,4,128]{2,1,0:T(4,128)S(1)} collective-permute-done((f32[7,4,128]{2,1,0:T(4,128)S(1)}, f32[7,4,128]{2,1,0:T(4,128)S(1)}, u32[]{:S(2)}, u32[]{:S(2)}) %collective-permute-start.6) | collective-permute-done | bytes 14368 | tf_op jit(solution)/shard_map/ppermute | solution.py:388
  49.1 1.8 %collective-permute-done.7.right_ref = f32[7,4,128]{2,1,0:T(4,128)S(1)} collective-permute-done((f32[7,4,128]{2,1,0:T(4,128)S(1)}, f32[7,4,128]{2,1,0:T(4,128)S(1)}, u32[]{:S(2)}, u32[]{:S(2)}) %collective-permute-start.7) | collective-permute-done | bytes 14368 | tf_op jit(solution)/shard_map/ppermute | solution.py:389
  50.9 0.0 collective-permute-done.4.up_ref
  51.0 3.8 %second_iteration.1 = (f32[1,6,4,8,128]{4,3,2,1,0:T(8,128)}, f32[384,128]{1,0:T(8,128)S(1)}) custom-call(s32[2,128]{1,0:T(2,128)S(1)} %copy-done.4, f32[6,4,8,128]{3,2,1,0:T(8,128)S(1)} %get-tuple-element.27.f1_ref, f32[6,4,8,128]{3,2,1,0:T(8,128)S(1)} %get-tuple-element.28.src_ref, f32[4,8,128]{2,1,0:T(8,128)S(1)} %get-tuple-element.22.tau_ref, ...), custom_call_target="tpu_custom_call" | custom-call | tf_op jit(solution)/shard_map/second_iteration/pallas_call | solution.py:439
  54.8 20.8 %all_to_all.10 = f32[128,1,384]{2,1,0:T(1,128)S(1)} all-to-all(f32[128,1,384]{2,1,0:T(1,128)S(1)} %bitcast.7), channel_id=1, replica_groups=mesh['row'=2,'span'=32,'pitch'=4] {'span','pitch'}, dimensions={0} | all-to-all | bytes 393216 | tf_op jit(solution)/shard_map/all_to_all | solution.py:454
  75.6 0.6 node_sums.1
  (17 shorter events, 0.0 us)
Async XLA Ops:
  0.6 0.9 %copy-start.1 = (f32[1,6,4,8,128]{4,3,2,1,0:T(8,128)S(1)}, f32[1,6,4,8,128]{4,3,2,1,0:T(8,128)}, u32[]{:S(2)}) copy-start(f32[1,6,4,8,128]{4,3,2,1,0:T(8,128)} %adj_ref.1) | copy-start | bytes 294916
  1.6 21.1 %collective-permute-start = (f32[6,8,128]{2,1,0:T(8,128)S(1)}, f32[6,8,128]{2,1,0:T(8,128)S(1)}, u32[]{:S(2)}, u32[]{:S(2)}) collective-permute-start(f32[6,8,128]{2,1,0:T(8,128)S(1)} %get-tuple-element.23), channel_id=1, source_target_pairs={{0,4},{4,8},{8,12},{12,16},{16,20},{20,24},{24,28},{28,32},{32,36}... | collective-permute-start | bytes 73736 | tf_op jit(solution)/shard_map/ppermute | solution.py:386
  5.0 17.7 %collective-permute-start.1 = (f32[6,8,128]{2,1,0:T(8,128)S(1)}, f32[6,8,128]{2,1,0:T(8,128)S(1)}, u32[]{:S(2)}, u32[]{:S(2)}) collective-permute-start(f32[6,8,128]{2,1,0:T(8,128)S(1)} %get-tuple-element.24), channel_id=1, source_target_pairs={{4,0},{8,4},{12,8},{16,12},{20,16},{24,20},{28,24},{32,28},{36,32}... | collective-permute-start | bytes 73736 | tf_op jit(solution)/shard_map/ppermute | solution.py:387
  11.7 11.0 %collective-permute-start.2 = (f32[6,4,128]{2,1,0:T(4,128)S(1)}, f32[6,4,128]{2,1,0:T(4,128)S(1)}, u32[]{:S(2)}, u32[]{:S(2)}) collective-permute-start(f32[6,4,128]{2,1,0:T(4,128)S(1)} %get-tuple-element.25), channel_id=1, source_target_pairs={{0,1},{1,2},{2,3},{3,0},{4,5},{5,6},{6,7},{7,4},{8,9},{9,10},{10,1... | collective-permute-start | bytes 36872 | tf_op jit(solution)/shard_map/ppermute | solution.py:388
  15.0 7.7 %collective-permute-start.3 = (f32[6,4,128]{2,1,0:T(4,128)S(1)}, f32[6,4,128]{2,1,0:T(4,128)S(1)}, u32[]{:S(2)}, u32[]{:S(2)}) collective-permute-start(f32[6,4,128]{2,1,0:T(4,128)S(1)} %get-tuple-element.26), channel_id=1, source_target_pairs={{1,0},{2,1},{3,2},{0,3},{5,4},{6,5},{7,6},{4,7},{9,8},{10,9},{11,1... | collective-permute-start | bytes 36872 | tf_op jit(solution)/shard_map/ppermute | solution.py:389
  17.2 1.6 %copy-start = (bf16[1,7,6,6,4,8,128]{6,5,4,3,2,1,0:T(8,128)(2,1)S(1)}, bf16[1,7,6,6,4,8,128]{6,5,4,3,2,1,0:T(8,128)(2,1)}, u32[]{:S(2)}) copy-start(bf16[1,7,6,6,4,8,128]{6,5,4,3,2,1,0:T(8,128)(2,1)} %jac_hbm.1) | copy-start | bytes 6193156
  18.8 0.9 %copy-start.2 = (f32[1,6,4,8,128]{4,3,2,1,0:T(8,128)S(1)}, f32[1,6,4,8,128]{4,3,2,1,0:T(8,128)}, u32[]{:S(2)}) copy-start(f32[1,6,4,8,128]{4,3,2,1,0:T(8,128)} %src_hbm.1) | copy-start | bytes 294916
  19.7 0.7 copy-start.3
  20.4 27.1 %copy-start.7 = (f32[1,1,1,18,128]{4,2,3,1,0:T(1,128)S(1)}, f32[1,1,1,18,128]{4,2,3,1,0:T(1,128)}, u32[]{:S(2)}) copy-start(f32[1,1,1,18,128]{4,2,3,1,0:T(1,128)} %param.15) | copy-start | bytes 27652
  20.4 30.5 %copy-start.4 = (s32[2,128]{1,0:T(2,128)S(1)}, s32[2,128]{1,0:T(2,128)}, u32[]{:S(2)}) copy-start(s32[2,128]{1,0:T(2,128)} %bands_ref.1) | copy-start | bytes 3076
  20.4 30.5 %copy-start.5 = (s32[1,1,1,128]{3,2,1,0:T(1,128)S(1)}, s32[1,1,1,128]{3,2,1,0:T(1,128)}, u32[]{:S(2)}) copy-start(s32[1,1,1,128]{3,2,1,0:T(1,128)} %cell_ref.1) | copy-start | bytes 1540
  20.4 30.5 %copy-start.6 = (s32[1,1,1,128]{3,2,1,0:T(1,128)S(1)}, s32[1,1,1,128]{3,2,1,0:T(1,128)}, u32[]{:S(2)}) copy-start(s32[1,1,1,128]{3,2,1,0:T(1,128)} %owner_ref.1) | copy-start | bytes 1540
  24.2 26.8 %all-to-all-start = ((f32[256,1,256]{2,1,0:T(1,128)}), f32[256,1,256]{2,1,0:T(1,128)S(1)}, u32[]{:S(2)}, u32[]{:S(2)}) async-start(f32[256,1,256]{2,1,0:T(1,128)} %bitcast), calls=%async_computation | async-start | bytes 524288 | tf_op jit(solution)/shard_map/all_to_all | solution.py:435
  33.0 18.0 %collective-permute-start.4 = (f32[7,8,128]{2,1,0:T(8,128)S(1)}, f32[7,8,128]{2,1,0:T(8,128)S(1)}, u32[]{:S(2)}, u32[]{:S(2)}) collective-permute-start(f32[7,8,128]{2,1,0:T(8,128)S(1)} %get-tuple-element.30), channel_id=1, source_target_pairs={{0,4},{4,8},{8,12},{12,16},{16,20},{20,24},{24,28},{28,32},{32,36}... | collective-permute-start | bytes 86024 | tf_op jit(solution)/shard_map/ppermute | solution.py:386
  36.4 14.6 %collective-permute-start.5 = (f32[7,8,128]{2,1,0:T(8,128)S(1)}, f32[7,8,128]{2,1,0:T(8,128)S(1)}, u32[]{:S(2)}, u32[]{:S(2)}) collective-permute-start(f32[7,8,128]{2,1,0:T(8,128)S(1)} %get-tuple-element.31), channel_id=1, source_target_pairs={{4,0},{8,4},{12,8},{16,12},{20,16},{24,20},{28,24},{32,28},{36,32}... | collective-permute-start | bytes 86024 | tf_op jit(solution)/shard_map/ppermute | solution.py:387
  43.1 6.1 %collective-permute-start.6 = (f32[7,4,128]{2,1,0:T(4,128)S(1)}, f32[7,4,128]{2,1,0:T(4,128)S(1)}, u32[]{:S(2)}, u32[]{:S(2)}) collective-permute-start(f32[7,4,128]{2,1,0:T(4,128)S(1)} %get-tuple-element.32), channel_id=1, source_target_pairs={{0,1},{1,2},{2,3},{3,0},{4,5},{5,6},{6,7},{7,4},{8,9},{9,10},{10,1... | collective-permute-start | bytes 43016 | tf_op jit(solution)/shard_map/ppermute | solution.py:388
  46.0 4.9 %collective-permute-start.7 = (f32[7,4,128]{2,1,0:T(4,128)S(1)}, f32[7,4,128]{2,1,0:T(4,128)S(1)}, u32[]{:S(2)}, u32[]{:S(2)}) collective-permute-start(f32[7,4,128]{2,1,0:T(4,128)S(1)} %get-tuple-element.33), channel_id=1, source_target_pairs={{1,0},{2,1},{3,2},{0,3},{5,4},{6,5},{7,6},{4,7},{9,8},{10,9},{11,1... | collective-permute-start | bytes 43016 | tf_op jit(solution)/shard_map/ppermute | solution.py:389

commit v4 on v3

--- a/solution.py
+++ b/solution.py
@@ -143,11 +143,20 @@
         rec_ref[j] = sums[j] + weights[j] * tau_out
 
 
+def inner_sides():
+    span = lax.axis_index("span")
+    return (
+        jnp.where(span > 0, 1.0, 0.0).astype(F32),
+        jnp.where(span < lax.axis_size("span") - 1, 1.0, 0.0).astype(F32),
+    )
+
+
 def edge_kernel(
     part_ref, rec_in, jac_ref, tau_ref, up_ref, down_ref, left_ref, right_ref,
     f1_ref, msg_ref, to_up_ref, to_down_ref, to_left_ref, to_right_ref, sides, rec,
 ):
     row = lax.axis_index("row")
+    keep = inner_sides()
     tile = (CP, LANES)
     lane, sub = lane_ids(tile), row_ids(tile)
     for d in range(NVAR):
@@ -173,9 +182,9 @@
         for j in range(CS):
             lost = acc[j]
             if j == 0:
-                lost = lost + first
+                lost = lost + first * keep[0]
             if j == CS - 1:
-                lost = lost + last
+                lost = lost + last * keep[1]
             new = part_ref[c, j] - tau_ref[j] * lost
             f1_ref[c, j] = new
             sums[j] = jnp.where(lane == at, pltpu.roll(new, at + 1 - row, 1), sums[j])
@@ -283,11 +292,12 @@
         return carry
 
     lax.fori_loop(0, NVAR, correct, 0)
+    keep = inner_sides()
     for n, (ref, at) in enumerate(((up_ref, 0), (down_ref, CS + 1))):
         moved = weight_sum(ref[NVAR] * spread0[at : at + 1])
         for c in range(NVAR):
             part = jnp.broadcast_to(moved[:, WEIGHT_AT + c : WEIGHT_AT + c + 1], tile)
-            edge[n, c] = ref[c] - jnp.where(at_outlet, part, 0.0)
+            edge[n, c] = (ref[c] - jnp.where(at_outlet, part, 0.0)) * keep[n]
     low = (CS, LANES)
     low_outlet = lane_ids(low) == outlet
     for n, ref in enumerate((left_ref, right_ref)):
@@ -362,6 +372,10 @@
 HBM = pl.BlockSpec(memory_space=pltpu.HBM)
 
 
+def in_hbm(x):
+    return pltpu.with_memory_space_constraint(x, pltpu.HBM)
+
+
 def call(kernel, name, outs, in_specs, scratch=(), cost=None):
     outs = [out if isinstance(out[0], tuple) else (out, F32) for out in outs]
     return pl.pallas_call(
@@ -378,8 +392,8 @@
 
 def exchange(to_up, to_down, to_left, to_right):
     spans, pitches = lax.axis_size("span"), lax.axis_size("pitch")
-    rising = [(i, i + 1) for i in range(spans - 1)]
-    falling = [(i + 1, i) for i in range(spans - 1)]
+    rising = [(i, (i + 1) % spans) for i in range(spans)]
+    falling = [((i + 1) % spans, i) for i in range(spans)]
     onward = [(i, (i + 1) % pitches) for i in range(pitches)]
     back = [((i + 1) % pitches, i) for i in range(pitches)]
     return (
@@ -405,7 +419,7 @@
         [edge, edge, side, side],
         in_specs=[HBM],
         scratch=[pltpu.SemaphoreType.DMA((4,))],
-    )(adjoint)
+    )(in_hbm(adjoint))
     halo = exchange(*edges)
     part, record, jac, src, tau = call(
         interior_kernel,
@@ -419,7 +433,7 @@
             pltpu.SemaphoreType.DMA((10,)),
         ],
         cost=pl.CostEstimate(flops=9_000_000, bytes_accessed=3_000_000, transcendentals=0),
-    )(adjoint, source, pseudo_step, jac_blocks)
+    )(*(in_hbm(x) for x in (adjoint, source, pseudo_step, jac_blocks)))
     edge = (NVAR + 1, CP, LANES)
     side = (NVAR + 1, CS, LANES)
     first, message, *sends = call(

time: 76.6 us -> 66 us (0.86)
  starting transfers between devices: 39 us -> 30.9 us
  local copies, waits for them, and re-layouts: 4.09 us -> 0.02 us
  waiting for transfers between devices: 3.44 us -> 5.38 us
  blocking collectives: 20.8 us -> 19.7 us
  Pallas kernels: 8.11 us -> 9.05 us
    unnamed x17 -> x9, local copies, waits for them, and re-layouts: 4.09 us -> 0.02 us
    ppermute x2, starting transfers between devices: 13.3 us -> 9.52 us  [exchange(): lax.ppermute(to_up, 'span', falling)]
    ppermute x2, starting transfers between devices: 6.79 us -> 3.13 us  [exchange(): lax.ppermute(to_down, 'span', rising)]
    all_to_all x1, waiting for transfers between devices: 0.01 us -> 1.17 us  [on_device(): lax.all_to_all(message.reshape(devices, 1, 2 * LANES), ('row', 'span', 'p...]
    all_to_all x1, blocking collectives: 20.8 us -> 19.7 us  [on_device(): lax.all_to_all(dense.reshape(peers, 1, 3 * LANES), ('span', 'pitch'), 0, 0)]
  transfers between devices with their start and end apart: 9 -> 9, of which waited for: 2 -> 4; matrix products, arithmetic and copies ran while one was open for 0% -> 0% of each run, Pallas kernels for 3% -> 4%
where the time goes in v4:
time: 66 us; the launch traced here: 65.7 us
  starting transfers between devices  30.9 us (47%)
  blocking collectives  19.7 us (30%)
  Pallas kernels  9.05 us (14%)
  waiting for transfers between devices  5.38 us (8%)
  between operations  0.68 us (1%)
    all_to_all x1, blocking collectives, on_device(): lax.all_to_all(dense.reshape(peers, 1, 3 * LANES), ('span', 'pitch'), 0, 0)  19.7 us
    ppermute x2, starting transfers between devices, exchange(): lax.ppermute(to_up, 'span', falling)  9.52 us
    all_to_all x1, starting transfers between devices, on_device(): lax.all_to_all(message.reshape(devices, 1, 2 * LANES), ('row', 'span', 'p...  8.46 us
    ppermute x2, starting transfers between devices, exchange(): lax.ppermute(to_right, 'pitch', onward)  6.17 us
    pallas_call x1, Pallas kernels, on_device(): call(second_kernel, 'second_iteration', [(1,) + block, (3 * peers, LANES)...  3.79 us
    ppermute x2, starting transfers between devices, exchange(): lax.ppermute(to_left, 'pitch', back)  3.61 us
    ppermute x2, starting transfers between devices, exchange(): lax.ppermute(to_down, 'span', rising)  3.13 us
    ppermute x2, waiting for transfers between devices, exchange(): lax.ppermute(to_left, 'pitch', back)  2.52 us
  transfers between devices with their start and end apart: 9, of which 4 were waited for; matrix products, arithmetic and copies ran while one was open for 0% of the time, Pallas kernels for 4%

profile of v4, /device:TPU:32, one launch (start us, length us, event | category | flops | bytes accessed | tf_op | source)
XLA Modules:
  0.0 65.7 jit_solution(16665022924384865496)
XLA Ops:
  0.6 0.8 %edges.1 = (f32[6,8,128]{2,1,0:T(8,128)S(1)}, f32[6,8,128]{2,1,0:T(8,128)S(1)}, f32[6,4,128]{2,1,0:T(4,128)S(1)}, f32[6,4,128]{2,1,0:T(4,128)S(1)}) custom-call(f32[1,6,4,8,128]{4,3,2,1,0:T(8,128)} %adj_ref.1), custom_call_target="tpu_custom_call" | custom-call | tf_op jit(solution)/shard_map/edges/pallas_call | solution.py:416
  1.5 1.6 %collective-permute-start = (f32[6,8,128]{2,1,0:T(8,128)S(1)}, f32[6,8,128]{2,1,0:T(8,128)S(1)}, u32[]{:S(2)}, u32[]{:S(2)}) collective-permute-start(f32[6,8,128]{2,1,0:T(8,128)S(1)} %get-tuple-element.23), channel_id=1, source_target_pairs={{0,4},{4,8},{8,12},{12,16},{16,20},{20,24},{24,28},{28,32},{32,36}... | collective-permute-start | bytes 73736 | tf_op jit(solution)/shard_map/ppermute | solution.py:400
  3.0 4.8 %collective-permute-start.1 = (f32[6,8,128]{2,1,0:T(8,128)S(1)}, f32[6,8,128]{2,1,0:T(8,128)S(1)}, u32[]{:S(2)}, u32[]{:S(2)}) collective-permute-start(f32[6,8,128]{2,1,0:T(8,128)S(1)} %get-tuple-element.24), channel_id=1, source_target_pairs={{4,0},{8,4},{12,8},{16,12},{20,16},{24,20},{28,24},{32,28},{36,32}... | collective-permute-start | bytes 73736 | tf_op jit(solution)/shard_map/ppermute | solution.py:401
  7.8 3.3 %collective-permute-start.2 = (f32[6,4,128]{2,1,0:T(4,128)S(1)}, f32[6,4,128]{2,1,0:T(4,128)S(1)}, u32[]{:S(2)}, u32[]{:S(2)}) collective-permute-start(f32[6,4,128]{2,1,0:T(4,128)S(1)} %get-tuple-element.25), channel_id=1, source_target_pairs={{0,1},{1,2},{2,3},{3,0},{4,5},{5,6},{6,7},{7,4},{8,9},{9,10},{10,1... | collective-permute-start | bytes 36872 | tf_op jit(solution)/shard_map/ppermute | solution.py:402
  11.1 2.2 %collective-permute-start.3 = (f32[6,4,128]{2,1,0:T(4,128)S(1)}, f32[6,4,128]{2,1,0:T(4,128)S(1)}, u32[]{:S(2)}, u32[]{:S(2)}) collective-permute-start(f32[6,4,128]{2,1,0:T(4,128)S(1)} %get-tuple-element.26), channel_id=1, source_target_pairs={{1,0},{2,1},{3,2},{0,3},{5,4},{6,5},{7,6},{4,7},{9,8},{10,9},{11,1... | collective-permute-start | bytes 36872 | tf_op jit(solution)/shard_map/ppermute | solution.py:403
  13.3 2.4 %interior.1 = (f32[6,4,8,128]{3,2,1,0:T(8,128)S(1)}, f32[4,8,128]{2,1,0:T(8,128)S(1)}, bf16[7,6,6,4,8,128]{5,4,3,2,1,0:T(8,128)(2,1)S(1)}, f32[6,4,8,128]{3,2,1,0:T(8,128)S(1)}, f32[4,8,128]{2,1,0:T(8,128)S(1)}) custom-call(f32[1,6,4,8,128]{4,3,2,1,0:T(8,128)} %adj_ref.1, f32[1,6,4,8,128]{4,3,2,1,0:T(8,128)} %src_hbm.1, f32[1,4,8,128]{3,2,1,0:T(8,128)} %tau_hbm.1, ...), custom_call_target="tpu_custom_call" | custom-call | flops 9000000 | bytes 3000000 | tf_op jit(solution)/shard_map/interior/pallas_call | solution.py:424
  15.7 0.0 collective-permute-done.2.left_ref
  15.7 0.7 %collective-permute-done.3.right_ref = f32[6,4,128]{2,1,0:T(4,128)S(1)} collective-permute-done((f32[6,4,128]{2,1,0:T(4,128)S(1)}, f32[6,4,128]{2,1,0:T(4,128)S(1)}, u32[]{:S(2)}, u32[]{:S(2)}) %collective-permute-start.3) | collective-permute-done | bytes 12320 | tf_op jit(solution)/shard_map/ppermute | solution.py:403
  16.4 0.0 collective-permute-done.up_ref
  16.4 0.0 collective-permute-done.1.down_ref
  16.4 1.4 %edge_update.1 = (f32[6,4,8,128]{3,2,1,0:T(8,128)S(1)}, f32[512,128]{1,0:T(8,128)}, f32[7,8,128]{2,1,0:T(8,128)S(1)}, f32[7,8,128]{2,1,0:T(8,128)S(1)}, f32[7,4,...) custom-call(f32[6,4,8,128]{3,2,1,0:T(8,128)S(1)} %get-tuple-element.19.part_ref, f32[4,8,128]{2,1,0:T(8,128)S(1)} %get-tuple-element.20.rec_in, ...), custom_call_target="tpu_custom_call" | custom-call | tf_op jit(solution)/shard_map/edge_update/pallas_call | solution.py:439
  17.9 8.5 %all-to-all-start = ((f32[256,1,256]{2,1,0:T(1,128)}), f32[256,1,256]{2,1,0:T(1,128)S(1)}, u32[]{:S(2)}, u32[]{:S(2)}) async-start(f32[256,1,256]{2,1,0:T(1,128)} %bitcast), calls=%async_computation | async-start | bytes 524288 | tf_op jit(solution)/shard_map/all_to_all | solution.py:449
  26.3 1.6 %collective-permute-start.4 = (f32[7,8,128]{2,1,0:T(8,128)S(1)}, f32[7,8,128]{2,1,0:T(8,128)S(1)}, u32[]{:S(2)}, u32[]{:S(2)}) collective-permute-start(f32[7,8,128]{2,1,0:T(8,128)S(1)} %get-tuple-element.30), channel_id=1, source_target_pairs={{0,4},{4,8},{8,12},{12,16},{16,20},{20,24},{24,28},{28,32},{32,36}... | collective-permute-start | bytes 86024 | tf_op jit(solution)/shard_map/ppermute | solution.py:400
  27.9 4.8 %collective-permute-start.5 = (f32[7,8,128]{2,1,0:T(8,128)S(1)}, f32[7,8,128]{2,1,0:T(8,128)S(1)}, u32[]{:S(2)}, u32[]{:S(2)}) collective-permute-start(f32[7,8,128]{2,1,0:T(8,128)S(1)} %get-tuple-element.31), channel_id=1, source_target_pairs={{4,0},{8,4},{12,8},{16,12},{20,16},{24,20},{28,24},{32,28},{36,32}... | collective-permute-start | bytes 86024 | tf_op jit(solution)/shard_map/ppermute | solution.py:401
  32.6 2.9 %collective-permute-start.6 = (f32[7,4,128]{2,1,0:T(4,128)S(1)}, f32[7,4,128]{2,1,0:T(4,128)S(1)}, u32[]{:S(2)}, u32[]{:S(2)}) collective-permute-start(f32[7,4,128]{2,1,0:T(4,128)S(1)} %get-tuple-element.32), channel_id=1, source_target_pairs={{0,1},{1,2},{2,3},{3,0},{4,5},{5,6},{6,7},{7,4},{8,9},{9,10},{10,1... | collective-permute-start | bytes 43016 | tf_op jit(solution)/shard_map/ppermute | solution.py:402
  35.5 1.4 %collective-permute-start.7 = (f32[7,4,128]{2,1,0:T(4,128)S(1)}, f32[7,4,128]{2,1,0:T(4,128)S(1)}, u32[]{:S(2)}, u32[]{:S(2)}) collective-permute-start(f32[7,4,128]{2,1,0:T(4,128)S(1)} %get-tuple-element.33), channel_id=1, source_target_pairs={{1,0},{2,1},{3,2},{0,3},{5,4},{6,5},{7,6},{4,7},{9,8},{10,9},{11,1... | collective-permute-start | bytes 43016 | tf_op jit(solution)/shard_map/ppermute | solution.py:403
  36.9 1.7 %collective-permute-done.6.left_ref = f32[7,4,128]{2,1,0:T(4,128)S(1)} collective-permute-done((f32[7,4,128]{2,1,0:T(4,128)S(1)}, f32[7,4,128]{2,1,0:T(4,128)S(1)}, u32[]{:S(2)}, u32[]{:S(2)}) %collective-permute-start.6) | collective-permute-done | bytes 14368 | tf_op jit(solution)/shard_map/ppermute | solution.py:402
  38.6 1.8 %collective-permute-done.7.right_ref = f32[7,4,128]{2,1,0:T(4,128)S(1)} collective-permute-done((f32[7,4,128]{2,1,0:T(4,128)S(1)}, f32[7,4,128]{2,1,0:T(4,128)S(1)}, u32[]{:S(2)}, u32[]{:S(2)}) %collective-permute-start.7) | collective-permute-done | bytes 14368 | tf_op jit(solution)/shard_map/ppermute | solution.py:403
  40.5 0.0 collective-permute-done.4.up_ref
  40.5 0.0 collective-permute-done.5.down_ref
  40.5 1.2 %all-to-all-done = f32[256,1,256]{2,1,0:T(1,128)S(1)} async-done(((f32[256,1,256]{2,1,0:T(1,128)}), f32[256,1,256]{2,1,0:T(1,128)S(1)}, u32[]{:S(2)}, u32[]{:S(2)}) %all-to-all-start) | async-done | bytes 262176 | tf_op jit(solution)/shard_map/all_to_all | solution.py:449
  41.6 3.8 %second_iteration.1 = (f32[1,6,4,8,128]{4,3,2,1,0:T(8,128)}, f32[384,128]{1,0:T(8,128)S(1)}) custom-call(s32[2,128]{1,0:T(2,128)S(1)} %copy-done, f32[6,4,8,128]{3,2,1,0:T(8,128)S(1)} %get-tuple-element.27.f1_ref, f32[6,4,8,128]{3,2,1,0:T(8,128)S(1)} %get-tuple-element.28.src_ref, f32[4,8,128]{2,1,0:T(8,128)S(1)} %get-tuple-element.22.tau_ref, ...), custom_call_target="tpu_custom_call" | custom-call | tf_op jit(solution)/shard_map/second_iteration/pallas_call | solution.py:453
  45.4 19.7 %all_to_all.10 = f32[128,1,384]{2,1,0:T(1,128)S(1)} all-to-all(f32[128,1,384]{2,1,0:T(1,128)S(1)} %bitcast.7), channel_id=1, replica_groups=mesh['row'=2,'span'=32,'pitch'=4] {'span','pitch'}, dimensions={0} | all-to-all | bytes 393216 | tf_op jit(solution)/shard_map/all_to_all | solution.py:468
  65.1 0.6 node_sums.1
  (9 shorter events, 0.0 us)
Async XLA Ops:
  1.5 14.9 %collective-permute-start = (f32[6,8,128]{2,1,0:T(8,128)S(1)}, f32[6,8,128]{2,1,0:T(8,128)S(1)}, u32[]{:S(2)}, u32[]{:S(2)}) collective-permute-start(f32[6,8,128]{2,1,0:T(8,128)S(1)} %get-tuple-element.23), channel_id=1, source_target_pairs={{0,4},{4,8},{8,12},{12,16},{16,20},{20,24},{24,28},{28,32},{32,36}... | collective-permute-start | bytes 73736 | tf_op jit(solution)/shard_map/ppermute | solution.py:400
  3.0 13.4 %collective-permute-start.1 = (f32[6,8,128]{2,1,0:T(8,128)S(1)}, f32[6,8,128]{2,1,0:T(8,128)S(1)}, u32[]{:S(2)}, u32[]{:S(2)}) collective-permute-start(f32[6,8,128]{2,1,0:T(8,128)S(1)} %get-tuple-element.24), channel_id=1, source_target_pairs={{4,0},{8,4},{12,8},{16,12},{20,16},{24,20},{28,24},{32,28},{36,32}... | collective-permute-start | bytes 73736 | tf_op jit(solution)/shard_map/ppermute | solution.py:401
  7.8 7.9 %collective-permute-start.2 = (f32[6,4,128]{2,1,0:T(4,128)S(1)}, f32[6,4,128]{2,1,0:T(4,128)S(1)}, u32[]{:S(2)}, u32[]{:S(2)}) collective-permute-start(f32[6,4,128]{2,1,0:T(4,128)S(1)} %get-tuple-element.25), channel_id=1, source_target_pairs={{0,1},{1,2},{2,3},{3,0},{4,5},{5,6},{6,7},{7,4},{8,9},{9,10},{10,1... | collective-permute-start | bytes 36872 | tf_op jit(solution)/shard_map/ppermute | solution.py:402
  11.1 25.9 %copy-start.3 = (f32[1,1,1,18,128]{4,2,3,1,0:T(1,128)S(1)}, f32[1,1,1,18,128]{4,2,3,1,0:T(1,128)}, u32[]{:S(2)}) copy-start(f32[1,1,1,18,128]{4,2,3,1,0:T(1,128)} %param.15) | copy-start | bytes 27652
  11.1 30.6 %copy-start = (s32[2,128]{1,0:T(2,128)S(1)}, s32[2,128]{1,0:T(2,128)}, u32[]{:S(2)}) copy-start(s32[2,128]{1,0:T(2,128)} %bands_ref.1) | copy-start | bytes 3076
  11.1 30.6 %copy-start.1 = (s32[1,1,1,128]{3,2,1,0:T(1,128)S(1)}, s32[1,1,1,128]{3,2,1,0:T(1,128)}, u32[]{:S(2)}) copy-start(s32[1,1,1,128]{3,2,1,0:T(1,128)} %cell_ref.1) | copy-start | bytes 1540
  11.1 30.6 %copy-start.2 = (s32[1,1,1,128]{3,2,1,0:T(1,128)S(1)}, s32[1,1,1,128]{3,2,1,0:T(1,128)}, u32[]{:S(2)}) copy-start(s32[1,1,1,128]{3,2,1,0:T(1,128)} %owner_ref.1) | copy-start | bytes 1540
  11.1 5.3 %collective-permute-start.3 = (f32[6,4,128]{2,1,0:T(4,128)S(1)}, f32[6,4,128]{2,1,0:T(4,128)S(1)}, u32[]{:S(2)}, u32[]{:S(2)}) collective-permute-start(f32[6,4,128]{2,1,0:T(4,128)S(1)} %get-tuple-element.26), channel_id=1, source_target_pairs={{1,0},{2,1},{3,2},{0,3},{5,4},{6,5},{7,6},{4,7},{9,8},{10,9},{11,1... | collective-permute-start | bytes 36872 | tf_op jit(solution)/shard_map/ppermute | solution.py:403
  17.9 23.8 %all-to-all-start = ((f32[256,1,256]{2,1,0:T(1,128)}), f32[256,1,256]{2,1,0:T(1,128)S(1)}, u32[]{:S(2)}, u32[]{:S(2)}) async-start(f32[256,1,256]{2,1,0:T(1,128)} %bitcast), calls=%async_computation | async-start | bytes 524288 | tf_op jit(solution)/shard_map/all_to_all | solution.py:449
  26.3 14.1 %collective-permute-start.4 = (f32[7,8,128]{2,1,0:T(8,128)S(1)}, f32[7,8,128]{2,1,0:T(8,128)S(1)}, u32[]{:S(2)}, u32[]{:S(2)}) collective-permute-start(f32[7,8,128]{2,1,0:T(8,128)S(1)} %get-tuple-element.30), channel_id=1, source_target_pairs={{0,4},{4,8},{8,12},{12,16},{16,20},{20,24},{24,28},{28,32},{32,36}... | collective-permute-start | bytes 86024 | tf_op jit(solution)/shard_map/ppermute | solution.py:400
  27.9 12.6 %collective-permute-start.5 = (f32[7,8,128]{2,1,0:T(8,128)S(1)}, f32[7,8,128]{2,1,0:T(8,128)S(1)}, u32[]{:S(2)}, u32[]{:S(2)}) collective-permute-start(f32[7,8,128]{2,1,0:T(8,128)S(1)} %get-tuple-element.31), channel_id=1, source_target_pairs={{4,0},{8,4},{12,8},{16,12},{20,16},{24,20},{28,24},{32,28},{36,32}... | collective-permute-start | bytes 86024 | tf_op jit(solution)/shard_map/ppermute | solution.py:401
  32.6 6.0 %collective-permute-start.6 = (f32[7,4,128]{2,1,0:T(4,128)S(1)}, f32[7,4,128]{2,1,0:T(4,128)S(1)}, u32[]{:S(2)}, u32[]{:S(2)}) collective-permute-start(f32[7,4,128]{2,1,0:T(4,128)S(1)} %get-tuple-element.32), channel_id=1, source_target_pairs={{0,1},{1,2},{2,3},{3,0},{4,5},{5,6},{6,7},{7,4},{8,9},{9,10},{10,1... | collective-permute-start | bytes 43016 | tf_op jit(solution)/shard_map/ppermute | solution.py:402
  35.5 4.9 %collective-permute-start.7 = (f32[7,4,128]{2,1,0:T(4,128)S(1)}, f32[7,4,128]{2,1,0:T(4,128)S(1)}, u32[]{:S(2)}, u32[]{:S(2)}) collective-permute-start(f32[7,4,128]{2,1,0:T(4,128)S(1)} %get-tuple-element.33), channel_id=1, source_target_pairs={{1,0},{2,1},{3,2},{0,3},{5,4},{6,5},{7,6},{4,7},{9,8},{10,9},{11,1... | collective-permute-start | bytes 43016 | tf_op jit(solution)/shard_map/ppermute | solution.py:403

commit v5 on v4

--- a/solution.py
+++ b/solution.py
@@ -14,6 +14,8 @@
 FIRST_AT = 8
 WEIGHT_AT = 16
 COUNT_AT = 6
+OWN_AT = 22
+OWN_COUNT_AT = 14
 
 
 def lane_ids(shape):
@@ -153,7 +155,7 @@
 
 def edge_kernel(
     part_ref, rec_in, jac_ref, tau_ref, up_ref, down_ref, left_ref, right_ref,
-    f1_ref, msg_ref, to_up_ref, to_down_ref, to_left_ref, to_right_ref, sides, rec,
+    f1_ref, swap_ref, own_ref, to_up_ref, to_down_ref, to_left_ref, to_right_ref, sides, rec,
 ):
     row = lax.axis_index("row")
     keep = inner_sides()
@@ -191,16 +193,20 @@
         return tuple(sums)
 
     sums = lax.fori_loop(0, NVAR, body, tuple(rec_in[j] for j in range(CS)))
-    rows = []
+    rows, own_rows = [], []
     for j in range(CS):
         rec[j] = sums[j]
         rows.append(jnp.sum(sums[j], axis=0, keepdims=True))
-    halves = [
-        jnp.broadcast_to(rows[2 * h] + pltpu.roll(rows[2 * h + 1], 64, 1), tile) for h in range(2)
-    ]
-    packed = jnp.where(sub % 2 == 0, halves[0], halves[1])
-    for i in range(msg_ref.shape[0] // CP):
-        msg_ref[CP * i : CP * (i + 1)] = packed
+        own = jnp.where(
+            lane[:1] == OWN_COUNT_AT, pltpu.roll(rows[j], OWN_COUNT_AT - COUNT_AT, 1), 0.0
+        )
+        for c in range(NVAR):
+            at = OWN_AT + 8 * c
+            own = jnp.where(lane[:1] == at, pltpu.roll(rows[j], at - c, 1), own)
+        own_rows.append(own)
+    for ref, lines in ((swap_ref, rows), (own_ref, own_rows)):
+        for h in range(2):
+            ref[h : h + 1] = lines[2 * h] + pltpu.roll(lines[2 * h + 1], 64, 1)
     to_up_ref[0:NVAR] = f1_ref[:, 0]
     to_up_ref[NVAR] = rec[0]
     to_down_ref[0:NVAR] = f1_ref[:, CS - 1]
@@ -218,13 +224,14 @@
     return x
 
 
-def spread(values):
+def spread(values, first, step):
     lane = lane_ids(values.shape)
     out = jnp.zeros(values.shape, F32)
     for d in range(NVAR):
+        at = first + step * d
         out = jnp.where(
             lane // 8 == d + WEIGHT_AT // 8,
-            jnp.broadcast_to(values[:, d : d + 1], values.shape),
+            jnp.broadcast_to(values[:, at : at + 1], values.shape),
             out,
         )
     return out
@@ -244,17 +251,15 @@
     wanted = [
         bands_ref[row, jnp.clip(span * CS - 1 + t, 0, last_cell)] for t in range(CS + 2)
     ]
-    half = all_ref.shape[0] // 2
+    lines = all_ref.shape[0]
     zero = jnp.zeros(tile, F32)
 
     second_half = lane >= LANES // 2
     odd = row_ids(tile) % 2 == 1
 
-    def gather_bands(of_row):
-        base = of_row * half
-
+    def gather_bands(of_row, count_at):
         def body(i, sums):
-            values = all_ref[pl.ds(pl.multiple_of(base + i * CP, CP), CP), :]
+            values = all_ref[pl.ds(pl.multiple_of(i * CP, CP), CP), :]
             cells = [bands_ref[of_row, i * CS + j] for j in range(CS)]
             ids = jnp.where(
                 odd,
@@ -265,18 +270,18 @@
                 total + jnp.where(ids == band, values, 0.0) for total, band in zip(sums, wanted)
             )
 
-        sums = lax.fori_loop(0, half // CP, body, (zero,) * (CS + 2), unroll=4)
+        sums = lax.fori_loop(0, lines // CP, body, (zero,) * (CS + 2), unroll=4)
         rows = [jnp.sum(x, axis=0, keepdims=True) for x in sums]
         rows = rows + [rows[-1]] * (CP - len(rows))
         folded = jnp.concatenate(rows, axis=0)
         folded = folded + pltpu.roll(folded, 64, 1)
-        return folded, jnp.broadcast_to(folded[:, COUNT_AT : COUNT_AT + 1], tile)
-
-    other, other_count = gather_bands(1 - row)
-    mine, my_count = gather_bands(row)
+        return folded, jnp.broadcast_to(folded[:, count_at : count_at + 1], tile)
+
+    other, other_count = gather_bands(1 - row, COUNT_AT)
+    mine, my_count = gather_bands(row, OWN_COUNT_AT)
     cycle0 = other / other_count
-    spread0 = spread(cycle0)
-    lost = weight_sum(other * spread(mine / my_count))
+    spread0 = spread(cycle0, 0, 1)
+    lost = weight_sum(other * spread(mine / my_count, OWN_AT, 8))
     cycle1 = (other - pltpu.roll(lost, LANES - (WEIGHT_AT - FIRST_AT), 1)) / other_count
     at_outlet = lane == outlet
 
@@ -408,7 +413,6 @@
     adjoint, source, pseudo_step, jac_blocks, band_map, face_cell, face_owner, face_weight
 ):
     rows, spans, pitches = (lax.axis_size(name) for name in ("row", "span", "pitch"))
-    devices = rows * spans * pitches
     peers = spans * pitches
     block = (NVAR, CS, CP, LANES)
     edge = (NVAR, CP, LANES)
@@ -436,19 +440,21 @@
     )(*(in_hbm(x) for x in (adjoint, source, pseudo_step, jac_blocks)))
     edge = (NVAR + 1, CP, LANES)
     side = (NVAR + 1, CS, LANES)
-    first, message, *sends = call(
+    first, swapped, own, *sends = call(
         edge_kernel,
         "edge_update",
-        [block, (2 * devices, LANES), edge, edge, side, side],
+        [block, (2, LANES), (2, LANES), edge, edge, side, side],
         in_specs=[VM] * 8,
         scratch=[
             pltpu.VMEM((2 * NVAR, CS, CP, LANES), F32),
             pltpu.VMEM((CS, CP, LANES), F32),
         ],
     )(part, record, jac, tau, *halo)
+    message = lax.ppermute(swapped, "row", [(i, rows - 1 - i) for i in range(rows)]) + own
     records = lax.all_to_all(
-        message.reshape(devices, 1, 2 * LANES), ("row", "span", "pitch"), 0, 0
-    ).reshape(2 * devices, LANES)
+        jnp.broadcast_to(message.reshape(1, 1, 2 * LANES), (peers, 1, 2 * LANES)),
+        ("span", "pitch"), 0, 0,
+    ).reshape(2 * peers, LANES)
     halo = exchange(*sends)
     field, dense = call(
         second_kernel,

time: 66 us -> 67.3 us (1.020)
  blocking collectives: 19.7 us -> 20.7 us
  starting transfers between devices: 30.9 us -> 31.7 us
  local copies, waits for them, and re-layouts: 0.02 us -> 0.76 us
  waiting for transfers between devices: 5.38 us -> 4.68 us
    all_to_all x1, waiting for transfers between devices: 1.17 us -> 0.01 us  [on_device(): lax.all_to_all(jnp.broadcast_to(message.reshape(1, 1, 2 * LANES), (peers,...]
    ppermute x0 -> x1, waiting for transfers between devices: none -> 1.13 us  [on_device(): lax.ppermute(swapped, 'row', [(i, rows - 1 - i) for i in range(rows)]) + own]
    all_to_all x1, blocking collectives: 19.7 us -> 20.7 us  [on_device(): lax.all_to_all(dense.reshape(peers, 1, 3 * LANES), ('span', 'pitch'), 0, 0)]
    all_to_all x1, starting transfers between devices: 8.46 us -> 9.39 us  [on_device(): lax.all_to_all(jnp.broadcast_to(message.reshape(1, 1, 2 * LANES), (peers,...]
    ppermute x2, waiting for transfers between devices: 2.52 us -> 1.7 us  [exchange(): lax.ppermute(to_left, 'pitch', back)]
    broadcast_in_dim x0 -> x1, local copies, waits for them, and re-layouts: none -> 0.74 us  [on_device(): jnp.broadcast_to(message.reshape(1, 1, 2 * LANES), (peers, 1, 2 * LANES))]
  transfers between devices with their start and end apart: 9 -> 10, of which waited for: 4 -> 4; matrix products, arithmetic and copies ran while one was open for 0% -> 0% of each run, Pallas kernels for 4% -> 4%
where the time goes in v5:
time: 67.3 us; the launch traced here: 67 us
  starting transfers between devices  31.7 us (47%)
  blocking collectives  20.7 us (31%)
  Pallas kernels  8.41 us (12%)
  waiting for transfers between devices  4.68 us (7%)
  local copies, waits for them, and re-layouts  0.76 us (1%)
  between operations  0.71 us (1%)
    all_to_all x1, blocking collectives, on_device(): lax.all_to_all(dense.reshape(peers, 1, 3 * LANES), ('span', 'pitch'), 0, 0)  20.7 us
    ppermute x2, starting transfers between devices, exchange(): lax.ppermute(to_up, 'span', falling)  9.51 us
    all_to_all x1, starting transfers between devices, on_device(): lax.all_to_all(jnp.broadcast_to(message.reshape(1, 1, 2 * LANES), (peers,...  9.39 us
    ppermute x2, starting transfers between devices, exchange(): lax.ppermute(to_right, 'pitch', onward)  5.64 us
    ppermute x2, starting transfers between devices, exchange(): lax.ppermute(to_left, 'pitch', back)  3.99 us
    pallas_call x1, Pallas kernels, on_device(): call(second_kernel, 'second_iteration', [(1,) + block, (3 * peers, LANES)...  3.78 us
    ppermute x2, starting transfers between devices, exchange(): lax.ppermute(to_down, 'span', rising)  3.14 us
    pallas_call x1, Pallas kernels, on_device(): call(interior_kernel, 'interior', [block, (CS, CP, LANES), ((7, NVAR) + b...  2.4 us
  transfers between devices with their start and end apart: 10, of which 4 were waited for; matrix products, arithmetic and copies ran while one was open for 0% of the time, Pallas kernels for 4%

profile of v5, /device:TPU:32, one launch (start us, length us, event | category | flops | bytes accessed | tf_op | source)
XLA Modules:
  0.0 67.0 jit_solution(660661716918576308)
XLA Ops:
  0.6 0.8 %edges.1 = (f32[6,8,128]{2,1,0:T(8,128)S(1)}, f32[6,8,128]{2,1,0:T(8,128)S(1)}, f32[6,4,128]{2,1,0:T(4,128)S(1)}, f32[6,4,128]{2,1,0:T(4,128)S(1)}) custom-call(f32[1,6,4,8,128]{4,3,2,1,0:T(8,128)} %adj_ref.1), custom_call_target="tpu_custom_call" | custom-call | tf_op jit(solution)/shard_map/edges/pallas_call | solution.py:420
  1.5 1.6 %collective-permute-start = (f32[6,8,128]{2,1,0:T(8,128)S(1)}, f32[6,8,128]{2,1,0:T(8,128)S(1)}, u32[]{:S(2)}, u32[]{:S(2)}) collective-permute-start(f32[6,8,128]{2,1,0:T(8,128)S(1)} %get-tuple-element.24), channel_id=1, source_target_pairs={{0,4},{4,8},{8,12},{12,16},{16,20},{20,24},{24,28},{28,32},{32,36}... | collective-permute-start | bytes 73736 | tf_op jit(solution)/shard_map/ppermute | solution.py:405
  3.0 4.8 %collective-permute-start.1 = (f32[6,8,128]{2,1,0:T(8,128)S(1)}, f32[6,8,128]{2,1,0:T(8,128)S(1)}, u32[]{:S(2)}, u32[]{:S(2)}) collective-permute-start(f32[6,8,128]{2,1,0:T(8,128)S(1)} %get-tuple-element.25), channel_id=1, source_target_pairs={{4,0},{8,4},{12,8},{16,12},{20,16},{24,20},{28,24},{32,28},{36,32}... | collective-permute-start | bytes 73736 | tf_op jit(solution)/shard_map/ppermute | solution.py:406
  7.8 3.3 %collective-permute-start.2 = (f32[6,4,128]{2,1,0:T(4,128)S(1)}, f32[6,4,128]{2,1,0:T(4,128)S(1)}, u32[]{:S(2)}, u32[]{:S(2)}) collective-permute-start(f32[6,4,128]{2,1,0:T(4,128)S(1)} %get-tuple-element.26), channel_id=1, source_target_pairs={{0,1},{1,2},{2,3},{3,0},{4,5},{5,6},{6,7},{7,4},{8,9},{9,10},{10,1... | collective-permute-start | bytes 36872 | tf_op jit(solution)/shard_map/ppermute | solution.py:407
  11.1 2.2 %collective-permute-start.3 = (f32[6,4,128]{2,1,0:T(4,128)S(1)}, f32[6,4,128]{2,1,0:T(4,128)S(1)}, u32[]{:S(2)}, u32[]{:S(2)}) collective-permute-start(f32[6,4,128]{2,1,0:T(4,128)S(1)} %get-tuple-element.27), channel_id=1, source_target_pairs={{1,0},{2,1},{3,2},{0,3},{5,4},{6,5},{7,6},{4,7},{9,8},{10,9},{11,1... | collective-permute-start | bytes 36872 | tf_op jit(solution)/shard_map/ppermute | solution.py:408
  13.3 2.4 %interior.1 = (f32[6,4,8,128]{3,2,1,0:T(8,128)S(1)}, f32[4,8,128]{2,1,0:T(8,128)S(1)}, bf16[7,6,6,4,8,128]{5,4,3,2,1,0:T(8,128)(2,1)S(1)}, f32[6,4,8,128]{3,2,1,0:T(8,128)S(1)}, f32[4,8,128]{2,1,0:T(8,128)S(1)}) custom-call(f32[1,6,4,8,128]{4,3,2,1,0:T(8,128)} %adj_ref.1, f32[1,6,4,8,128]{4,3,2,1,0:T(8,128)} %src_hbm.1, f32[1,4,8,128]{3,2,1,0:T(8,128)} %tau_hbm.1, ...), custom_call_target="tpu_custom_call" | custom-call | flops 9000000 | bytes 3000000 | tf_op jit(solution)/shard_map/interior/pallas_call | solution.py:428
  15.7 0.7 %collective-permute-done.3.right_ref = f32[6,4,128]{2,1,0:T(4,128)S(1)} collective-permute-done((f32[6,4,128]{2,1,0:T(4,128)S(1)}, f32[6,4,128]{2,1,0:T(4,128)S(1)}, u32[]{:S(2)}, u32[]{:S(2)}) %collective-permute-start.3) | collective-permute-done | bytes 12320 | tf_op jit(solution)/shard_map/ppermute | solution.py:408
  16.4 0.8 %edge_update.1 = (f32[6,4,8,128]{3,2,1,0:T(8,128)S(1)}, f32[2,128]{1,0:T(2,128)S(1)}, f32[2,128]{1,0:T(2,128)S(1)}, f32[7,8,128]{2,1,0:T(8,128)S(1)}, f32[7,8,12...) custom-call(f32[6,4,8,128]{3,2,1,0:T(8,128)S(1)} %get-tuple-element.20.part_ref, ...), custom_call_target="tpu_custom_call" | custom-call | tf_op jit(solution)/shard_map/edge_update/pallas_call | solution.py:443
  17.2 0.0 collective-permute-start.4
  17.3 1.1 %collective-permute-done.4 = f32[2,128]{1,0:T(2,128)S(1)} collective-permute-done((f32[2,128]{1,0:T(2,128)S(1)}, f32[2,128]{1,0:T(2,128)S(1)}, u32[]{:S(2)}, u32[]{:S(2)}) %collective-permute-start.4) | collective-permute-done | bytes 1056 | tf_op jit(solution)/shard_map/ppermute | solution.py:453
  18.4 0.7 %broadcast_in_dim.8 = f32[128,1,256]{2,1,0:T(1,128)} broadcast(f32[256]{0:T(256)S(1)} %add_bitcast_fusion), dimensions={2} | broadcast | bytes 132096 | tf_op jit(solution)/shard_map/broadcast_in_dim | solution.py:455
  19.1 9.4 %all-to-all-start = ((f32[128,1,256]{2,1,0:T(1,128)}), f32[128,1,256]{2,1,0:T(1,128)S(1)}, u32[]{:S(2)}, u32[]{:S(2)}) async-start(f32[128,1,256]{2,1,0:T(1,128)} %broadcast_in_dim.8), calls=%async_computation | async-start | bytes 262144 | tf_op jit(solution)/shard_map/all_to_all | solution.py:454
  28.5 1.6 %collective-permute-start.5 = (f32[7,8,128]{2,1,0:T(8,128)S(1)}, f32[7,8,128]{2,1,0:T(8,128)S(1)}, u32[]{:S(2)}, u32[]{:S(2)}) collective-permute-start(f32[7,8,128]{2,1,0:T(8,128)S(1)} %get-tuple-element.32), channel_id=1, source_target_pairs={{0,4},{4,8},{8,12},{12,16},{16,20},{20,24},{24,28},{28,32},{32,36}... | collective-permute-start | bytes 86024 | tf_op jit(solution)/shard_map/ppermute | solution.py:405
  30.1 4.8 %collective-permute-start.6 = (f32[7,8,128]{2,1,0:T(8,128)S(1)}, f32[7,8,128]{2,1,0:T(8,128)S(1)}, u32[]{:S(2)}, u32[]{:S(2)}) collective-permute-start(f32[7,8,128]{2,1,0:T(8,128)S(1)} %get-tuple-element.33), channel_id=1, source_target_pairs={{4,0},{8,4},{12,8},{16,12},{20,16},{24,20},{28,24},{32,28},{36,32}... | collective-permute-start | bytes 86024 | tf_op jit(solution)/shard_map/ppermute | solution.py:406
  34.9 2.4 %collective-permute-start.7 = (f32[7,4,128]{2,1,0:T(4,128)S(1)}, f32[7,4,128]{2,1,0:T(4,128)S(1)}, u32[]{:S(2)}, u32[]{:S(2)}) collective-permute-start(f32[7,4,128]{2,1,0:T(4,128)S(1)} %get-tuple-element.34), channel_id=1, source_target_pairs={{0,1},{1,2},{2,3},{3,0},{4,5},{5,6},{6,7},{7,4},{8,9},{9,10},{10,1... | collective-permute-start | bytes 43016 | tf_op jit(solution)/shard_map/ppermute | solution.py:407
  37.2 1.8 %collective-permute-start.8 = (f32[7,4,128]{2,1,0:T(4,128)S(1)}, f32[7,4,128]{2,1,0:T(4,128)S(1)}, u32[]{:S(2)}, u32[]{:S(2)}) collective-permute-start(f32[7,4,128]{2,1,0:T(4,128)S(1)} %get-tuple-element.35), channel_id=1, source_target_pairs={{1,0},{2,1},{3,2},{0,3},{5,4},{6,5},{7,6},{4,7},{9,8},{10,9},{11,1... | collective-permute-start | bytes 43016 | tf_op jit(solution)/shard_map/ppermute | solution.py:408
  39.0 1.8 %collective-permute-done.7.left_ref = f32[7,4,128]{2,1,0:T(4,128)S(1)} collective-permute-done((f32[7,4,128]{2,1,0:T(4,128)S(1)}, f32[7,4,128]{2,1,0:T(4,128)S(1)}, u32[]{:S(2)}, u32[]{:S(2)}) %collective-permute-start.7) | collective-permute-done | bytes 14368 | tf_op jit(solution)/shard_map/ppermute | solution.py:407
  40.9 1.0 %collective-permute-done.8.right_ref = f32[7,4,128]{2,1,0:T(4,128)S(1)} collective-permute-done((f32[7,4,128]{2,1,0:T(4,128)S(1)}, f32[7,4,128]{2,1,0:T(4,128)S(1)}, u32[]{:S(2)}, u32[]{:S(2)}) %collective-permute-start.8) | collective-permute-done | bytes 14368 | tf_op jit(solution)/shard_map/ppermute | solution.py:408
  41.9 0.0 collective-permute-done.5.up_ref
  41.9 0.0 collective-permute-done.6.down_ref
  41.9 0.0 all-to-all-done
  41.9 3.8 %second_iteration.1 = (f32[1,6,4,8,128]{4,3,2,1,0:T(8,128)}, f32[384,128]{1,0:T(8,128)S(1)}) custom-call(s32[2,128]{1,0:T(2,128)S(1)} %copy-done, f32[6,4,8,128]{3,2,1,0:T(8,128)S(1)} %get-tuple-element.28.f1_ref, f32[6,4,8,128]{3,2,1,0:T(8,128)S(1)} %get-tuple-element.29.src_ref, f32[4,8,128]{2,1,0:T(8,128)S(1)} %get-tuple-element.23.tau_ref, ...), custom_call_target="tpu_custom_call" | custom-call | tf_op jit(solution)/shard_map/second_iteration/pallas_call | solution.py:459
  45.7 20.7 %all_to_all.10 = f32[128,1,384]{2,1,0:T(1,128)S(1)} all-to-all(f32[128,1,384]{2,1,0:T(1,128)S(1)} %bitcast.8), channel_id=1, replica_groups=mesh['row'=2,'span'=32,'pitch'=4] {'span','pitch'}, dimensions={0} | all-to-all | bytes 393216 | tf_op jit(solution)/shard_map/all_to_all | solution.py:474
  66.4 0.6 node_sums.1
  (13 shorter events, 0.0 us)
Async XLA Ops:
  1.5 14.9 %collective-permute-start = (f32[6,8,128]{2,1,0:T(8,128)S(1)}, f32[6,8,128]{2,1,0:T(8,128)S(1)}, u32[]{:S(2)}, u32[]{:S(2)}) collective-permute-start(f32[6,8,128]{2,1,0:T(8,128)S(1)} %get-tuple-element.24), channel_id=1, source_target_pairs={{0,4},{4,8},{8,12},{12,16},{16,20},{20,24},{24,28},{28,32},{32,36}... | collective-permute-start | bytes 73736 | tf_op jit(solution)/shard_map/ppermute | solution.py:405
  3.0 13.4 %collective-permute-start.1 = (f32[6,8,128]{2,1,0:T(8,128)S(1)}, f32[6,8,128]{2,1,0:T(8,128)S(1)}, u32[]{:S(2)}, u32[]{:S(2)}) collective-permute-start(f32[6,8,128]{2,1,0:T(8,128)S(1)} %get-tuple-element.25), channel_id=1, source_target_pairs={{4,0},{8,4},{12,8},{16,12},{20,16},{24,20},{28,24},{32,28},{36,32}... | collective-permute-start | bytes 73736 | tf_op jit(solution)/shard_map/ppermute | solution.py:406
  7.8 7.9 %collective-permute-start.2 = (f32[6,4,128]{2,1,0:T(4,128)S(1)}, f32[6,4,128]{2,1,0:T(4,128)S(1)}, u32[]{:S(2)}, u32[]{:S(2)}) collective-permute-start(f32[6,4,128]{2,1,0:T(4,128)S(1)} %get-tuple-element.26), channel_id=1, source_target_pairs={{0,1},{1,2},{2,3},{3,0},{4,5},{5,6},{6,7},{7,4},{8,9},{9,10},{10,1... | collective-permute-start | bytes 36872 | tf_op jit(solution)/shard_map/ppermute | solution.py:407
  11.1 28.0 %copy-start.3 = (f32[1,1,1,18,128]{4,2,3,1,0:T(1,128)S(1)}, f32[1,1,1,18,128]{4,2,3,1,0:T(1,128)}, u32[]{:S(2)}) copy-start(f32[1,1,1,18,128]{4,2,3,1,0:T(1,128)} %param.15) | copy-start | bytes 27652
  11.1 30.8 %copy-start = (s32[2,128]{1,0:T(2,128)S(1)}, s32[2,128]{1,0:T(2,128)}, u32[]{:S(2)}) copy-start(s32[2,128]{1,0:T(2,128)} %bands_ref.1) | copy-start | bytes 3076
  11.1 30.8 %copy-start.1 = (s32[1,1,1,128]{3,2,1,0:T(1,128)S(1)}, s32[1,1,1,128]{3,2,1,0:T(1,128)}, u32[]{:S(2)}) copy-start(s32[1,1,1,128]{3,2,1,0:T(1,128)} %cell_ref.1) | copy-start | bytes 1540
  11.1 30.8 %copy-start.2 = (s32[1,1,1,128]{3,2,1,0:T(1,128)S(1)}, s32[1,1,1,128]{3,2,1,0:T(1,128)}, u32[]{:S(2)}) copy-start(s32[1,1,1,128]{3,2,1,0:T(1,128)} %owner_ref.1) | copy-start | bytes 1540
  11.1 5.3 %collective-permute-start.3 = (f32[6,4,128]{2,1,0:T(4,128)S(1)}, f32[6,4,128]{2,1,0:T(4,128)S(1)}, u32[]{:S(2)}, u32[]{:S(2)}) collective-permute-start(f32[6,4,128]{2,1,0:T(4,128)S(1)} %get-tuple-element.27), channel_id=1, source_target_pairs={{1,0},{2,1},{3,2},{0,3},{5,4},{6,5},{7,6},{4,7},{9,8},{10,9},{11,1... | collective-permute-start | bytes 36872 | tf_op jit(solution)/shard_map/ppermute | solution.py:408
  17.2 1.2 %collective-permute-start.4 = (f32[2,128]{1,0:T(2,128)S(1)}, f32[2,128]{1,0:T(2,128)S(1)}, u32[]{:S(2)}, u32[]{:S(2)}) collective-permute-start(f32[2,128]{1,0:T(2,128)S(1)} %get-tuple-element.30), channel_id=1, source_target_pairs={{0,128},{128,0},{1,129},{129,1},{2,130},{130,2},{3,131},{131,3},{4... | collective-permute-start | bytes 3080 | tf_op jit(solution)/shard_map/ppermute | solution.py:453
  19.1 22.7 %all-to-all-start = ((f32[128,1,256]{2,1,0:T(1,128)}), f32[128,1,256]{2,1,0:T(1,128)S(1)}, u32[]{:S(2)}, u32[]{:S(2)}) async-start(f32[128,1,256]{2,1,0:T(1,128)} %broadcast_in_dim.8), calls=%async_computation | async-start | bytes 262144 | tf_op jit(solution)/shard_map/all_to_all | solution.py:454
  28.5 13.3 %collective-permute-start.5 = (f32[7,8,128]{2,1,0:T(8,128)S(1)}, f32[7,8,128]{2,1,0:T(8,128)S(1)}, u32[]{:S(2)}, u32[]{:S(2)}) collective-permute-start(f32[7,8,128]{2,1,0:T(8,128)S(1)} %get-tuple-element.32), channel_id=1, source_target_pairs={{0,4},{4,8},{8,12},{12,16},{16,20},{20,24},{24,28},{28,32},{32,36}... | collective-permute-start | bytes 86024 | tf_op jit(solution)/shard_map/ppermute | solution.py:405
  30.1 11.7 %collective-permute-start.6 = (f32[7,8,128]{2,1,0:T(8,128)S(1)}, f32[7,8,128]{2,1,0:T(8,128)S(1)}, u32[]{:S(2)}, u32[]{:S(2)}) collective-permute-start(f32[7,8,128]{2,1,0:T(8,128)S(1)} %get-tuple-element.33), channel_id=1, source_target_pairs={{4,0},{8,4},{12,8},{16,12},{20,16},{24,20},{28,24},{32,28},{36,32}... | collective-permute-start | bytes 86024 | tf_op jit(solution)/shard_map/ppermute | solution.py:406
  34.9 6.0 %collective-permute-start.7 = (f32[7,4,128]{2,1,0:T(4,128)S(1)}, f32[7,4,128]{2,1,0:T(4,128)S(1)}, u32[]{:S(2)}, u32[]{:S(2)}) collective-permute-start(f32[7,4,128]{2,1,0:T(4,128)S(1)} %get-tuple-element.34), channel_id=1, source_target_pairs={{0,1},{1,2},{2,3},{3,0},{4,5},{5,6},{6,7},{7,4},{8,9},{9,10},{10,1... | collective-permute-start | bytes 43016 | tf_op jit(solution)/shard_map/ppermute | solution.py:407
  37.2 4.6 %collective-permute-start.8 = (f32[7,4,128]{2,1,0:T(4,128)S(1)}, f32[7,4,128]{2,1,0:T(4,128)S(1)}, u32[]{:S(2)}, u32[]{:S(2)}) collective-permute-start(f32[7,4,128]{2,1,0:T(4,128)S(1)} %get-tuple-element.35), channel_id=1, source_target_pairs={{1,0},{2,1},{3,2},{0,3},{5,4},{6,5},{7,6},{4,7},{9,8},{10,9},{11,1... | collective-permute-start | bytes 43016 | tf_op jit(solution)/shard_map/ppermute | solution.py:408

commit v6 on v4

--- a/solution.py
+++ b/solution.py
@@ -151,14 +151,9 @@
     )
 
 
-def edge_kernel(
-    part_ref, rec_in, jac_ref, tau_ref, up_ref, down_ref, left_ref, right_ref,
-    f1_ref, msg_ref, to_up_ref, to_down_ref, to_left_ref, to_right_ref, sides, rec,
-):
-    row = lax.axis_index("row")
-    keep = inner_sides()
-    tile = (CP, LANES)
-    lane, sub = lane_ids(tile), row_ids(tile)
+def fill_sides(sides, left_ref, right_ref):
+    tile = (CP, LANES)
+    sub = row_ids(tile)
     for d in range(NVAR):
         for j in range(CS):
             sides[d, j] = jnp.where(
@@ -168,24 +163,38 @@
                 sub == CP - 1, jnp.broadcast_to(right_ref[d, j : j + 1], tile), 0.0
             )
 
+
+def edge_terms(jac_ref, sides, up_ref, down_ref, keep, c):
+    acc = jnp.zeros((CS, CP, LANES), F32)
+    first = jnp.zeros((CP, LANES), F32)
+    last = jnp.zeros((CP, LANES), F32)
+    for d in range(NVAR):
+        acc = acc + jac_ref[3, c, d].astype(F32) * sides[d]
+        acc = acc + jac_ref[4, c, d].astype(F32) * sides[NVAR + d]
+        first = first + jac_ref[1, c, d, 0].astype(F32) * up_ref[d]
+        last = last + jac_ref[2, c, d, CS - 1].astype(F32) * down_ref[d]
+    lost = [acc[j] for j in range(CS)]
+    lost[0] = lost[0] + first * keep[0]
+    lost[CS - 1] = lost[CS - 1] + last * keep[1]
+    return lost
+
+
+def edge_kernel(
+    part_ref, rec_in, jac_ref, tau_ref, up_ref, down_ref, left_ref, right_ref,
+    f1_ref, msg_ref, rec, to_up_ref, to_down_ref, to_left_ref, to_right_ref, sides,
+):
+    row = lax.axis_index("row")
+    keep = inner_sides()
+    tile = (CP, LANES)
+    lane, sub = lane_ids(tile), row_ids(tile)
+    fill_sides(sides, left_ref, right_ref)
+
     def body(c, sums):
         sums = list(sums)
-        acc = jnp.zeros((CS, CP, LANES), F32)
-        first = jnp.zeros(tile, F32)
-        last = jnp.zeros(tile, F32)
-        for d in range(NVAR):
-            acc = acc + jac_ref[3, c, d].astype(F32) * sides[d]
-            acc = acc + jac_ref[4, c, d].astype(F32) * sides[NVAR + d]
-            first = first + jac_ref[1, c, d, 0].astype(F32) * up_ref[d]
-            last = last + jac_ref[2, c, d, CS - 1].astype(F32) * down_ref[d]
+        lost = edge_terms(jac_ref, sides, up_ref, down_ref, keep, c)
         at = FIRST_AT + c
         for j in range(CS):
-            lost = acc[j]
-            if j == 0:
-                lost = lost + first * keep[0]
-            if j == CS - 1:
-                lost = lost + last * keep[1]
-            new = part_ref[c, j] - tau_ref[j] * lost
+            new = part_ref[c, j] - tau_ref[j] * lost[j]
             f1_ref[c, j] = new
             sums[j] = jnp.where(lane == at, pltpu.roll(new, at + 1 - row, 1), sums[j])
         return tuple(sums)
@@ -218,28 +227,130 @@
     return x
 
 
-def spread(values):
+def spread(values, first):
     lane = lane_ids(values.shape)
     out = jnp.zeros(values.shape, F32)
     for d in range(NVAR):
+        at = first + d
         out = jnp.where(
             lane // 8 == d + WEIGHT_AT // 8,
-            jnp.broadcast_to(values[:, d : d + 1], values.shape),
+            jnp.broadcast_to(values[:, at : at + 1], values.shape),
             out,
         )
     return out
 
 
-def second_kernel(
-    bands_ref, f1_ref, src_ref, tau_ref, jac_ref, all_ref, up_ref, down_ref, left_ref, right_ref,
-    cell_ref, owner_ref, weight_ref, out_ref, dense_ref, vs, field, cycle, edge, side,
+def outlet_lanes(row):
+    return (1 - row) * (LANES - 1), (1 - row) * (LANES - 2) + row
+
+
+def settle_kernel(
+    bands_ref, f1_ref, src_ref, tau_ref, jac_ref, cell_ref, owner_ref,
+    part_ref, pack_ref, ids_ref, seen_ref, node_ref, vs,
+):
+    row = lax.axis_index("row")
+    outlet, inner = outlet_lanes(row)
+    ghost = 6 - row
+    tile = (CP, LANES)
+    zero = jnp.zeros(tile, F32)
+    lane = lane_ids(tile)
+    fill_stencil(
+        vs,
+        lambda d, j: f1_ref[d, j],
+        lambda d: zero,
+        lambda d: zero,
+        lambda d, j: zero,
+        lambda d, j: zero,
+        lambda d, j: zero,
+        lambda d, j: zero,
+    )
+    for n in range(6):
+        for j in range(CS):
+            pack_ref[n, j] = zero
+
+    def advance(c, carry):
+        part_ref[c] = f1_ref[c] + tau_ref[...] * (src_ref[c] - image_of(jac_ref, vs, c))
+        for n in range(6):
+            point = n if n < 5 else ghost
+            extra = 1 - row if n < 5 else 2 - 3 * row
+            for j in range(CS):
+                pack = pack_ref[n, j]
+                for d in range(NVAR):
+                    at = WEIGHT_AT + 8 * d + c
+                    moved = pltpu.roll(jac_ref[point, c, d, j].astype(F32), at + extra, 1)
+                    pack = jnp.where(lane == at, moved, pack)
+                pack_ref[n, j] = pack
+        return carry
+
+    lax.fori_loop(0, NVAR, advance, 0)
+    for j in range(CS):
+        steps = [
+            jnp.sum(jnp.where(lane == at, tau_ref[j], 0.0), axis=1, keepdims=True)
+            for at in (outlet, inner)
+        ]
+        for n in range(6):
+            pack_ref[n, j] = pack_ref[n, j] * steps[n // 5]
+    second_half = lane >= LANES // 2
+    odd = row_ids(tile) % 2 == 1
+    spans = bands_ref.shape[1] // CS
+
+    def label(i, carry):
+        of_row = i // spans
+        cells = [bands_ref[of_row, (i % spans) * CS + j] for j in range(CS)]
+        ids_ref[pl.ds(pl.multiple_of(i * CP, CP), CP), :] = jnp.where(
+            odd,
+            jnp.where(second_half, cells[3], cells[2]),
+            jnp.where(second_half, cells[1], cells[0]),
+        )
+        return carry
+
+    lax.fori_loop(0, 2 * spans, label, 0)
+    cells = cell_ref[0, 0]
+    for j in range(CS):
+        here = row_ids(tile) + CP * j == cells // LANES
+        for n, at in enumerate((outlet, inner)):
+            seen_ref[n, j] = jnp.where(here & (cells % LANES == at), 1.0, 0.0).astype(F32)
+    square = (LANES, LANES)
+    picked = (row_ids(square) == owner_ref[0, 0] % LANES).astype(F32).astype(BF16)
+    for n in range(3):
+        node_ref[:, LANES * n : LANES * (n + 1)] = picked
+
+
+def settle_edges_kernel(
+    part_ref, jac_ref, tau_ref, up_ref, down_ref, left_ref, right_ref, cell_ref,
+    part2_ref, face_ref, sides,
+):
+    keep = inner_sides()
+    tile = (CP, LANES)
+    fill_sides(sides, left_ref, right_ref)
+
+    def body(c, carry):
+        lost = edge_terms(jac_ref, sides, up_ref, down_ref, keep, c)
+        for j in range(CS):
+            part2_ref[c, j] = part_ref[c, j] - tau_ref[j] * lost[j]
+        return carry
+
+    lax.fori_loop(0, NVAR, body, 0)
+    cells = cell_ref[0, 0]
+    square = (LANES, LANES)
+    axial_pick = (row_ids(square) == cells % LANES).astype(F32).astype(BF16)
+    picked = dot3(part2_ref[...].reshape(NVAR * CS * CP, LANES), axial_pick, ((1,), (0,)))
+    here = row_ids((CS * CP, LANES)) == cells // LANES
+    for c in range(NVAR):
+        block = picked[c * CS * CP : (c + 1) * CS * CP]
+        face_ref[c : c + 1] = jnp.sum(jnp.where(here, block, 0.0), axis=0, keepdims=True)
+
+
+def cycle_kernel(
+    bands_ref, part_ref, rec_ref, pack_ref, ids_ref, all_ref, up_ref, down_ref, left_ref, right_ref,
+    seen_ref, node_ref, face_ref, owner_ref, weight_ref, out_ref, dense_ref,
 ):
     row = lax.axis_index("row")
     span = lax.axis_index("span")
-    outlet = (1 - row) * (LANES - 1)
-    ghost = 6 - row
-    tile = (CP, LANES)
-    lane = lane_ids(tile)
+    outlet, inner = outlet_lanes(row)
+    keep = inner_sides()
+    tile = (CP, LANES)
+    lane, sub = lane_ids(tile), row_ids(tile)
     last_cell = bands_ref.shape[1] - 1
     wanted = [
         bands_ref[row, jnp.clip(span * CS - 1 + t, 0, last_cell)] for t in range(CS + 2)
@@ -247,114 +358,84 @@
     half = all_ref.shape[0] // 2
     zero = jnp.zeros(tile, F32)
 
-    second_half = lane >= LANES // 2
-    odd = row_ids(tile) % 2 == 1
-
-    def gather_bands(of_row):
-        base = of_row * half
-
-        def body(i, sums):
-            values = all_ref[pl.ds(pl.multiple_of(base + i * CP, CP), CP), :]
-            cells = [bands_ref[of_row, i * CS + j] for j in range(CS)]
-            ids = jnp.where(
-                odd,
-                jnp.where(second_half, cells[3], cells[2]),
-                jnp.where(second_half, cells[1], cells[0]),
-            )
-            return tuple(
-                total + jnp.where(ids == band, values, 0.0) for total, band in zip(sums, wanted)
-            )
-
-        sums = lax.fori_loop(0, half // CP, body, (zero,) * (CS + 2), unroll=4)
-        rows = [jnp.sum(x, axis=0, keepdims=True) for x in sums]
-        rows = rows + [rows[-1]] * (CP - len(rows))
-        folded = jnp.concatenate(rows, axis=0)
-        folded = folded + pltpu.roll(folded, 64, 1)
-        return folded, jnp.broadcast_to(folded[:, COUNT_AT : COUNT_AT + 1], tile)
-
-    other, other_count = gather_bands(1 - row)
-    mine, my_count = gather_bands(row)
-    cycle0 = other / other_count
-    spread0 = spread(cycle0)
-    lost = weight_sum(other * spread(mine / my_count))
+    def body(i, sums):
+        sums = list(sums)
+        for n, of_row in enumerate((1 - row, row)):
+            at = pl.multiple_of(of_row * half + i * CP, CP)
+            ids, values = ids_ref[pl.ds(at, CP), :], all_ref[pl.ds(at, CP), :]
+            for t, band in enumerate(wanted):
+                k = (CS + 2) * n + t
+                sums[k] = sums[k] + jnp.where(ids == band, values, 0.0)
+        return tuple(sums)
+
+    sums = lax.fori_loop(0, half // CP, body, (zero,) * (2 * CS + 4), unroll=2)
+
+    def folded(parts):
+        rows = [jnp.sum(x, axis=0, keepdims=True) for x in parts]
+        whole = jnp.concatenate(rows + [rows[-1]] * (CP - len(rows)), axis=0)
+        whole = whole + pltpu.roll(whole, 64, 1)
+        return whole, jnp.broadcast_to(whole[:, COUNT_AT : COUNT_AT + 1], tile)
+
+    other, other_count = folded(sums[: CS + 2])
+    mine, my_count = folded(sums[CS + 2 :])
+    spread0 = spread(other / other_count, 0)
+    lost = weight_sum(other * spread(mine / my_count, 0))
     cycle1 = (other - pltpu.roll(lost, LANES - (WEIGHT_AT - FIRST_AT), 1)) / other_count
-    at_outlet = lane == outlet
-
+    spread1 = spread(cycle1, FIRST_AT)
+
+    def shift_of(record, values):
+        moved = weight_sum(record * values)
+        return moved, spread(moved, WEIGHT_AT)
+
+    own = [shift_of(rec_ref[j], spread0[j + 1 : j + 2]) for j in range(CS)]
+    above = shift_of(up_ref[NVAR], spread0[:1])[1] * keep[0]
+    below = shift_of(down_ref[NVAR], spread0[CS + 1 : CS + 2])[1] * keep[1]
+    left = shift_of(left_ref[NVAR], spread0[1 : 1 + CS])[1]
+    right = shift_of(right_ref[NVAR], spread0[1 : 1 + CS])[1]
+    changes = []
     for j in range(CS):
-        for d in range(NVAR):
-            cycle[d, j] = jnp.broadcast_to(cycle0[j + 1 : j + 2, d : d + 1], tile)
-
-    def correct(c, carry):
-        acc = jnp.zeros((CS, CP, LANES), F32)
-        for d in range(NVAR):
-            acc = acc + jac_ref[ghost, c, d].astype(F32) * cycle[d]
-        field[c] = f1_ref[c] - jnp.where(at_outlet[None], tau_ref[...] * acc, 0.0)
-        return carry
-
-    lax.fori_loop(0, NVAR, correct, 0)
-    keep = inner_sides()
-    for n, (ref, at) in enumerate(((up_ref, 0), (down_ref, CS + 1))):
-        moved = weight_sum(ref[NVAR] * spread0[at : at + 1])
-        for c in range(NVAR):
-            part = jnp.broadcast_to(moved[:, WEIGHT_AT + c : WEIGHT_AT + c + 1], tile)
-            edge[n, c] = (ref[c] - jnp.where(at_outlet, part, 0.0)) * keep[n]
-    low = (CS, LANES)
-    low_outlet = lane_ids(low) == outlet
-    for n, ref in enumerate((left_ref, right_ref)):
-        moved = weight_sum(ref[NVAR] * spread0[1 : 1 + CS])
-        for c in range(NVAR):
-            part = jnp.broadcast_to(moved[:, WEIGHT_AT + c : WEIGHT_AT + c + 1], low)
-            side[n, c] = ref[c] - jnp.where(low_outlet, part, 0.0)
-    is_upper = jnp.where(row == 0, 1.0, 0.0).astype(F32)
-
-    def cycled(d, j):
-        at = FIRST_AT + d
-        return jnp.broadcast_to(cycle1[j + 1 : j + 2, at : at + 1], tile)
-
-    fill_stencil(
-        vs,
-        lambda d, j: field[d, j],
-        lambda d: edge[0, d],
-        lambda d: edge[1, d],
-        lambda d, j: side[0, d, j : j + 1],
-        lambda d, j: side[1, d, j : j + 1],
-        lambda d, j: cycled(d, j) * (1.0 - is_upper),
-        lambda d, j: cycled(d, j) * is_upper,
-    )
-
-    def advance(c, carry):
-        new = field[c] + tau_ref[...] * (src_ref[c] - image_of(jac_ref, vs, c))
-        out_ref[0, c] = new
-        return carry
-
-    lax.fori_loop(0, NVAR, advance, 0)
-
-    cells = cell_ref[0, 0]
-    square = (LANES, LANES)
-    axial_pick = (row_ids(square) == cells % LANES).astype(F32).astype(BF16)
-    flat = out_ref[0].reshape(NVAR * CS * CP, LANES)
-    picked = dot3(flat, axial_pick, ((1,), (0,)))
-    here = row_ids((CS * CP, LANES)) == cells // LANES
+        x = own[j][1]
+        total = pack_ref[0, j] * x - rec_ref[j] * spread1[j + 1 : j + 2]
+        total = total + pack_ref[1, j] * (own[j - 1][1] if j > 0 else above)
+        total = total + pack_ref[2, j] * (own[j + 1][1] if j < CS - 1 else below)
+        total = total + pack_ref[3, j] * jnp.where(
+            sub == 0, jnp.broadcast_to(left[j : j + 1], tile), pltpu.roll(x, 1, 0)
+        )
+        total = total + pack_ref[4, j] * jnp.where(
+            sub == CP - 1, jnp.broadcast_to(right[j : j + 1], tile), pltpu.roll(x, CP - 1, 0)
+        )
+        changes.append((weight_sum(total) - own[j][0], weight_sum(pack_ref[5, j] * x)))
     terms = [jnp.zeros((1, LANES), F32)] * 3
     for c in range(NVAR):
-        block = picked[c * CS * CP : (c + 1) * CS * CP]
-        value = jnp.sum(jnp.where(here, block, 0.0), axis=0, keepdims=True)
+        at = WEIGHT_AT + c
+        seen = zero
+        for j in range(CS):
+            first, second = (jnp.broadcast_to(x[:, at : at + 1], tile) for x in changes[j])
+            moved = jnp.where(lane == outlet, first, jnp.where(lane == inner, second, 0.0))
+            out_ref[0, c, j] = part_ref[c, j] + moved
+            seen = seen + (seen_ref[0, j] * first + seen_ref[1, j] * second)
+        value = face_ref[c : c + 1] + jnp.sum(seen, axis=0, keepdims=True)
         for k in range(3):
             at = NVAR * k + c
             terms[k] = terms[k] + weight_ref[0, 0, 0, at : at + 1] * value
-    owners = owner_ref[0, 0]
     shape = dense_ref.shape
     line = row_ids(shape)
     device = (line * 43691) >> 17
-    coord = line - 3 * device
-    value = jnp.where(
-        coord == 0,
-        jnp.broadcast_to(terms[0], shape),
-        jnp.where(coord == 1, jnp.broadcast_to(terms[1], shape), jnp.broadcast_to(terms[2], shape)),
-    )
-    placed = jnp.where(device == owners // LANES, value, 0.0)
-    node_pick = (row_ids(square) == owners % LANES).astype(F32).astype(BF16)
-    dense_ref[...] = dot3(placed, node_pick, ((1,), (1,)))
+    here = device == owner_ref[0, 0] // LANES
+    cycle_rows = (24, LANES)
+    coord = row_ids(cycle_rows) % 3
+    pieces = []
+    for parts in zip(*(split3(x) for x in terms)):
+        wide = [jnp.broadcast_to(x.astype(F32), cycle_rows) for x in parts]
+        pattern = jnp.where(coord == 0, wide[0], jnp.where(coord == 1, wide[1], wide[2]))
+        pattern = jnp.concatenate([pattern] * (shape[0] // 24), axis=0)
+        pieces.append(jnp.where(here, pattern, 0.0).astype(BF16))
+    dense_ref[...] = lax.dot_general(
+        jnp.concatenate(pieces, axis=1),
+        node_ref[...],
+        (((1,), (1,)), ((), ())),
+        preferred_element_type=F32,
+    )
 
 
 def third_kernel(parts_ref, out_ref):
@@ -436,34 +517,44 @@
     )(*(in_hbm(x) for x in (adjoint, source, pseudo_step, jac_blocks)))
     edge = (NVAR + 1, CP, LANES)
     side = (NVAR + 1, CS, LANES)
-    first, message, *sends = call(
+    first, message, full_record, *sends = call(
         edge_kernel,
         "edge_update",
-        [block, (2 * devices, LANES), edge, edge, side, side],
+        [block, (2 * devices, LANES), (CS, CP, LANES), edge, edge, side, side],
         in_specs=[VM] * 8,
-        scratch=[
-            pltpu.VMEM((2 * NVAR, CS, CP, LANES), F32),
-            pltpu.VMEM((CS, CP, LANES), F32),
-        ],
+        scratch=[pltpu.VMEM((2 * NVAR, CS, CP, LANES), F32)],
     )(part, record, jac, tau, *halo)
     records = lax.all_to_all(
         message.reshape(devices, 1, 2 * LANES), ("row", "span", "pitch"), 0, 0
     ).reshape(2 * devices, LANES)
     halo = exchange(*sends)
+    part, packs, ids, seen, picks = call(
+        settle_kernel,
+        "settle",
+        [
+            block, (6, CS, CP, LANES), ((2 * devices, LANES), jnp.int32), (2, CS, CP, LANES),
+            ((LANES, 3 * LANES), BF16),
+        ],
+        in_specs=[SM] + [VM] * 6,
+        scratch=[pltpu.VMEM((7 * NVAR, CS, CP, LANES), F32)],
+        cost=pl.CostEstimate(flops=9_000_000, bytes_accessed=3_000_000, transcendentals=0),
+    )(band_map, first, src, tau, jac, face_cell, face_owner)
+    part, faces = call(
+        settle_edges_kernel,
+        "settle_edges",
+        [block, (CP, LANES)],
+        in_specs=[VM] * 8,
+        scratch=[pltpu.VMEM((2 * NVAR, CS, CP, LANES), F32)],
+        cost=pl.CostEstimate(flops=3_000_000, bytes_accessed=2_000_000, transcendentals=0),
+    )(part, jac, tau, *halo, face_cell)
     field, dense = call(
-        second_kernel,
-        "second_iteration",
+        cycle_kernel,
+        "cycle_update",
         [(1,) + block, (3 * peers, LANES)],
-        in_specs=[SM] + [VM] * 12,
-        scratch=[
-            pltpu.VMEM((7 * NVAR, CS, CP, LANES), F32),
-            pltpu.VMEM(block, F32),
-            pltpu.VMEM(block, F32),
-            pltpu.VMEM((2, NVAR, CP, LANES), F32),
-            pltpu.VMEM((2, NVAR, CS, LANES), F32),
-        ],
+        in_specs=[SM] + [VM] * 14,
     )(
-        band_map, first, src, tau, jac, records, *halo, face_cell, face_owner, face_weight,
+        band_map, part, full_record, packs, ids, records, *halo, seen, picks, faces, face_owner,
+        face_weight,
     )
     parts = lax.all_to_all(dense.reshape(peers, 1, 3 * LANES), ("span", "pitch"), 0, 0)
     (nodes,) = call(third_kernel, "node_sums", [(3, 1, LANES)], in_specs=[VM])(

time: 66 us -> 66 us (level)
  waiting for transfers between devices: 5.38 us -> 1.63 us
  Pallas kernels: 9.05 us -> 11.5 us
  blocking collectives: 19.7 us -> 21 us
    pallas_call x2 -> x4, Pallas kernels: 5.24 us -> 7.68 us  [the longest x1 3.28 us: on_device(): call(settle_kernel, 'settle', [block, (6, CS, CP, LANES), ((2 * devices,...]
    ppermute x2, waiting for transfers between devices: 1.69 us -> 0.01 us  [exchange(): lax.ppermute(to_right, 'pitch', onward)]
    ppermute x2, waiting for transfers between devices: 2.52 us -> 0.88 us  [exchange(): lax.ppermute(to_left, 'pitch', back)]
    all_to_all x1, blocking collectives: 19.7 us -> 21 us  [on_device(): lax.all_to_all(dense.reshape(peers, 1, 3 * LANES), ('span', 'pitch'), 0, 0)]
  transfers between devices with their start and end apart: 9 -> 9, of which waited for: 4 -> 3; matrix products, arithmetic and copies ran while one was open for 0% -> 0% of each run, Pallas kernels for 4% -> 9%
where the time goes in v6:
time: 66 us; the launch traced here: 65.7 us
  starting transfers between devices  30.9 us (47%)
  blocking collectives  21 us (32%)
  Pallas kernels  11.5 us (17%)
  waiting for transfers between devices  1.63 us (2%)
  between operations  0.71 us (1%)
    all_to_all x1, blocking collectives, on_device(): lax.all_to_all(dense.reshape(peers, 1, 3 * LANES), ('span', 'pitch'), 0, 0)  21 us
    ppermute x2, starting transfers between devices, exchange(): lax.ppermute(to_up, 'span', falling)  9.52 us
    all_to_all x1, starting transfers between devices, on_device(): lax.all_to_all(message.reshape(devices, 1, 2 * LANES), ('row', 'span', 'p...  8.46 us
    ppermute x2, starting transfers between devices, exchange(): lax.ppermute(to_right, 'pitch', onward)  6.17 us
    ppermute x2, starting transfers between devices, exchange(): lax.ppermute(to_left, 'pitch', back)  3.61 us
    pallas_call x1, Pallas kernels, on_device(): call(settle_kernel, 'settle', [block, (6, CS, CP, LANES), ((2 * devices,...  3.28 us
    ppermute x2, starting transfers between devices, exchange(): lax.ppermute(to_down, 'span', rising)  3.13 us
    pallas_call x1, Pallas kernels, on_device(): call(cycle_kernel, 'cycle_update', [(1,) + block, (3 * peers, LANES)], in...  2.53 us
  transfers between devices with their start and end apart: 9, of which 3 were waited for; matrix products, arithmetic and copies ran while one was open for 0% of the time, Pallas kernels for 9%

profile of v6, /device:TPU:32, one launch (start us, length us, event | category | flops | bytes accessed | tf_op | source)
XLA Modules:
  0.0 65.7 jit_solution(1540832843715115960)
XLA Ops:
  0.6 0.8 %edges.1 = (f32[6,8,128]{2,1,0:T(8,128)S(1)}, f32[6,8,128]{2,1,0:T(8,128)S(1)}, f32[6,4,128]{2,1,0:T(4,128)S(1)}, f32[6,4,128]{2,1,0:T(4,128)S(1)}) custom-call(f32[1,6,4,8,128]{4,3,2,1,0:T(8,128)} %adj_ref.1), custom_call_target="tpu_custom_call" | custom-call | tf_op jit(solution)/shard_map/edges/pallas_call | solution.py:497
  1.5 1.6 %collective-permute-start = (f32[6,8,128]{2,1,0:T(8,128)S(1)}, f32[6,8,128]{2,1,0:T(8,128)S(1)}, u32[]{:S(2)}, u32[]{:S(2)}) collective-permute-start(f32[6,8,128]{2,1,0:T(8,128)S(1)} %get-tuple-element.31), channel_id=1, source_target_pairs={{0,4},{4,8},{8,12},{12,16},{16,20},{20,24},{24,28},{28,32},{32,36}... | collective-permute-start | bytes 73736 | tf_op jit(solution)/shard_map/ppermute | solution.py:481
  3.0 4.8 %collective-permute-start.1 = (f32[6,8,128]{2,1,0:T(8,128)S(1)}, f32[6,8,128]{2,1,0:T(8,128)S(1)}, u32[]{:S(2)}, u32[]{:S(2)}) collective-permute-start(f32[6,8,128]{2,1,0:T(8,128)S(1)} %get-tuple-element.32), channel_id=1, source_target_pairs={{4,0},{8,4},{12,8},{16,12},{20,16},{24,20},{28,24},{32,28},{36,32}... | collective-permute-start | bytes 73736 | tf_op jit(solution)/shard_map/ppermute | solution.py:482
  7.8 3.3 %collective-permute-start.2 = (f32[6,4,128]{2,1,0:T(4,128)S(1)}, f32[6,4,128]{2,1,0:T(4,128)S(1)}, u32[]{:S(2)}, u32[]{:S(2)}) collective-permute-start(f32[6,4,128]{2,1,0:T(4,128)S(1)} %get-tuple-element.33), channel_id=1, source_target_pairs={{0,1},{1,2},{2,3},{3,0},{4,5},{5,6},{6,7},{7,4},{8,9},{9,10},{10,1... | collective-permute-start | bytes 36872 | tf_op jit(solution)/shard_map/ppermute | solution.py:483
  11.1 2.2 %collective-permute-start.3 = (f32[6,4,128]{2,1,0:T(4,128)S(1)}, f32[6,4,128]{2,1,0:T(4,128)S(1)}, u32[]{:S(2)}, u32[]{:S(2)}) collective-permute-start(f32[6,4,128]{2,1,0:T(4,128)S(1)} %get-tuple-element.34), channel_id=1, source_target_pairs={{1,0},{2,1},{3,2},{0,3},{5,4},{6,5},{7,6},{4,7},{9,8},{10,9},{11,1... | collective-permute-start | bytes 36872 | tf_op jit(solution)/shard_map/ppermute | solution.py:484
  13.3 2.4 %interior.1 = (f32[6,4,8,128]{3,2,1,0:T(8,128)S(1)}, f32[4,8,128]{2,1,0:T(8,128)S(1)}, bf16[7,6,6,4,8,128]{5,4,3,2,1,0:T(8,128)(2,1)S(1)}, f32[6,4,8,128]{3,2,1,0:T(8,128)S(1)}, f32[4,8,128]{2,1,0:T(8,128)S(1)}) custom-call(f32[1,6,4,8,128]{4,3,2,1,0:T(8,128)} %adj_ref.1, f32[1,6,4,8,128]{4,3,2,1,0:T(8,128)} %src_hbm.1, f32[1,4,8,128]{3,2,1,0:T(8,128)} %tau_hbm.1, ...), custom_call_target="tpu_custom_call" | custom-call | flops 9000000 | bytes 3000000 | tf_op jit(solution)/shard_map/interior/pallas_call | solution.py:505
  15.7 0.0 collective-permute-done.2.left_ref
  15.7 0.7 %collective-permute-done.3.right_ref = f32[6,4,128]{2,1,0:T(4,128)S(1)} collective-permute-done((f32[6,4,128]{2,1,0:T(4,128)S(1)}, f32[6,4,128]{2,1,0:T(4,128)S(1)}, u32[]{:S(2)}, u32[]{:S(2)}) %collective-permute-start.3) | collective-permute-done | bytes 12320 | tf_op jit(solution)/shard_map/ppermute | solution.py:484
  16.4 0.0 collective-permute-done.up_ref
  16.4 1.4 %edge_update.1 = (f32[6,4,8,128]{3,2,1,0:T(8,128)S(1)}, f32[512,128]{1,0:T(8,128)}, f32[4,8,128]{2,1,0:T(8,128)S(1)}, f32[7,8,128]{2,1,0:T(8,128)S(1)}, f32[7,8,...) custom-call(f32[6,4,8,128]{3,2,1,0:T(8,128)S(1)} %get-tuple-element.27.part_ref, ...), custom_call_target="tpu_custom_call" | custom-call | tf_op jit(solution)/shard_map/edge_update/pallas_call | solution.py:520
  17.9 8.5 %all-to-all-start = ((f32[256,1,256]{2,1,0:T(1,128)}), f32[256,1,256]{2,1,0:T(1,128)S(1)}, u32[]{:S(2)}, u32[]{:S(2)}) async-start(f32[256,1,256]{2,1,0:T(1,128)} %bitcast), calls=%async_computation | async-start | bytes 524288 | tf_op jit(solution)/shard_map/all_to_all | solution.py:527
  26.3 1.6 %collective-permute-start.4 = (f32[7,8,128]{2,1,0:T(8,128)S(1)}, f32[7,8,128]{2,1,0:T(8,128)S(1)}, u32[]{:S(2)}, u32[]{:S(2)}) collective-permute-start(f32[7,8,128]{2,1,0:T(8,128)S(1)} %get-tuple-element.38), channel_id=1, source_target_pairs={{0,4},{4,8},{8,12},{12,16},{16,20},{20,24},{24,28},{28,32},{32,36}... | collective-permute-start | bytes 86024 | tf_op jit(solution)/shard_map/ppermute | solution.py:481
  27.9 4.8 %collective-permute-start.5 = (f32[7,8,128]{2,1,0:T(8,128)S(1)}, f32[7,8,128]{2,1,0:T(8,128)S(1)}, u32[]{:S(2)}, u32[]{:S(2)}) collective-permute-start(f32[7,8,128]{2,1,0:T(8,128)S(1)} %get-tuple-element.39), channel_id=1, source_target_pairs={{4,0},{8,4},{12,8},{16,12},{20,16},{24,20},{28,24},{32,28},{36,32}... | collective-permute-start | bytes 86024 | tf_op jit(solution)/shard_map/ppermute | solution.py:482
  32.6 2.9 %collective-permute-start.6 = (f32[7,4,128]{2,1,0:T(4,128)S(1)}, f32[7,4,128]{2,1,0:T(4,128)S(1)}, u32[]{:S(2)}, u32[]{:S(2)}) collective-permute-start(f32[7,4,128]{2,1,0:T(4,128)S(1)} %get-tuple-element.40), channel_id=1, source_target_pairs={{0,1},{1,2},{2,3},{3,0},{4,5},{5,6},{6,7},{7,4},{8,9},{9,10},{10,1... | collective-permute-start | bytes 43016 | tf_op jit(solution)/shard_map/ppermute | solution.py:483
  35.5 1.4 %collective-permute-start.7 = (f32[7,4,128]{2,1,0:T(4,128)S(1)}, f32[7,4,128]{2,1,0:T(4,128)S(1)}, u32[]{:S(2)}, u32[]{:S(2)}) collective-permute-start(f32[7,4,128]{2,1,0:T(4,128)S(1)} %get-tuple-element.41), channel_id=1, source_target_pairs={{1,0},{2,1},{3,2},{0,3},{5,4},{6,5},{7,6},{4,7},{9,8},{10,9},{11,1... | collective-permute-start | bytes 43016 | tf_op jit(solution)/shard_map/ppermute | solution.py:484
  37.0 3.3 %settle.1 = (f32[6,4,8,128]{3,2,1,0:T(8,128)S(1)}, f32[6,4,8,128]{3,2,1,0:T(8,128)S(1)}, s32[512,128]{1,0:T(8,128)S(1)}, f32[2,4,8,128]{3,2,1,0:T(8,128)S(1)}, bf16[128,384]{1,0:T(8,128)(2,1)S(1)}) custom-call(s32[2,128]{1,0:T(2,128)S(1)} %copy-done, f32[6,4,8,128]{3,2,1,0:T(8,128)S(1)} %get-tuple-element.35.f1_ref, ...), custom_call_target="tpu_custom_call" | custom-call | flops 9000000 | bytes 3000000 | tf_op jit(solution)/shard_map/settle/pallas_call | solution.py:531
  40.3 0.2 collective-permute-done.7.right_ref
  40.4 0.0 collective-permute-done.4.up_ref
  40.5 0.0 collective-permute-done.5.down_ref
  40.5 0.4 settle_edges.1
  40.9 0.7 %all-to-all-done = f32[256,1,256]{2,1,0:T(1,128)S(1)} async-done(((f32[256,1,256]{2,1,0:T(1,128)}), f32[256,1,256]{2,1,0:T(1,128)S(1)}, u32[]{:S(2)}, u32[]{:S(2)}) %all-to-all-start) | async-done | bytes 262176 | tf_op jit(solution)/shard_map/all_to_all | solution.py:527
  41.6 2.5 %cycle_update.1 = (f32[1,6,4,8,128]{4,3,2,1,0:T(8,128)}, f32[384,128]{1,0:T(8,128)S(1)}) custom-call(s32[2,128]{1,0:T(2,128)S(1)} %copy-done, f32[6,4,8,128]{3,2,1,0:T(8,128)S(1)} %get-tuple-element.42.part_ref, f32[4,8,128]{2,1,0:T(8,128)S(1)} %get-tuple-element.43.rec_ref, f32[6,4,8,128]{3,2,1,0:T(8,128)S(1)} %get-tuple-element.44.pack_ref, ...), custom_call_target="tpu_custom_call" | custom-call | tf_op jit(solution)/shard_map/cycle_update/pallas_call | solution.py:550
  44.2 21.0 %all_to_all.10 = f32[128,1,384]{2,1,0:T(1,128)S(1)} all-to-all(f32[128,1,384]{2,1,0:T(1,128)S(1)} %bitcast.7), channel_id=1, replica_groups=mesh['row'=2,'span'=32,'pitch'=4] {'span','pitch'}, dimensions={0} | all-to-all | bytes 393216 | tf_op jit(solution)/shard_map/all_to_all | solution.py:559
  65.1 0.6 node_sums.1
  (11 shorter events, 0.0 us)
Async XLA Ops:
  1.5 14.9 %collective-permute-start = (f32[6,8,128]{2,1,0:T(8,128)S(1)}, f32[6,8,128]{2,1,0:T(8,128)S(1)}, u32[]{:S(2)}, u32[]{:S(2)}) collective-permute-start(f32[6,8,128]{2,1,0:T(8,128)S(1)} %get-tuple-element.31), channel_id=1, source_target_pairs={{0,4},{4,8},{8,12},{12,16},{16,20},{20,24},{24,28},{28,32},{32,36}... | collective-permute-start | bytes 73736 | tf_op jit(solution)/shard_map/ppermute | solution.py:481
  3.0 13.4 %collective-permute-start.1 = (f32[6,8,128]{2,1,0:T(8,128)S(1)}, f32[6,8,128]{2,1,0:T(8,128)S(1)}, u32[]{:S(2)}, u32[]{:S(2)}) collective-permute-start(f32[6,8,128]{2,1,0:T(8,128)S(1)} %get-tuple-element.32), channel_id=1, source_target_pairs={{4,0},{8,4},{12,8},{16,12},{20,16},{24,20},{28,24},{32,28},{36,32}... | collective-permute-start | bytes 73736 | tf_op jit(solution)/shard_map/ppermute | solution.py:482
  7.8 7.9 %collective-permute-start.2 = (f32[6,4,128]{2,1,0:T(4,128)S(1)}, f32[6,4,128]{2,1,0:T(4,128)S(1)}, u32[]{:S(2)}, u32[]{:S(2)}) collective-permute-start(f32[6,4,128]{2,1,0:T(4,128)S(1)} %get-tuple-element.33), channel_id=1, source_target_pairs={{0,1},{1,2},{2,3},{3,0},{4,5},{5,6},{6,7},{7,4},{8,9},{9,10},{10,1... | collective-permute-start | bytes 36872 | tf_op jit(solution)/shard_map/ppermute | solution.py:483
  11.1 25.9 %copy-start.3 = (f32[1,1,1,18,128]{4,2,3,1,0:T(1,128)S(1)}, f32[1,1,1,18,128]{4,2,3,1,0:T(1,128)}, u32[]{:S(2)}) copy-start(f32[1,1,1,18,128]{4,2,3,1,0:T(1,128)} %param.15) | copy-start | bytes 27652
  11.1 25.9 %copy-start = (s32[2,128]{1,0:T(2,128)S(1)}, s32[2,128]{1,0:T(2,128)}, u32[]{:S(2)}) copy-start(s32[2,128]{1,0:T(2,128)} %bands_ref.3) | copy-start | bytes 3076
  11.1 25.9 %copy-start.1 = (s32[1,1,1,128]{3,2,1,0:T(1,128)S(1)}, s32[1,1,1,128]{3,2,1,0:T(1,128)}, u32[]{:S(2)}) copy-start(s32[1,1,1,128]{3,2,1,0:T(1,128)} %cell_ref.3) | copy-start | bytes 1540
  11.1 25.9 %copy-start.2 = (s32[1,1,1,128]{3,2,1,0:T(1,128)S(1)}, s32[1,1,1,128]{3,2,1,0:T(1,128)}, u32[]{:S(2)}) copy-start(s32[1,1,1,128]{3,2,1,0:T(1,128)} %owner_ref.3) | copy-start | bytes 1540
  11.1 5.3 %collective-permute-start.3 = (f32[6,4,128]{2,1,0:T(4,128)S(1)}, f32[6,4,128]{2,1,0:T(4,128)S(1)}, u32[]{:S(2)}, u32[]{:S(2)}) collective-permute-start(f32[6,4,128]{2,1,0:T(4,128)S(1)} %get-tuple-element.34), channel_id=1, source_target_pairs={{1,0},{2,1},{3,2},{0,3},{5,4},{6,5},{7,6},{4,7},{9,8},{10,9},{11,1... | collective-permute-start | bytes 36872 | tf_op jit(solution)/shard_map/ppermute | solution.py:484
  17.9 23.8 %all-to-all-start = ((f32[256,1,256]{2,1,0:T(1,128)}), f32[256,1,256]{2,1,0:T(1,128)S(1)}, u32[]{:S(2)}, u32[]{:S(2)}) async-start(f32[256,1,256]{2,1,0:T(1,128)} %bitcast), calls=%async_computation | async-start | bytes 524288 | tf_op jit(solution)/shard_map/all_to_all | solution.py:527
  26.3 14.1 %collective-permute-start.4 = (f32[7,8,128]{2,1,0:T(8,128)S(1)}, f32[7,8,128]{2,1,0:T(8,128)S(1)}, u32[]{:S(2)}, u32[]{:S(2)}) collective-permute-start(f32[7,8,128]{2,1,0:T(8,128)S(1)} %get-tuple-element.38), channel_id=1, source_target_pairs={{0,4},{4,8},{8,12},{12,16},{16,20},{20,24},{24,28},{28,32},{32,36}... | collective-permute-start | bytes 86024 | tf_op jit(solution)/shard_map/ppermute | solution.py:481
  27.9 12.6 %collective-permute-start.5 = (f32[7,8,128]{2,1,0:T(8,128)S(1)}, f32[7,8,128]{2,1,0:T(8,128)S(1)}, u32[]{:S(2)}, u32[]{:S(2)}) collective-permute-start(f32[7,8,128]{2,1,0:T(8,128)S(1)} %get-tuple-element.39), channel_id=1, source_target_pairs={{4,0},{8,4},{12,8},{16,12},{20,16},{24,20},{28,24},{32,28},{36,32}... | collective-permute-start | bytes 86024 | tf_op jit(solution)/shard_map/ppermute | solution.py:482
  32.6 7.6 %collective-permute-start.6 = (f32[7,4,128]{2,1,0:T(4,128)S(1)}, f32[7,4,128]{2,1,0:T(4,128)S(1)}, u32[]{:S(2)}, u32[]{:S(2)}) collective-permute-start(f32[7,4,128]{2,1,0:T(4,128)S(1)} %get-tuple-element.40), channel_id=1, source_target_pairs={{0,1},{1,2},{2,3},{3,0},{4,5},{5,6},{6,7},{7,4},{8,9},{9,10},{10,1... | collective-permute-start | bytes 43016 | tf_op jit(solution)/shard_map/ppermute | solution.py:483
  35.5 4.9 %collective-permute-start.7 = (f32[7,4,128]{2,1,0:T(4,128)S(1)}, f32[7,4,128]{2,1,0:T(4,128)S(1)}, u32[]{:S(2)}, u32[]{:S(2)}) collective-permute-start(f32[7,4,128]{2,1,0:T(4,128)S(1)} %get-tuple-element.41), channel_id=1, source_target_pairs={{1,0},{2,1},{3,2},{0,3},{5,4},{6,5},{7,6},{4,7},{9,8},{10,9},{11,1... | collective-permute-start | bytes 43016 | tf_op jit(solution)/shard_map/ppermute | solution.py:484

commit v7 on v6

--- a/solution.py
+++ b/solution.py
@@ -290,27 +290,24 @@
         ]
         for n in range(6):
             pack_ref[n, j] = pack_ref[n, j] * steps[n // 5]
-    second_half = lane >= LANES // 2
-    odd = row_ids(tile) % 2 == 1
-    spans = bands_ref.shape[1] // CS
-
-    def label(i, carry):
-        of_row = i // spans
-        cells = [bands_ref[of_row, (i % spans) * CS + j] for j in range(CS)]
-        ids_ref[pl.ds(pl.multiple_of(i * CP, CP), CP), :] = jnp.where(
-            odd,
-            jnp.where(second_half, cells[3], cells[2]),
-            jnp.where(second_half, cells[1], cells[0]),
+    square = (LANES, LANES)
+    lines = ids_ref.shape[0] // 2
+    even_cell = (lane_ids((lines, LANES)) == 2 * row_ids((lines, LANES))).astype(F32).astype(BF16)
+    for of_row in range(2):
+        bands = bands_ref[of_row : of_row + 1].astype(F32)
+        pair = jnp.where(
+            row_ids(square) < LANES // 2,
+            jnp.broadcast_to(bands, square),
+            jnp.broadcast_to(pltpu.roll(bands, LANES - 1, 1), square),
         )
-        return carry
-
-    lax.fori_loop(0, 2 * spans, label, 0)
+        ids_ref[lines * of_row : lines * (of_row + 1)] = lax.dot_general(
+            even_cell, pair.astype(BF16), (((1,), (1,)), ((), ())), preferred_element_type=F32
+        )
     cells = cell_ref[0, 0]
     for j in range(CS):
         here = row_ids(tile) + CP * j == cells // LANES
         for n, at in enumerate((outlet, inner)):
             seen_ref[n, j] = jnp.where(here & (cells % LANES == at), 1.0, 0.0).astype(F32)
-    square = (LANES, LANES)
     picked = (row_ids(square) == owner_ref[0, 0] % LANES).astype(F32).astype(BF16)
     for n in range(3):
         node_ref[:, LANES * n : LANES * (n + 1)] = picked
@@ -341,43 +338,55 @@
         face_ref[c : c + 1] = jnp.sum(jnp.where(here, block, 0.0), axis=0, keepdims=True)
 
 
-def cycle_kernel(
-    bands_ref, part_ref, rec_ref, pack_ref, ids_ref, all_ref, up_ref, down_ref, left_ref, right_ref,
-    seen_ref, node_ref, face_ref, owner_ref, weight_ref, out_ref, dense_ref,
+def bands_kernel(
+    bands_ref, ids_ref, all_ref, to_left_ref, to_right_ref, sum_ref, left_ref, right_ref
 ):
     row = lax.axis_index("row")
     span = lax.axis_index("span")
+    tile = (CP, LANES)
+    last_cell = bands_ref.shape[1] - 1
+    wanted = [
+        bands_ref[row, jnp.clip(span * CS - 1 + t, 0, last_cell)].astype(F32)
+        for t in range(CS + 2)
+    ]
+    half = all_ref.shape[0] // 2
+
+    def folded(of_row):
+        sums = [jnp.zeros(tile, F32)] * (CS + 2)
+        for i in range(half // CP):
+            at = pl.multiple_of(of_row * half + i * CP, CP)
+            ids, values = ids_ref[pl.ds(at, CP), :], all_ref[pl.ds(at, CP), :]
+            sums = [x + jnp.where(ids == band, values, 0.0) for x, band in zip(sums, wanted)]
+        rows = [jnp.sum(x, axis=0, keepdims=True) for x in sums]
+        whole = jnp.concatenate(rows + [rows[-1]] * (CP - len(rows)), axis=0)
+        return whole + pltpu.roll(whole, 64, 1)
+
+    total = jnp.where(lane_ids(tile) < LANES // 2, folded(1 - row), folded(row))
+    sum_ref[...] = total
+    for out_ref, in_ref in ((left_ref, to_left_ref), (right_ref, to_right_ref)):
+        out_ref[: NVAR + 1] = in_ref[...]
+        out_ref[NVAR + 1] = total[:CS]
+        out_ref[NVAR + 2] = total[CS:]
+
+
+def cycle_kernel(
+    part_ref, rec_ref, pack_ref, sum_ref, far_ref, up_ref, down_ref, left_ref, right_ref,
+    seen_ref, node_ref, face_ref, owner_ref, weight_ref, out_hbm, dense_ref, field, sem,
+):
+    row = lax.axis_index("row")
     outlet, inner = outlet_lanes(row)
     keep = inner_sides()
     tile = (CP, LANES)
     lane, sub = lane_ids(tile), row_ids(tile)
-    last_cell = bands_ref.shape[1] - 1
-    wanted = [
-        bands_ref[row, jnp.clip(span * CS - 1 + t, 0, last_cell)] for t in range(CS + 2)
+    zero = jnp.zeros(tile, F32)
+    sides = [
+        jnp.concatenate([ref[NVAR + 1], ref[NVAR + 2]], axis=0) for ref in (left_ref, right_ref)
     ]
-    half = all_ref.shape[0] // 2
-    zero = jnp.zeros(tile, F32)
-
-    def body(i, sums):
-        sums = list(sums)
-        for n, of_row in enumerate((1 - row, row)):
-            at = pl.multiple_of(of_row * half + i * CP, CP)
-            ids, values = ids_ref[pl.ds(at, CP), :], all_ref[pl.ds(at, CP), :]
-            for t, band in enumerate(wanted):
-                k = (CS + 2) * n + t
-                sums[k] = sums[k] + jnp.where(ids == band, values, 0.0)
-        return tuple(sums)
-
-    sums = lax.fori_loop(0, half // CP, body, (zero,) * (2 * CS + 4), unroll=2)
-
-    def folded(parts):
-        rows = [jnp.sum(x, axis=0, keepdims=True) for x in parts]
-        whole = jnp.concatenate(rows + [rows[-1]] * (CP - len(rows)), axis=0)
-        whole = whole + pltpu.roll(whole, 64, 1)
-        return whole, jnp.broadcast_to(whole[:, COUNT_AT : COUNT_AT + 1], tile)
-
-    other, other_count = folded(sums[: CS + 2])
-    mine, my_count = folded(sums[CS + 2 :])
+    other = (sum_ref[...] + far_ref[...]) + (sides[0] + sides[1])
+    mine = pltpu.roll(other, LANES // 2, 1)
+    other_count, my_count = (
+        jnp.broadcast_to(x[:, COUNT_AT : COUNT_AT + 1], tile) for x in (other, mine)
+    )
     spread0 = spread(other / other_count, 0)
     lost = weight_sum(other * spread(mine / my_count, 0))
     cycle1 = (other - pltpu.roll(lost, LANES - (WEIGHT_AT - FIRST_AT), 1)) / other_count
@@ -412,12 +421,14 @@
         for j in range(CS):
             first, second = (jnp.broadcast_to(x[:, at : at + 1], tile) for x in changes[j])
             moved = jnp.where(lane == outlet, first, jnp.where(lane == inner, second, 0.0))
-            out_ref[0, c, j] = part_ref[c, j] + moved
+            field[0, c, j] = part_ref[c, j] + moved
             seen = seen + (seen_ref[0, j] * first + seen_ref[1, j] * second)
         value = face_ref[c : c + 1] + jnp.sum(seen, axis=0, keepdims=True)
         for k in range(3):
             at = NVAR * k + c
             terms[k] = terms[k] + weight_ref[0, 0, 0, at : at + 1] * value
+    write = pltpu.make_async_copy(field, out_hbm, sem)
+    write.start()
     shape = dense_ref.shape
     line = row_ids(shape)
     device = (line * 43691) >> 17
@@ -436,6 +447,7 @@
         (((1,), (1,)), ((), ())),
         preferred_element_type=F32,
     )
+    write.wait()
 
 
 def third_kernel(parts_ref, out_ref):
@@ -457,13 +469,13 @@
     return pltpu.with_memory_space_constraint(x, pltpu.HBM)
 
 
-def call(kernel, name, outs, in_specs, scratch=(), cost=None):
+def call(kernel, name, outs, in_specs, scratch=(), cost=None, out_specs=None):
     outs = [out if isinstance(out[0], tuple) else (out, F32) for out in outs]
     return pl.pallas_call(
         kernel,
         out_shape=tuple(jax.ShapeDtypeStruct(shape, dtype) for shape, dtype in outs),
         in_specs=in_specs,
-        out_specs=(VM,) * len(outs),
+        out_specs=out_specs or (VM,) * len(outs),
         scratch_shapes=list(scratch),
         compiler_params=PARAMS,
         cost_estimate=cost,
@@ -471,25 +483,24 @@
     )
 
 
-def exchange(to_up, to_down, to_left, to_right):
-    spans, pitches = lax.axis_size("span"), lax.axis_size("pitch")
-    rising = [(i, (i + 1) % spans) for i in range(spans)]
-    falling = [((i + 1) % spans, i) for i in range(spans)]
-    onward = [(i, (i + 1) % pitches) for i in range(pitches)]
-    back = [((i + 1) % pitches, i) for i in range(pitches)]
-    return (
-        lax.ppermute(to_down, "span", rising),
-        lax.ppermute(to_up, "span", falling),
-        lax.ppermute(to_right, "pitch", onward),
-        lax.ppermute(to_left, "pitch", back),
-    )
+def shifted(value, axis, by):
+    devices = lax.axis_size(axis)
+    return lax.ppermute(value, axis, [(i, (i + by) % devices) for i in range(devices)])
+
+
+def over_span(to_up, to_down):
+    return shifted(to_down, "span", 1), shifted(to_up, "span", -1)
+
+
+def over_pitch(to_left, to_right):
+    return shifted(to_right, "pitch", 1), shifted(to_left, "pitch", -1)
 
 
 def on_device(
     adjoint, source, pseudo_step, jac_blocks, band_map, face_cell, face_owner, face_weight
 ):
     rows, spans, pitches = (lax.axis_size(name) for name in ("row", "span", "pitch"))
-    devices = rows * spans * pitches
+    groups = rows * spans
     peers = spans * pitches
     block = (NVAR, CS, CP, LANES)
     edge = (NVAR, CP, LANES)
@@ -501,7 +512,7 @@
         in_specs=[HBM],
         scratch=[pltpu.SemaphoreType.DMA((4,))],
     )(in_hbm(adjoint))
-    halo = exchange(*edges)
+    halo = over_span(*edges[:2]) + over_pitch(*edges[2:])
     part, record, jac, src, tau = call(
         interior_kernel,
         "interior",
@@ -520,25 +531,31 @@
     first, message, full_record, *sends = call(
         edge_kernel,
         "edge_update",
-        [block, (2 * devices, LANES), (CS, CP, LANES), edge, edge, side, side],
+        [block, (2 * groups, LANES), (CS, CP, LANES), edge, edge, side, side],
         in_specs=[VM] * 8,
         scratch=[pltpu.VMEM((2 * NVAR, CS, CP, LANES), F32)],
     )(part, record, jac, tau, *halo)
     records = lax.all_to_all(
-        message.reshape(devices, 1, 2 * LANES), ("row", "span", "pitch"), 0, 0
-    ).reshape(2 * devices, LANES)
-    halo = exchange(*sends)
+        message.reshape(groups, 1, 2 * LANES), ("row", "span"), 0, 0
+    ).reshape(2 * groups, LANES)
+    halo = over_span(*sends[:2])
     part, packs, ids, seen, picks = call(
         settle_kernel,
         "settle",
         [
-            block, (6, CS, CP, LANES), ((2 * devices, LANES), jnp.int32), (2, CS, CP, LANES),
+            block, (6, CS, CP, LANES), ((2 * groups, LANES), F32), (2, CS, CP, LANES),
             ((LANES, 3 * LANES), BF16),
         ],
-        in_specs=[SM] + [VM] * 6,
+        in_specs=[VM] * 7,
         scratch=[pltpu.VMEM((7 * NVAR, CS, CP, LANES), F32)],
         cost=pl.CostEstimate(flops=9_000_000, bytes_accessed=3_000_000, transcendentals=0),
     )(band_map, first, src, tau, jac, face_cell, face_owner)
+    tail = (NVAR + 3, CS, LANES)
+    sums, *sides = call(
+        bands_kernel, "band_sums", [(CP, LANES), tail, tail], in_specs=[SM] + [VM] * 4
+    )(band_map, ids, records, *sends[2:])
+    halo = halo + over_pitch(*sides)
+    far = shifted(sums, "pitch", 2)
     part, faces = call(
         settle_edges_kernel,
         "settle_edges",
@@ -551,10 +568,11 @@
         cycle_kernel,
         "cycle_update",
         [(1,) + block, (3 * peers, LANES)],
-        in_specs=[SM] + [VM] * 14,
+        in_specs=[VM] * 14,
+        out_specs=(HBM, VM),
+        scratch=[pltpu.VMEM((1,) + block, F32), pltpu.SemaphoreType.DMA],
     )(
-        band_map, part, full_record, packs, ids, records, *halo, seen, picks, faces, face_owner,
-        face_weight,
+        part, full_record, packs, sums, far, *halo, seen, picks, faces, face_owner, face_weight,
     )
     parts = lax.all_to_all(dense.reshape(peers, 1, 3 * LANES), ("span", "pitch"), 0, 0)
     (nodes,) = call(third_kernel, "node_sums", [(3, 1, LANES)], in_specs=[VM])(

time: 66 us -> 66.8 us (1.012)
  Pallas kernels: 11.5 us -> 9.63 us
  waiting for transfers between devices: 1.63 us -> 3.33 us
  starting transfers between devices: 30.9 us -> 31.8 us
    ppermute x8 -> x9, starting transfers between devices: 22.4 us -> 26.6 us  [shifted(): lax.ppermute(value, axis, [(i, (i + by) % devices) for i in range(devices)])]
    all_to_all x1, starting transfers between devices: 8.46 us -> 5.16 us  [on_device(): lax.all_to_all(message.reshape(groups, 1, 2 * LANES), ('row', 'span'), 0, 0)]
    ppermute x8 -> x9, waiting for transfers between devices: 0.9 us -> 3.31 us  [shifted(): lax.ppermute(value, axis, [(i, (i + by) % devices) for i in range(devices)])]
    pallas_call x2 -> x3, Pallas kernels: 4.72 us -> 3.65 us  [the longest x1 1.58 us: on_device(): call(settle_kernel, 'settle', [block, (6, CS, CP, LANES), ((2 * groups, L...]
    pallas_call x1, Pallas kernels: 2.53 us -> 1.72 us  [on_device(): call(cycle_kernel, 'cycle_update', [(1,) + block, (3 * peers, LANES)], in...]
    all_to_all x1, waiting for transfers between devices: 0.73 us -> 0.01 us  [on_device(): lax.all_to_all(message.reshape(groups, 1, 2 * LANES), ('row', 'span'), 0, 0)]
  transfers between devices with their start and end apart: 9 -> 10, of which waited for: 3 -> 3; matrix products, arithmetic and copies ran while one was open for 0% -> 0% of each run, Pallas kernels for 9% -> 8%
where the time goes in v7:
time: 66.8 us; the launch traced here: 66.5 us
  starting transfers between devices  31.8 us (48%)
  blocking collectives  21 us (31%)
  Pallas kernels  9.63 us (14%)
  waiting for transfers between devices  3.33 us (5%)
  between operations  0.72 us (1%)
    ppermute x9, starting transfers between devices, shifted(): lax.ppermute(value, axis, [(i, (i + by) % devices) for i in range(devices)])  26.6 us
    all_to_all x1, blocking collectives, on_device(): lax.all_to_all(dense.reshape(peers, 1, 3 * LANES), ('span', 'pitch'), 0, 0)  21 us
    all_to_all x1, starting transfers between devices, on_device(): lax.all_to_all(message.reshape(groups, 1, 2 * LANES), ('row', 'span'), 0, 0)  5.16 us
    ppermute x9, waiting for transfers between devices, shifted(): lax.ppermute(value, axis, [(i, (i + by) % devices) for i in range(devices)])  3.31 us
    pallas_call x1, Pallas kernels, on_device(): call(interior_kernel, 'interior', [block, (CS, CP, LANES), ((7, NVAR) + b...  2.4 us
    pallas_call x1, Pallas kernels, on_device(): call(cycle_kernel, 'cycle_update', [(1,) + block, (3 * peers, LANES)], in...  1.72 us
    pallas_call x1, Pallas kernels, on_device(): call(settle_kernel, 'settle', [block, (6, CS, CP, LANES), ((2 * groups, L...  1.58 us
    pallas_call x1, Pallas kernels, on_device(): call(edge_kernel, 'edge_update', [block, (2 * groups, LANES), (CS, CP, LA...  1.37 us
  transfers between devices with their start and end apart: 10, of which 3 were waited for; matrix products, arithmetic and copies ran while one was open for 0% of the time, Pallas kernels for 8%

profile of v7, /device:TPU:32, one launch (start us, length us, event | category | flops | bytes accessed | tf_op | source)
XLA Modules:
  0.0 66.5 jit_solution(15656510774299807701)
XLA Ops:
  0.6 0.8 %edges.1 = (f32[6,8,128]{2,1,0:T(8,128)S(1)}, f32[6,8,128]{2,1,0:T(8,128)S(1)}, f32[6,4,128]{2,1,0:T(4,128)S(1)}, f32[6,4,128]{2,1,0:T(4,128)S(1)}) custom-call(f32[1,6,4,8,128]{4,3,2,1,0:T(8,128)} %adj_ref.1), custom_call_target="tpu_custom_call" | custom-call | tf_op jit(solution)/shard_map/edges/pallas_call | solution.py:508
  1.5 1.6 %collective-permute-start = (f32[6,8,128]{2,1,0:T(8,128)S(1)}, f32[6,8,128]{2,1,0:T(8,128)S(1)}, u32[]{:S(2)}, u32[]{:S(2)}) collective-permute-start(f32[6,8,128]{2,1,0:T(8,128)S(1)} %get-tuple-element.34), channel_id=1, source_target_pairs={{0,4},{4,8},{8,12},{12,16},{16,20},{20,24},{24,28},{28,32},{32,36}... | collective-permute-start | bytes 73736 | tf_op jit(solution)/shard_map/ppermute | solution.py:488
  3.0 4.8 %collective-permute-start.1 = (f32[6,8,128]{2,1,0:T(8,128)S(1)}, f32[6,8,128]{2,1,0:T(8,128)S(1)}, u32[]{:S(2)}, u32[]{:S(2)}) collective-permute-start(f32[6,8,128]{2,1,0:T(8,128)S(1)} %get-tuple-element.35), channel_id=1, source_target_pairs={{0,124},{4,0},{8,4},{12,8},{16,12},{20,16},{24,20},{28,24},{32,28}... | collective-permute-start | bytes 73736 | tf_op jit(solution)/shard_map/ppermute | solution.py:488
  7.8 3.3 %collective-permute-start.2 = (f32[6,4,128]{2,1,0:T(4,128)S(1)}, f32[6,4,128]{2,1,0:T(4,128)S(1)}, u32[]{:S(2)}, u32[]{:S(2)}) collective-permute-start(f32[6,4,128]{2,1,0:T(4,128)S(1)} %get-tuple-element.36), channel_id=1, source_target_pairs={{0,1},{1,2},{2,3},{3,0},{4,5},{5,6},{6,7},{7,4},{8,9},{9,10},{10,1... | collective-permute-start | bytes 36872 | tf_op jit(solution)/shard_map/ppermute | solution.py:488
  11.1 2.2 %collective-permute-start.3 = (f32[6,4,128]{2,1,0:T(4,128)S(1)}, f32[6,4,128]{2,1,0:T(4,128)S(1)}, u32[]{:S(2)}, u32[]{:S(2)}) collective-permute-start(f32[6,4,128]{2,1,0:T(4,128)S(1)} %get-tuple-element.37), channel_id=1, source_target_pairs={{0,3},{1,0},{2,1},{3,2},{4,7},{5,4},{6,5},{7,6},{8,11},{9,8},{10,9... | collective-permute-start | bytes 36872 | tf_op jit(solution)/shard_map/ppermute | solution.py:488
  13.3 2.4 %interior.1 = (f32[6,4,8,128]{3,2,1,0:T(8,128)S(1)}, f32[4,8,128]{2,1,0:T(8,128)S(1)}, bf16[7,6,6,4,8,128]{5,4,3,2,1,0:T(8,128)(2,1)S(1)}, f32[6,4,8,128]{3,2,1,0:T(8,128)S(1)}, f32[4,8,128]{2,1,0:T(8,128)S(1)}) custom-call(f32[1,6,4,8,128]{4,3,2,1,0:T(8,128)} %adj_ref.1, f32[1,6,4,8,128]{4,3,2,1,0:T(8,128)} %src_hbm.1, f32[1,4,8,128]{3,2,1,0:T(8,128)} %tau_hbm.1, ...), custom_call_target="tpu_custom_call" | custom-call | flops 9000000 | bytes 3000000 | tf_op jit(solution)/shard_map/interior/pallas_call | solution.py:516
  15.7 0.0 collective-permute-done.2.left_ref
  15.7 0.6 collective-permute-done.3.right_ref
  16.3 1.4 %edge_update.1 = (f32[6,4,8,128]{3,2,1,0:T(8,128)S(1)}, f32[128,128]{1,0:T(8,128)}, f32[4,8,128]{2,1,0:T(8,128)S(1)}, f32[7,8,128]{2,1,0:T(8,128)S(1)}, f32[7,8,...) custom-call(f32[6,4,8,128]{3,2,1,0:T(8,128)S(1)} %get-tuple-element.30.part_ref, ...), custom_call_target="tpu_custom_call" | custom-call | tf_op jit(solution)/shard_map/edge_update/pallas_call | solution.py:531
  17.7 5.2 %all-to-all-start = ((f32[64,1,256]{2,1,0:T(1,128)}), f32[64,1,256]{2,1,0:T(1,128)S(1)}, u32[]{:S(2)}, u32[]{:S(2)}) async-start(f32[64,1,256]{2,1,0:T(1,128)} %bitcast), calls=%async_computation | async-start | bytes 131072 | tf_op jit(solution)/shard_map/all_to_all | solution.py:538
  22.9 1.5 %collective-permute-start.4 = (f32[7,8,128]{2,1,0:T(8,128)S(1)}, f32[7,8,128]{2,1,0:T(8,128)S(1)}, u32[]{:S(2)}, u32[]{:S(2)}) collective-permute-start(f32[7,8,128]{2,1,0:T(8,128)S(1)} %get-tuple-element.41), channel_id=1, source_target_pairs={{0,4},{4,8},{8,12},{12,16},{16,20},{20,24},{24,28},{28,32},{32,36}... | collective-permute-start | bytes 86024 | tf_op jit(solution)/shard_map/ppermute | solution.py:488
  24.4 4.8 %collective-permute-start.5 = (f32[7,8,128]{2,1,0:T(8,128)S(1)}, f32[7,8,128]{2,1,0:T(8,128)S(1)}, u32[]{:S(2)}, u32[]{:S(2)}) collective-permute-start(f32[7,8,128]{2,1,0:T(8,128)S(1)} %get-tuple-element.42), channel_id=1, source_target_pairs={{0,124},{4,0},{8,4},{12,8},{16,12},{20,16},{24,20},{28,24},{32,28}... | collective-permute-start | bytes 86024 | tf_op jit(solution)/shard_map/ppermute | solution.py:488
  29.2 1.6 %settle.1 = (f32[6,4,8,128]{3,2,1,0:T(8,128)S(1)}, f32[6,4,8,128]{3,2,1,0:T(8,128)S(1)}, f32[128,128]{1,0:T(8,128)S(1)}, f32[2,4,8,128]{3,2,1,0:T(8,128)S(1)}, bf16[128,384]{1,0:T(8,128)(2,1)S(1)}) custom-call(s32[2,128]{1,0:T(2,128)S(1)} %copy-done, f32[6,4,8,128]{3,2,1,0:T(8,128)S(1)} %get-tuple-element.38.f1_ref, ...), custom_call_target="tpu_custom_call" | custom-call | flops 9000000 | bytes 3000000 | tf_op jit(solution)/shard_map/settle/pallas_call | solution.py:542
  30.8 0.0 all-to-all-done
  30.8 0.7 %band_sums.1 = (f32[8,128]{1,0:T(8,128)S(1)}, f32[9,4,128]{2,1,0:T(4,128)S(1)}, f32[9,4,128]{2,1,0:T(4,128)S(1)}) custom-call(s32[2,128]{1,0:T(2,128)S(1)} %copy-done, f32[128,128]{1,0:T(8,128)S(1)} %get-tuple-element.43.ids_ref, f32[128,128]{1,0:T(8,128)S(1)} %bitcast.6, f32[7,4,128]{2,1,0:T(4,128)S(1)} %get-tuple-element.45.to_left_ref, ...), custom_call_target="tpu_custom_call" | custom-call | tf_op jit(solution)/shard_map/band_sums/pallas_call | solution.py:554
  31.5 4.2 %collective-permute-start.6 = (f32[9,4,128]{2,1,0:T(4,128)S(1)}, f32[9,4,128]{2,1,0:T(4,128)S(1)}, u32[]{:S(2)}, u32[]{:S(2)}) collective-permute-start(f32[9,4,128]{2,1,0:T(4,128)S(1)} %get-tuple-element.47), channel_id=1, source_target_pairs={{0,1},{1,2},{2,3},{3,0},{4,5},{5,6},{6,7},{7,4},{8,9},{9,10},{10,1... | collective-permute-start | bytes 55304 | tf_op jit(solution)/shard_map/ppermute | solution.py:488
  35.7 0.0 collective-permute-start.7
  35.7 4.4 %collective-permute-start.8 = (f32[8,128]{1,0:T(8,128)S(1)}, f32[8,128]{1,0:T(8,128)S(1)}, u32[]{:S(2)}, u32[]{:S(2)}) collective-permute-start(f32[8,128]{1,0:T(8,128)S(1)} %get-tuple-element.52.sum_ref), channel_id=1, source_target_pairs={{0,2},{1,3},{2,0},{3,1},{4,6},{5,7},{6,4},{7,5},{8,10},{9,11},{10,... | collective-permute-start | bytes 12296 | tf_op jit(solution)/shard_map/ppermute | solution.py:488
  40.0 0.3 collective-permute-done.7.right_ref
  40.3 0.4 settle_edges.1
  40.8 2.4 %collective-permute-done.8.far_ref = f32[8,128]{1,0:T(8,128)S(1)} collective-permute-done((f32[8,128]{1,0:T(8,128)S(1)}, f32[8,128]{1,0:T(8,128)S(1)}, u32[]{:S(2)}, u32[]{:S(2)}) %collective-permute-start.8) | collective-permute-done | bytes 4128 | tf_op jit(solution)/shard_map/ppermute | solution.py:488
  43.2 1.7 %cycle_update.1 = (f32[1,6,4,8,128]{4,3,2,1,0:T(8,128)}, f32[384,128]{1,0:T(8,128)S(1)}) custom-call(f32[6,4,8,128]{3,2,1,0:T(8,128)S(1)} %get-tuple-element.49.part_ref, f32[4,8,128]{2,1,0:T(8,128)S(1)} %get-tuple-element.50.rec_ref, f32[6,4,8,128]{3,2,1,0:T(8,128)S(1)} %get-tuple-element.51.pack_ref, f32[8,128]{1,0:T(8,128)S(1)} %get-tuple-element.52.sum_ref, ...), custom_call_target="tpu_custom_call" | custom-call | tf_op jit(solution)/shard_map/cycle_update/pallas_call | solution.py:567
  44.9 21.0 %all_to_all.10 = f32[128,1,384]{2,1,0:T(1,128)S(1)} all-to-all(f32[128,1,384]{2,1,0:T(1,128)S(1)} %bitcast.7), channel_id=1, replica_groups=mesh['row'=2,'span'=32,'pitch'=4] {'span','pitch'}, dimensions={0} | all-to-all | bytes 393216 | tf_op jit(solution)/shard_map/all_to_all | solution.py:577
  65.9 0.6 node_sums.1
  (14 shorter events, 0.0 us)
Async XLA Ops:
  1.5 14.9 %collective-permute-start = (f32[6,8,128]{2,1,0:T(8,128)S(1)}, f32[6,8,128]{2,1,0:T(8,128)S(1)}, u32[]{:S(2)}, u32[]{:S(2)}) collective-permute-start(f32[6,8,128]{2,1,0:T(8,128)S(1)} %get-tuple-element.34), channel_id=1, source_target_pairs={{0,4},{4,8},{8,12},{12,16},{16,20},{20,24},{24,28},{28,32},{32,36}... | collective-permute-start | bytes 73736 | tf_op jit(solution)/shard_map/ppermute | solution.py:488
  3.0 13.3 %collective-permute-start.1 = (f32[6,8,128]{2,1,0:T(8,128)S(1)}, f32[6,8,128]{2,1,0:T(8,128)S(1)}, u32[]{:S(2)}, u32[]{:S(2)}) collective-permute-start(f32[6,8,128]{2,1,0:T(8,128)S(1)} %get-tuple-element.35), channel_id=1, source_target_pairs={{0,124},{4,0},{8,4},{12,8},{16,12},{20,16},{24,20},{28,24},{32,28}... | collective-permute-start | bytes 73736 | tf_op jit(solution)/shard_map/ppermute | solution.py:488
  7.8 7.9 %collective-permute-start.2 = (f32[6,4,128]{2,1,0:T(4,128)S(1)}, f32[6,4,128]{2,1,0:T(4,128)S(1)}, u32[]{:S(2)}, u32[]{:S(2)}) collective-permute-start(f32[6,4,128]{2,1,0:T(4,128)S(1)} %get-tuple-element.36), channel_id=1, source_target_pairs={{0,1},{1,2},{2,3},{3,0},{4,5},{5,6},{6,7},{7,4},{8,9},{9,10},{10,1... | collective-permute-start | bytes 36872 | tf_op jit(solution)/shard_map/ppermute | solution.py:488
  11.1 18.1 %copy-start = (s32[2,128]{1,0:T(2,128)S(1)}, s32[2,128]{1,0:T(2,128)}, u32[]{:S(2)}) copy-start(s32[2,128]{1,0:T(2,128)} %bands_ref.3) | copy-start | bytes 3076
  11.1 18.1 %copy-start.1 = (s32[1,1,1,128]{3,2,1,0:T(1,128)S(1)}, s32[1,1,1,128]{3,2,1,0:T(1,128)}, u32[]{:S(2)}) copy-start(s32[1,1,1,128]{3,2,1,0:T(1,128)} %cell_ref.3) | copy-start | bytes 1540
  11.1 18.1 %copy-start.2 = (s32[1,1,1,128]{3,2,1,0:T(1,128)S(1)}, s32[1,1,1,128]{3,2,1,0:T(1,128)}, u32[]{:S(2)}) copy-start(s32[1,1,1,128]{3,2,1,0:T(1,128)} %owner_ref.3) | copy-start | bytes 1540
  11.1 5.3 %collective-permute-start.3 = (f32[6,4,128]{2,1,0:T(4,128)S(1)}, f32[6,4,128]{2,1,0:T(4,128)S(1)}, u32[]{:S(2)}, u32[]{:S(2)}) collective-permute-start(f32[6,4,128]{2,1,0:T(4,128)S(1)} %get-tuple-element.37), channel_id=1, source_target_pairs={{0,3},{1,0},{2,1},{3,2},{4,7},{5,4},{6,5},{7,6},{8,11},{9,8},{10,9... | collective-permute-start | bytes 36872 | tf_op jit(solution)/shard_map/ppermute | solution.py:488
  16.3 23.7 %copy-start.3 = (f32[1,1,1,18,128]{4,2,3,1,0:T(1,128)S(1)}, f32[1,1,1,18,128]{4,2,3,1,0:T(1,128)}, u32[]{:S(2)}) copy-start(f32[1,1,1,18,128]{4,2,3,1,0:T(1,128)} %param.15) | copy-start | bytes 27652
  17.7 13.1 %all-to-all-start = ((f32[64,1,256]{2,1,0:T(1,128)}), f32[64,1,256]{2,1,0:T(1,128)S(1)}, u32[]{:S(2)}, u32[]{:S(2)}) async-start(f32[64,1,256]{2,1,0:T(1,128)} %bitcast), calls=%async_computation | async-start | bytes 131072 | tf_op jit(solution)/shard_map/all_to_all | solution.py:538
  22.9 17.2 %collective-permute-start.4 = (f32[7,8,128]{2,1,0:T(8,128)S(1)}, f32[7,8,128]{2,1,0:T(8,128)S(1)}, u32[]{:S(2)}, u32[]{:S(2)}) collective-permute-start(f32[7,8,128]{2,1,0:T(8,128)S(1)} %get-tuple-element.41), channel_id=1, source_target_pairs={{0,4},{4,8},{8,12},{12,16},{16,20},{20,24},{24,28},{28,32},{32,36}... | collective-permute-start | bytes 86024 | tf_op jit(solution)/shard_map/ppermute | solution.py:488
  24.4 15.6 %collective-permute-start.5 = (f32[7,8,128]{2,1,0:T(8,128)S(1)}, f32[7,8,128]{2,1,0:T(8,128)S(1)}, u32[]{:S(2)}, u32[]{:S(2)}) collective-permute-start(f32[7,8,128]{2,1,0:T(8,128)S(1)} %get-tuple-element.42), channel_id=1, source_target_pairs={{0,124},{4,0},{8,4},{12,8},{16,12},{20,16},{24,20},{28,24},{32,28}... | collective-permute-start | bytes 86024 | tf_op jit(solution)/shard_map/ppermute | solution.py:488
  31.5 8.5 %collective-permute-start.6 = (f32[9,4,128]{2,1,0:T(4,128)S(1)}, f32[9,4,128]{2,1,0:T(4,128)S(1)}, u32[]{:S(2)}, u32[]{:S(2)}) collective-permute-start(f32[9,4,128]{2,1,0:T(4,128)S(1)} %get-tuple-element.47), channel_id=1, source_target_pairs={{0,1},{1,2},{2,3},{3,0},{4,5},{5,6},{6,7},{7,4},{8,9},{9,10},{10,1... | collective-permute-start | bytes 55304 | tf_op jit(solution)/shard_map/ppermute | solution.py:488
  35.7 4.7 %collective-permute-start.7 = (f32[9,4,128]{2,1,0:T(4,128)S(1)}, f32[9,4,128]{2,1,0:T(4,128)S(1)}, u32[]{:S(2)}, u32[]{:S(2)}) collective-permute-start(f32[9,4,128]{2,1,0:T(4,128)S(1)} %get-tuple-element.48), channel_id=1, source_target_pairs={{0,3},{1,0},{2,1},{3,2},{4,7},{5,4},{6,5},{7,6},{8,11},{9,8},{10,9... | collective-permute-start | bytes 55304 | tf_op jit(solution)/shard_map/ppermute | solution.py:488
  35.7 7.5 %collective-permute-start.8 = (f32[8,128]{1,0:T(8,128)S(1)}, f32[8,128]{1,0:T(8,128)S(1)}, u32[]{:S(2)}, u32[]{:S(2)}) collective-permute-start(f32[8,128]{1,0:T(8,128)S(1)} %get-tuple-element.52.sum_ref), channel_id=1, source_target_pairs={{0,2},{1,3},{2,0},{3,1},{4,6},{5,7},{6,4},{7,5},{8,10},{9,11},{10,... | collective-permute-start | bytes 12296 | tf_op jit(solution)/shard_map/ppermute | solution.py:488

commit v8 on v6

--- a/solution.py
+++ b/solution.py
@@ -290,27 +290,26 @@
         ]
         for n in range(6):
             pack_ref[n, j] = pack_ref[n, j] * steps[n // 5]
-    second_half = lane >= LANES // 2
-    odd = row_ids(tile) % 2 == 1
-    spans = bands_ref.shape[1] // CS
-
-    def label(i, carry):
-        of_row = i // spans
-        cells = [bands_ref[of_row, (i % spans) * CS + j] for j in range(CS)]
-        ids_ref[pl.ds(pl.multiple_of(i * CP, CP), CP), :] = jnp.where(
-            odd,
-            jnp.where(second_half, cells[3], cells[2]),
-            jnp.where(second_half, cells[1], cells[0]),
+    square = (LANES, LANES)
+    lines = ids_ref.shape[0] // 2
+    line = row_ids((lines, LANES))
+    first_cell = CS * (line // CP) + 2 * (line % 2)
+    even_cell = (lane_ids((lines, LANES)) == first_cell).astype(F32).astype(BF16)
+    for of_row in range(2):
+        bands = bands_ref[of_row : of_row + 1].astype(F32)
+        pair = jnp.where(
+            row_ids(square) < LANES // 2,
+            jnp.broadcast_to(bands, square),
+            jnp.broadcast_to(pltpu.roll(bands, LANES - 1, 1), square),
         )
-        return carry
-
-    lax.fori_loop(0, 2 * spans, label, 0)
+        ids_ref[lines * of_row : lines * (of_row + 1)] = lax.dot_general(
+            even_cell, pair.astype(BF16), (((1,), (1,)), ((), ())), preferred_element_type=F32
+        )
     cells = cell_ref[0, 0]
     for j in range(CS):
         here = row_ids(tile) + CP * j == cells // LANES
         for n, at in enumerate((outlet, inner)):
             seen_ref[n, j] = jnp.where(here & (cells % LANES == at), 1.0, 0.0).astype(F32)
-    square = (LANES, LANES)
     picked = (row_ids(square) == owner_ref[0, 0] % LANES).astype(F32).astype(BF16)
     for n in range(3):
         node_ref[:, LANES * n : LANES * (n + 1)] = picked
@@ -343,7 +342,7 @@
 
 def cycle_kernel(
     bands_ref, part_ref, rec_ref, pack_ref, ids_ref, all_ref, up_ref, down_ref, left_ref, right_ref,
-    seen_ref, node_ref, face_ref, owner_ref, weight_ref, out_ref, dense_ref,
+    seen_ref, node_ref, face_ref, owner_ref, weight_ref, out_hbm, dense_ref, field, sem,
 ):
     row = lax.axis_index("row")
     span = lax.axis_index("span")
@@ -353,7 +352,8 @@
     lane, sub = lane_ids(tile), row_ids(tile)
     last_cell = bands_ref.shape[1] - 1
     wanted = [
-        bands_ref[row, jnp.clip(span * CS - 1 + t, 0, last_cell)] for t in range(CS + 2)
+        bands_ref[row, jnp.clip(span * CS - 1 + t, 0, last_cell)].astype(F32)
+        for t in range(CS + 2)
     ]
     half = all_ref.shape[0] // 2
     zero = jnp.zeros(tile, F32)
@@ -368,7 +368,7 @@
                 sums[k] = sums[k] + jnp.where(ids == band, values, 0.0)
         return tuple(sums)
 
-    sums = lax.fori_loop(0, half // CP, body, (zero,) * (2 * CS + 4), unroll=2)
+    sums = lax.fori_loop(0, half // CP, body, (zero,) * (2 * CS + 4), unroll=4)
 
     def folded(parts):
         rows = [jnp.sum(x, axis=0, keepdims=True) for x in parts]
@@ -412,12 +412,14 @@
         for j in range(CS):
             first, second = (jnp.broadcast_to(x[:, at : at + 1], tile) for x in changes[j])
             moved = jnp.where(lane == outlet, first, jnp.where(lane == inner, second, 0.0))
-            out_ref[0, c, j] = part_ref[c, j] + moved
+            field[0, c, j] = part_ref[c, j] + moved
             seen = seen + (seen_ref[0, j] * first + seen_ref[1, j] * second)
         value = face_ref[c : c + 1] + jnp.sum(seen, axis=0, keepdims=True)
         for k in range(3):
             at = NVAR * k + c
             terms[k] = terms[k] + weight_ref[0, 0, 0, at : at + 1] * value
+    write = pltpu.make_async_copy(field, out_hbm, sem)
+    write.start()
     shape = dense_ref.shape
     line = row_ids(shape)
     device = (line * 43691) >> 17
@@ -436,6 +438,7 @@
         (((1,), (1,)), ((), ())),
         preferred_element_type=F32,
     )
+    write.wait()
 
 
 def third_kernel(parts_ref, out_ref):
@@ -457,13 +460,13 @@
     return pltpu.with_memory_space_constraint(x, pltpu.HBM)
 
 
-def call(kernel, name, outs, in_specs, scratch=(), cost=None):
+def call(kernel, name, outs, in_specs, scratch=(), cost=None, out_specs=None):
     outs = [out if isinstance(out[0], tuple) else (out, F32) for out in outs]
     return pl.pallas_call(
         kernel,
         out_shape=tuple(jax.ShapeDtypeStruct(shape, dtype) for shape, dtype in outs),
         in_specs=in_specs,
-        out_specs=(VM,) * len(outs),
+        out_specs=out_specs or (VM,) * len(outs),
         scratch_shapes=list(scratch),
         compiler_params=PARAMS,
         cost_estimate=cost,
@@ -471,18 +474,17 @@
     )
 
 
-def exchange(to_up, to_down, to_left, to_right):
-    spans, pitches = lax.axis_size("span"), lax.axis_size("pitch")
-    rising = [(i, (i + 1) % spans) for i in range(spans)]
-    falling = [((i + 1) % spans, i) for i in range(spans)]
-    onward = [(i, (i + 1) % pitches) for i in range(pitches)]
-    back = [((i + 1) % pitches, i) for i in range(pitches)]
-    return (
-        lax.ppermute(to_down, "span", rising),
-        lax.ppermute(to_up, "span", falling),
-        lax.ppermute(to_right, "pitch", onward),
-        lax.ppermute(to_left, "pitch", back),
-    )
+def shifted(value, axis, by):
+    devices = lax.axis_size(axis)
+    return lax.ppermute(value, axis, [(i, (i + by) % devices) for i in range(devices)])
+
+
+def over_span(to_up, to_down):
+    return shifted(to_down, "span", 1), shifted(to_up, "span", -1)
+
+
+def over_pitch(to_left, to_right):
+    return shifted(to_right, "pitch", 1), shifted(to_left, "pitch", -1)
 
 
 def on_device(
@@ -501,7 +503,7 @@
         in_specs=[HBM],
         scratch=[pltpu.SemaphoreType.DMA((4,))],
     )(in_hbm(adjoint))
-    halo = exchange(*edges)
+    halo = over_span(*edges[:2]) + over_pitch(*edges[2:])
     part, record, jac, src, tau = call(
         interior_kernel,
         "interior",
@@ -527,15 +529,15 @@
     records = lax.all_to_all(
         message.reshape(devices, 1, 2 * LANES), ("row", "span", "pitch"), 0, 0
     ).reshape(2 * devices, LANES)
-    halo = exchange(*sends)
+    halo = over_span(*sends[:2]) + over_pitch(*sends[2:])
     part, packs, ids, seen, picks = call(
         settle_kernel,
         "settle",
         [
-            block, (6, CS, CP, LANES), ((2 * devices, LANES), jnp.int32), (2, CS, CP, LANES),
+            block, (6, CS, CP, LANES), ((2 * devices, LANES), F32), (2, CS, CP, LANES),
             ((LANES, 3 * LANES), BF16),
         ],
-        in_specs=[SM] + [VM] * 6,
+        in_specs=[VM] * 7,
         scratch=[pltpu.VMEM((7 * NVAR, CS, CP, LANES), F32)],
         cost=pl.CostEstimate(flops=9_000_000, bytes_accessed=3_000_000, transcendentals=0),
     )(band_map, first, src, tau, jac, face_cell, face_owner)
@@ -552,6 +554,8 @@
         "cycle_update",
         [(1,) + block, (3 * peers, LANES)],
         in_specs=[SM] + [VM] * 14,
+        out_specs=(HBM, VM),
+        scratch=[pltpu.VMEM((1,) + block, F32), pltpu.SemaphoreType.DMA],
     )(
         band_map, part, full_record, packs, ids, records, *halo, seen, picks, faces, face_owner,
         face_weight,

time: 66 us -> 65.1 us (0.986)
  Pallas kernels: 11.5 us -> 9.82 us
  waiting for transfers between devices: 1.63 us -> 3.28 us
  blocking collectives: 21 us -> 20.2 us
    ppermute x8, waiting for transfers between devices: 0.9 us -> 2.55 us  [shifted(): lax.ppermute(value, axis, [(i, (i + by) % devices) for i in range(devices)])]
    pallas_call x1, Pallas kernels: 3.28 us -> 1.63 us  [on_device(): call(settle_kernel, 'settle', [block, (6, CS, CP, LANES), ((2 * devices,...]
    all_to_all x1, blocking collectives: 21 us -> 20.2 us  [on_device(): lax.all_to_all(dense.reshape(peers, 1, 3 * LANES), ('span', 'pitch'), 0, 0)]
  transfers between devices with their start and end apart: 9 -> 9, of which waited for: 3 -> 3; matrix products, arithmetic and copies ran while one was open for 0% -> 0% of each run, Pallas kernels for 9% -> 7%
where the time goes in v8:
time: 65.1 us; the launch traced here: 64.9 us
  starting transfers between devices  30.9 us (47%)
  blocking collectives  20.2 us (31%)
  Pallas kernels  9.82 us (15%)
  waiting for transfers between devices  3.28 us (5%)
  between operations  0.71 us (1%)
    ppermute x8, starting transfers between devices, shifted(): lax.ppermute(value, axis, [(i, (i + by) % devices) for i in range(devices)])  22.4 us
    all_to_all x1, blocking collectives, on_device(): lax.all_to_all(dense.reshape(peers, 1, 3 * LANES), ('span', 'pitch'), 0, 0)  20.2 us
    all_to_all x1, starting transfers between devices, on_device(): lax.all_to_all(message.reshape(devices, 1, 2 * LANES), ('row', 'span', 'p...  8.46 us
    ppermute x8, waiting for transfers between devices, shifted(): lax.ppermute(value, axis, [(i, (i + by) % devices) for i in range(devices)])  2.55 us
    pallas_call x1, Pallas kernels, on_device(): call(cycle_kernel, 'cycle_update', [(1,) + block, (3 * peers, LANES)], in...  2.5 us
    pallas_call x1, Pallas kernels, on_device(): call(interior_kernel, 'interior', [block, (CS, CP, LANES), ((7, NVAR) + b...  2.4 us
    pallas_call x1, Pallas kernels, on_device(): call(settle_kernel, 'settle', [block, (6, CS, CP, LANES), ((2 * devices,...  1.63 us
    pallas_call x1, Pallas kernels, on_device(): call(edge_kernel, 'edge_update', [block, (2 * devices, LANES), (CS, CP, L...  1.44 us
  transfers between devices with their start and end apart: 9, of which 3 were waited for; matrix products, arithmetic and copies ran while one was open for 0% of the time, Pallas kernels for 7%

profile of v8, /device:TPU:32, one launch (start us, length us, event | category | flops | bytes accessed | tf_op | source)
XLA Modules:
  0.0 64.9 jit_solution(15758313635551537191)
XLA Ops:
  0.6 0.8 %edges.1 = (f32[6,8,128]{2,1,0:T(8,128)S(1)}, f32[6,8,128]{2,1,0:T(8,128)S(1)}, f32[6,4,128]{2,1,0:T(4,128)S(1)}, f32[6,4,128]{2,1,0:T(4,128)S(1)}) custom-call(f32[1,6,4,8,128]{4,3,2,1,0:T(8,128)} %adj_ref.1), custom_call_target="tpu_custom_call" | custom-call | tf_op jit(solution)/shard_map/edges/pallas_call | solution.py:499
  1.5 1.6 %collective-permute-start = (f32[6,8,128]{2,1,0:T(8,128)S(1)}, f32[6,8,128]{2,1,0:T(8,128)S(1)}, u32[]{:S(2)}, u32[]{:S(2)}) collective-permute-start(f32[6,8,128]{2,1,0:T(8,128)S(1)} %get-tuple-element.31), channel_id=1, source_target_pairs={{0,4},{4,8},{8,12},{12,16},{16,20},{20,24},{24,28},{28,32},{32,36}... | collective-permute-start | bytes 73736 | tf_op jit(solution)/shard_map/ppermute | solution.py:479
  3.0 4.8 %collective-permute-start.1 = (f32[6,8,128]{2,1,0:T(8,128)S(1)}, f32[6,8,128]{2,1,0:T(8,128)S(1)}, u32[]{:S(2)}, u32[]{:S(2)}) collective-permute-start(f32[6,8,128]{2,1,0:T(8,128)S(1)} %get-tuple-element.32), channel_id=1, source_target_pairs={{0,124},{4,0},{8,4},{12,8},{16,12},{20,16},{24,20},{28,24},{32,28}... | collective-permute-start | bytes 73736 | tf_op jit(solution)/shard_map/ppermute | solution.py:479
  7.8 3.3 %collective-permute-start.2 = (f32[6,4,128]{2,1,0:T(4,128)S(1)}, f32[6,4,128]{2,1,0:T(4,128)S(1)}, u32[]{:S(2)}, u32[]{:S(2)}) collective-permute-start(f32[6,4,128]{2,1,0:T(4,128)S(1)} %get-tuple-element.33), channel_id=1, source_target_pairs={{0,1},{1,2},{2,3},{3,0},{4,5},{5,6},{6,7},{7,4},{8,9},{9,10},{10,1... | collective-permute-start | bytes 36872 | tf_op jit(solution)/shard_map/ppermute | solution.py:479
  11.1 2.2 %collective-permute-start.3 = (f32[6,4,128]{2,1,0:T(4,128)S(1)}, f32[6,4,128]{2,1,0:T(4,128)S(1)}, u32[]{:S(2)}, u32[]{:S(2)}) collective-permute-start(f32[6,4,128]{2,1,0:T(4,128)S(1)} %get-tuple-element.34), channel_id=1, source_target_pairs={{0,3},{1,0},{2,1},{3,2},{4,7},{5,4},{6,5},{7,6},{8,11},{9,8},{10,9... | collective-permute-start | bytes 36872 | tf_op jit(solution)/shard_map/ppermute | solution.py:479
  13.3 2.4 %interior.1 = (f32[6,4,8,128]{3,2,1,0:T(8,128)S(1)}, f32[4,8,128]{2,1,0:T(8,128)S(1)}, bf16[7,6,6,4,8,128]{5,4,3,2,1,0:T(8,128)(2,1)S(1)}, f32[6,4,8,128]{3,2,1,0:T(8,128)S(1)}, f32[4,8,128]{2,1,0:T(8,128)S(1)}) custom-call(f32[1,6,4,8,128]{4,3,2,1,0:T(8,128)} %adj_ref.1, f32[1,6,4,8,128]{4,3,2,1,0:T(8,128)} %src_hbm.1, f32[1,4,8,128]{3,2,1,0:T(8,128)} %tau_hbm.1, ...), custom_call_target="tpu_custom_call" | custom-call | flops 9000000 | bytes 3000000 | tf_op jit(solution)/shard_map/interior/pallas_call | solution.py:507
  15.7 0.0 collective-permute-done.2.left_ref
  15.7 0.7 %collective-permute-done.3.right_ref = f32[6,4,128]{2,1,0:T(4,128)S(1)} collective-permute-done((f32[6,4,128]{2,1,0:T(4,128)S(1)}, f32[6,4,128]{2,1,0:T(4,128)S(1)}, u32[]{:S(2)}, u32[]{:S(2)}) %collective-permute-start.3) | collective-permute-done | bytes 12320 | tf_op jit(solution)/shard_map/ppermute | solution.py:479
  16.4 1.4 %edge_update.1 = (f32[6,4,8,128]{3,2,1,0:T(8,128)S(1)}, f32[512,128]{1,0:T(8,128)}, f32[4,8,128]{2,1,0:T(8,128)S(1)}, f32[7,8,128]{2,1,0:T(8,128)S(1)}, f32[7,8,...) custom-call(f32[6,4,8,128]{3,2,1,0:T(8,128)S(1)} %get-tuple-element.27.part_ref, ...), custom_call_target="tpu_custom_call" | custom-call | tf_op jit(solution)/shard_map/edge_update/pallas_call | solution.py:522
  17.9 8.5 %all-to-all-start = ((f32[256,1,256]{2,1,0:T(1,128)}), f32[256,1,256]{2,1,0:T(1,128)S(1)}, u32[]{:S(2)}, u32[]{:S(2)}) async-start(f32[256,1,256]{2,1,0:T(1,128)} %bitcast), calls=%async_computation | async-start | bytes 524288 | tf_op jit(solution)/shard_map/all_to_all | solution.py:529
  26.3 1.6 %collective-permute-start.4 = (f32[7,8,128]{2,1,0:T(8,128)S(1)}, f32[7,8,128]{2,1,0:T(8,128)S(1)}, u32[]{:S(2)}, u32[]{:S(2)}) collective-permute-start(f32[7,8,128]{2,1,0:T(8,128)S(1)} %get-tuple-element.38), channel_id=1, source_target_pairs={{0,4},{4,8},{8,12},{12,16},{16,20},{20,24},{24,28},{28,32},{32,36}... | collective-permute-start | bytes 86024 | tf_op jit(solution)/shard_map/ppermute | solution.py:479
  27.9 4.8 %collective-permute-start.5 = (f32[7,8,128]{2,1,0:T(8,128)S(1)}, f32[7,8,128]{2,1,0:T(8,128)S(1)}, u32[]{:S(2)}, u32[]{:S(2)}) collective-permute-start(f32[7,8,128]{2,1,0:T(8,128)S(1)} %get-tuple-element.39), channel_id=1, source_target_pairs={{0,124},{4,0},{8,4},{12,8},{16,12},{20,16},{24,20},{28,24},{32,28}... | collective-permute-start | bytes 86024 | tf_op jit(solution)/shard_map/ppermute | solution.py:479
  32.6 2.9 %collective-permute-start.6 = (f32[7,4,128]{2,1,0:T(4,128)S(1)}, f32[7,4,128]{2,1,0:T(4,128)S(1)}, u32[]{:S(2)}, u32[]{:S(2)}) collective-permute-start(f32[7,4,128]{2,1,0:T(4,128)S(1)} %get-tuple-element.40), channel_id=1, source_target_pairs={{0,1},{1,2},{2,3},{3,0},{4,5},{5,6},{6,7},{7,4},{8,9},{9,10},{10,1... | collective-permute-start | bytes 43016 | tf_op jit(solution)/shard_map/ppermute | solution.py:479
  35.5 1.4 %collective-permute-start.7 = (f32[7,4,128]{2,1,0:T(4,128)S(1)}, f32[7,4,128]{2,1,0:T(4,128)S(1)}, u32[]{:S(2)}, u32[]{:S(2)}) collective-permute-start(f32[7,4,128]{2,1,0:T(4,128)S(1)} %get-tuple-element.41), channel_id=1, source_target_pairs={{0,3},{1,0},{2,1},{3,2},{4,7},{5,4},{6,5},{7,6},{8,11},{9,8},{10,9... | collective-permute-start | bytes 43016 | tf_op jit(solution)/shard_map/ppermute | solution.py:479
  37.0 1.6 %settle.1 = (f32[6,4,8,128]{3,2,1,0:T(8,128)S(1)}, f32[6,4,8,128]{3,2,1,0:T(8,128)S(1)}, f32[512,128]{1,0:T(8,128)S(1)}, f32[2,4,8,128]{3,2,1,0:T(8,128)S(1)}, bf16[128,384]{1,0:T(8,128)(2,1)S(1)}) custom-call(s32[2,128]{1,0:T(2,128)S(1)} %copy-done, f32[6,4,8,128]{3,2,1,0:T(8,128)S(1)} %get-tuple-element.35.f1_ref, ...), custom_call_target="tpu_custom_call" | custom-call | flops 9000000 | bytes 3000000 | tf_op jit(solution)/shard_map/settle/pallas_call | solution.py:533
  38.6 0.0 collective-permute-done.6.left_ref
  38.6 1.8 %collective-permute-done.7.right_ref = f32[7,4,128]{2,1,0:T(4,128)S(1)} collective-permute-done((f32[7,4,128]{2,1,0:T(4,128)S(1)}, f32[7,4,128]{2,1,0:T(4,128)S(1)}, u32[]{:S(2)}, u32[]{:S(2)}) %collective-permute-start.7) | collective-permute-done | bytes 14368 | tf_op jit(solution)/shard_map/ppermute | solution.py:479
  40.4 0.0 collective-permute-done.4.up_ref
  40.5 0.0 collective-permute-done.5.down_ref
  40.5 0.4 settle_edges.1
  40.9 0.7 %all-to-all-done = f32[256,1,256]{2,1,0:T(1,128)S(1)} async-done(((f32[256,1,256]{2,1,0:T(1,128)}), f32[256,1,256]{2,1,0:T(1,128)S(1)}, u32[]{:S(2)}, u32[]{:S(2)}) %all-to-all-start) | async-done | bytes 262176 | tf_op jit(solution)/shard_map/all_to_all | solution.py:529
  41.6 2.5 %cycle_update.1 = (f32[1,6,4,8,128]{4,3,2,1,0:T(8,128)}, f32[384,128]{1,0:T(8,128)S(1)}) custom-call(s32[2,128]{1,0:T(2,128)S(1)} %copy-done, f32[6,4,8,128]{3,2,1,0:T(8,128)S(1)} %get-tuple-element.42.part_ref, f32[4,8,128]{2,1,0:T(8,128)S(1)} %get-tuple-element.43.rec_ref, f32[6,4,8,128]{3,2,1,0:T(8,128)S(1)} %get-tuple-element.44.pack_ref, ...), custom_call_target="tpu_custom_call" | custom-call | tf_op jit(solution)/shard_map/cycle_update/pallas_call | solution.py:552
  44.1 20.2 %all_to_all.10 = f32[128,1,384]{2,1,0:T(1,128)S(1)} all-to-all(f32[128,1,384]{2,1,0:T(1,128)S(1)} %bitcast.7), channel_id=1, replica_groups=mesh['row'=2,'span'=32,'pitch'=4] {'span','pitch'}, dimensions={0} | all-to-all | bytes 393216 | tf_op jit(solution)/shard_map/all_to_all | solution.py:563
  64.3 0.6 node_sums.1
  (11 shorter events, 0.0 us)
Async XLA Ops:
  1.5 14.9 %collective-permute-start = (f32[6,8,128]{2,1,0:T(8,128)S(1)}, f32[6,8,128]{2,1,0:T(8,128)S(1)}, u32[]{:S(2)}, u32[]{:S(2)}) collective-permute-start(f32[6,8,128]{2,1,0:T(8,128)S(1)} %get-tuple-element.31), channel_id=1, source_target_pairs={{0,4},{4,8},{8,12},{12,16},{16,20},{20,24},{24,28},{28,32},{32,36}... | collective-permute-start | bytes 73736 | tf_op jit(solution)/shard_map/ppermute | solution.py:479
  3.0 13.4 %collective-permute-start.1 = (f32[6,8,128]{2,1,0:T(8,128)S(1)}, f32[6,8,128]{2,1,0:T(8,128)S(1)}, u32[]{:S(2)}, u32[]{:S(2)}) collective-permute-start(f32[6,8,128]{2,1,0:T(8,128)S(1)} %get-tuple-element.32), channel_id=1, source_target_pairs={{0,124},{4,0},{8,4},{12,8},{16,12},{20,16},{24,20},{28,24},{32,28}... | collective-permute-start | bytes 73736 | tf_op jit(solution)/shard_map/ppermute | solution.py:479
  7.8 7.9 %collective-permute-start.2 = (f32[6,4,128]{2,1,0:T(4,128)S(1)}, f32[6,4,128]{2,1,0:T(4,128)S(1)}, u32[]{:S(2)}, u32[]{:S(2)}) collective-permute-start(f32[6,4,128]{2,1,0:T(4,128)S(1)} %get-tuple-element.33), channel_id=1, source_target_pairs={{0,1},{1,2},{2,3},{3,0},{4,5},{5,6},{6,7},{7,4},{8,9},{9,10},{10,1... | collective-permute-start | bytes 36872 | tf_op jit(solution)/shard_map/ppermute | solution.py:479
  11.1 25.9 %copy-start.3 = (f32[1,1,1,18,128]{4,2,3,1,0:T(1,128)S(1)}, f32[1,1,1,18,128]{4,2,3,1,0:T(1,128)}, u32[]{:S(2)}) copy-start(f32[1,1,1,18,128]{4,2,3,1,0:T(1,128)} %param.15) | copy-start | bytes 27652
  11.1 25.9 %copy-start = (s32[2,128]{1,0:T(2,128)S(1)}, s32[2,128]{1,0:T(2,128)}, u32[]{:S(2)}) copy-start(s32[2,128]{1,0:T(2,128)} %bands_ref.3) | copy-start | bytes 3076
  11.1 25.9 %copy-start.1 = (s32[1,1,1,128]{3,2,1,0:T(1,128)S(1)}, s32[1,1,1,128]{3,2,1,0:T(1,128)}, u32[]{:S(2)}) copy-start(s32[1,1,1,128]{3,2,1,0:T(1,128)} %cell_ref.3) | copy-start | bytes 1540
  11.1 25.9 %copy-start.2 = (s32[1,1,1,128]{3,2,1,0:T(1,128)S(1)}, s32[1,1,1,128]{3,2,1,0:T(1,128)}, u32[]{:S(2)}) copy-start(s32[1,1,1,128]{3,2,1,0:T(1,128)} %owner_ref.3) | copy-start | bytes 1540
  11.1 5.3 %collective-permute-start.3 = (f32[6,4,128]{2,1,0:T(4,128)S(1)}, f32[6,4,128]{2,1,0:T(4,128)S(1)}, u32[]{:S(2)}, u32[]{:S(2)}) collective-permute-start(f32[6,4,128]{2,1,0:T(4,128)S(1)} %get-tuple-element.34), channel_id=1, source_target_pairs={{0,3},{1,0},{2,1},{3,2},{4,7},{5,4},{6,5},{7,6},{8,11},{9,8},{10,9... | collective-permute-start | bytes 36872 | tf_op jit(solution)/shard_map/ppermute | solution.py:479
  17.9 23.8 %all-to-all-start = ((f32[256,1,256]{2,1,0:T(1,128)}), f32[256,1,256]{2,1,0:T(1,128)S(1)}, u32[]{:S(2)}, u32[]{:S(2)}) async-start(f32[256,1,256]{2,1,0:T(1,128)} %bitcast), calls=%async_computation | async-start | bytes 524288 | tf_op jit(solution)/shard_map/all_to_all | solution.py:529
  26.3 14.1 %collective-permute-start.4 = (f32[7,8,128]{2,1,0:T(8,128)S(1)}, f32[7,8,128]{2,1,0:T(8,128)S(1)}, u32[]{:S(2)}, u32[]{:S(2)}) collective-permute-start(f32[7,8,128]{2,1,0:T(8,128)S(1)} %get-tuple-element.38), channel_id=1, source_target_pairs={{0,4},{4,8},{8,12},{12,16},{16,20},{20,24},{24,28},{28,32},{32,36}... | collective-permute-start | bytes 86024 | tf_op jit(solution)/shard_map/ppermute | solution.py:479
  27.9 12.6 %collective-permute-start.5 = (f32[7,8,128]{2,1,0:T(8,128)S(1)}, f32[7,8,128]{2,1,0:T(8,128)S(1)}, u32[]{:S(2)}, u32[]{:S(2)}) collective-permute-start(f32[7,8,128]{2,1,0:T(8,128)S(1)} %get-tuple-element.39), channel_id=1, source_target_pairs={{0,124},{4,0},{8,4},{12,8},{16,12},{20,16},{24,20},{28,24},{32,28}... | collective-permute-start | bytes 86024 | tf_op jit(solution)/shard_map/ppermute | solution.py:479
  32.6 6.0 %collective-permute-start.6 = (f32[7,4,128]{2,1,0:T(4,128)S(1)}, f32[7,4,128]{2,1,0:T(4,128)S(1)}, u32[]{:S(2)}, u32[]{:S(2)}) collective-permute-start(f32[7,4,128]{2,1,0:T(4,128)S(1)} %get-tuple-element.40), channel_id=1, source_target_pairs={{0,1},{1,2},{2,3},{3,0},{4,5},{5,6},{6,7},{7,4},{8,9},{9,10},{10,1... | collective-permute-start | bytes 43016 | tf_op jit(solution)/shard_map/ppermute | solution.py:479
  35.5 4.9 %collective-permute-start.7 = (f32[7,4,128]{2,1,0:T(4,128)S(1)}, f32[7,4,128]{2,1,0:T(4,128)S(1)}, u32[]{:S(2)}, u32[]{:S(2)}) collective-permute-start(f32[7,4,128]{2,1,0:T(4,128)S(1)} %get-tuple-element.41), channel_id=1, source_target_pairs={{0,3},{1,0},{2,1},{3,2},{4,7},{5,4},{6,5},{7,6},{8,11},{9,8},{10,9... | collective-permute-start | bytes 43016 | tf_op jit(solution)/shard_map/ppermute | solution.py:479

commit v9 on v8

--- a/solution.py
+++ b/solution.py
@@ -14,6 +14,7 @@
 FIRST_AT = 8
 WEIGHT_AT = 16
 COUNT_AT = 6
+PITCH_PAD = 7
 
 
 def lane_ids(shape):
@@ -67,16 +68,19 @@
     return acc
 
 
-def edges_kernel(adj_ref, up_ref, down_ref, left_ref, right_ref, sems):
+def edges_kernel(adj_ref, left_ref, right_ref, up_ref, down_ref, sems):
     adj = adj_ref.at[0]
+    left_rows, right_rows = (ref.at[:NVAR] for ref in (left_ref, right_ref))
     copies = [
         pltpu.make_async_copy(adj.at[:, 0], up_ref, sems.at[0]),
         pltpu.make_async_copy(adj.at[:, CS - 1], down_ref, sems.at[1]),
-        pltpu.make_async_copy(adj.at[:, :, 0], left_ref, sems.at[2]),
-        pltpu.make_async_copy(adj.at[:, :, CP - 1], right_ref, sems.at[3]),
+        pltpu.make_async_copy(adj.at[:, :, 0], left_rows, sems.at[2]),
+        pltpu.make_async_copy(adj.at[:, :, CP - 1], right_rows, sems.at[3]),
     ]
     for copy in copies:
         copy.start()
+    for ref in (left_ref, right_ref):
+        ref[NVAR:] = jnp.zeros((PITCH_PAD, CS, LANES), F32)
     for copy in copies:
         copy.wait()
 
@@ -180,8 +184,8 @@
 
 
 def edge_kernel(
-    part_ref, rec_in, jac_ref, tau_ref, up_ref, down_ref, left_ref, right_ref,
-    f1_ref, msg_ref, rec, to_up_ref, to_down_ref, to_left_ref, to_right_ref, sides,
+    part_ref, rec_in, jac_ref, tau_ref, left_ref, right_ref, up_ref, down_ref,
+    f1_ref, msg_ref, rec, to_left_ref, to_right_ref, to_up_ref, to_down_ref, sides,
 ):
     row = lax.axis_index("row")
     keep = inner_sides()
@@ -219,6 +223,8 @@
         to_right_ref[c] = f1_ref[c, :, CP - 1, :]
     to_left_ref[NVAR] = rec[:, 0, :]
     to_right_ref[NVAR] = rec[:, CP - 1, :]
+    for ref in (to_left_ref, to_right_ref):
+        ref[NVAR + 1 :] = jnp.zeros((PITCH_PAD + 1, CS, LANES), F32)
 
 
 def weight_sum(x):
@@ -316,7 +322,7 @@
 
 
 def settle_edges_kernel(
-    part_ref, jac_ref, tau_ref, up_ref, down_ref, left_ref, right_ref, cell_ref,
+    part_ref, jac_ref, tau_ref, left_ref, right_ref, up_ref, down_ref, cell_ref,
     part2_ref, face_ref, sides,
 ):
     keep = inner_sides()
@@ -341,7 +347,7 @@
 
 
 def cycle_kernel(
-    bands_ref, part_ref, rec_ref, pack_ref, ids_ref, all_ref, up_ref, down_ref, left_ref, right_ref,
+    bands_ref, part_ref, rec_ref, pack_ref, ids_ref, all_ref, left_ref, right_ref, up_ref, down_ref,
     seen_ref, node_ref, face_ref, owner_ref, weight_ref, out_hbm, dense_ref, field, sem,
 ):
     row = lax.axis_index("row")
@@ -495,15 +501,15 @@
     peers = spans * pitches
     block = (NVAR, CS, CP, LANES)
     edge = (NVAR, CP, LANES)
-    side = (NVAR, CS, LANES)
+    side = (NVAR + PITCH_PAD, CS, LANES)
     edges = call(
         edges_kernel,
         "edges",
-        [edge, edge, side, side],
+        [side, side, edge, edge],
         in_specs=[HBM],
         scratch=[pltpu.SemaphoreType.DMA((4,))],
     )(in_hbm(adjoint))
-    halo = over_span(*edges[:2]) + over_pitch(*edges[2:])
+    halo = over_pitch(*edges[:2]) + over_span(*edges[2:])
     part, record, jac, src, tau = call(
         interior_kernel,
         "interior",
@@ -518,18 +524,18 @@
         cost=pl.CostEstimate(flops=9_000_000, bytes_accessed=3_000_000, transcendentals=0),
     )(*(in_hbm(x) for x in (adjoint, source, pseudo_step, jac_blocks)))
     edge = (NVAR + 1, CP, LANES)
-    side = (NVAR + 1, CS, LANES)
+    side = (NVAR + 1 + PITCH_PAD + 1, CS, LANES)
     first, message, full_record, *sends = call(
         edge_kernel,
         "edge_update",
-        [block, (2 * devices, LANES), (CS, CP, LANES), edge, edge, side, side],
+        [block, (2 * devices, LANES), (CS, CP, LANES), side, side, edge, edge],
         in_specs=[VM] * 8,
         scratch=[pltpu.VMEM((2 * NVAR, CS, CP, LANES), F32)],
     )(part, record, jac, tau, *halo)
     records = lax.all_to_all(
         message.reshape(devices, 1, 2 * LANES), ("row", "span", "pitch"), 0, 0
     ).reshape(2 * devices, LANES)
-    halo = over_span(*sends[:2]) + over_pitch(*sends[2:])
+    halo = over_pitch(*sends[:2]) + over_span(*sends[2:])
     part, packs, ids, seen, picks = call(
         settle_kernel,
         "settle",

time: 65.1 us -> 72.2 us (1.11)
  starting transfers between devices: 30.9 us -> 35.1 us
  blocking collectives: 20.2 us -> 24.1 us
  waiting for transfers between devices: 3.28 us -> 2.21 us
    all_to_all x1, starting transfers between devices: 8.46 us -> 12.5 us  [on_device(): lax.all_to_all(message.reshape(devices, 1, 2 * LANES), ('row', 'span', 'p...]
    all_to_all x1, blocking collectives: 20.2 us -> 24.1 us  [on_device(): lax.all_to_all(dense.reshape(peers, 1, 3 * LANES), ('span', 'pitch'), 0, 0)]
    ppermute x8, waiting for transfers between devices: 2.55 us -> 0.48 us  [shifted(): lax.ppermute(value, axis, [(i, (i + by) % devices) for i in range(devices)])]
    all_to_all x1, waiting for transfers between devices: 0.73 us -> 1.72 us  [on_device(): lax.all_to_all(message.reshape(devices, 1, 2 * LANES), ('row', 'span', 'p...]
  transfers between devices with their start and end apart: 9 -> 9, of which waited for: 3 -> 2; matrix products, arithmetic and copies ran while one was open for 0% -> 0% of each run, Pallas kernels for 7% -> 6%
where the time goes in v9:
time: 72.2 us; the launch traced here: 72 us
  starting transfers between devices  35.1 us (49%)
  blocking collectives  24.1 us (33%)
  Pallas kernels  9.83 us (14%)
  waiting for transfers between devices  2.21 us (3%)
  between operations  0.74 us (1%)
    all_to_all x1, blocking collectives, on_device(): lax.all_to_all(dense.reshape(peers, 1, 3 * LANES), ('span', 'pitch'), 0, 0)  24.1 us
    ppermute x8, starting transfers between devices, shifted(): lax.ppermute(value, axis, [(i, (i + by) % devices) for i in range(devices)])  22.6 us
    all_to_all x1, starting transfers between devices, on_device(): lax.all_to_all(message.reshape(devices, 1, 2 * LANES), ('row', 'span', 'p...  12.5 us
    pallas_call x1, Pallas kernels, on_device(): call(cycle_kernel, 'cycle_update', [(1,) + block, (3 * peers, LANES)], in...  2.5 us
    pallas_call x1, Pallas kernels, on_device(): call(interior_kernel, 'interior', [block, (CS, CP, LANES), ((7, NVAR) + b...  2.4 us
    all_to_all x1, waiting for transfers between devices, on_device(): lax.all_to_all(message.reshape(devices, 1, 2 * LANES), ('row', 'span', 'p...  1.72 us
    pallas_call x1, Pallas kernels, on_device(): call(settle_kernel, 'settle', [block, (6, CS, CP, LANES), ((2 * devices,...  1.63 us
  transfers between devices with their start and end apart: 9, of which 2 were waited for; matrix products, arithmetic and copies ran while one was open for 0% of the time, Pallas kernels for 6%

profile of v9, /device:TPU:32, one launch (start us, length us, event | category | flops | bytes accessed | tf_op | source)
XLA Modules:
  0.0 72.0 jit_solution(13957373836584449333)
XLA Ops:
  0.6 0.8 %edges.1 = (f32[13,4,128]{2,1,0:T(4,128)S(1)}, f32[13,4,128]{2,1,0:T(4,128)S(1)}, f32[6,8,128]{2,1,0:T(8,128)S(1)}, f32[6,8,128]{2,1,0:T(8,128)S(1)}) custom-call(f32[1,6,4,8,128]{4,3,2,1,0:T(8,128)} %adj_ref.1), custom_call_target="tpu_custom_call" | custom-call | tf_op jit(solution)/shard_map/edges/pallas_call | solution.py:505
  1.5 3.3 %collective-permute-start = (f32[13,4,128]{2,1,0:T(4,128)S(1)}, f32[13,4,128]{2,1,0:T(4,128)S(1)}, u32[]{:S(2)}, u32[]{:S(2)}) collective-permute-start(f32[13,4,128]{2,1,0:T(4,128)S(1)} %get-tuple-element.31), channel_id=1, source_target_pairs={{0,1},{1,2},{2,3},{3,0},{4,5},{5,6},{6,7},{7,4},{8,9},{9,10},{10,1... | collective-permute-start | bytes 79880 | tf_op jit(solution)/shard_map/ppermute | solution.py:485
  4.8 2.2 %collective-permute-start.1 = (f32[13,4,128]{2,1,0:T(4,128)S(1)}, f32[13,4,128]{2,1,0:T(4,128)S(1)}, u32[]{:S(2)}, u32[]{:S(2)}) collective-permute-start(f32[13,4,128]{2,1,0:T(4,128)S(1)} %get-tuple-element.32), channel_id=1, source_target_pairs={{0,3},{1,0},{2,1},{3,2},{4,7},{5,4},{6,5},{7,6},{8,11},{9,8},{10,9... | collective-permute-start | bytes 79880 | tf_op jit(solution)/shard_map/ppermute | solution.py:485
  7.0 1.5 %collective-permute-start.2 = (f32[6,8,128]{2,1,0:T(8,128)S(1)}, f32[6,8,128]{2,1,0:T(8,128)S(1)}, u32[]{:S(2)}, u32[]{:S(2)}) collective-permute-start(f32[6,8,128]{2,1,0:T(8,128)S(1)} %get-tuple-element.33), channel_id=1, source_target_pairs={{0,4},{4,8},{8,12},{12,16},{16,20},{20,24},{24,28},{28,32},{32,36}... | collective-permute-start | bytes 73736 | tf_op jit(solution)/shard_map/ppermute | solution.py:485
  8.5 4.8 %collective-permute-start.3 = (f32[6,8,128]{2,1,0:T(8,128)S(1)}, f32[6,8,128]{2,1,0:T(8,128)S(1)}, u32[]{:S(2)}, u32[]{:S(2)}) collective-permute-start(f32[6,8,128]{2,1,0:T(8,128)S(1)} %get-tuple-element.34), channel_id=1, source_target_pairs={{0,124},{4,0},{8,4},{12,8},{16,12},{20,16},{24,20},{28,24},{32,28}... | collective-permute-start | bytes 73736 | tf_op jit(solution)/shard_map/ppermute | solution.py:485
  13.4 2.4 %interior.1 = (f32[6,4,8,128]{3,2,1,0:T(8,128)S(1)}, f32[4,8,128]{2,1,0:T(8,128)S(1)}, bf16[7,6,6,4,8,128]{5,4,3,2,1,0:T(8,128)(2,1)S(1)}, f32[6,4,8,128]{3,2,1,0:T(8,128)S(1)}, f32[4,8,128]{2,1,0:T(8,128)S(1)}) custom-call(f32[1,6,4,8,128]{4,3,2,1,0:T(8,128)} %adj_ref.1, f32[1,6,4,8,128]{4,3,2,1,0:T(8,128)} %src_hbm.1, f32[1,4,8,128]{3,2,1,0:T(8,128)} %tau_hbm.1, ...), custom_call_target="tpu_custom_call" | custom-call | flops 9000000 | bytes 3000000 | tf_op jit(solution)/shard_map/interior/pallas_call | solution.py:513
  15.8 0.0 collective-permute-done.3.down_ref
  15.8 0.0 collective-permute-done.left_ref
  15.8 1.4 %edge_update.1 = (f32[6,4,8,128]{3,2,1,0:T(8,128)S(1)}, f32[512,128]{1,0:T(8,128)}, f32[4,8,128]{2,1,0:T(8,128)S(1)}, f32[15,4,128]{2,1,0:T(4,128)S(1)}, f32[15,...) custom-call(f32[6,4,8,128]{3,2,1,0:T(8,128)S(1)} %get-tuple-element.27.part_ref, ...), custom_call_target="tpu_custom_call" | custom-call | tf_op jit(solution)/shard_map/edge_update/pallas_call | solution.py:528
  17.3 12.5 %all-to-all-start = ((f32[256,1,256]{2,1,0:T(1,128)}), f32[256,1,256]{2,1,0:T(1,128)S(1)}, u32[]{:S(2)}, u32[]{:S(2)}) async-start(f32[256,1,256]{2,1,0:T(1,128)} %bitcast), calls=%async_computation | async-start | bytes 524288 | tf_op jit(solution)/shard_map/all_to_all | solution.py:535
  29.8 3.0 %collective-permute-start.4 = (f32[15,4,128]{2,1,0:T(4,128)S(1)}, f32[15,4,128]{2,1,0:T(4,128)S(1)}, u32[]{:S(2)}, u32[]{:S(2)}) collective-permute-start(f32[15,4,128]{2,1,0:T(4,128)S(1)} %get-tuple-element.38), channel_id=1, source_target_pairs={{0,1},{1,2},{2,3},{3,0},{4,5},{5,6},{6,7},{7,4},{8,9},{9,10},{10,1... | collective-permute-start | bytes 92168 | tf_op jit(solution)/shard_map/ppermute | solution.py:485
  32.8 1.5 %collective-permute-start.5 = (f32[15,4,128]{2,1,0:T(4,128)S(1)}, f32[15,4,128]{2,1,0:T(4,128)S(1)}, u32[]{:S(2)}, u32[]{:S(2)}) collective-permute-start(f32[15,4,128]{2,1,0:T(4,128)S(1)} %get-tuple-element.39), channel_id=1, source_target_pairs={{0,3},{1,0},{2,1},{3,2},{4,7},{5,4},{6,5},{7,6},{8,11},{9,8},{10,9... | collective-permute-start | bytes 92168 | tf_op jit(solution)/shard_map/ppermute | solution.py:485
  34.2 1.5 %collective-permute-start.6 = (f32[7,8,128]{2,1,0:T(8,128)S(1)}, f32[7,8,128]{2,1,0:T(8,128)S(1)}, u32[]{:S(2)}, u32[]{:S(2)}) collective-permute-start(f32[7,8,128]{2,1,0:T(8,128)S(1)} %get-tuple-element.40), channel_id=1, source_target_pairs={{0,4},{4,8},{8,12},{12,16},{16,20},{20,24},{24,28},{28,32},{32,36}... | collective-permute-start | bytes 86024 | tf_op jit(solution)/shard_map/ppermute | solution.py:485
  35.7 4.8 %collective-permute-start.7 = (f32[7,8,128]{2,1,0:T(8,128)S(1)}, f32[7,8,128]{2,1,0:T(8,128)S(1)}, u32[]{:S(2)}, u32[]{:S(2)}) collective-permute-start(f32[7,8,128]{2,1,0:T(8,128)S(1)} %get-tuple-element.41), channel_id=1, source_target_pairs={{0,124},{4,0},{8,4},{12,8},{16,12},{20,16},{24,20},{28,24},{32,28}... | collective-permute-start | bytes 86024 | tf_op jit(solution)/shard_map/ppermute | solution.py:485
  40.5 1.6 %settle.1 = (f32[6,4,8,128]{3,2,1,0:T(8,128)S(1)}, f32[6,4,8,128]{3,2,1,0:T(8,128)S(1)}, f32[512,128]{1,0:T(8,128)S(1)}, f32[2,4,8,128]{3,2,1,0:T(8,128)S(1)}, bf16[128,384]{1,0:T(8,128)(2,1)S(1)}) custom-call(s32[2,128]{1,0:T(2,128)S(1)} %copy-done, f32[6,4,8,128]{3,2,1,0:T(8,128)S(1)} %get-tuple-element.35.f1_ref, ...), custom_call_target="tpu_custom_call" | custom-call | flops 9000000 | bytes 3000000 | tf_op jit(solution)/shard_map/settle/pallas_call | solution.py:539
  42.2 0.5 collective-permute-done.6.up_ref
  42.6 0.0 collective-permute-done.7.down_ref
  42.6 0.0 collective-permute-done.4.left_ref
  42.6 0.0 collective-permute-done.5.right_ref
  42.6 0.4 settle_edges.1
  43.1 1.7 %all-to-all-done = f32[256,1,256]{2,1,0:T(1,128)S(1)} async-done(((f32[256,1,256]{2,1,0:T(1,128)}), f32[256,1,256]{2,1,0:T(1,128)S(1)}, u32[]{:S(2)}, u32[]{:S(2)}) %all-to-all-start) | async-done | bytes 262176 | tf_op jit(solution)/shard_map/all_to_all | solution.py:535
  44.8 2.5 %cycle_update.1 = (f32[1,6,4,8,128]{4,3,2,1,0:T(8,128)}, f32[384,128]{1,0:T(8,128)S(1)}) custom-call(s32[2,128]{1,0:T(2,128)S(1)} %copy-done, f32[6,4,8,128]{3,2,1,0:T(8,128)S(1)} %get-tuple-element.42.part_ref, f32[4,8,128]{2,1,0:T(8,128)S(1)} %get-tuple-element.43.rec_ref, f32[6,4,8,128]{3,2,1,0:T(8,128)S(1)} %get-tuple-element.44.pack_ref, ...), custom_call_target="tpu_custom_call" | custom-call | tf_op jit(solution)/shard_map/cycle_update/pallas_call | solution.py:558
  47.3 24.1 %all_to_all.10 = f32[128,1,384]{2,1,0:T(1,128)S(1)} all-to-all(f32[128,1,384]{2,1,0:T(1,128)S(1)} %bitcast.7), channel_id=1, replica_groups=mesh['row'=2,'span'=32,'pitch'=4] {'span','pitch'}, dimensions={0} | all-to-all | bytes 393216 | tf_op jit(solution)/shard_map/all_to_all | solution.py:569
  71.4 0.6 node_sums.1
  (11 shorter events, 0.0 us)
Async XLA Ops:
  1.5 14.3 %collective-permute-start = (f32[13,4,128]{2,1,0:T(4,128)S(1)}, f32[13,4,128]{2,1,0:T(4,128)S(1)}, u32[]{:S(2)}, u32[]{:S(2)}) collective-permute-start(f32[13,4,128]{2,1,0:T(4,128)S(1)} %get-tuple-element.31), channel_id=1, source_target_pairs={{0,1},{1,2},{2,3},{3,0},{4,5},{5,6},{6,7},{7,4},{8,9},{9,10},{10,1... | collective-permute-start | bytes 79880 | tf_op jit(solution)/shard_map/ppermute | solution.py:485
  4.8 11.0 %collective-permute-start.1 = (f32[13,4,128]{2,1,0:T(4,128)S(1)}, f32[13,4,128]{2,1,0:T(4,128)S(1)}, u32[]{:S(2)}, u32[]{:S(2)}) collective-permute-start(f32[13,4,128]{2,1,0:T(4,128)S(1)} %get-tuple-element.32), channel_id=1, source_target_pairs={{0,3},{1,0},{2,1},{3,2},{4,7},{5,4},{6,5},{7,6},{8,11},{9,8},{10,9... | collective-permute-start | bytes 79880 | tf_op jit(solution)/shard_map/ppermute | solution.py:485
  7.0 8.7 %collective-permute-start.2 = (f32[6,8,128]{2,1,0:T(8,128)S(1)}, f32[6,8,128]{2,1,0:T(8,128)S(1)}, u32[]{:S(2)}, u32[]{:S(2)}) collective-permute-start(f32[6,8,128]{2,1,0:T(8,128)S(1)} %get-tuple-element.33), channel_id=1, source_target_pairs={{0,4},{4,8},{8,12},{12,16},{16,20},{20,24},{24,28},{28,32},{32,36}... | collective-permute-start | bytes 73736 | tf_op jit(solution)/shard_map/ppermute | solution.py:485
  8.5 32.0 %copy-start.3 = (f32[1,1,1,18,128]{4,2,3,1,0:T(1,128)S(1)}, f32[1,1,1,18,128]{4,2,3,1,0:T(1,128)}, u32[]{:S(2)}) copy-start(f32[1,1,1,18,128]{4,2,3,1,0:T(1,128)} %param.15) | copy-start | bytes 27652
  8.5 32.0 %copy-start = (s32[2,128]{1,0:T(2,128)S(1)}, s32[2,128]{1,0:T(2,128)}, u32[]{:S(2)}) copy-start(s32[2,128]{1,0:T(2,128)} %bands_ref.3) | copy-start | bytes 3076
  8.5 32.0 %copy-start.1 = (s32[1,1,1,128]{3,2,1,0:T(1,128)S(1)}, s32[1,1,1,128]{3,2,1,0:T(1,128)}, u32[]{:S(2)}) copy-start(s32[1,1,1,128]{3,2,1,0:T(1,128)} %cell_ref.3) | copy-start | bytes 1540
  8.5 32.0 %copy-start.2 = (s32[1,1,1,128]{3,2,1,0:T(1,128)S(1)}, s32[1,1,1,128]{3,2,1,0:T(1,128)}, u32[]{:S(2)}) copy-start(s32[1,1,1,128]{3,2,1,0:T(1,128)} %owner_ref.3) | copy-start | bytes 1540
  8.5 7.3 %collective-permute-start.3 = (f32[6,8,128]{2,1,0:T(8,128)S(1)}, f32[6,8,128]{2,1,0:T(8,128)S(1)}, u32[]{:S(2)}, u32[]{:S(2)}) collective-permute-start(f32[6,8,128]{2,1,0:T(8,128)S(1)} %get-tuple-element.34), channel_id=1, source_target_pairs={{0,124},{4,0},{8,4},{12,8},{16,12},{20,16},{24,20},{28,24},{32,28}... | collective-permute-start | bytes 73736 | tf_op jit(solution)/shard_map/ppermute | solution.py:485
  17.3 27.5 %all-to-all-start = ((f32[256,1,256]{2,1,0:T(1,128)}), f32[256,1,256]{2,1,0:T(1,128)S(1)}, u32[]{:S(2)}, u32[]{:S(2)}) async-start(f32[256,1,256]{2,1,0:T(1,128)} %bitcast), calls=%async_computation | async-start | bytes 524288 | tf_op jit(solution)/shard_map/all_to_all | solution.py:535
  29.8 12.8 %collective-permute-start.4 = (f32[15,4,128]{2,1,0:T(4,128)S(1)}, f32[15,4,128]{2,1,0:T(4,128)S(1)}, u32[]{:S(2)}, u32[]{:S(2)}) collective-permute-start(f32[15,4,128]{2,1,0:T(4,128)S(1)} %get-tuple-element.38), channel_id=1, source_target_pairs={{0,1},{1,2},{2,3},{3,0},{4,5},{5,6},{6,7},{7,4},{8,9},{9,10},{10,1... | collective-permute-start | bytes 92168 | tf_op jit(solution)/shard_map/ppermute | solution.py:485
  32.8 9.9 %collective-permute-start.5 = (f32[15,4,128]{2,1,0:T(4,128)S(1)}, f32[15,4,128]{2,1,0:T(4,128)S(1)}, u32[]{:S(2)}, u32[]{:S(2)}) collective-permute-start(f32[15,4,128]{2,1,0:T(4,128)S(1)} %get-tuple-element.39), channel_id=1, source_target_pairs={{0,3},{1,0},{2,1},{3,2},{4,7},{5,4},{6,5},{7,6},{8,11},{9,8},{10,9... | collective-permute-start | bytes 92168 | tf_op jit(solution)/shard_map/ppermute | solution.py:485
  34.2 8.4 %collective-permute-start.6 = (f32[7,8,128]{2,1,0:T(8,128)S(1)}, f32[7,8,128]{2,1,0:T(8,128)S(1)}, u32[]{:S(2)}, u32[]{:S(2)}) collective-permute-start(f32[7,8,128]{2,1,0:T(8,128)S(1)} %get-tuple-element.40), channel_id=1, source_target_pairs={{0,4},{4,8},{8,12},{12,16},{16,20},{20,24},{24,28},{28,32},{32,36}... | collective-permute-start | bytes 86024 | tf_op jit(solution)/shard_map/ppermute | solution.py:485
  35.7 6.9 %collective-permute-start.7 = (f32[7,8,128]{2,1,0:T(8,128)S(1)}, f32[7,8,128]{2,1,0:T(8,128)S(1)}, u32[]{:S(2)}, u32[]{:S(2)}) collective-permute-start(f32[7,8,128]{2,1,0:T(8,128)S(1)} %get-tuple-element.41), channel_id=1, source_target_pairs={{0,124},{4,0},{8,4},{12,8},{16,12},{20,16},{24,20},{28,24},{32,28}... | collective-permute-start | bytes 86024 | tf_op jit(solution)/shard_map/ppermute | solution.py:485

commit v10 on v8

--- a/solution.py
+++ b/solution.py
@@ -181,7 +181,7 @@
 
 def edge_kernel(
     part_ref, rec_in, jac_ref, tau_ref, up_ref, down_ref, left_ref, right_ref,
-    f1_ref, msg_ref, rec, to_up_ref, to_down_ref, to_left_ref, to_right_ref, sides,
+    f1_ref, msg_hbm, rec, to_up_ref, to_down_ref, to_left_ref, to_right_ref, sides, copies, sems,
 ):
     row = lax.axis_index("row")
     keep = inner_sides()
@@ -208,8 +208,15 @@
         jnp.broadcast_to(rows[2 * h] + pltpu.roll(rows[2 * h + 1], 64, 1), tile) for h in range(2)
     ]
     packed = jnp.where(sub % 2 == 0, halves[0], halves[1])
-    for i in range(msg_ref.shape[0] // CP):
-        msg_ref[CP * i : CP * (i + 1)] = packed
+    lines = copies.shape[0]
+    for i in range(lines // CP):
+        copies[CP * i : CP * (i + 1)] = packed
+    writes = [
+        pltpu.make_async_copy(copies, msg_hbm.at[pl.ds(lines * i, lines)], sems.at[i])
+        for i in range(msg_hbm.shape[0] // lines)
+    ]
+    for write in writes:
+        write.start()
     to_up_ref[0:NVAR] = f1_ref[:, 0]
     to_up_ref[NVAR] = rec[0]
     to_down_ref[0:NVAR] = f1_ref[:, CS - 1]
@@ -219,6 +226,8 @@
         to_right_ref[c] = f1_ref[c, :, CP - 1, :]
     to_left_ref[NVAR] = rec[:, 0, :]
     to_right_ref[NVAR] = rec[:, CP - 1, :]
+    for write in writes:
+        write.wait()
 
 
 def weight_sum(x):
@@ -405,21 +414,30 @@
             sub == CP - 1, jnp.broadcast_to(right[j : j + 1], tile), pltpu.roll(x, CP - 1, 0)
         )
         changes.append((weight_sum(total) - own[j][0], weight_sum(pack_ref[5, j] * x)))
+    wide = [
+        [
+            [jnp.broadcast_to(x[:, WEIGHT_AT + c : WEIGHT_AT + c + 1], tile) for x in changes[j]]
+            for j in range(CS)
+        ]
+        for c in range(NVAR)
+    ]
+    for c in range(NVAR):
+        for j in range(CS):
+            first, second = wide[c][j]
+            moved = jnp.where(lane == outlet, first, jnp.where(lane == inner, second, 0.0))
+            field[0, c, j] = part_ref[c, j] + moved
+    write = pltpu.make_async_copy(field, out_hbm, sem)
+    write.start()
     terms = [jnp.zeros((1, LANES), F32)] * 3
     for c in range(NVAR):
-        at = WEIGHT_AT + c
         seen = zero
         for j in range(CS):
-            first, second = (jnp.broadcast_to(x[:, at : at + 1], tile) for x in changes[j])
-            moved = jnp.where(lane == outlet, first, jnp.where(lane == inner, second, 0.0))
-            field[0, c, j] = part_ref[c, j] + moved
+            first, second = wide[c][j]
             seen = seen + (seen_ref[0, j] * first + seen_ref[1, j] * second)
         value = face_ref[c : c + 1] + jnp.sum(seen, axis=0, keepdims=True)
         for k in range(3):
             at = NVAR * k + c
             terms[k] = terms[k] + weight_ref[0, 0, 0, at : at + 1] * value
-    write = pltpu.make_async_copy(field, out_hbm, sem)
-    write.start()
     shape = dense_ref.shape
     line = row_ids(shape)
     device = (line * 43691) >> 17
@@ -439,13 +457,6 @@
         preferred_element_type=F32,
     )
     write.wait()
-
-
-def third_kernel(parts_ref, out_ref):
-    folded = jnp.sum(parts_ref[...].reshape(-1, 24, LANES), axis=0)
-    coord = row_ids(folded.shape) % 3
-    for k in range(3):
-        out_ref[k] = jnp.sum(jnp.where(coord == k, folded, 0.0), axis=0, keepdims=True)
 
 
 VM = pl.BlockSpec(memory_space=pltpu.VMEM)
@@ -524,7 +535,12 @@
         "edge_update",
         [block, (2 * devices, LANES), (CS, CP, LANES), edge, edge, side, side],
         in_specs=[VM] * 8,
-        scratch=[pltpu.VMEM((2 * NVAR, CS, CP, LANES), F32)],
+        out_specs=(VM, HBM) + (VM,) * 5,
+        scratch=[
+            pltpu.VMEM((2 * NVAR, CS, CP, LANES), F32),
+            pltpu.VMEM((2 * devices // 8, LANES), F32),
+            pltpu.SemaphoreType.DMA((8,)),
+        ],
     )(part, record, jac, tau, *halo)
     records = lax.all_to_all(
         message.reshape(devices, 1, 2 * LANES), ("row", "span", "pitch"), 0, 0
@@ -561,10 +577,8 @@
         face_weight,
     )
     parts = lax.all_to_all(dense.reshape(peers, 1, 3 * LANES), ("span", "pitch"), 0, 0)
-    (nodes,) = call(third_kernel, "node_sums", [(3, 1, LANES)], in_specs=[VM])(
-        parts.reshape(3 * peers, LANES)
-    )
-    return field, nodes.transpose(1, 0, 2)
+    nodes = jnp.sum(parts, axis=(0, 1)).reshape(1, 3, LANES)
+    return field, nodes
 
 
 def solution(mesh):

time: 65.1 us -> 65.4 us (level)
  no operation moved by 1% of the time
where the time goes in v10:
time: 65.4 us; the launch traced here: 65.1 us
  starting transfers between devices  30.9 us (47%)
  blocking collectives  20.2 us (31%)
  Pallas kernels  9.3 us (14%)
  waiting for transfers between devices  3.28 us (5%)
  between operations  0.72 us (1%)
    ppermute x8, starting transfers between devices, shifted(): lax.ppermute(value, axis, [(i, (i + by) % devices) for i in range(devices)])  22.4 us
    all_to_all x1, blocking collectives, on_device(): lax.all_to_all(dense.reshape(peers, 1, 3 * LANES), ('span', 'pitch'), 0, 0)  20.2 us
    all_to_all x1, starting transfers between devices, on_device(): lax.all_to_all(message.reshape(devices, 1, 2 * LANES), ('row', 'span', 'p...  8.46 us
    ppermute x8, waiting for transfers between devices, shifted(): lax.ppermute(value, axis, [(i, (i + by) % devices) for i in range(devices)])  2.55 us
    pallas_call x1, Pallas kernels, on_device(): call(cycle_kernel, 'cycle_update', [(1,) + block, (3 * peers, LANES)], in...  2.5 us
    pallas_call x1, Pallas kernels, on_device(): call(interior_kernel, 'interior', [block, (CS, CP, LANES), ((7, NVAR) + b...  2.4 us
    pallas_call x1, Pallas kernels, on_device(): call(settle_kernel, 'settle', [block, (6, CS, CP, LANES), ((2 * devices,...  1.63 us
    pallas_call x1, Pallas kernels, on_device(): call(edge_kernel, 'edge_update', [block, (2 * devices, LANES), (CS, CP, L...  1.5 us
  transfers between devices with their start and end apart: 9, of which 3 were waited for; matrix products, arithmetic and copies ran while one was open for 0% of the time, Pallas kernels for 7%

profile of v10, /device:TPU:32, one launch (start us, length us, event | category | flops | bytes accessed | tf_op | source)
XLA Modules:
  0.0 65.1 jit_solution(14940573009217446692)
XLA Ops:
  0.6 0.8 %edges.1 = (f32[6,8,128]{2,1,0:T(8,128)S(1)}, f32[6,8,128]{2,1,0:T(8,128)S(1)}, f32[6,4,128]{2,1,0:T(4,128)S(1)}, f32[6,4,128]{2,1,0:T(4,128)S(1)}) custom-call(f32[1,6,4,8,128]{4,3,2,1,0:T(8,128)} %adj_ref.1), custom_call_target="tpu_custom_call" | custom-call | tf_op jit(solution)/shard_map/edges/pallas_call | solution.py:510
  1.5 1.6 %collective-permute-start = (f32[6,8,128]{2,1,0:T(8,128)S(1)}, f32[6,8,128]{2,1,0:T(8,128)S(1)}, u32[]{:S(2)}, u32[]{:S(2)}) collective-permute-start(f32[6,8,128]{2,1,0:T(8,128)S(1)} %get-tuple-element.31), channel_id=1, source_target_pairs={{0,4},{4,8},{8,12},{12,16},{16,20},{20,24},{24,28},{28,32},{32,36}... | collective-permute-start | bytes 73736 | tf_op jit(solution)/shard_map/ppermute | solution.py:490
  3.0 4.8 %collective-permute-start.1 = (f32[6,8,128]{2,1,0:T(8,128)S(1)}, f32[6,8,128]{2,1,0:T(8,128)S(1)}, u32[]{:S(2)}, u32[]{:S(2)}) collective-permute-start(f32[6,8,128]{2,1,0:T(8,128)S(1)} %get-tuple-element.32), channel_id=1, source_target_pairs={{0,124},{4,0},{8,4},{12,8},{16,12},{20,16},{24,20},{28,24},{32,28}... | collective-permute-start | bytes 73736 | tf_op jit(solution)/shard_map/ppermute | solution.py:490
  7.8 3.3 %collective-permute-start.2 = (f32[6,4,128]{2,1,0:T(4,128)S(1)}, f32[6,4,128]{2,1,0:T(4,128)S(1)}, u32[]{:S(2)}, u32[]{:S(2)}) collective-permute-start(f32[6,4,128]{2,1,0:T(4,128)S(1)} %get-tuple-element.33), channel_id=1, source_target_pairs={{0,1},{1,2},{2,3},{3,0},{4,5},{5,6},{6,7},{7,4},{8,9},{9,10},{10,1... | collective-permute-start | bytes 36872 | tf_op jit(solution)/shard_map/ppermute | solution.py:490
  11.1 2.2 %collective-permute-start.3 = (f32[6,4,128]{2,1,0:T(4,128)S(1)}, f32[6,4,128]{2,1,0:T(4,128)S(1)}, u32[]{:S(2)}, u32[]{:S(2)}) collective-permute-start(f32[6,4,128]{2,1,0:T(4,128)S(1)} %get-tuple-element.34), channel_id=1, source_target_pairs={{0,3},{1,0},{2,1},{3,2},{4,7},{5,4},{6,5},{7,6},{8,11},{9,8},{10,9... | collective-permute-start | bytes 36872 | tf_op jit(solution)/shard_map/ppermute | solution.py:490
  13.3 2.4 %interior.1 = (f32[6,4,8,128]{3,2,1,0:T(8,128)S(1)}, f32[4,8,128]{2,1,0:T(8,128)S(1)}, bf16[7,6,6,4,8,128]{5,4,3,2,1,0:T(8,128)(2,1)S(1)}, f32[6,4,8,128]{3,2,1,0:T(8,128)S(1)}, f32[4,8,128]{2,1,0:T(8,128)S(1)}) custom-call(f32[1,6,4,8,128]{4,3,2,1,0:T(8,128)} %adj_ref.1, f32[1,6,4,8,128]{4,3,2,1,0:T(8,128)} %src_hbm.1, f32[1,4,8,128]{3,2,1,0:T(8,128)} %tau_hbm.1, ...), custom_call_target="tpu_custom_call" | custom-call | flops 9000000 | bytes 3000000 | tf_op jit(solution)/shard_map/interior/pallas_call | solution.py:518
  15.7 0.0 collective-permute-done.2.left_ref
  15.7 0.7 %collective-permute-done.3.right_ref = f32[6,4,128]{2,1,0:T(4,128)S(1)} collective-permute-done((f32[6,4,128]{2,1,0:T(4,128)S(1)}, f32[6,4,128]{2,1,0:T(4,128)S(1)}, u32[]{:S(2)}, u32[]{:S(2)}) %collective-permute-start.3) | collective-permute-done | bytes 12320 | tf_op jit(solution)/shard_map/ppermute | solution.py:490
  16.4 0.0 collective-permute-done.up_ref
  16.4 1.5 %edge_update.1 = (f32[6,4,8,128]{3,2,1,0:T(8,128)S(1)}, f32[512,128]{1,0:T(8,128)}, f32[4,8,128]{2,1,0:T(8,128)S(1)}, f32[7,8,128]{2,1,0:T(8,128)S(1)}, f32[7,8,...) custom-call(f32[6,4,8,128]{3,2,1,0:T(8,128)S(1)} %get-tuple-element.27.part_ref, ...), custom_call_target="tpu_custom_call" | custom-call | tf_op jit(solution)/shard_map/edge_update/pallas_call | solution.py:533
  17.9 8.5 %all-to-all-start = ((f32[256,1,256]{2,1,0:T(1,128)}), f32[256,1,256]{2,1,0:T(1,128)S(1)}, u32[]{:S(2)}, u32[]{:S(2)}) async-start(f32[256,1,256]{2,1,0:T(1,128)} %bitcast), calls=%async_computation | async-start | bytes 524288 | tf_op jit(solution)/shard_map/all_to_all | solution.py:545
  26.4 1.6 %collective-permute-start.4 = (f32[7,8,128]{2,1,0:T(8,128)S(1)}, f32[7,8,128]{2,1,0:T(8,128)S(1)}, u32[]{:S(2)}, u32[]{:S(2)}) collective-permute-start(f32[7,8,128]{2,1,0:T(8,128)S(1)} %get-tuple-element.38), channel_id=1, source_target_pairs={{0,4},{4,8},{8,12},{12,16},{16,20},{20,24},{24,28},{28,32},{32,36}... | collective-permute-start | bytes 86024 | tf_op jit(solution)/shard_map/ppermute | solution.py:490
  27.9 4.8 %collective-permute-start.5 = (f32[7,8,128]{2,1,0:T(8,128)S(1)}, f32[7,8,128]{2,1,0:T(8,128)S(1)}, u32[]{:S(2)}, u32[]{:S(2)}) collective-permute-start(f32[7,8,128]{2,1,0:T(8,128)S(1)} %get-tuple-element.39), channel_id=1, source_target_pairs={{0,124},{4,0},{8,4},{12,8},{16,12},{20,16},{24,20},{28,24},{32,28}... | collective-permute-start | bytes 86024 | tf_op jit(solution)/shard_map/ppermute | solution.py:490
  32.7 2.9 %collective-permute-start.6 = (f32[7,4,128]{2,1,0:T(4,128)S(1)}, f32[7,4,128]{2,1,0:T(4,128)S(1)}, u32[]{:S(2)}, u32[]{:S(2)}) collective-permute-start(f32[7,4,128]{2,1,0:T(4,128)S(1)} %get-tuple-element.40), channel_id=1, source_target_pairs={{0,1},{1,2},{2,3},{3,0},{4,5},{5,6},{6,7},{7,4},{8,9},{9,10},{10,1... | collective-permute-start | bytes 43016 | tf_op jit(solution)/shard_map/ppermute | solution.py:490
  35.6 1.4 %collective-permute-start.7 = (f32[7,4,128]{2,1,0:T(4,128)S(1)}, f32[7,4,128]{2,1,0:T(4,128)S(1)}, u32[]{:S(2)}, u32[]{:S(2)}) collective-permute-start(f32[7,4,128]{2,1,0:T(4,128)S(1)} %get-tuple-element.41), channel_id=1, source_target_pairs={{0,3},{1,0},{2,1},{3,2},{4,7},{5,4},{6,5},{7,6},{8,11},{9,8},{10,9... | collective-permute-start | bytes 43016 | tf_op jit(solution)/shard_map/ppermute | solution.py:490
  37.0 1.6 %settle.1 = (f32[6,4,8,128]{3,2,1,0:T(8,128)S(1)}, f32[6,4,8,128]{3,2,1,0:T(8,128)S(1)}, f32[512,128]{1,0:T(8,128)S(1)}, f32[2,4,8,128]{3,2,1,0:T(8,128)S(1)}, bf16[128,384]{1,0:T(8,128)(2,1)S(1)}) custom-call(s32[2,128]{1,0:T(2,128)S(1)} %copy-done, f32[6,4,8,128]{3,2,1,0:T(8,128)S(1)} %get-tuple-element.35.f1_ref, ...), custom_call_target="tpu_custom_call" | custom-call | flops 9000000 | bytes 3000000 | tf_op jit(solution)/shard_map/settle/pallas_call | solution.py:549
  38.7 0.0 collective-permute-done.6.left_ref
  38.7 1.8 %collective-permute-done.7.right_ref = f32[7,4,128]{2,1,0:T(4,128)S(1)} collective-permute-done((f32[7,4,128]{2,1,0:T(4,128)S(1)}, f32[7,4,128]{2,1,0:T(4,128)S(1)}, u32[]{:S(2)}, u32[]{:S(2)}) %collective-permute-start.7) | collective-permute-done | bytes 14368 | tf_op jit(solution)/shard_map/ppermute | solution.py:490
  40.5 0.4 settle_edges.1
  41.0 0.7 %all-to-all-done = f32[256,1,256]{2,1,0:T(1,128)S(1)} async-done(((f32[256,1,256]{2,1,0:T(1,128)}), f32[256,1,256]{2,1,0:T(1,128)S(1)}, u32[]{:S(2)}, u32[]{:S(2)}) %all-to-all-start) | async-done | bytes 262176 | tf_op jit(solution)/shard_map/all_to_all | solution.py:545
  41.7 2.5 %cycle_update.1 = (f32[1,6,4,8,128]{4,3,2,1,0:T(8,128)}, f32[384,128]{1,0:T(8,128)S(1)}) custom-call(s32[2,128]{1,0:T(2,128)S(1)} %copy-done, f32[6,4,8,128]{3,2,1,0:T(8,128)S(1)} %get-tuple-element.42.part_ref, f32[4,8,128]{2,1,0:T(8,128)S(1)} %get-tuple-element.43.rec_ref, f32[6,4,8,128]{3,2,1,0:T(8,128)S(1)} %get-tuple-element.44.pack_ref, ...), custom_call_target="tpu_custom_call" | custom-call | tf_op jit(solution)/shard_map/cycle_update/pallas_call | solution.py:568
  44.2 20.2 %all_to_all.10 = f32[128,1,384]{2,1,0:T(1,128)S(1)} all-to-all(f32[128,1,384]{2,1,0:T(1,128)S(1)} %bitcast.4), channel_id=1, replica_groups=mesh['row'=2,'span'=32,'pitch'=4] {'span','pitch'}, dimensions={0} | all-to-all | bytes 393216 | tf_op jit(solution)/shard_map/all_to_all | solution.py:579
  64.4 0.2 reduce_sum.9
  64.5 0.6 reshape.19
  (12 shorter events, 0.0 us)
Async XLA Ops:
  1.5 14.9 %collective-permute-start = (f32[6,8,128]{2,1,0:T(8,128)S(1)}, f32[6,8,128]{2,1,0:T(8,128)S(1)}, u32[]{:S(2)}, u32[]{:S(2)}) collective-permute-start(f32[6,8,128]{2,1,0:T(8,128)S(1)} %get-tuple-element.31), channel_id=1, source_target_pairs={{0,4},{4,8},{8,12},{12,16},{16,20},{20,24},{24,28},{28,32},{32,36}... | collective-permute-start | bytes 73736 | tf_op jit(solution)/shard_map/ppermute | solution.py:490
  3.0 13.4 %collective-permute-start.1 = (f32[6,8,128]{2,1,0:T(8,128)S(1)}, f32[6,8,128]{2,1,0:T(8,128)S(1)}, u32[]{:S(2)}, u32[]{:S(2)}) collective-permute-start(f32[6,8,128]{2,1,0:T(8,128)S(1)} %get-tuple-element.32), channel_id=1, source_target_pairs={{0,124},{4,0},{8,4},{12,8},{16,12},{20,16},{24,20},{28,24},{32,28}... | collective-permute-start | bytes 73736 | tf_op jit(solution)/shard_map/ppermute | solution.py:490
  7.8 7.9 %collective-permute-start.2 = (f32[6,4,128]{2,1,0:T(4,128)S(1)}, f32[6,4,128]{2,1,0:T(4,128)S(1)}, u32[]{:S(2)}, u32[]{:S(2)}) collective-permute-start(f32[6,4,128]{2,1,0:T(4,128)S(1)} %get-tuple-element.33), channel_id=1, source_target_pairs={{0,1},{1,2},{2,3},{3,0},{4,5},{5,6},{6,7},{7,4},{8,9},{9,10},{10,1... | collective-permute-start | bytes 36872 | tf_op jit(solution)/shard_map/ppermute | solution.py:490
  11.1 26.0 %copy-start.3 = (f32[1,1,1,18,128]{4,2,3,1,0:T(1,128)S(1)}, f32[1,1,1,18,128]{4,2,3,1,0:T(1,128)}, u32[]{:S(2)}) copy-start(f32[1,1,1,18,128]{4,2,3,1,0:T(1,128)} %param.15) | copy-start | bytes 27652
  11.1 26.0 %copy-start = (s32[2,128]{1,0:T(2,128)S(1)}, s32[2,128]{1,0:T(2,128)}, u32[]{:S(2)}) copy-start(s32[2,128]{1,0:T(2,128)} %bands_ref.3) | copy-start | bytes 3076
  11.1 26.0 %copy-start.1 = (s32[1,1,1,128]{3,2,1,0:T(1,128)S(1)}, s32[1,1,1,128]{3,2,1,0:T(1,128)}, u32[]{:S(2)}) copy-start(s32[1,1,1,128]{3,2,1,0:T(1,128)} %cell_ref.3) | copy-start | bytes 1540
  11.1 26.0 %copy-start.2 = (s32[1,1,1,128]{3,2,1,0:T(1,128)S(1)}, s32[1,1,1,128]{3,2,1,0:T(1,128)}, u32[]{:S(2)}) copy-start(s32[1,1,1,128]{3,2,1,0:T(1,128)} %owner_ref.3) | copy-start | bytes 1540
  11.1 5.3 %collective-permute-start.3 = (f32[6,4,128]{2,1,0:T(4,128)S(1)}, f32[6,4,128]{2,1,0:T(4,128)S(1)}, u32[]{:S(2)}, u32[]{:S(2)}) collective-permute-start(f32[6,4,128]{2,1,0:T(4,128)S(1)} %get-tuple-element.34), channel_id=1, source_target_pairs={{0,3},{1,0},{2,1},{3,2},{4,7},{5,4},{6,5},{7,6},{8,11},{9,8},{10,9... | collective-permute-start | bytes 36872 | tf_op jit(solution)/shard_map/ppermute | solution.py:490
  17.9 23.8 %all-to-all-start = ((f32[256,1,256]{2,1,0:T(1,128)}), f32[256,1,256]{2,1,0:T(1,128)S(1)}, u32[]{:S(2)}, u32[]{:S(2)}) async-start(f32[256,1,256]{2,1,0:T(1,128)} %bitcast), calls=%async_computation | async-start | bytes 524288 | tf_op jit(solution)/shard_map/all_to_all | solution.py:545
  26.4 14.1 %collective-permute-start.4 = (f32[7,8,128]{2,1,0:T(8,128)S(1)}, f32[7,8,128]{2,1,0:T(8,128)S(1)}, u32[]{:S(2)}, u32[]{:S(2)}) collective-permute-start(f32[7,8,128]{2,1,0:T(8,128)S(1)} %get-tuple-element.38), channel_id=1, source_target_pairs={{0,4},{4,8},{8,12},{12,16},{16,20},{20,24},{24,28},{28,32},{32,36}... | collective-permute-start | bytes 86024 | tf_op jit(solution)/shard_map/ppermute | solution.py:490
  27.9 12.6 %collective-permute-start.5 = (f32[7,8,128]{2,1,0:T(8,128)S(1)}, f32[7,8,128]{2,1,0:T(8,128)S(1)}, u32[]{:S(2)}, u32[]{:S(2)}) collective-permute-start(f32[7,8,128]{2,1,0:T(8,128)S(1)} %get-tuple-element.39), channel_id=1, source_target_pairs={{0,124},{4,0},{8,4},{12,8},{16,12},{20,16},{24,20},{28,24},{32,28}... | collective-permute-start | bytes 86024 | tf_op jit(solution)/shard_map/ppermute | solution.py:490
  32.7 6.0 %collective-permute-start.6 = (f32[7,4,128]{2,1,0:T(4,128)S(1)}, f32[7,4,128]{2,1,0:T(4,128)S(1)}, u32[]{:S(2)}, u32[]{:S(2)}) collective-permute-start(f32[7,4,128]{2,1,0:T(4,128)S(1)} %get-tuple-element.40), channel_id=1, source_target_pairs={{0,1},{1,2},{2,3},{3,0},{4,5},{5,6},{6,7},{7,4},{8,9},{9,10},{10,1... | collective-permute-start | bytes 43016 | tf_op jit(solution)/shard_map/ppermute | solution.py:490
  35.6 4.9 %collective-permute-start.7 = (f32[7,4,128]{2,1,0:T(4,128)S(1)}, f32[7,4,128]{2,1,0:T(4,128)S(1)}, u32[]{:S(2)}, u32[]{:S(2)}) collective-permute-start(f32[7,4,128]{2,1,0:T(4,128)S(1)} %get-tuple-element.41), channel_id=1, source_target_pairs={{0,3},{1,0},{2,1},{3,2},{4,7},{5,4},{6,5},{7,6},{8,11},{9,8},{10,9... | collective-permute-start | bytes 43016 | tf_op jit(solution)/shard_map/ppermute | solution.py:490

commit v11 on v10

--- a/solution.py
+++ b/solution.py
@@ -97,7 +97,8 @@
     ]
     load_tau = pltpu.make_async_copy(tau_hbm.at[0], tau_ref, sems.at[8])
     load_src = pltpu.make_async_copy(src_hbm.at[0], src_ref, sems.at[9])
-    for copy in [load_adj] + load_jac + [load_tau, load_src]:
+    order = (5, 6, 0, 1, 2, 3, 4)
+    for copy in [load_adj] + [load_jac[s] for s in order] + [load_tau, load_src]:
         copy.start()
     load_adj.wait()
     fill_stencil(
@@ -110,37 +111,43 @@
         lambda d, j: zero,
         lambda d, j: zero,
     )
-    for s in range(7):
-        load_jac[s].wait()
-
-        def apply(c, carry):
-            acc = jnp.zeros((CS, CP, LANES), F32) if s == 0 else image[c]
+
+    def image_part(c, points, acc):
+        for s in points:
             for d in range(NVAR):
                 acc = acc + jac_ref[s, c, d].astype(F32) * vs[6 * s + d]
-            image[c] = acc
-            return carry
-
-        lax.fori_loop(0, NVAR, apply, 0)
-    load_tau.wait()
-    load_src.wait()
-
-    def finish(c, carry):
+        return acc
+
+    load_jac[5].wait()
+    load_jac[6].wait()
+
+    def axial(c, carry):
         weights, sums = (list(x) for x in carry)
-        f0 = adj_ref[c]
-        part_ref[c] = f0 + tau_ref[...] * (src_ref[c] - image[c])
+        image[c] = image_part(c, (5, 6), jnp.zeros((CS, CP, LANES), F32))
         for j in range(CS):
             for d in range(NVAR):
                 at = WEIGHT_AT + 8 * d + c
                 moved = pltpu.roll(jac_ref[ghost, c, d, j].astype(F32), at + 1 - row, 1)
                 weights[j] = jnp.where(lane == at, moved, weights[j])
-            sums[j] = jnp.where(lane == c, pltpu.roll(f0[j], c + 1 - row, 1), sums[j])
+            sums[j] = jnp.where(lane == c, pltpu.roll(adj_ref[c, j], c + 1 - row, 1), sums[j])
         return tuple(weights), tuple(sums)
 
     ones = jnp.where(lane == COUNT_AT, 1.0, 0.0).astype(F32)
-    weights, sums = lax.fori_loop(0, NVAR, finish, ((zero,) * CS, (ones,) * CS))
+    weights, sums = lax.fori_loop(0, NVAR, axial, ((zero,) * CS, (ones,) * CS))
+    load_tau.wait()
     for j in range(CS):
         tau_out = jnp.sum(jnp.where(lane == outlet, tau_ref[j], 0.0), axis=1, keepdims=True)
         rec_ref[j] = sums[j] + weights[j] * tau_out
+    for s in range(5):
+        load_jac[s].wait()
+    load_src.wait()
+
+    def finish(c, carry):
+        lost = image_part(c, range(5), image[c])
+        part_ref[c] = adj_ref[c] + tau_ref[...] * (src_ref[c] - lost)
+        return carry
+
+    lax.fori_loop(0, NVAR, finish, 0)
 
 
 def inner_sides():
@@ -231,9 +238,8 @@
 
 
 def weight_sum(x):
-    for by in (32, 16, 8):
-        x = x + pltpu.roll(x, LANES - by, 1)
-    return x
+    moved = [pltpu.roll(x, LANES - 8 * d, 1) for d in range(1, NVAR)]
+    return ((x + moved[0]) + (moved[1] + moved[2])) + (moved[3] + moved[4])
 
 
 def spread(values, first):
@@ -377,7 +383,7 @@
                 sums[k] = sums[k] + jnp.where(ids == band, values, 0.0)
         return tuple(sums)
 
-    sums = lax.fori_loop(0, half // CP, body, (zero,) * (2 * CS + 4), unroll=4)
+    sums = lax.fori_loop(0, half // CP, body, (zero,) * (2 * CS + 4), unroll=8)
 
     def folded(parts):
         rows = [jnp.sum(x, axis=0, keepdims=True) for x in parts]

time: 65.4 us -> 65 us (level)
  no operation moved by 1% of the time
where the time goes in v11:
time: 65 us; the launch traced here: 64.7 us
  starting transfers between devices  30.9 us (48%)
  blocking collectives  20.2 us (31%)
  Pallas kernels  8.78 us (14%)
  waiting for transfers between devices  3.43 us (5%)
  between operations  0.72 us (1%)
    ppermute x8, starting transfers between devices, shifted(): lax.ppermute(value, axis, [(i, (i + by) % devices) for i in range(devices)])  22.4 us
    all_to_all x1, blocking collectives, on_device(): lax.all_to_all(dense.reshape(peers, 1, 3 * LANES), ('span', 'pitch'), 0, 0)  20.2 us
    all_to_all x1, starting transfers between devices, on_device(): lax.all_to_all(message.reshape(devices, 1, 2 * LANES), ('row', 'span', 'p...  8.46 us
    ppermute x8, waiting for transfers between devices, shifted(): lax.ppermute(value, axis, [(i, (i + by) % devices) for i in range(devices)])  2.71 us
    pallas_call x1, Pallas kernels, on_device(): call(interior_kernel, 'interior', [block, (CS, CP, LANES), ((7, NVAR) + b...  2.25 us
    pallas_call x1, Pallas kernels, on_device(): call(cycle_kernel, 'cycle_update', [(1,) + block, (3 * peers, LANES)], in...  2.14 us
    pallas_call x1, Pallas kernels, on_device(): call(settle_kernel, 'settle', [block, (6, CS, CP, LANES), ((2 * devices,...  1.63 us
    pallas_call x1, Pallas kernels, on_device(): call(edge_kernel, 'edge_update', [block, (2 * devices, LANES), (CS, CP, L...  1.5 us
  transfers between devices with their start and end apart: 9, of which 3 were waited for; matrix products, arithmetic and copies ran while one was open for 0% of the time, Pallas kernels for 7%

profile of v11, /device:TPU:32, one launch (start us, length us, event | category | flops | bytes accessed | tf_op | source)
XLA Modules:
  0.0 64.7 jit_solution(5153407874008083401)
XLA Ops:
  0.6 0.8 %edges.1 = (f32[6,8,128]{2,1,0:T(8,128)S(1)}, f32[6,8,128]{2,1,0:T(8,128)S(1)}, f32[6,4,128]{2,1,0:T(4,128)S(1)}, f32[6,4,128]{2,1,0:T(4,128)S(1)}) custom-call(f32[1,6,4,8,128]{4,3,2,1,0:T(8,128)} %adj_ref.1), custom_call_target="tpu_custom_call" | custom-call | tf_op jit(solution)/shard_map/edges/pallas_call | solution.py:516
  1.5 1.6 %collective-permute-start = (f32[6,8,128]{2,1,0:T(8,128)S(1)}, f32[6,8,128]{2,1,0:T(8,128)S(1)}, u32[]{:S(2)}, u32[]{:S(2)}) collective-permute-start(f32[6,8,128]{2,1,0:T(8,128)S(1)} %get-tuple-element.31), channel_id=1, source_target_pairs={{0,4},{4,8},{8,12},{12,16},{16,20},{20,24},{24,28},{28,32},{32,36}... | collective-permute-start | bytes 73736 | tf_op jit(solution)/shard_map/ppermute | solution.py:496
  3.0 4.8 %collective-permute-start.1 = (f32[6,8,128]{2,1,0:T(8,128)S(1)}, f32[6,8,128]{2,1,0:T(8,128)S(1)}, u32[]{:S(2)}, u32[]{:S(2)}) collective-permute-start(f32[6,8,128]{2,1,0:T(8,128)S(1)} %get-tuple-element.32), channel_id=1, source_target_pairs={{0,124},{4,0},{8,4},{12,8},{16,12},{20,16},{24,20},{28,24},{32,28}... | collective-permute-start | bytes 73736 | tf_op jit(solution)/shard_map/ppermute | solution.py:496
  7.8 3.3 %collective-permute-start.2 = (f32[6,4,128]{2,1,0:T(4,128)S(1)}, f32[6,4,128]{2,1,0:T(4,128)S(1)}, u32[]{:S(2)}, u32[]{:S(2)}) collective-permute-start(f32[6,4,128]{2,1,0:T(4,128)S(1)} %get-tuple-element.33), channel_id=1, source_target_pairs={{0,1},{1,2},{2,3},{3,0},{4,5},{5,6},{6,7},{7,4},{8,9},{9,10},{10,1... | collective-permute-start | bytes 36872 | tf_op jit(solution)/shard_map/ppermute | solution.py:496
  11.1 2.2 %collective-permute-start.3 = (f32[6,4,128]{2,1,0:T(4,128)S(1)}, f32[6,4,128]{2,1,0:T(4,128)S(1)}, u32[]{:S(2)}, u32[]{:S(2)}) collective-permute-start(f32[6,4,128]{2,1,0:T(4,128)S(1)} %get-tuple-element.34), channel_id=1, source_target_pairs={{0,3},{1,0},{2,1},{3,2},{4,7},{5,4},{6,5},{7,6},{8,11},{9,8},{10,9... | collective-permute-start | bytes 36872 | tf_op jit(solution)/shard_map/ppermute | solution.py:496
  13.3 2.2 %interior.1 = (f32[6,4,8,128]{3,2,1,0:T(8,128)S(1)}, f32[4,8,128]{2,1,0:T(8,128)S(1)}, bf16[7,6,6,4,8,128]{5,4,3,2,1,0:T(8,128)(2,1)S(1)}, f32[6,4,8,128]{3,2,1,0:T(8,128)S(1)}, f32[4,8,128]{2,1,0:T(8,128)S(1)}) custom-call(f32[1,6,4,8,128]{4,3,2,1,0:T(8,128)} %adj_ref.1, f32[1,6,4,8,128]{4,3,2,1,0:T(8,128)} %src_hbm.1, f32[1,4,8,128]{3,2,1,0:T(8,128)} %tau_hbm.1, ...), custom_call_target="tpu_custom_call" | custom-call | flops 9000000 | bytes 3000000 | tf_op jit(solution)/shard_map/interior/pallas_call | solution.py:524
  15.5 0.0 collective-permute-done.2.left_ref
  15.6 0.8 %collective-permute-done.3.right_ref = f32[6,4,128]{2,1,0:T(4,128)S(1)} collective-permute-done((f32[6,4,128]{2,1,0:T(4,128)S(1)}, f32[6,4,128]{2,1,0:T(4,128)S(1)}, u32[]{:S(2)}, u32[]{:S(2)}) %collective-permute-start.3) | collective-permute-done | bytes 12320 | tf_op jit(solution)/shard_map/ppermute | solution.py:496
  16.4 0.0 collective-permute-done.up_ref
  16.4 1.5 %edge_update.1 = (f32[6,4,8,128]{3,2,1,0:T(8,128)S(1)}, f32[512,128]{1,0:T(8,128)}, f32[4,8,128]{2,1,0:T(8,128)S(1)}, f32[7,8,128]{2,1,0:T(8,128)S(1)}, f32[7,8,...) custom-call(f32[6,4,8,128]{3,2,1,0:T(8,128)S(1)} %get-tuple-element.27.part_ref, ...), custom_call_target="tpu_custom_call" | custom-call | tf_op jit(solution)/shard_map/edge_update/pallas_call | solution.py:539
  17.9 8.5 %all-to-all-start = ((f32[256,1,256]{2,1,0:T(1,128)}), f32[256,1,256]{2,1,0:T(1,128)S(1)}, u32[]{:S(2)}, u32[]{:S(2)}) async-start(f32[256,1,256]{2,1,0:T(1,128)} %bitcast), calls=%async_computation | async-start | bytes 524288 | tf_op jit(solution)/shard_map/all_to_all | solution.py:551
  26.4 1.6 %collective-permute-start.4 = (f32[7,8,128]{2,1,0:T(8,128)S(1)}, f32[7,8,128]{2,1,0:T(8,128)S(1)}, u32[]{:S(2)}, u32[]{:S(2)}) collective-permute-start(f32[7,8,128]{2,1,0:T(8,128)S(1)} %get-tuple-element.38), channel_id=1, source_target_pairs={{0,4},{4,8},{8,12},{12,16},{16,20},{20,24},{24,28},{28,32},{32,36}... | collective-permute-start | bytes 86024 | tf_op jit(solution)/shard_map/ppermute | solution.py:496
  27.9 4.8 %collective-permute-start.5 = (f32[7,8,128]{2,1,0:T(8,128)S(1)}, f32[7,8,128]{2,1,0:T(8,128)S(1)}, u32[]{:S(2)}, u32[]{:S(2)}) collective-permute-start(f32[7,8,128]{2,1,0:T(8,128)S(1)} %get-tuple-element.39), channel_id=1, source_target_pairs={{0,124},{4,0},{8,4},{12,8},{16,12},{20,16},{24,20},{28,24},{32,28}... | collective-permute-start | bytes 86024 | tf_op jit(solution)/shard_map/ppermute | solution.py:496
  32.7 2.9 %collective-permute-start.6 = (f32[7,4,128]{2,1,0:T(4,128)S(1)}, f32[7,4,128]{2,1,0:T(4,128)S(1)}, u32[]{:S(2)}, u32[]{:S(2)}) collective-permute-start(f32[7,4,128]{2,1,0:T(4,128)S(1)} %get-tuple-element.40), channel_id=1, source_target_pairs={{0,1},{1,2},{2,3},{3,0},{4,5},{5,6},{6,7},{7,4},{8,9},{9,10},{10,1... | collective-permute-start | bytes 43016 | tf_op jit(solution)/shard_map/ppermute | solution.py:496
  35.6 1.4 %collective-permute-start.7 = (f32[7,4,128]{2,1,0:T(4,128)S(1)}, f32[7,4,128]{2,1,0:T(4,128)S(1)}, u32[]{:S(2)}, u32[]{:S(2)}) collective-permute-start(f32[7,4,128]{2,1,0:T(4,128)S(1)} %get-tuple-element.41), channel_id=1, source_target_pairs={{0,3},{1,0},{2,1},{3,2},{4,7},{5,4},{6,5},{7,6},{8,11},{9,8},{10,9... | collective-permute-start | bytes 43016 | tf_op jit(solution)/shard_map/ppermute | solution.py:496
  37.0 1.6 %settle.1 = (f32[6,4,8,128]{3,2,1,0:T(8,128)S(1)}, f32[6,4,8,128]{3,2,1,0:T(8,128)S(1)}, f32[512,128]{1,0:T(8,128)S(1)}, f32[2,4,8,128]{3,2,1,0:T(8,128)S(1)}, bf16[128,384]{1,0:T(8,128)(2,1)S(1)}) custom-call(s32[2,128]{1,0:T(2,128)S(1)} %copy-done, f32[6,4,8,128]{3,2,1,0:T(8,128)S(1)} %get-tuple-element.35.f1_ref, ...), custom_call_target="tpu_custom_call" | custom-call | flops 9000000 | bytes 3000000 | tf_op jit(solution)/shard_map/settle/pallas_call | solution.py:555
  38.7 0.0 collective-permute-done.6.left_ref
  38.7 1.8 %collective-permute-done.7.right_ref = f32[7,4,128]{2,1,0:T(4,128)S(1)} collective-permute-done((f32[7,4,128]{2,1,0:T(4,128)S(1)}, f32[7,4,128]{2,1,0:T(4,128)S(1)}, u32[]{:S(2)}, u32[]{:S(2)}) %collective-permute-start.7) | collective-permute-done | bytes 14368 | tf_op jit(solution)/shard_map/ppermute | solution.py:496
  40.5 0.4 settle_edges.1
  41.0 0.7 %all-to-all-done = f32[256,1,256]{2,1,0:T(1,128)S(1)} async-done(((f32[256,1,256]{2,1,0:T(1,128)}), f32[256,1,256]{2,1,0:T(1,128)S(1)}, u32[]{:S(2)}, u32[]{:S(2)}) %all-to-all-start) | async-done | bytes 262176 | tf_op jit(solution)/shard_map/all_to_all | solution.py:551
  41.7 2.1 %cycle_update.1 = (f32[1,6,4,8,128]{4,3,2,1,0:T(8,128)}, f32[384,128]{1,0:T(8,128)S(1)}) custom-call(s32[2,128]{1,0:T(2,128)S(1)} %copy-done, f32[6,4,8,128]{3,2,1,0:T(8,128)S(1)} %get-tuple-element.42.part_ref, f32[4,8,128]{2,1,0:T(8,128)S(1)} %get-tuple-element.43.rec_ref, f32[6,4,8,128]{3,2,1,0:T(8,128)S(1)} %get-tuple-element.44.pack_ref, ...), custom_call_target="tpu_custom_call" | custom-call | tf_op jit(solution)/shard_map/cycle_update/pallas_call | solution.py:574
  43.8 20.2 %all_to_all.10 = f32[128,1,384]{2,1,0:T(1,128)S(1)} all-to-all(f32[128,1,384]{2,1,0:T(1,128)S(1)} %bitcast.4), channel_id=1, replica_groups=mesh['row'=2,'span'=32,'pitch'=4] {'span','pitch'}, dimensions={0} | all-to-all | bytes 393216 | tf_op jit(solution)/shard_map/all_to_all | solution.py:585
  64.0 0.2 reduce_sum.9
  64.2 0.6 reshape.19
  (12 shorter events, 0.0 us)
Async XLA Ops:
  1.5 14.9 %collective-permute-start = (f32[6,8,128]{2,1,0:T(8,128)S(1)}, f32[6,8,128]{2,1,0:T(8,128)S(1)}, u32[]{:S(2)}, u32[]{:S(2)}) collective-permute-start(f32[6,8,128]{2,1,0:T(8,128)S(1)} %get-tuple-element.31), channel_id=1, source_target_pairs={{0,4},{4,8},{8,12},{12,16},{16,20},{20,24},{24,28},{28,32},{32,36}... | collective-permute-start | bytes 73736 | tf_op jit(solution)/shard_map/ppermute | solution.py:496
  3.0 13.4 %collective-permute-start.1 = (f32[6,8,128]{2,1,0:T(8,128)S(1)}, f32[6,8,128]{2,1,0:T(8,128)S(1)}, u32[]{:S(2)}, u32[]{:S(2)}) collective-permute-start(f32[6,8,128]{2,1,0:T(8,128)S(1)} %get-tuple-element.32), channel_id=1, source_target_pairs={{0,124},{4,0},{8,4},{12,8},{16,12},{20,16},{24,20},{28,24},{32,28}... | collective-permute-start | bytes 73736 | tf_op jit(solution)/shard_map/ppermute | solution.py:496
  7.8 7.8 %collective-permute-start.2 = (f32[6,4,128]{2,1,0:T(4,128)S(1)}, f32[6,4,128]{2,1,0:T(4,128)S(1)}, u32[]{:S(2)}, u32[]{:S(2)}) collective-permute-start(f32[6,4,128]{2,1,0:T(4,128)S(1)} %get-tuple-element.33), channel_id=1, source_target_pairs={{0,1},{1,2},{2,3},{3,0},{4,5},{5,6},{6,7},{7,4},{8,9},{9,10},{10,1... | collective-permute-start | bytes 36872 | tf_op jit(solution)/shard_map/ppermute | solution.py:496
  11.1 26.0 %copy-start.3 = (f32[1,1,1,18,128]{4,2,3,1,0:T(1,128)S(1)}, f32[1,1,1,18,128]{4,2,3,1,0:T(1,128)}, u32[]{:S(2)}) copy-start(f32[1,1,1,18,128]{4,2,3,1,0:T(1,128)} %param.15) | copy-start | bytes 27652
  11.1 26.0 %copy-start = (s32[2,128]{1,0:T(2,128)S(1)}, s32[2,128]{1,0:T(2,128)}, u32[]{:S(2)}) copy-start(s32[2,128]{1,0:T(2,128)} %bands_ref.3) | copy-start | bytes 3076
  11.1 26.0 %copy-start.1 = (s32[1,1,1,128]{3,2,1,0:T(1,128)S(1)}, s32[1,1,1,128]{3,2,1,0:T(1,128)}, u32[]{:S(2)}) copy-start(s32[1,1,1,128]{3,2,1,0:T(1,128)} %cell_ref.3) | copy-start | bytes 1540
  11.1 26.0 %copy-start.2 = (s32[1,1,1,128]{3,2,1,0:T(1,128)S(1)}, s32[1,1,1,128]{3,2,1,0:T(1,128)}, u32[]{:S(2)}) copy-start(s32[1,1,1,128]{3,2,1,0:T(1,128)} %owner_ref.3) | copy-start | bytes 1540
  11.1 5.3 %collective-permute-start.3 = (f32[6,4,128]{2,1,0:T(4,128)S(1)}, f32[6,4,128]{2,1,0:T(4,128)S(1)}, u32[]{:S(2)}, u32[]{:S(2)}) collective-permute-start(f32[6,4,128]{2,1,0:T(4,128)S(1)} %get-tuple-element.34), channel_id=1, source_target_pairs={{0,3},{1,0},{2,1},{3,2},{4,7},{5,4},{6,5},{7,6},{8,11},{9,8},{10,9... | collective-permute-start | bytes 36872 | tf_op jit(solution)/shard_map/ppermute | solution.py:496
  17.9 23.8 %all-to-all-start = ((f32[256,1,256]{2,1,0:T(1,128)}), f32[256,1,256]{2,1,0:T(1,128)S(1)}, u32[]{:S(2)}, u32[]{:S(2)}) async-start(f32[256,1,256]{2,1,0:T(1,128)} %bitcast), calls=%async_computation | async-start | bytes 524288 | tf_op jit(solution)/shard_map/all_to_all | solution.py:551
  26.4 14.1 %collective-permute-start.4 = (f32[7,8,128]{2,1,0:T(8,128)S(1)}, f32[7,8,128]{2,1,0:T(8,128)S(1)}, u32[]{:S(2)}, u32[]{:S(2)}) collective-permute-start(f32[7,8,128]{2,1,0:T(8,128)S(1)} %get-tuple-element.38), channel_id=1, source_target_pairs={{0,4},{4,8},{8,12},{12,16},{16,20},{20,24},{24,28},{28,32},{32,36}... | collective-permute-start | bytes 86024 | tf_op jit(solution)/shard_map/ppermute | solution.py:496
  27.9 12.6 %collective-permute-start.5 = (f32[7,8,128]{2,1,0:T(8,128)S(1)}, f32[7,8,128]{2,1,0:T(8,128)S(1)}, u32[]{:S(2)}, u32[]{:S(2)}) collective-permute-start(f32[7,8,128]{2,1,0:T(8,128)S(1)} %get-tuple-element.39), channel_id=1, source_target_pairs={{0,124},{4,0},{8,4},{12,8},{16,12},{20,16},{24,20},{28,24},{32,28}... | collective-permute-start | bytes 86024 | tf_op jit(solution)/shard_map/ppermute | solution.py:496
  32.7 6.0 %collective-permute-start.6 = (f32[7,4,128]{2,1,0:T(4,128)S(1)}, f32[7,4,128]{2,1,0:T(4,128)S(1)}, u32[]{:S(2)}, u32[]{:S(2)}) collective-permute-start(f32[7,4,128]{2,1,0:T(4,128)S(1)} %get-tuple-element.40), channel_id=1, source_target_pairs={{0,1},{1,2},{2,3},{3,0},{4,5},{5,6},{6,7},{7,4},{8,9},{9,10},{10,1... | collective-permute-start | bytes 43016 | tf_op jit(solution)/shard_map/ppermute | solution.py:496
  35.6 4.9 %collective-permute-start.7 = (f32[7,4,128]{2,1,0:T(4,128)S(1)}, f32[7,4,128]{2,1,0:T(4,128)S(1)}, u32[]{:S(2)}, u32[]{:S(2)}) collective-permute-start(f32[7,4,128]{2,1,0:T(4,128)S(1)} %get-tuple-element.41), channel_id=1, source_target_pairs={{0,3},{1,0},{2,1},{3,2},{4,7},{5,4},{6,5},{7,6},{8,11},{9,8},{10,9... | collective-permute-start | bytes 43016 | tf_op jit(solution)/shard_map/ppermute | solution.py:496

commit v12 on v11

--- a/solution.py
+++ b/solution.py
@@ -81,26 +81,13 @@
         copy.wait()
 
 
-def interior_kernel(
-    adj_hbm, src_hbm, tau_hbm, jac_hbm, part_ref, rec_ref, jac_ref, src_ref, tau_ref, adj_ref, vs,
-    image, sems,
-):
+def interior_kernel(adj_ref, src_ref, tau_ref, jac_ref, part_ref, rec_ref, vs):
     row = lax.axis_index("row")
     outlet = (1 - row) * (LANES - 1)
     ghost = 6 - row
     tile = (CP, LANES)
     zero = jnp.zeros(tile, F32)
     lane = lane_ids(tile)
-    load_adj = pltpu.make_async_copy(adj_hbm.at[0], adj_ref, sems.at[0])
-    load_jac = [
-        pltpu.make_async_copy(jac_hbm.at[0, s], jac_ref.at[s], sems.at[1 + s]) for s in range(7)
-    ]
-    load_tau = pltpu.make_async_copy(tau_hbm.at[0], tau_ref, sems.at[8])
-    load_src = pltpu.make_async_copy(src_hbm.at[0], src_ref, sems.at[9])
-    order = (5, 6, 0, 1, 2, 3, 4)
-    for copy in [load_adj] + [load_jac[s] for s in order] + [load_tau, load_src]:
-        copy.start()
-    load_adj.wait()
     fill_stencil(
         vs,
         lambda d, j: adj_ref[d, j],
@@ -112,18 +99,9 @@
         lambda d, j: zero,
     )
 
-    def image_part(c, points, acc):
-        for s in points:
-            for d in range(NVAR):
-                acc = acc + jac_ref[s, c, d].astype(F32) * vs[6 * s + d]
-        return acc
-
-    load_jac[5].wait()
-    load_jac[6].wait()
-
-    def axial(c, carry):
+    def advance(c, carry):
         weights, sums = (list(x) for x in carry)
-        image[c] = image_part(c, (5, 6), jnp.zeros((CS, CP, LANES), F32))
+        part_ref[c] = adj_ref[c] + tau_ref[...] * (src_ref[c] - image_of(jac_ref, vs, c))
         for j in range(CS):
             for d in range(NVAR):
                 at = WEIGHT_AT + 8 * d + c
@@ -133,21 +111,10 @@
         return tuple(weights), tuple(sums)
 
     ones = jnp.where(lane == COUNT_AT, 1.0, 0.0).astype(F32)
-    weights, sums = lax.fori_loop(0, NVAR, axial, ((zero,) * CS, (ones,) * CS))
-    load_tau.wait()
+    weights, sums = lax.fori_loop(0, NVAR, advance, ((zero,) * CS, (ones,) * CS))
     for j in range(CS):
         tau_out = jnp.sum(jnp.where(lane == outlet, tau_ref[j], 0.0), axis=1, keepdims=True)
         rec_ref[j] = sums[j] + weights[j] * tau_out
-    for s in range(5):
-        load_jac[s].wait()
-    load_src.wait()
-
-    def finish(c, carry):
-        lost = image_part(c, range(5), image[c])
-        part_ref[c] = adj_ref[c] + tau_ref[...] * (src_ref[c] - lost)
-        return carry
-
-    lax.fori_loop(0, NVAR, finish, 0)
 
 
 def inner_sides():
@@ -519,21 +486,18 @@
         [edge, edge, side, side],
         in_specs=[HBM],
         scratch=[pltpu.SemaphoreType.DMA((4,))],
+        cost=pl.CostEstimate(flops=2_000_000_000, bytes_accessed=30_000_000, transcendentals=0),
     )(in_hbm(adjoint))
     halo = over_span(*edges[:2]) + over_pitch(*edges[2:])
-    part, record, jac, src, tau = call(
+    jac, src, tau = jac_blocks[0], source[0], pseudo_step[0]
+    part, record = call(
         interior_kernel,
         "interior",
-        [block, (CS, CP, LANES), ((7, NVAR) + block, BF16), block, (CS, CP, LANES)],
-        in_specs=[HBM] * 4,
-        scratch=[
-            pltpu.VMEM(block, F32),
-            pltpu.VMEM((7 * NVAR, CS, CP, LANES), F32),
-            pltpu.VMEM(block, F32),
-            pltpu.SemaphoreType.DMA((10,)),
-        ],
+        [block, (CS, CP, LANES)],
+        in_specs=[VM] * 4,
+        scratch=[pltpu.VMEM((7 * NVAR, CS, CP, LANES), F32)],
         cost=pl.CostEstimate(flops=9_000_000, bytes_accessed=3_000_000, transcendentals=0),
-    )(*(in_hbm(x) for x in (adjoint, source, pseudo_step, jac_blocks)))
+    )(adjoint[0], src, tau, jac)
     edge = (NVAR + 1, CP, LANES)
     side = (NVAR + 1, CS, LANES)
     first, message, full_record, *sends = call(

time: 65 us -> 65 us (level)
  waiting for transfers between devices: 3.43 us -> 4.59 us
  Pallas kernels: 8.78 us -> 7.7 us
    pallas_call x1, Pallas kernels: 2.25 us -> 1.06 us  [on_device(): call(interior_kernel, 'interior', [block, (CS, CP, LANES)], in_specs=[VM]...]
    ppermute x8, waiting for transfers between devices: 2.71 us -> 3.86 us  [shifted(): lax.ppermute(value, axis, [(i, (i + by) % devices) for i in range(devices)])]
  transfers between devices with their start and end apart: 9 -> 9, of which waited for: 3 -> 4; matrix products, arithmetic and copies ran while one was open for 0% -> 0% of each run, Pallas kernels for 7% -> 5%
where the time goes in v12:
time: 65 us; the launch traced here: 64.8 us
  starting transfers between devices  30.8 us (47%)
  blocking collectives  20.2 us (31%)
  Pallas kernels  7.7 us (12%)
  waiting for transfers between devices  4.59 us (7%)
  between operations  0.77 us (1%)
    ppermute x8, starting transfers between devices, shifted(): lax.ppermute(value, axis, [(i, (i + by) % devices) for i in range(devices)])  22.3 us
    all_to_all x1, blocking collectives, on_device(): lax.all_to_all(dense.reshape(peers, 1, 3 * LANES), ('span', 'pitch'), 0, 0)  20.2 us
    all_to_all x1, starting transfers between devices, on_device(): lax.all_to_all(message.reshape(devices, 1, 2 * LANES), ('row', 'span', 'p...  8.47 us
    ppermute x8, waiting for transfers between devices, shifted(): lax.ppermute(value, axis, [(i, (i + by) % devices) for i in range(devices)])  3.86 us
    pallas_call x1, Pallas kernels, on_device(): call(cycle_kernel, 'cycle_update', [(1,) + block, (3 * peers, LANES)], in...  2.14 us
    pallas_call x1, Pallas kernels, on_device(): call(settle_kernel, 'settle', [block, (6, CS, CP, LANES), ((2 * devices,...  1.63 us
    pallas_call x1, Pallas kernels, on_device(): call(edge_kernel, 'edge_update', [block, (2 * devices, LANES), (CS, CP, L...  1.5 us
  transfers between devices with their start and end apart: 9, of which 4 were waited for; matrix products, arithmetic and copies ran while one was open for 0% of the time, Pallas kernels for 5%

profile of v12, /device:TPU:32, one launch (start us, length us, event | category | flops | bytes accessed | tf_op | source)
XLA Modules:
  0.0 64.8 jit_solution(8784369928123130614)
XLA Ops:
  0.7 0.9 %edges.1 = (f32[6,8,128]{2,1,0:T(8,128)S(1)}, f32[6,8,128]{2,1,0:T(8,128)S(1)}, f32[6,4,128]{2,1,0:T(4,128)S(1)}, f32[6,4,128]{2,1,0:T(4,128)S(1)}) custom-call(f32[1,6,4,8,128]{4,3,2,1,0:T(8,128)} %adj_ref.1), custom_call_target="tpu_custom_call" | custom-call | flops 2000000000 | bytes 30000000 | tf_op jit(solution)/shard_map/edges/pallas_call | solution.py:483
  1.6 1.6 %collective-permute-start = (f32[6,8,128]{2,1,0:T(8,128)S(1)}, f32[6,8,128]{2,1,0:T(8,128)S(1)}, u32[]{:S(2)}, u32[]{:S(2)}) collective-permute-start(f32[6,8,128]{2,1,0:T(8,128)S(1)} %get-tuple-element.26), channel_id=1, source_target_pairs={{0,4},{4,8},{8,12},{12,16},{16,20},{20,24},{24,28},{28,32},{32,36}... | collective-permute-start | bytes 73736 | tf_op jit(solution)/shard_map/ppermute | solution.py:463
  3.2 4.8 %collective-permute-start.1 = (f32[6,8,128]{2,1,0:T(8,128)S(1)}, f32[6,8,128]{2,1,0:T(8,128)S(1)}, u32[]{:S(2)}, u32[]{:S(2)}) collective-permute-start(f32[6,8,128]{2,1,0:T(8,128)S(1)} %get-tuple-element.27), channel_id=1, source_target_pairs={{0,124},{4,0},{8,4},{12,8},{16,12},{20,16},{24,20},{28,24},{32,28}... | collective-permute-start | bytes 73736 | tf_op jit(solution)/shard_map/ppermute | solution.py:463
  7.9 3.3 %collective-permute-start.2 = (f32[6,4,128]{2,1,0:T(4,128)S(1)}, f32[6,4,128]{2,1,0:T(4,128)S(1)}, u32[]{:S(2)}, u32[]{:S(2)}) collective-permute-start(f32[6,4,128]{2,1,0:T(4,128)S(1)} %get-tuple-element.28), channel_id=1, source_target_pairs={{0,1},{1,2},{2,3},{3,0},{4,5},{5,6},{6,7},{7,4},{8,9},{9,10},{10,1... | collective-permute-start | bytes 36872 | tf_op jit(solution)/shard_map/ppermute | solution.py:463
  11.2 2.1 %collective-permute-start.3 = (f32[6,4,128]{2,1,0:T(4,128)S(1)}, f32[6,4,128]{2,1,0:T(4,128)S(1)}, u32[]{:S(2)}, u32[]{:S(2)}) collective-permute-start(f32[6,4,128]{2,1,0:T(4,128)S(1)} %get-tuple-element.29), channel_id=1, source_target_pairs={{0,3},{1,0},{2,1},{3,2},{4,7},{5,4},{6,5},{7,6},{8,11},{9,8},{10,9... | collective-permute-start | bytes 36872 | tf_op jit(solution)/shard_map/ppermute | solution.py:463
  13.4 0.0 copy-start.5
  13.4 1.1 %interior.1 = (f32[6,4,8,128]{3,2,1,0:T(8,128)S(1)}, f32[4,8,128]{2,1,0:T(8,128)S(1)}) custom-call(f32[6,4,8,128]{3,2,1,0:T(8,128)S(1)} %bitcast.19, f32[6,4,8,128]{3,2,1,0:T(8,128)S(1)} %bitcast.12, f32[4,8,128]{2,1,0:T(8,128)S(1)} %bitcast.14, bf16[7,6,6,4,8,128]{5,4,3,2,1,0:T(8,128)(2,1)S(1)} %bitcast.7), custom_call_target="tpu_custom_call" | custom-call | flops 9000000 | bytes 3000000 | tf_op jit(solution)/shard_map/interior/pallas_call | solution.py:493
  14.5 0.6 collective-permute-done.2.left_ref
  15.0 1.5 %collective-permute-done.3.right_ref = f32[6,4,128]{2,1,0:T(4,128)S(1)} collective-permute-done((f32[6,4,128]{2,1,0:T(4,128)S(1)}, f32[6,4,128]{2,1,0:T(4,128)S(1)}, u32[]{:S(2)}, u32[]{:S(2)}) %collective-permute-start.3) | collective-permute-done | bytes 12320 | tf_op jit(solution)/shard_map/ppermute | solution.py:463
  16.5 1.5 %edge_update.1 = (f32[6,4,8,128]{3,2,1,0:T(8,128)S(1)}, f32[512,128]{1,0:T(8,128)}, f32[4,8,128]{2,1,0:T(8,128)S(1)}, f32[7,8,128]{2,1,0:T(8,128)S(1)}, f32[7,8,...) custom-call(f32[6,4,8,128]{3,2,1,0:T(8,128)S(1)} %get-tuple-element.24.part_ref, ...), custom_call_target="tpu_custom_call" | custom-call | tf_op jit(solution)/shard_map/edge_update/pallas_call | solution.py:503
  18.0 8.5 %all-to-all-start = ((f32[256,1,256]{2,1,0:T(1,128)}), f32[256,1,256]{2,1,0:T(1,128)S(1)}, u32[]{:S(2)}, u32[]{:S(2)}) async-start(f32[256,1,256]{2,1,0:T(1,128)} %bitcast.4), calls=%async_computation | async-start | bytes 524288 | tf_op jit(solution)/shard_map/all_to_all | solution.py:515
  26.5 1.6 %collective-permute-start.4 = (f32[7,8,128]{2,1,0:T(8,128)S(1)}, f32[7,8,128]{2,1,0:T(8,128)S(1)}, u32[]{:S(2)}, u32[]{:S(2)}) collective-permute-start(f32[7,8,128]{2,1,0:T(8,128)S(1)} %get-tuple-element.32), channel_id=1, source_target_pairs={{0,4},{4,8},{8,12},{12,16},{16,20},{20,24},{24,28},{28,32},{32,36}... | collective-permute-start | bytes 86024 | tf_op jit(solution)/shard_map/ppermute | solution.py:463
  28.0 4.8 %collective-permute-start.5 = (f32[7,8,128]{2,1,0:T(8,128)S(1)}, f32[7,8,128]{2,1,0:T(8,128)S(1)}, u32[]{:S(2)}, u32[]{:S(2)}) collective-permute-start(f32[7,8,128]{2,1,0:T(8,128)S(1)} %get-tuple-element.33), channel_id=1, source_target_pairs={{0,124},{4,0},{8,4},{12,8},{16,12},{20,16},{24,20},{28,24},{32,28}... | collective-permute-start | bytes 86024 | tf_op jit(solution)/shard_map/ppermute | solution.py:463
  32.8 2.9 %collective-permute-start.6 = (f32[7,4,128]{2,1,0:T(4,128)S(1)}, f32[7,4,128]{2,1,0:T(4,128)S(1)}, u32[]{:S(2)}, u32[]{:S(2)}) collective-permute-start(f32[7,4,128]{2,1,0:T(4,128)S(1)} %get-tuple-element.34), channel_id=1, source_target_pairs={{0,1},{1,2},{2,3},{3,0},{4,5},{5,6},{6,7},{7,4},{8,9},{9,10},{10,1... | collective-permute-start | bytes 43016 | tf_op jit(solution)/shard_map/ppermute | solution.py:463
  35.7 1.4 %collective-permute-start.7 = (f32[7,4,128]{2,1,0:T(4,128)S(1)}, f32[7,4,128]{2,1,0:T(4,128)S(1)}, u32[]{:S(2)}, u32[]{:S(2)}) collective-permute-start(f32[7,4,128]{2,1,0:T(4,128)S(1)} %get-tuple-element.35), channel_id=1, source_target_pairs={{0,3},{1,0},{2,1},{3,2},{4,7},{5,4},{6,5},{7,6},{8,11},{9,8},{10,9... | collective-permute-start | bytes 43016 | tf_op jit(solution)/shard_map/ppermute | solution.py:463
  37.1 1.6 %settle.1 = (f32[6,4,8,128]{3,2,1,0:T(8,128)S(1)}, f32[6,4,8,128]{3,2,1,0:T(8,128)S(1)}, f32[512,128]{1,0:T(8,128)S(1)}, f32[2,4,8,128]{3,2,1,0:T(8,128)S(1)}, bf16[128,384]{1,0:T(8,128)(2,1)S(1)}) custom-call(s32[2,128]{1,0:T(2,128)S(1)} %copy-done.4, f32[6,4,8,128]{3,2,1,0:T(8,128)S(1)} %get-tuple-element.30.f1_ref, f32[6,4,8,128]{3,2,1,0:T(8,128)S(1)} %bitcast.13, ...), custom_call_target="tpu_custom_call" | custom-call | flops 9000000 | bytes 3000000 | tf_op jit(solution)/shard_map/settle/pallas_call | solution.py:519
  38.7 0.0 collective-permute-done.6.left_ref
  38.8 1.8 %collective-permute-done.7.right_ref = f32[7,4,128]{2,1,0:T(4,128)S(1)} collective-permute-done((f32[7,4,128]{2,1,0:T(4,128)S(1)}, f32[7,4,128]{2,1,0:T(4,128)S(1)}, u32[]{:S(2)}, u32[]{:S(2)}) %collective-permute-start.7) | collective-permute-done | bytes 14368 | tf_op jit(solution)/shard_map/ppermute | solution.py:463
  40.6 0.4 settle_edges.1
  41.0 0.7 %all-to-all-done = f32[256,1,256]{2,1,0:T(1,128)S(1)} async-done(((f32[256,1,256]{2,1,0:T(1,128)}), f32[256,1,256]{2,1,0:T(1,128)S(1)}, u32[]{:S(2)}, u32[]{:S(2)}) %all-to-all-start) | async-done | bytes 262176 | tf_op jit(solution)/shard_map/all_to_all | solution.py:515
  41.8 2.1 %cycle_update.1 = (f32[1,6,4,8,128]{4,3,2,1,0:T(8,128)}, f32[384,128]{1,0:T(8,128)S(1)}) custom-call(s32[2,128]{1,0:T(2,128)S(1)} %copy-done.4, f32[6,4,8,128]{3,2,1,0:T(8,128)S(1)} %get-tuple-element.36.part_ref, f32[4,8,128]{2,1,0:T(8,128)S(1)} %get-tuple-element.37.rec_ref, f32[6,4,8,128]{3,2,1,0:T(8,128)S(1)} %get-tuple-element.38.pack_ref, ...), custom_call_target="tpu_custom_call" | custom-call | tf_op jit(solution)/shard_map/cycle_update/pallas_call | solution.py:538
  43.9 20.2 %all_to_all.10 = f32[128,1,384]{2,1,0:T(1,128)S(1)} all-to-all(f32[128,1,384]{2,1,0:T(1,128)S(1)} %bitcast.18), channel_id=1, replica_groups=mesh['row'=2,'span'=32,'pitch'=4] {'span','pitch'}, dimensions={0} | all-to-all | bytes 393216 | tf_op jit(solution)/shard_map/all_to_all | solution.py:549
  64.1 0.2 reduce_sum.9
  64.2 0.6 reshape.19
  (20 shorter events, 0.1 us)
Async XLA Ops:
  0.6 12.7 %copy-start.3 = (f32[1,6,4,8,128]{4,3,2,1,0:T(8,128)S(1)}, f32[1,6,4,8,128]{4,3,2,1,0:T(8,128)}, u32[]{:S(2)}) copy-start(f32[1,6,4,8,128]{4,3,2,1,0:T(8,128)} %adj_ref.1) | copy-start | bytes 294916
  0.6 12.7 %copy-start = (bf16[1,7,6,6,4,8,128]{6,5,4,3,2,1,0:T(8,128)(2,1)S(1)}, bf16[1,7,6,6,4,8,128]{6,5,4,3,2,1,0:T(8,128)(2,1)}, u32[]{:S(2)}) copy-start(bf16[1,7,6,6,4,8,128]{6,5,4,3,2,1,0:T(8,128)(2,1)} %param.11) | copy-start | bytes 6193156
  0.7 12.7 %copy-start.2 = (f32[1,4,8,128]{3,2,1,0:T(8,128)S(1)}, f32[1,4,8,128]{3,2,1,0:T(8,128)}, u32[]{:S(2)}) copy-start(f32[1,4,8,128]{3,2,1,0:T(8,128)} %param.10) | copy-start | bytes 49156
  0.7 12.7 %copy-start.1 = (f32[1,6,4,8,128]{4,3,2,1,0:T(8,128)S(1)}, f32[1,6,4,8,128]{4,3,2,1,0:T(8,128)}, u32[]{:S(2)}) copy-start(f32[1,6,4,8,128]{4,3,2,1,0:T(8,128)} %param.9) | copy-start | bytes 294916
  1.6 14.9 %collective-permute-start = (f32[6,8,128]{2,1,0:T(8,128)S(1)}, f32[6,8,128]{2,1,0:T(8,128)S(1)}, u32[]{:S(2)}, u32[]{:S(2)}) collective-permute-start(f32[6,8,128]{2,1,0:T(8,128)S(1)} %get-tuple-element.26), channel_id=1, source_target_pairs={{0,4},{4,8},{8,12},{12,16},{16,20},{20,24},{24,28},{28,32},{32,36}... | collective-permute-start | bytes 73736 | tf_op jit(solution)/shard_map/ppermute | solution.py:463
  3.2 13.3 %collective-permute-start.1 = (f32[6,8,128]{2,1,0:T(8,128)S(1)}, f32[6,8,128]{2,1,0:T(8,128)S(1)}, u32[]{:S(2)}, u32[]{:S(2)}) collective-permute-start(f32[6,8,128]{2,1,0:T(8,128)S(1)} %get-tuple-element.27), channel_id=1, source_target_pairs={{0,124},{4,0},{8,4},{12,8},{16,12},{20,16},{24,20},{28,24},{32,28}... | collective-permute-start | bytes 73736 | tf_op jit(solution)/shard_map/ppermute | solution.py:463
  7.9 7.1 %collective-permute-start.2 = (f32[6,4,128]{2,1,0:T(4,128)S(1)}, f32[6,4,128]{2,1,0:T(4,128)S(1)}, u32[]{:S(2)}, u32[]{:S(2)}) collective-permute-start(f32[6,4,128]{2,1,0:T(4,128)S(1)} %get-tuple-element.28), channel_id=1, source_target_pairs={{0,1},{1,2},{2,3},{3,0},{4,5},{5,6},{6,7},{7,4},{8,9},{9,10},{10,1... | collective-permute-start | bytes 36872 | tf_op jit(solution)/shard_map/ppermute | solution.py:463
  11.2 5.3 %collective-permute-start.3 = (f32[6,4,128]{2,1,0:T(4,128)S(1)}, f32[6,4,128]{2,1,0:T(4,128)S(1)}, u32[]{:S(2)}, u32[]{:S(2)}) collective-permute-start(f32[6,4,128]{2,1,0:T(4,128)S(1)} %get-tuple-element.29), channel_id=1, source_target_pairs={{0,3},{1,0},{2,1},{3,2},{4,7},{5,4},{6,5},{7,6},{8,11},{9,8},{10,9... | collective-permute-start | bytes 36872 | tf_op jit(solution)/shard_map/ppermute | solution.py:463
  13.4 23.7 %copy-start.7 = (f32[1,1,1,18,128]{4,2,3,1,0:T(1,128)S(1)}, f32[1,1,1,18,128]{4,2,3,1,0:T(1,128)}, u32[]{:S(2)}) copy-start(f32[1,1,1,18,128]{4,2,3,1,0:T(1,128)} %param.15) | copy-start | bytes 27652
  13.4 23.7 %copy-start.4 = (s32[2,128]{1,0:T(2,128)S(1)}, s32[2,128]{1,0:T(2,128)}, u32[]{:S(2)}) copy-start(s32[2,128]{1,0:T(2,128)} %bands_ref.3) | copy-start | bytes 3076
  13.4 23.7 %copy-start.5 = (s32[1,1,1,128]{3,2,1,0:T(1,128)S(1)}, s32[1,1,1,128]{3,2,1,0:T(1,128)}, u32[]{:S(2)}) copy-start(s32[1,1,1,128]{3,2,1,0:T(1,128)} %cell_ref.3) | copy-start | bytes 1540
  13.4 23.7 %copy-start.6 = (s32[1,1,1,128]{3,2,1,0:T(1,128)S(1)}, s32[1,1,1,128]{3,2,1,0:T(1,128)}, u32[]{:S(2)}) copy-start(s32[1,1,1,128]{3,2,1,0:T(1,128)} %owner_ref.3) | copy-start | bytes 1540
  18.0 23.8 %all-to-all-start = ((f32[256,1,256]{2,1,0:T(1,128)}), f32[256,1,256]{2,1,0:T(1,128)S(1)}, u32[]{:S(2)}, u32[]{:S(2)}) async-start(f32[256,1,256]{2,1,0:T(1,128)} %bitcast.4), calls=%async_computation | async-start | bytes 524288 | tf_op jit(solution)/shard_map/all_to_all | solution.py:515
  26.5 14.1 %collective-permute-start.4 = (f32[7,8,128]{2,1,0:T(8,128)S(1)}, f32[7,8,128]{2,1,0:T(8,128)S(1)}, u32[]{:S(2)}, u32[]{:S(2)}) collective-permute-start(f32[7,8,128]{2,1,0:T(8,128)S(1)} %get-tuple-element.32), channel_id=1, source_target_pairs={{0,4},{4,8},{8,12},{12,16},{16,20},{20,24},{24,28},{28,32},{32,36}... | collective-permute-start | bytes 86024 | tf_op jit(solution)/shard_map/ppermute | solution.py:463
  28.0 12.6 %collective-permute-start.5 = (f32[7,8,128]{2,1,0:T(8,128)S(1)}, f32[7,8,128]{2,1,0:T(8,128)S(1)}, u32[]{:S(2)}, u32[]{:S(2)}) collective-permute-start(f32[7,8,128]{2,1,0:T(8,128)S(1)} %get-tuple-element.33), channel_id=1, source_target_pairs={{0,124},{4,0},{8,4},{12,8},{16,12},{20,16},{24,20},{28,24},{32,28}... | collective-permute-start | bytes 86024 | tf_op jit(solution)/shard_map/ppermute | solution.py:463
  32.8 6.0 %collective-permute-start.6 = (f32[7,4,128]{2,1,0:T(4,128)S(1)}, f32[7,4,128]{2,1,0:T(4,128)S(1)}, u32[]{:S(2)}, u32[]{:S(2)}) collective-permute-start(f32[7,4,128]{2,1,0:T(4,128)S(1)} %get-tuple-element.34), channel_id=1, source_target_pairs={{0,1},{1,2},{2,3},{3,0},{4,5},{5,6},{6,7},{7,4},{8,9},{9,10},{10,1... | collective-permute-start | bytes 43016 | tf_op jit(solution)/shard_map/ppermute | solution.py:463
  35.7 4.9 %collective-permute-start.7 = (f32[7,4,128]{2,1,0:T(4,128)S(1)}, f32[7,4,128]{2,1,0:T(4,128)S(1)}, u32[]{:S(2)}, u32[]{:S(2)}) collective-permute-start(f32[7,4,128]{2,1,0:T(4,128)S(1)} %get-tuple-element.35), channel_id=1, source_target_pairs={{0,3},{1,0},{2,1},{3,2},{4,7},{5,4},{6,5},{7,6},{8,11},{9,8},{10,9... | collective-permute-start | bytes 43016 | tf_op jit(solution)/shard_map/ppermute | solution.py:463

commit v13 on v7

--- a/solution.py
+++ b/solution.py
@@ -14,6 +14,7 @@
 FIRST_AT = 8
 WEIGHT_AT = 16
 COUNT_AT = 6
+FAR_COPIES = 5
 
 
 def lane_ids(shape):
@@ -81,25 +82,13 @@
         copy.wait()
 
 
-def interior_kernel(
-    adj_hbm, src_hbm, tau_hbm, jac_hbm, part_ref, rec_ref, jac_ref, src_ref, tau_ref, adj_ref, vs,
-    image, sems,
-):
+def interior_kernel(adj_ref, src_ref, tau_ref, jac_ref, part_ref, rec_ref, vs):
     row = lax.axis_index("row")
     outlet = (1 - row) * (LANES - 1)
     ghost = 6 - row
     tile = (CP, LANES)
     zero = jnp.zeros(tile, F32)
     lane = lane_ids(tile)
-    load_adj = pltpu.make_async_copy(adj_hbm.at[0], adj_ref, sems.at[0])
-    load_jac = [
-        pltpu.make_async_copy(jac_hbm.at[0, s], jac_ref.at[s], sems.at[1 + s]) for s in range(7)
-    ]
-    load_tau = pltpu.make_async_copy(tau_hbm.at[0], tau_ref, sems.at[8])
-    load_src = pltpu.make_async_copy(src_hbm.at[0], src_ref, sems.at[9])
-    for copy in [load_adj] + load_jac + [load_tau, load_src]:
-        copy.start()
-    load_adj.wait()
     fill_stencil(
         vs,
         lambda d, j: adj_ref[d, j],
@@ -110,34 +99,20 @@
         lambda d, j: zero,
         lambda d, j: zero,
     )
-    for s in range(7):
-        load_jac[s].wait()
-
-        def apply(c, carry):
-            acc = jnp.zeros((CS, CP, LANES), F32) if s == 0 else image[c]
-            for d in range(NVAR):
-                acc = acc + jac_ref[s, c, d].astype(F32) * vs[6 * s + d]
-            image[c] = acc
-            return carry
-
-        lax.fori_loop(0, NVAR, apply, 0)
-    load_tau.wait()
-    load_src.wait()
-
-    def finish(c, carry):
+
+    def advance(c, carry):
         weights, sums = (list(x) for x in carry)
-        f0 = adj_ref[c]
-        part_ref[c] = f0 + tau_ref[...] * (src_ref[c] - image[c])
+        part_ref[c] = adj_ref[c] + tau_ref[...] * (src_ref[c] - image_of(jac_ref, vs, c))
         for j in range(CS):
             for d in range(NVAR):
                 at = WEIGHT_AT + 8 * d + c
                 moved = pltpu.roll(jac_ref[ghost, c, d, j].astype(F32), at + 1 - row, 1)
                 weights[j] = jnp.where(lane == at, moved, weights[j])
-            sums[j] = jnp.where(lane == c, pltpu.roll(f0[j], c + 1 - row, 1), sums[j])
+            sums[j] = jnp.where(lane == c, pltpu.roll(adj_ref[c, j], c + 1 - row, 1), sums[j])
         return tuple(weights), tuple(sums)
 
     ones = jnp.where(lane == COUNT_AT, 1.0, 0.0).astype(F32)
-    weights, sums = lax.fori_loop(0, NVAR, finish, ((zero,) * CS, (ones,) * CS))
+    weights, sums = lax.fori_loop(0, NVAR, advance, ((zero,) * CS, (ones,) * CS))
     for j in range(CS):
         tau_out = jnp.sum(jnp.where(lane == outlet, tau_ref[j], 0.0), axis=1, keepdims=True)
         rec_ref[j] = sums[j] + weights[j] * tau_out
@@ -222,9 +197,8 @@
 
 
 def weight_sum(x):
-    for by in (32, 16, 8):
-        x = x + pltpu.roll(x, LANES - by, 1)
-    return x
+    moved = [pltpu.roll(x, LANES - 8 * d, 1) for d in range(1, NVAR)]
+    return ((x + moved[0]) + (moved[1] + moved[2])) + (moved[3] + moved[4])
 
 
 def spread(values, first):
@@ -362,7 +336,8 @@
         return whole + pltpu.roll(whole, 64, 1)
 
     total = jnp.where(lane_ids(tile) < LANES // 2, folded(1 - row), folded(row))
-    sum_ref[...] = total
+    for n in range(FAR_COPIES):
+        sum_ref[n] = total
     for out_ref, in_ref in ((left_ref, to_left_ref), (right_ref, to_right_ref)):
         out_ref[: NVAR + 1] = in_ref[...]
         out_ref[NVAR + 1] = total[:CS]
@@ -382,7 +357,7 @@
     sides = [
         jnp.concatenate([ref[NVAR + 1], ref[NVAR + 2]], axis=0) for ref in (left_ref, right_ref)
     ]
-    other = (sum_ref[...] + far_ref[...]) + (sides[0] + sides[1])
+    other = (sum_ref[0] + far_ref[0]) + (sides[0] + sides[1])
     mine = pltpu.roll(other, LANES // 2, 1)
     other_count, my_count = (
         jnp.broadcast_to(x[:, COUNT_AT : COUNT_AT + 1], tile) for x in (other, mine)
@@ -511,21 +486,18 @@
         [edge, edge, side, side],
         in_specs=[HBM],
         scratch=[pltpu.SemaphoreType.DMA((4,))],
+        cost=pl.CostEstimate(flops=2_000_000_000, bytes_accessed=30_000_000, transcendentals=0),
     )(in_hbm(adjoint))
     halo = over_span(*edges[:2]) + over_pitch(*edges[2:])
-    part, record, jac, src, tau = call(
+    jac, src, tau = jac_blocks[0], source[0], pseudo_step[0]
+    part, record = call(
         interior_kernel,
         "interior",
-        [block, (CS, CP, LANES), ((7, NVAR) + block, BF16), block, (CS, CP, LANES)],
-        in_specs=[HBM] * 4,
-        scratch=[
-            pltpu.VMEM(block, F32),
-            pltpu.VMEM((7 * NVAR, CS, CP, LANES), F32),
-            pltpu.VMEM(block, F32),
-            pltpu.SemaphoreType.DMA((10,)),
-        ],
+        [block, (CS, CP, LANES)],
+        in_specs=[VM] * 4,
+        scratch=[pltpu.VMEM((7 * NVAR, CS, CP, LANES), F32)],
         cost=pl.CostEstimate(flops=9_000_000, bytes_accessed=3_000_000, transcendentals=0),
-    )(*(in_hbm(x) for x in (adjoint, source, pseudo_step, jac_blocks)))
+    )(adjoint[0], src, tau, jac)
     edge = (NVAR + 1, CP, LANES)
     side = (NVAR + 1, CS, LANES)
     first, message, full_record, *sends = call(
@@ -552,7 +524,7 @@
     )(band_map, first, src, tau, jac, face_cell, face_owner)
     tail = (NVAR + 3, CS, LANES)
     sums, *sides = call(
-        bands_kernel, "band_sums", [(CP, LANES), tail, tail], in_specs=[SM] + [VM] * 4
+        bands_kernel, "band_sums", [(FAR_COPIES, CP, LANES), tail, tail], in_specs=[SM] + [VM] * 4
     )(band_map, ids, records, *sends[2:])
     halo = halo + over_pitch(*sides)
     far = shifted(sums, "pitch", 2)

time: 66.8 us -> 65.8 us (0.985)
  Pallas kernels: 9.63 us -> 8.04 us
    pallas_call x2, Pallas kernels: 3.1 us -> 1.76 us  [the longest x1 1.06 us: on_device(): call(interior_kernel, 'interior', [block, (CS, CP, LANES)], in_specs=[VM]...]
  transfers between devices with their start and end apart: 10 -> 10, of which waited for: 3 -> 3; matrix products, arithmetic and copies ran while one was open for 0% -> 0% of each run, Pallas kernels for 8% -> 6%
where the time goes in v13:
time: 65.8 us; the launch traced here: 65.6 us
  starting transfers between devices  31.2 us (47%)
  blocking collectives  21.6 us (33%)
  Pallas kernels  8.04 us (12%)
  waiting for transfers between devices  3.95 us (6%)
  between operations  0.77 us (1%)
    ppermute x9, starting transfers between devices, shifted(): lax.ppermute(value, axis, [(i, (i + by) % devices) for i in range(devices)])  26 us
    all_to_all x1, blocking collectives, on_device(): lax.all_to_all(dense.reshape(peers, 1, 3 * LANES), ('span', 'pitch'), 0, 0)  21.6 us
    all_to_all x1, starting transfers between devices, on_device(): lax.all_to_all(message.reshape(groups, 1, 2 * LANES), ('row', 'span'), 0, 0)  5.16 us
    ppermute x9, waiting for transfers between devices, shifted(): lax.ppermute(value, axis, [(i, (i + by) % devices) for i in range(devices)])  3.93 us
    pallas_call x1, Pallas kernels, on_device(): call(settle_kernel, 'settle', [block, (6, CS, CP, LANES), ((2 * groups, L...  1.58 us
    pallas_call x1, Pallas kernels, on_device(): call(edge_kernel, 'edge_update', [block, (2 * groups, LANES), (CS, CP, LA...  1.37 us
    pallas_call x1, Pallas kernels, on_device(): call(cycle_kernel, 'cycle_update', [(1,) + block, (3 * peers, LANES)], in...  1.34 us
  transfers between devices with their start and end apart: 10, of which 3 were waited for; matrix products, arithmetic and copies ran while one was open for 0% of the time, Pallas kernels for 6%

profile of v13, /device:TPU:32, one launch (start us, length us, event | category | flops | bytes accessed | tf_op | source)
XLA Modules:
  0.0 65.6 jit_solution(10437158522871944681)
XLA Ops:
  0.7 0.9 %edges.1 = (f32[6,8,128]{2,1,0:T(8,128)S(1)}, f32[6,8,128]{2,1,0:T(8,128)S(1)}, f32[6,4,128]{2,1,0:T(4,128)S(1)}, f32[6,4,128]{2,1,0:T(4,128)S(1)}) custom-call(f32[1,6,4,8,128]{4,3,2,1,0:T(8,128)} %adj_ref.1), custom_call_target="tpu_custom_call" | custom-call | flops 2000000000 | bytes 30000000 | tf_op jit(solution)/shard_map/edges/pallas_call | solution.py:483
  1.6 1.6 %collective-permute-start = (f32[6,8,128]{2,1,0:T(8,128)S(1)}, f32[6,8,128]{2,1,0:T(8,128)S(1)}, u32[]{:S(2)}, u32[]{:S(2)}) collective-permute-start(f32[6,8,128]{2,1,0:T(8,128)S(1)} %get-tuple-element.29), channel_id=1, source_target_pairs={{0,4},{4,8},{8,12},{12,16},{16,20},{20,24},{24,28},{28,32},{32,36}... | collective-permute-start | bytes 73736 | tf_op jit(solution)/shard_map/ppermute | solution.py:463
  3.2 4.8 %collective-permute-start.1 = (f32[6,8,128]{2,1,0:T(8,128)S(1)}, f32[6,8,128]{2,1,0:T(8,128)S(1)}, u32[]{:S(2)}, u32[]{:S(2)}) collective-permute-start(f32[6,8,128]{2,1,0:T(8,128)S(1)} %get-tuple-element.30), channel_id=1, source_target_pairs={{0,124},{4,0},{8,4},{12,8},{16,12},{20,16},{24,20},{28,24},{32,28}... | collective-permute-start | bytes 73736 | tf_op jit(solution)/shard_map/ppermute | solution.py:463
  7.9 3.3 %collective-permute-start.2 = (f32[6,4,128]{2,1,0:T(4,128)S(1)}, f32[6,4,128]{2,1,0:T(4,128)S(1)}, u32[]{:S(2)}, u32[]{:S(2)}) collective-permute-start(f32[6,4,128]{2,1,0:T(4,128)S(1)} %get-tuple-element.31), channel_id=1, source_target_pairs={{0,1},{1,2},{2,3},{3,0},{4,5},{5,6},{6,7},{7,4},{8,9},{9,10},{10,1... | collective-permute-start | bytes 36872 | tf_op jit(solution)/shard_map/ppermute | solution.py:463
  11.2 2.1 %collective-permute-start.3 = (f32[6,4,128]{2,1,0:T(4,128)S(1)}, f32[6,4,128]{2,1,0:T(4,128)S(1)}, u32[]{:S(2)}, u32[]{:S(2)}) collective-permute-start(f32[6,4,128]{2,1,0:T(4,128)S(1)} %get-tuple-element.32), channel_id=1, source_target_pairs={{0,3},{1,0},{2,1},{3,2},{4,7},{5,4},{6,5},{7,6},{8,11},{9,8},{10,9... | collective-permute-start | bytes 36872 | tf_op jit(solution)/shard_map/ppermute | solution.py:463
  13.4 1.1 %interior.1 = (f32[6,4,8,128]{3,2,1,0:T(8,128)S(1)}, f32[4,8,128]{2,1,0:T(8,128)S(1)}) custom-call(f32[6,4,8,128]{3,2,1,0:T(8,128)S(1)} %bitcast.22, f32[6,4,8,128]{3,2,1,0:T(8,128)S(1)} %bitcast.14, f32[4,8,128]{2,1,0:T(8,128)S(1)} %bitcast.16, bf16[7,6,6,4,8,128]{5,4,3,2,1,0:T(8,128)(2,1)S(1)} %bitcast.9), custom_call_target="tpu_custom_call" | custom-call | flops 9000000 | bytes 3000000 | tf_op jit(solution)/shard_map/interior/pallas_call | solution.py:493
  14.5 0.6 collective-permute-done.2.left_ref
  15.0 1.5 %collective-permute-done.3.right_ref = f32[6,4,128]{2,1,0:T(4,128)S(1)} collective-permute-done((f32[6,4,128]{2,1,0:T(4,128)S(1)}, f32[6,4,128]{2,1,0:T(4,128)S(1)}, u32[]{:S(2)}, u32[]{:S(2)}) %collective-permute-start.3) | collective-permute-done | bytes 12320 | tf_op jit(solution)/shard_map/ppermute | solution.py:463
  16.5 1.4 %edge_update.1 = (f32[6,4,8,128]{3,2,1,0:T(8,128)S(1)}, f32[128,128]{1,0:T(8,128)}, f32[4,8,128]{2,1,0:T(8,128)S(1)}, f32[7,8,128]{2,1,0:T(8,128)S(1)}, f32[7,8,...) custom-call(f32[6,4,8,128]{3,2,1,0:T(8,128)S(1)} %get-tuple-element.27.part_ref, ...), custom_call_target="tpu_custom_call" | custom-call | tf_op jit(solution)/shard_map/edge_update/pallas_call | solution.py:503
  17.9 5.2 %all-to-all-start = ((f32[64,1,256]{2,1,0:T(1,128)}), f32[64,1,256]{2,1,0:T(1,128)S(1)}, u32[]{:S(2)}, u32[]{:S(2)}) async-start(f32[64,1,256]{2,1,0:T(1,128)} %bitcast.4), calls=%async_computation | async-start | bytes 131072 | tf_op jit(solution)/shard_map/all_to_all | solution.py:510
  23.0 1.5 %collective-permute-start.4 = (f32[7,8,128]{2,1,0:T(8,128)S(1)}, f32[7,8,128]{2,1,0:T(8,128)S(1)}, u32[]{:S(2)}, u32[]{:S(2)}) collective-permute-start(f32[7,8,128]{2,1,0:T(8,128)S(1)} %get-tuple-element.35), channel_id=1, source_target_pairs={{0,4},{4,8},{8,12},{12,16},{16,20},{20,24},{24,28},{28,32},{32,36}... | collective-permute-start | bytes 86024 | tf_op jit(solution)/shard_map/ppermute | solution.py:463
  24.6 4.8 %collective-permute-start.5 = (f32[7,8,128]{2,1,0:T(8,128)S(1)}, f32[7,8,128]{2,1,0:T(8,128)S(1)}, u32[]{:S(2)}, u32[]{:S(2)}) collective-permute-start(f32[7,8,128]{2,1,0:T(8,128)S(1)} %get-tuple-element.36), channel_id=1, source_target_pairs={{0,124},{4,0},{8,4},{12,8},{16,12},{20,16},{24,20},{28,24},{32,28}... | collective-permute-start | bytes 86024 | tf_op jit(solution)/shard_map/ppermute | solution.py:463
  29.4 1.6 %settle.1 = (f32[6,4,8,128]{3,2,1,0:T(8,128)S(1)}, f32[6,4,8,128]{3,2,1,0:T(8,128)S(1)}, f32[128,128]{1,0:T(8,128)S(1)}, f32[2,4,8,128]{3,2,1,0:T(8,128)S(1)}, bf16[128,384]{1,0:T(8,128)(2,1)S(1)}) custom-call(s32[2,128]{1,0:T(2,128)S(1)} %copy-done.4, f32[6,4,8,128]{3,2,1,0:T(8,128)S(1)} %get-tuple-element.33.f1_ref, f32[6,4,8,128]{3,2,1,0:T(8,128)S(1)} %bitcast.15, ...), custom_call_target="tpu_custom_call" | custom-call | flops 9000000 | bytes 3000000 | tf_op jit(solution)/shard_map/settle/pallas_call | solution.py:514
  30.9 0.0 all-to-all-done
  31.0 0.7 %band_sums.1 = (f32[5,8,128]{2,1,0:T(8,128)S(1)}, f32[9,4,128]{2,1,0:T(4,128)S(1)}, f32[9,4,128]{2,1,0:T(4,128)S(1)}) custom-call(s32[2,128]{1,0:T(2,128)S(1)} %copy-done.4, f32[128,128]{1,0:T(8,128)S(1)} %get-tuple-element.37.ids_ref, f32[128,128]{1,0:T(8,128)S(1)} %bitcast.20, f32[7,4,128]{2,1,0:T(4,128)S(1)} %get-tuple-element.39.to_left_ref, ...), custom_call_target="tpu_custom_call" | custom-call | tf_op jit(solution)/shard_map/band_sums/pallas_call | solution.py:526
  31.7 3.9 %collective-permute-start.8 = (f32[5,8,128]{2,1,0:T(8,128)S(1)}, f32[5,8,128]{2,1,0:T(8,128)S(1)}, u32[]{:S(2)}, u32[]{:S(2)}) collective-permute-start(f32[5,8,128]{2,1,0:T(8,128)S(1)} %get-tuple-element.46.sum_ref), channel_id=1, source_target_pairs={{0,2},{1,3},{2,0},{3,1},{4,6},{5,7},{6,4},{7,5},{8,10},{9,11},{10,... | collective-permute-start | bytes 61448 | tf_op jit(solution)/shard_map/ppermute | solution.py:463
  35.5 1.2 %collective-permute-start.6 = (f32[9,4,128]{2,1,0:T(4,128)S(1)}, f32[9,4,128]{2,1,0:T(4,128)S(1)}, u32[]{:S(2)}, u32[]{:S(2)}) collective-permute-start(f32[9,4,128]{2,1,0:T(4,128)S(1)} %get-tuple-element.41), channel_id=1, source_target_pairs={{0,1},{1,2},{2,3},{3,0},{4,5},{5,6},{6,7},{7,4},{8,9},{9,10},{10,1... | collective-permute-start | bytes 55304 | tf_op jit(solution)/shard_map/ppermute | solution.py:463
  36.7 2.9 %collective-permute-start.7 = (f32[9,4,128]{2,1,0:T(4,128)S(1)}, f32[9,4,128]{2,1,0:T(4,128)S(1)}, u32[]{:S(2)}, u32[]{:S(2)}) collective-permute-start(f32[9,4,128]{2,1,0:T(4,128)S(1)} %get-tuple-element.42), channel_id=1, source_target_pairs={{0,3},{1,0},{2,1},{3,2},{4,7},{5,4},{6,5},{7,6},{8,11},{9,8},{10,9... | collective-permute-start | bytes 55304 | tf_op jit(solution)/shard_map/ppermute | solution.py:463
  39.7 1.9 %collective-permute-done.6.left_ref = f32[9,4,128]{2,1,0:T(4,128)S(1)} collective-permute-done((f32[9,4,128]{2,1,0:T(4,128)S(1)}, f32[9,4,128]{2,1,0:T(4,128)S(1)}, u32[]{:S(2)}, u32[]{:S(2)}) %collective-permute-start.6) | collective-permute-done | bytes 18464 | tf_op jit(solution)/shard_map/ppermute | solution.py:463
  41.6 0.0 collective-permute-done.7.right_ref
  41.6 0.4 settle_edges.1
  42.1 1.3 %cycle_update.1 = (f32[1,6,4,8,128]{4,3,2,1,0:T(8,128)}, f32[384,128]{1,0:T(8,128)S(1)}) custom-call(f32[6,4,8,128]{3,2,1,0:T(8,128)S(1)} %get-tuple-element.43.part_ref, f32[4,8,128]{2,1,0:T(8,128)S(1)} %get-tuple-element.44.rec_ref, f32[6,4,8,128]{3,2,1,0:T(8,128)S(1)} %get-tuple-element.45.pack_ref, f32[5,8,128]{2,1,0:T(8,128)S(1)} %get-tuple-element.46.sum_ref, ...), custom_call_target="tpu_custom_call" | custom-call | tf_op jit(solution)/shard_map/cycle_update/pallas_call | solution.py:539
  43.4 21.6 %all_to_all.10 = f32[128,1,384]{2,1,0:T(1,128)S(1)} all-to-all(f32[128,1,384]{2,1,0:T(1,128)S(1)} %bitcast.21), channel_id=1, replica_groups=mesh['row'=2,'span'=32,'pitch'=4] {'span','pitch'}, dimensions={0} | all-to-all | bytes 393216 | tf_op jit(solution)/shard_map/all_to_all | solution.py:549
  65.1 0.6 node_sums.1
  (22 shorter events, 0.1 us)
Async XLA Ops:
  0.6 12.7 %copy-start.3 = (f32[1,6,4,8,128]{4,3,2,1,0:T(8,128)S(1)}, f32[1,6,4,8,128]{4,3,2,1,0:T(8,128)}, u32[]{:S(2)}) copy-start(f32[1,6,4,8,128]{4,3,2,1,0:T(8,128)} %adj_ref.1) | copy-start | bytes 294916
  0.6 12.7 %copy-start = (bf16[1,7,6,6,4,8,128]{6,5,4,3,2,1,0:T(8,128)(2,1)S(1)}, bf16[1,7,6,6,4,8,128]{6,5,4,3,2,1,0:T(8,128)(2,1)}, u32[]{:S(2)}) copy-start(bf16[1,7,6,6,4,8,128]{6,5,4,3,2,1,0:T(8,128)(2,1)} %param.11) | copy-start | bytes 6193156
  0.7 12.7 %copy-start.2 = (f32[1,4,8,128]{3,2,1,0:T(8,128)S(1)}, f32[1,4,8,128]{3,2,1,0:T(8,128)}, u32[]{:S(2)}) copy-start(f32[1,4,8,128]{3,2,1,0:T(8,128)} %param.10) | copy-start | bytes 49156
  0.7 12.7 %copy-start.1 = (f32[1,6,4,8,128]{4,3,2,1,0:T(8,128)S(1)}, f32[1,6,4,8,128]{4,3,2,1,0:T(8,128)}, u32[]{:S(2)}) copy-start(f32[1,6,4,8,128]{4,3,2,1,0:T(8,128)} %param.9) | copy-start | bytes 294916
  1.6 14.9 %collective-permute-start = (f32[6,8,128]{2,1,0:T(8,128)S(1)}, f32[6,8,128]{2,1,0:T(8,128)S(1)}, u32[]{:S(2)}, u32[]{:S(2)}) collective-permute-start(f32[6,8,128]{2,1,0:T(8,128)S(1)} %get-tuple-element.29), channel_id=1, source_target_pairs={{0,4},{4,8},{8,12},{12,16},{16,20},{20,24},{24,28},{28,32},{32,36}... | collective-permute-start | bytes 73736 | tf_op jit(solution)/shard_map/ppermute | solution.py:463
  3.2 13.3 %collective-permute-start.1 = (f32[6,8,128]{2,1,0:T(8,128)S(1)}, f32[6,8,128]{2,1,0:T(8,128)S(1)}, u32[]{:S(2)}, u32[]{:S(2)}) collective-permute-start(f32[6,8,128]{2,1,0:T(8,128)S(1)} %get-tuple-element.30), channel_id=1, source_target_pairs={{0,124},{4,0},{8,4},{12,8},{16,12},{20,16},{24,20},{28,24},{32,28}... | collective-permute-start | bytes 73736 | tf_op jit(solution)/shard_map/ppermute | solution.py:463
  7.9 7.1 %collective-permute-start.2 = (f32[6,4,128]{2,1,0:T(4,128)S(1)}, f32[6,4,128]{2,1,0:T(4,128)S(1)}, u32[]{:S(2)}, u32[]{:S(2)}) collective-permute-start(f32[6,4,128]{2,1,0:T(4,128)S(1)} %get-tuple-element.31), channel_id=1, source_target_pairs={{0,1},{1,2},{2,3},{3,0},{4,5},{5,6},{6,7},{7,4},{8,9},{9,10},{10,1... | collective-permute-start | bytes 36872 | tf_op jit(solution)/shard_map/ppermute | solution.py:463
  11.2 5.3 %collective-permute-start.3 = (f32[6,4,128]{2,1,0:T(4,128)S(1)}, f32[6,4,128]{2,1,0:T(4,128)S(1)}, u32[]{:S(2)}, u32[]{:S(2)}) collective-permute-start(f32[6,4,128]{2,1,0:T(4,128)S(1)} %get-tuple-element.32), channel_id=1, source_target_pairs={{0,3},{1,0},{2,1},{3,2},{4,7},{5,4},{6,5},{7,6},{8,11},{9,8},{10,9... | collective-permute-start | bytes 36872 | tf_op jit(solution)/shard_map/ppermute | solution.py:463
  13.4 16.0 %copy-start.4 = (s32[2,128]{1,0:T(2,128)S(1)}, s32[2,128]{1,0:T(2,128)}, u32[]{:S(2)}) copy-start(s32[2,128]{1,0:T(2,128)} %bands_ref.3) | copy-start | bytes 3076
  13.4 16.0 %copy-start.5 = (s32[1,1,1,128]{3,2,1,0:T(1,128)S(1)}, s32[1,1,1,128]{3,2,1,0:T(1,128)}, u32[]{:S(2)}) copy-start(s32[1,1,1,128]{3,2,1,0:T(1,128)} %cell_ref.3) | copy-start | bytes 1540
  13.4 16.0 %copy-start.6 = (s32[1,1,1,128]{3,2,1,0:T(1,128)S(1)}, s32[1,1,1,128]{3,2,1,0:T(1,128)}, u32[]{:S(2)}) copy-start(s32[1,1,1,128]{3,2,1,0:T(1,128)} %owner_ref.3) | copy-start | bytes 1540
  16.5 23.2 %copy-start.7 = (f32[1,1,1,18,128]{4,2,3,1,0:T(1,128)S(1)}, f32[1,1,1,18,128]{4,2,3,1,0:T(1,128)}, u32[]{:S(2)}) copy-start(f32[1,1,1,18,128]{4,2,3,1,0:T(1,128)} %param.15) | copy-start | bytes 27652
  17.9 13.1 %all-to-all-start = ((f32[64,1,256]{2,1,0:T(1,128)}), f32[64,1,256]{2,1,0:T(1,128)S(1)}, u32[]{:S(2)}, u32[]{:S(2)}) async-start(f32[64,1,256]{2,1,0:T(1,128)} %bitcast.4), calls=%async_computation | async-start | bytes 131072 | tf_op jit(solution)/shard_map/all_to_all | solution.py:510
  23.0 16.6 %collective-permute-start.4 = (f32[7,8,128]{2,1,0:T(8,128)S(1)}, f32[7,8,128]{2,1,0:T(8,128)S(1)}, u32[]{:S(2)}, u32[]{:S(2)}) collective-permute-start(f32[7,8,128]{2,1,0:T(8,128)S(1)} %get-tuple-element.35), channel_id=1, source_target_pairs={{0,4},{4,8},{8,12},{12,16},{16,20},{20,24},{24,28},{28,32},{32,36}... | collective-permute-start | bytes 86024 | tf_op jit(solution)/shard_map/ppermute | solution.py:463
  24.6 15.1 %collective-permute-start.5 = (f32[7,8,128]{2,1,0:T(8,128)S(1)}, f32[7,8,128]{2,1,0:T(8,128)S(1)}, u32[]{:S(2)}, u32[]{:S(2)}) collective-permute-start(f32[7,8,128]{2,1,0:T(8,128)S(1)} %get-tuple-element.36), channel_id=1, source_target_pairs={{0,124},{4,0},{8,4},{12,8},{16,12},{20,16},{24,20},{28,24},{32,28}... | collective-permute-start | bytes 86024 | tf_op jit(solution)/shard_map/ppermute | solution.py:463
  31.7 10.4 %collective-permute-start.8 = (f32[5,8,128]{2,1,0:T(8,128)S(1)}, f32[5,8,128]{2,1,0:T(8,128)S(1)}, u32[]{:S(2)}, u32[]{:S(2)}) collective-permute-start(f32[5,8,128]{2,1,0:T(8,128)S(1)} %get-tuple-element.46.sum_ref), channel_id=1, source_target_pairs={{0,2},{1,3},{2,0},{3,1},{4,6},{5,7},{6,4},{7,5},{8,10},{9,11},{10,... | collective-permute-start | bytes 61448 | tf_op jit(solution)/shard_map/ppermute | solution.py:463
  35.5 6.0 %collective-permute-start.6 = (f32[9,4,128]{2,1,0:T(4,128)S(1)}, f32[9,4,128]{2,1,0:T(4,128)S(1)}, u32[]{:S(2)}, u32[]{:S(2)}) collective-permute-start(f32[9,4,128]{2,1,0:T(4,128)S(1)} %get-tuple-element.41), channel_id=1, source_target_pairs={{0,1},{1,2},{2,3},{3,0},{4,5},{5,6},{6,7},{7,4},{8,9},{9,10},{10,1... | collective-permute-start | bytes 55304 | tf_op jit(solution)/shard_map/ppermute | solution.py:463
  36.7 4.9 %collective-permute-start.7 = (f32[9,4,128]{2,1,0:T(4,128)S(1)}, f32[9,4,128]{2,1,0:T(4,128)S(1)}, u32[]{:S(2)}, u32[]{:S(2)}) collective-permute-start(f32[9,4,128]{2,1,0:T(4,128)S(1)} %get-tuple-element.42), channel_id=1, source_target_pairs={{0,3},{1,0},{2,1},{3,2},{4,7},{5,4},{6,5},{7,6},{8,11},{9,8},{10,9... | collective-permute-start | bytes 55304 | tf_op jit(solution)/shard_map/ppermute | solution.py:463

commit v14 on v12

--- a/solution.py
+++ b/solution.py
@@ -32,12 +32,12 @@
     return hi, mid, low
 
 
-def dot3(x, onehot, dims):
-    parts = [
-        lax.dot_general(part, onehot, (dims, ((), ())), preferred_element_type=F32)
-        for part in split3(x)
-    ]
-    return parts[0] + (parts[1] + parts[2])
+def dot3(x, onehot):
+    return jnp.dot(
+        jnp.concatenate(split3(x), axis=1),
+        jnp.concatenate([onehot] * 3, axis=0),
+        preferred_element_type=F32,
+    )
 
 
 def fill_stencil(vs, field, up, down, left, right, lower, upper):
@@ -315,7 +315,7 @@
     cells = cell_ref[0, 0]
     square = (LANES, LANES)
     axial_pick = (row_ids(square) == cells % LANES).astype(F32).astype(BF16)
-    picked = dot3(part2_ref[...].reshape(NVAR * CS * CP, LANES), axial_pick, ((1,), (0,)))
+    picked = dot3(part2_ref[...].reshape(NVAR * CS * CP, LANES), axial_pick)
     here = row_ids((CS * CP, LANES)) == cells // LANES
     for c in range(NVAR):
         block = picked[c * CS * CP : (c + 1) * CS * CP]
@@ -430,6 +430,13 @@
         preferred_element_type=F32,
     )
     write.wait()
+
+
+def third_kernel(parts_ref, out_ref):
+    folded = jnp.sum(parts_ref[...].reshape(-1, 24, LANES), axis=0)
+    coord = row_ids(folded.shape) % 3
+    for k in range(3):
+        out_ref[k] = jnp.sum(jnp.where(coord == k, folded, 0.0), axis=0, keepdims=True)
 
 
 VM = pl.BlockSpec(memory_space=pltpu.VMEM)
@@ -547,8 +554,10 @@
         face_weight,
     )
     parts = lax.all_to_all(dense.reshape(peers, 1, 3 * LANES), ("span", "pitch"), 0, 0)
-    nodes = jnp.sum(parts, axis=(0, 1)).reshape(1, 3, LANES)
-    return field, nodes
+    (nodes,) = call(third_kernel, "node_sums", [(3, 1, LANES)], in_specs=[VM])(
+        parts.reshape(3 * peers, LANES)
+    )
+    return field, nodes.transpose(1, 0, 2)
 
 
 def solution(mesh):

time: 65 us -> 64.8 us (level)
  no operation moved by 1% of the time
where the time goes in v14:
time: 64.8 us; the launch traced here: 64.7 us
  starting transfers between devices  30.8 us (48%)
  blocking collectives  20.2 us (31%)
  Pallas kernels  8.3 us (13%)
  waiting for transfers between devices  4.58 us (7%)
  between operations  0.76 us (1%)
    ppermute x8, starting transfers between devices, shifted(): lax.ppermute(value, axis, [(i, (i + by) % devices) for i in range(devices)])  22.3 us
    all_to_all x1, blocking collectives, on_device(): lax.all_to_all(dense.reshape(peers, 1, 3 * LANES), ('span', 'pitch'), 0, 0)  20.2 us
    all_to_all x1, starting transfers between devices, on_device(): lax.all_to_all(message.reshape(devices, 1, 2 * LANES), ('row', 'span', 'p...  8.47 us
    ppermute x8, waiting for transfers between devices, shifted(): lax.ppermute(value, axis, [(i, (i + by) % devices) for i in range(devices)])  3.86 us
    pallas_call x1, Pallas kernels, on_device(): call(cycle_kernel, 'cycle_update', [(1,) + block, (3 * peers, LANES)], in...  2.14 us
    pallas_call x1, Pallas kernels, on_device(): call(settle_kernel, 'settle', [block, (6, CS, CP, LANES), ((2 * devices,...  1.63 us
    pallas_call x1, Pallas kernels, on_device(): call(edge_kernel, 'edge_update', [block, (2 * devices, LANES), (CS, CP, L...  1.5 us
  transfers between devices with their start and end apart: 9, of which 4 were waited for; matrix products, arithmetic and copies ran while one was open for 0% of the time, Pallas kernels for 5%

profile of v14, /device:TPU:32, one launch (start us, length us, event | category | flops | bytes accessed | tf_op | source)
XLA Modules:
  0.0 64.7 jit_solution(8567187837612649979)
XLA Ops:
  0.7 0.9 %edges.1 = (f32[6,8,128]{2,1,0:T(8,128)S(1)}, f32[6,8,128]{2,1,0:T(8,128)S(1)}, f32[6,4,128]{2,1,0:T(4,128)S(1)}, f32[6,4,128]{2,1,0:T(4,128)S(1)}) custom-call(f32[1,6,4,8,128]{4,3,2,1,0:T(8,128)} %adj_ref.1), custom_call_target="tpu_custom_call" | custom-call | flops 2000000000 | bytes 30000000 | tf_op jit(solution)/shard_map/edges/pallas_call | solution.py:490
  1.6 1.6 %collective-permute-start = (f32[6,8,128]{2,1,0:T(8,128)S(1)}, f32[6,8,128]{2,1,0:T(8,128)S(1)}, u32[]{:S(2)}, u32[]{:S(2)}) collective-permute-start(f32[6,8,128]{2,1,0:T(8,128)S(1)} %get-tuple-element.26), channel_id=1, source_target_pairs={{0,4},{4,8},{8,12},{12,16},{16,20},{20,24},{24,28},{28,32},{32,36}... | collective-permute-start | bytes 73736 | tf_op jit(solution)/shard_map/ppermute | solution.py:470
  3.2 4.8 %collective-permute-start.1 = (f32[6,8,128]{2,1,0:T(8,128)S(1)}, f32[6,8,128]{2,1,0:T(8,128)S(1)}, u32[]{:S(2)}, u32[]{:S(2)}) collective-permute-start(f32[6,8,128]{2,1,0:T(8,128)S(1)} %get-tuple-element.27), channel_id=1, source_target_pairs={{0,124},{4,0},{8,4},{12,8},{16,12},{20,16},{24,20},{28,24},{32,28}... | collective-permute-start | bytes 73736 | tf_op jit(solution)/shard_map/ppermute | solution.py:470
  7.9 3.3 %collective-permute-start.2 = (f32[6,4,128]{2,1,0:T(4,128)S(1)}, f32[6,4,128]{2,1,0:T(4,128)S(1)}, u32[]{:S(2)}, u32[]{:S(2)}) collective-permute-start(f32[6,4,128]{2,1,0:T(4,128)S(1)} %get-tuple-element.28), channel_id=1, source_target_pairs={{0,1},{1,2},{2,3},{3,0},{4,5},{5,6},{6,7},{7,4},{8,9},{9,10},{10,1... | collective-permute-start | bytes 36872 | tf_op jit(solution)/shard_map/ppermute | solution.py:470
  11.2 2.1 %collective-permute-start.3 = (f32[6,4,128]{2,1,0:T(4,128)S(1)}, f32[6,4,128]{2,1,0:T(4,128)S(1)}, u32[]{:S(2)}, u32[]{:S(2)}) collective-permute-start(f32[6,4,128]{2,1,0:T(4,128)S(1)} %get-tuple-element.29), channel_id=1, source_target_pairs={{0,3},{1,0},{2,1},{3,2},{4,7},{5,4},{6,5},{7,6},{8,11},{9,8},{10,9... | collective-permute-start | bytes 36872 | tf_op jit(solution)/shard_map/ppermute | solution.py:470
  13.4 0.0 copy-start.5
  13.4 0.0 copy-start.6
  13.4 1.1 %interior.1 = (f32[6,4,8,128]{3,2,1,0:T(8,128)S(1)}, f32[4,8,128]{2,1,0:T(8,128)S(1)}) custom-call(f32[6,4,8,128]{3,2,1,0:T(8,128)S(1)} %bitcast.22, f32[6,4,8,128]{3,2,1,0:T(8,128)S(1)} %bitcast.15, f32[4,8,128]{2,1,0:T(8,128)S(1)} %bitcast.17, bf16[7,6,6,4,8,128]{5,4,3,2,1,0:T(8,128)(2,1)S(1)} %bitcast.9), custom_call_target="tpu_custom_call" | custom-call | flops 9000000 | bytes 3000000 | tf_op jit(solution)/shard_map/interior/pallas_call | solution.py:500
  14.5 0.6 collective-permute-done.2.left_ref
  15.0 1.5 %collective-permute-done.3.right_ref = f32[6,4,128]{2,1,0:T(4,128)S(1)} collective-permute-done((f32[6,4,128]{2,1,0:T(4,128)S(1)}, f32[6,4,128]{2,1,0:T(4,128)S(1)}, u32[]{:S(2)}, u32[]{:S(2)}) %collective-permute-start.3) | collective-permute-done | bytes 12320 | tf_op jit(solution)/shard_map/ppermute | solution.py:470
  16.5 1.5 %edge_update.1 = (f32[6,4,8,128]{3,2,1,0:T(8,128)S(1)}, f32[512,128]{1,0:T(8,128)}, f32[4,8,128]{2,1,0:T(8,128)S(1)}, f32[7,8,128]{2,1,0:T(8,128)S(1)}, f32[7,8,...) custom-call(f32[6,4,8,128]{3,2,1,0:T(8,128)S(1)} %get-tuple-element.24.part_ref, ...), custom_call_target="tpu_custom_call" | custom-call | tf_op jit(solution)/shard_map/edge_update/pallas_call | solution.py:510
  18.0 8.5 %all-to-all-start = ((f32[256,1,256]{2,1,0:T(1,128)}), f32[256,1,256]{2,1,0:T(1,128)S(1)}, u32[]{:S(2)}, u32[]{:S(2)}) async-start(f32[256,1,256]{2,1,0:T(1,128)} %bitcast.4), calls=%async_computation | async-start | bytes 524288 | tf_op jit(solution)/shard_map/all_to_all | solution.py:522
  26.5 1.6 %collective-permute-start.4 = (f32[7,8,128]{2,1,0:T(8,128)S(1)}, f32[7,8,128]{2,1,0:T(8,128)S(1)}, u32[]{:S(2)}, u32[]{:S(2)}) collective-permute-start(f32[7,8,128]{2,1,0:T(8,128)S(1)} %get-tuple-element.32), channel_id=1, source_target_pairs={{0,4},{4,8},{8,12},{12,16},{16,20},{20,24},{24,28},{28,32},{32,36}... | collective-permute-start | bytes 86024 | tf_op jit(solution)/shard_map/ppermute | solution.py:470
  28.0 4.8 %collective-permute-start.5 = (f32[7,8,128]{2,1,0:T(8,128)S(1)}, f32[7,8,128]{2,1,0:T(8,128)S(1)}, u32[]{:S(2)}, u32[]{:S(2)}) collective-permute-start(f32[7,8,128]{2,1,0:T(8,128)S(1)} %get-tuple-element.33), channel_id=1, source_target_pairs={{0,124},{4,0},{8,4},{12,8},{16,12},{20,16},{24,20},{28,24},{32,28}... | collective-permute-start | bytes 86024 | tf_op jit(solution)/shard_map/ppermute | solution.py:470
  32.8 2.9 %collective-permute-start.6 = (f32[7,4,128]{2,1,0:T(4,128)S(1)}, f32[7,4,128]{2,1,0:T(4,128)S(1)}, u32[]{:S(2)}, u32[]{:S(2)}) collective-permute-start(f32[7,4,128]{2,1,0:T(4,128)S(1)} %get-tuple-element.34), channel_id=1, source_target_pairs={{0,1},{1,2},{2,3},{3,0},{4,5},{5,6},{6,7},{7,4},{8,9},{9,10},{10,1... | collective-permute-start | bytes 43016 | tf_op jit(solution)/shard_map/ppermute | solution.py:470
  35.7 1.4 %collective-permute-start.7 = (f32[7,4,128]{2,1,0:T(4,128)S(1)}, f32[7,4,128]{2,1,0:T(4,128)S(1)}, u32[]{:S(2)}, u32[]{:S(2)}) collective-permute-start(f32[7,4,128]{2,1,0:T(4,128)S(1)} %get-tuple-element.35), channel_id=1, source_target_pairs={{0,3},{1,0},{2,1},{3,2},{4,7},{5,4},{6,5},{7,6},{8,11},{9,8},{10,9... | collective-permute-start | bytes 43016 | tf_op jit(solution)/shard_map/ppermute | solution.py:470
  37.1 1.6 %settle.1 = (f32[6,4,8,128]{3,2,1,0:T(8,128)S(1)}, f32[6,4,8,128]{3,2,1,0:T(8,128)S(1)}, f32[512,128]{1,0:T(8,128)S(1)}, f32[2,4,8,128]{3,2,1,0:T(8,128)S(1)}, bf16[128,384]{1,0:T(8,128)(2,1)S(1)}) custom-call(s32[2,128]{1,0:T(2,128)S(1)} %copy-done.4, f32[6,4,8,128]{3,2,1,0:T(8,128)S(1)} %get-tuple-element.30.f1_ref, f32[6,4,8,128]{3,2,1,0:T(8,128)S(1)} %bitcast.16, ...), custom_call_target="tpu_custom_call" | custom-call | flops 9000000 | bytes 3000000 | tf_op jit(solution)/shard_map/settle/pallas_call | solution.py:526
  38.7 0.0 collective-permute-done.6.left_ref
  38.8 1.8 %collective-permute-done.7.right_ref = f32[7,4,128]{2,1,0:T(4,128)S(1)} collective-permute-done((f32[7,4,128]{2,1,0:T(4,128)S(1)}, f32[7,4,128]{2,1,0:T(4,128)S(1)}, u32[]{:S(2)}, u32[]{:S(2)}) %collective-permute-start.7) | collective-permute-done | bytes 14368 | tf_op jit(solution)/shard_map/ppermute | solution.py:470
  40.6 0.4 settle_edges.1
  41.0 0.7 %all-to-all-done = f32[256,1,256]{2,1,0:T(1,128)S(1)} async-done(((f32[256,1,256]{2,1,0:T(1,128)}), f32[256,1,256]{2,1,0:T(1,128)S(1)}, u32[]{:S(2)}, u32[]{:S(2)}) %all-to-all-start) | async-done | bytes 262176 | tf_op jit(solution)/shard_map/all_to_all | solution.py:522
  41.8 2.1 %cycle_update.1 = (f32[1,6,4,8,128]{4,3,2,1,0:T(8,128)}, f32[384,128]{1,0:T(8,128)S(1)}) custom-call(s32[2,128]{1,0:T(2,128)S(1)} %copy-done.4, f32[6,4,8,128]{3,2,1,0:T(8,128)S(1)} %get-tuple-element.36.part_ref, f32[4,8,128]{2,1,0:T(8,128)S(1)} %get-tuple-element.37.rec_ref, f32[6,4,8,128]{3,2,1,0:T(8,128)S(1)} %get-tuple-element.38.pack_ref, ...), custom_call_target="tpu_custom_call" | custom-call | tf_op jit(solution)/shard_map/cycle_update/pallas_call | solution.py:545
  43.9 20.2 %all_to_all.10 = f32[128,1,384]{2,1,0:T(1,128)S(1)} all-to-all(f32[128,1,384]{2,1,0:T(1,128)S(1)} %bitcast.21), channel_id=1, replica_groups=mesh['row'=2,'span'=32,'pitch'=4] {'span','pitch'}, dimensions={0} | all-to-all | bytes 393216 | tf_op jit(solution)/shard_map/all_to_all | solution.py:556
  64.1 0.6 node_sums.1
  (19 shorter events, 0.0 us)
Async XLA Ops:
  0.6 12.7 %copy-start.3 = (f32[1,6,4,8,128]{4,3,2,1,0:T(8,128)S(1)}, f32[1,6,4,8,128]{4,3,2,1,0:T(8,128)}, u32[]{:S(2)}) copy-start(f32[1,6,4,8,128]{4,3,2,1,0:T(8,128)} %adj_ref.1) | copy-start | bytes 294916
  0.6 12.7 %copy-start = (bf16[1,7,6,6,4,8,128]{6,5,4,3,2,1,0:T(8,128)(2,1)S(1)}, bf16[1,7,6,6,4,8,128]{6,5,4,3,2,1,0:T(8,128)(2,1)}, u32[]{:S(2)}) copy-start(bf16[1,7,6,6,4,8,128]{6,5,4,3,2,1,0:T(8,128)(2,1)} %param.11) | copy-start | bytes 6193156
  0.7 12.7 %copy-start.2 = (f32[1,4,8,128]{3,2,1,0:T(8,128)S(1)}, f32[1,4,8,128]{3,2,1,0:T(8,128)}, u32[]{:S(2)}) copy-start(f32[1,4,8,128]{3,2,1,0:T(8,128)} %param.10) | copy-start | bytes 49156
  0.7 12.7 %copy-start.1 = (f32[1,6,4,8,128]{4,3,2,1,0:T(8,128)S(1)}, f32[1,6,4,8,128]{4,3,2,1,0:T(8,128)}, u32[]{:S(2)}) copy-start(f32[1,6,4,8,128]{4,3,2,1,0:T(8,128)} %param.9) | copy-start | bytes 294916
  1.6 14.9 %collective-permute-start = (f32[6,8,128]{2,1,0:T(8,128)S(1)}, f32[6,8,128]{2,1,0:T(8,128)S(1)}, u32[]{:S(2)}, u32[]{:S(2)}) collective-permute-start(f32[6,8,128]{2,1,0:T(8,128)S(1)} %get-tuple-element.26), channel_id=1, source_target_pairs={{0,4},{4,8},{8,12},{12,16},{16,20},{20,24},{24,28},{28,32},{32,36}... | collective-permute-start | bytes 73736 | tf_op jit(solution)/shard_map/ppermute | solution.py:470
  3.2 13.3 %collective-permute-start.1 = (f32[6,8,128]{2,1,0:T(8,128)S(1)}, f32[6,8,128]{2,1,0:T(8,128)S(1)}, u32[]{:S(2)}, u32[]{:S(2)}) collective-permute-start(f32[6,8,128]{2,1,0:T(8,128)S(1)} %get-tuple-element.27), channel_id=1, source_target_pairs={{0,124},{4,0},{8,4},{12,8},{16,12},{20,16},{24,20},{28,24},{32,28}... | collective-permute-start | bytes 73736 | tf_op jit(solution)/shard_map/ppermute | solution.py:470
  7.9 7.1 %collective-permute-start.2 = (f32[6,4,128]{2,1,0:T(4,128)S(1)}, f32[6,4,128]{2,1,0:T(4,128)S(1)}, u32[]{:S(2)}, u32[]{:S(2)}) collective-permute-start(f32[6,4,128]{2,1,0:T(4,128)S(1)} %get-tuple-element.28), channel_id=1, source_target_pairs={{0,1},{1,2},{2,3},{3,0},{4,5},{5,6},{6,7},{7,4},{8,9},{9,10},{10,1... | collective-permute-start | bytes 36872 | tf_op jit(solution)/shard_map/ppermute | solution.py:470
  11.2 5.3 %collective-permute-start.3 = (f32[6,4,128]{2,1,0:T(4,128)S(1)}, f32[6,4,128]{2,1,0:T(4,128)S(1)}, u32[]{:S(2)}, u32[]{:S(2)}) collective-permute-start(f32[6,4,128]{2,1,0:T(4,128)S(1)} %get-tuple-element.29), channel_id=1, source_target_pairs={{0,3},{1,0},{2,1},{3,2},{4,7},{5,4},{6,5},{7,6},{8,11},{9,8},{10,9... | collective-permute-start | bytes 36872 | tf_op jit(solution)/shard_map/ppermute | solution.py:470
  13.4 23.7 %copy-start.7 = (f32[1,1,1,18,128]{4,2,3,1,0:T(1,128)S(1)}, f32[1,1,1,18,128]{4,2,3,1,0:T(1,128)}, u32[]{:S(2)}) copy-start(f32[1,1,1,18,128]{4,2,3,1,0:T(1,128)} %param.15) | copy-start | bytes 27652
  13.4 23.7 %copy-start.4 = (s32[2,128]{1,0:T(2,128)S(1)}, s32[2,128]{1,0:T(2,128)}, u32[]{:S(2)}) copy-start(s32[2,128]{1,0:T(2,128)} %bands_ref.3) | copy-start | bytes 3076
  13.4 23.7 %copy-start.5 = (s32[1,1,1,128]{3,2,1,0:T(1,128)S(1)}, s32[1,1,1,128]{3,2,1,0:T(1,128)}, u32[]{:S(2)}) copy-start(s32[1,1,1,128]{3,2,1,0:T(1,128)} %cell_ref.3) | copy-start | bytes 1540
  13.4 23.7 %copy-start.6 = (s32[1,1,1,128]{3,2,1,0:T(1,128)S(1)}, s32[1,1,1,128]{3,2,1,0:T(1,128)}, u32[]{:S(2)}) copy-start(s32[1,1,1,128]{3,2,1,0:T(1,128)} %owner_ref.3) | copy-start | bytes 1540
  18.0 23.8 %all-to-all-start = ((f32[256,1,256]{2,1,0:T(1,128)}), f32[256,1,256]{2,1,0:T(1,128)S(1)}, u32[]{:S(2)}, u32[]{:S(2)}) async-start(f32[256,1,256]{2,1,0:T(1,128)} %bitcast.4), calls=%async_computation | async-start | bytes 524288 | tf_op jit(solution)/shard_map/all_to_all | solution.py:522
  26.5 14.1 %collective-permute-start.4 = (f32[7,8,128]{2,1,0:T(8,128)S(1)}, f32[7,8,128]{2,1,0:T(8,128)S(1)}, u32[]{:S(2)}, u32[]{:S(2)}) collective-permute-start(f32[7,8,128]{2,1,0:T(8,128)S(1)} %get-tuple-element.32), channel_id=1, source_target_pairs={{0,4},{4,8},{8,12},{12,16},{16,20},{20,24},{24,28},{28,32},{32,36}... | collective-permute-start | bytes 86024 | tf_op jit(solution)/shard_map/ppermute | solution.py:470
  28.0 12.6 %collective-permute-start.5 = (f32[7,8,128]{2,1,0:T(8,128)S(1)}, f32[7,8,128]{2,1,0:T(8,128)S(1)}, u32[]{:S(2)}, u32[]{:S(2)}) collective-permute-start(f32[7,8,128]{2,1,0:T(8,128)S(1)} %get-tuple-element.33), channel_id=1, source_target_pairs={{0,124},{4,0},{8,4},{12,8},{16,12},{20,16},{24,20},{28,24},{32,28}... | collective-permute-start | bytes 86024 | tf_op jit(solution)/shard_map/ppermute | solution.py:470
  32.8 6.0 %collective-permute-start.6 = (f32[7,4,128]{2,1,0:T(4,128)S(1)}, f32[7,4,128]{2,1,0:T(4,128)S(1)}, u32[]{:S(2)}, u32[]{:S(2)}) collective-permute-start(f32[7,4,128]{2,1,0:T(4,128)S(1)} %get-tuple-element.34), channel_id=1, source_target_pairs={{0,1},{1,2},{2,3},{3,0},{4,5},{5,6},{6,7},{7,4},{8,9},{9,10},{10,1... | collective-permute-start | bytes 43016 | tf_op jit(solution)/shard_map/ppermute | solution.py:470
  35.7 4.9 %collective-permute-start.7 = (f32[7,4,128]{2,1,0:T(4,128)S(1)}, f32[7,4,128]{2,1,0:T(4,128)S(1)}, u32[]{:S(2)}, u32[]{:S(2)}) collective-permute-start(f32[7,4,128]{2,1,0:T(4,128)S(1)} %get-tuple-element.35), channel_id=1, source_target_pairs={{0,3},{1,0},{2,1},{3,2},{4,7},{5,4},{6,5},{7,6},{8,11},{9,8},{10,9... | collective-permute-start | bytes 43016 | tf_op jit(solution)/shard_map/ppermute | solution.py:470

commit v15 on v12

--- a/solution.py
+++ b/solution.py
@@ -173,7 +173,7 @@
             sums[j] = jnp.where(lane == at, pltpu.roll(new, at + 1 - row, 1), sums[j])
         return tuple(sums)
 
-    sums = lax.fori_loop(0, NVAR, body, tuple(rec_in[j] for j in range(CS)))
+    sums = lax.fori_loop(0, NVAR, body, tuple(rec_in[j] for j in range(CS)), unroll=True)
     rows = []
     for j in range(CS):
         rec[j] = sums[j]
@@ -311,7 +311,7 @@
             part2_ref[c, j] = part_ref[c, j] - tau_ref[j] * lost[j]
         return carry
 
-    lax.fori_loop(0, NVAR, body, 0)
+    lax.fori_loop(0, NVAR, body, 0, unroll=True)
     cells = cell_ref[0, 0]
     square = (LANES, LANES)
     axial_pick = (row_ids(square) == cells % LANES).astype(F32).astype(BF16)

time: 65 us -> 64.5 us (level)
  no operation moved by 1% of the time
where the time goes in v15:
time: 64.5 us; the launch traced here: 64.3 us
  starting transfers between devices  30.8 us (48%)
  blocking collectives  20.1 us (31%)
  Pallas kernels  7.15 us (11%)
  waiting for transfers between devices  4.69 us (7%)
  between operations  0.77 us (1%)
    ppermute x8, starting transfers between devices, shifted(): lax.ppermute(value, axis, [(i, (i + by) % devices) for i in range(devices)])  22.3 us
    all_to_all x1, blocking collectives, on_device(): lax.all_to_all(dense.reshape(peers, 1, 3 * LANES), ('span', 'pitch'), 0, 0)  20.1 us
    all_to_all x1, starting transfers between devices, on_device(): lax.all_to_all(message.reshape(devices, 1, 2 * LANES), ('row', 'span', 'p...  8.47 us
    ppermute x8, waiting for transfers between devices, shifted(): lax.ppermute(value, axis, [(i, (i + by) % devices) for i in range(devices)])  3.86 us
    pallas_call x1, Pallas kernels, on_device(): call(cycle_kernel, 'cycle_update', [(1,) + block, (3 * peers, LANES)], in...  2.14 us
    pallas_call x1, Pallas kernels, on_device(): call(settle_kernel, 'settle', [block, (6, CS, CP, LANES), ((2 * devices,...  1.63 us
  transfers between devices with their start and end apart: 9, of which 4 were waited for; matrix products, arithmetic and copies ran while one was open for 0% of the time, Pallas kernels for 5%

profile of v15, /device:TPU:32, one launch (start us, length us, event | category | flops | bytes accessed | tf_op | source)
XLA Modules:
  0.0 64.3 jit_solution(72196762460711345)
XLA Ops:
  0.7 0.9 %edges.1 = (f32[6,8,128]{2,1,0:T(8,128)S(1)}, f32[6,8,128]{2,1,0:T(8,128)S(1)}, f32[6,4,128]{2,1,0:T(4,128)S(1)}, f32[6,4,128]{2,1,0:T(4,128)S(1)}) custom-call(f32[1,6,4,8,128]{4,3,2,1,0:T(8,128)} %adj_ref.1), custom_call_target="tpu_custom_call" | custom-call | flops 2000000000 | bytes 30000000 | tf_op jit(solution)/shard_map/edges/pallas_call | solution.py:483
  1.6 1.6 %collective-permute-start = (f32[6,8,128]{2,1,0:T(8,128)S(1)}, f32[6,8,128]{2,1,0:T(8,128)S(1)}, u32[]{:S(2)}, u32[]{:S(2)}) collective-permute-start(f32[6,8,128]{2,1,0:T(8,128)S(1)} %get-tuple-element.26), channel_id=1, source_target_pairs={{0,4},{4,8},{8,12},{12,16},{16,20},{20,24},{24,28},{28,32},{32,36}... | collective-permute-start | bytes 73736 | tf_op jit(solution)/shard_map/ppermute | solution.py:463
  3.2 4.8 %collective-permute-start.1 = (f32[6,8,128]{2,1,0:T(8,128)S(1)}, f32[6,8,128]{2,1,0:T(8,128)S(1)}, u32[]{:S(2)}, u32[]{:S(2)}) collective-permute-start(f32[6,8,128]{2,1,0:T(8,128)S(1)} %get-tuple-element.27), channel_id=1, source_target_pairs={{0,124},{4,0},{8,4},{12,8},{16,12},{20,16},{24,20},{28,24},{32,28}... | collective-permute-start | bytes 73736 | tf_op jit(solution)/shard_map/ppermute | solution.py:463
  7.9 3.3 %collective-permute-start.2 = (f32[6,4,128]{2,1,0:T(4,128)S(1)}, f32[6,4,128]{2,1,0:T(4,128)S(1)}, u32[]{:S(2)}, u32[]{:S(2)}) collective-permute-start(f32[6,4,128]{2,1,0:T(4,128)S(1)} %get-tuple-element.28), channel_id=1, source_target_pairs={{0,1},{1,2},{2,3},{3,0},{4,5},{5,6},{6,7},{7,4},{8,9},{9,10},{10,1... | collective-permute-start | bytes 36872 | tf_op jit(solution)/shard_map/ppermute | solution.py:463
  11.2 2.1 %collective-permute-start.3 = (f32[6,4,128]{2,1,0:T(4,128)S(1)}, f32[6,4,128]{2,1,0:T(4,128)S(1)}, u32[]{:S(2)}, u32[]{:S(2)}) collective-permute-start(f32[6,4,128]{2,1,0:T(4,128)S(1)} %get-tuple-element.29), channel_id=1, source_target_pairs={{0,3},{1,0},{2,1},{3,2},{4,7},{5,4},{6,5},{7,6},{8,11},{9,8},{10,9... | collective-permute-start | bytes 36872 | tf_op jit(solution)/shard_map/ppermute | solution.py:463
  13.4 0.0 copy-start.5
  13.4 1.1 %interior.1 = (f32[6,4,8,128]{3,2,1,0:T(8,128)S(1)}, f32[4,8,128]{2,1,0:T(8,128)S(1)}) custom-call(f32[6,4,8,128]{3,2,1,0:T(8,128)S(1)} %bitcast.19, f32[6,4,8,128]{3,2,1,0:T(8,128)S(1)} %bitcast.12, f32[4,8,128]{2,1,0:T(8,128)S(1)} %bitcast.14, bf16[7,6,6,4,8,128]{5,4,3,2,1,0:T(8,128)(2,1)S(1)} %bitcast.7), custom_call_target="tpu_custom_call" | custom-call | flops 9000000 | bytes 3000000 | tf_op jit(solution)/shard_map/interior/pallas_call | solution.py:493
  14.5 0.6 collective-permute-done.2.left_ref
  15.0 1.5 %collective-permute-done.3.right_ref = f32[6,4,128]{2,1,0:T(4,128)S(1)} collective-permute-done((f32[6,4,128]{2,1,0:T(4,128)S(1)}, f32[6,4,128]{2,1,0:T(4,128)S(1)}, u32[]{:S(2)}, u32[]{:S(2)}) %collective-permute-start.3) | collective-permute-done | bytes 12320 | tf_op jit(solution)/shard_map/ppermute | solution.py:463
  16.5 1.0 %edge_update.1 = (f32[6,4,8,128]{3,2,1,0:T(8,128)S(1)}, f32[512,128]{1,0:T(8,128)}, f32[4,8,128]{2,1,0:T(8,128)S(1)}, f32[7,8,128]{2,1,0:T(8,128)S(1)}, f32[7,8,...) custom-call(f32[6,4,8,128]{3,2,1,0:T(8,128)S(1)} %get-tuple-element.24.part_ref, ...), custom_call_target="tpu_custom_call" | custom-call | tf_op jit(solution)/shard_map/edge_update/pallas_call | solution.py:503
  17.5 8.5 %all-to-all-start = ((f32[256,1,256]{2,1,0:T(1,128)}), f32[256,1,256]{2,1,0:T(1,128)S(1)}, u32[]{:S(2)}, u32[]{:S(2)}) async-start(f32[256,1,256]{2,1,0:T(1,128)} %bitcast.4), calls=%async_computation | async-start | bytes 524288 | tf_op jit(solution)/shard_map/all_to_all | solution.py:515
  26.0 1.6 %collective-permute-start.4 = (f32[7,8,128]{2,1,0:T(8,128)S(1)}, f32[7,8,128]{2,1,0:T(8,128)S(1)}, u32[]{:S(2)}, u32[]{:S(2)}) collective-permute-start(f32[7,8,128]{2,1,0:T(8,128)S(1)} %get-tuple-element.32), channel_id=1, source_target_pairs={{0,4},{4,8},{8,12},{12,16},{16,20},{20,24},{24,28},{28,32},{32,36}... | collective-permute-start | bytes 86024 | tf_op jit(solution)/shard_map/ppermute | solution.py:463
  27.6 4.8 %collective-permute-start.5 = (f32[7,8,128]{2,1,0:T(8,128)S(1)}, f32[7,8,128]{2,1,0:T(8,128)S(1)}, u32[]{:S(2)}, u32[]{:S(2)}) collective-permute-start(f32[7,8,128]{2,1,0:T(8,128)S(1)} %get-tuple-element.33), channel_id=1, source_target_pairs={{0,124},{4,0},{8,4},{12,8},{16,12},{20,16},{24,20},{28,24},{32,28}... | collective-permute-start | bytes 86024 | tf_op jit(solution)/shard_map/ppermute | solution.py:463
  32.3 2.9 %collective-permute-start.6 = (f32[7,4,128]{2,1,0:T(4,128)S(1)}, f32[7,4,128]{2,1,0:T(4,128)S(1)}, u32[]{:S(2)}, u32[]{:S(2)}) collective-permute-start(f32[7,4,128]{2,1,0:T(4,128)S(1)} %get-tuple-element.34), channel_id=1, source_target_pairs={{0,1},{1,2},{2,3},{3,0},{4,5},{5,6},{6,7},{7,4},{8,9},{9,10},{10,1... | collective-permute-start | bytes 43016 | tf_op jit(solution)/shard_map/ppermute | solution.py:463
  35.2 1.4 %collective-permute-start.7 = (f32[7,4,128]{2,1,0:T(4,128)S(1)}, f32[7,4,128]{2,1,0:T(4,128)S(1)}, u32[]{:S(2)}, u32[]{:S(2)}) collective-permute-start(f32[7,4,128]{2,1,0:T(4,128)S(1)} %get-tuple-element.35), channel_id=1, source_target_pairs={{0,3},{1,0},{2,1},{3,2},{4,7},{5,4},{6,5},{7,6},{8,11},{9,8},{10,9... | collective-permute-start | bytes 43016 | tf_op jit(solution)/shard_map/ppermute | solution.py:463
  36.6 1.6 %settle.1 = (f32[6,4,8,128]{3,2,1,0:T(8,128)S(1)}, f32[6,4,8,128]{3,2,1,0:T(8,128)S(1)}, f32[512,128]{1,0:T(8,128)S(1)}, f32[2,4,8,128]{3,2,1,0:T(8,128)S(1)}, bf16[128,384]{1,0:T(8,128)(2,1)S(1)}) custom-call(s32[2,128]{1,0:T(2,128)S(1)} %copy-done.4, f32[6,4,8,128]{3,2,1,0:T(8,128)S(1)} %get-tuple-element.30.f1_ref, f32[6,4,8,128]{3,2,1,0:T(8,128)S(1)} %bitcast.13, ...), custom_call_target="tpu_custom_call" | custom-call | flops 9000000 | bytes 3000000 | tf_op jit(solution)/shard_map/settle/pallas_call | solution.py:519
  38.3 0.0 collective-permute-done.6.left_ref
  38.3 1.8 %collective-permute-done.7.right_ref = f32[7,4,128]{2,1,0:T(4,128)S(1)} collective-permute-done((f32[7,4,128]{2,1,0:T(4,128)S(1)}, f32[7,4,128]{2,1,0:T(4,128)S(1)}, u32[]{:S(2)}, u32[]{:S(2)}) %collective-permute-start.7) | collective-permute-done | bytes 14368 | tf_op jit(solution)/shard_map/ppermute | solution.py:463
  40.1 0.3 settle_edges.1
  40.5 0.8 %all-to-all-done = f32[256,1,256]{2,1,0:T(1,128)S(1)} async-done(((f32[256,1,256]{2,1,0:T(1,128)}), f32[256,1,256]{2,1,0:T(1,128)S(1)}, u32[]{:S(2)}, u32[]{:S(2)}) %all-to-all-start) | async-done | bytes 262176 | tf_op jit(solution)/shard_map/all_to_all | solution.py:515
  41.3 2.1 %cycle_update.1 = (f32[1,6,4,8,128]{4,3,2,1,0:T(8,128)}, f32[384,128]{1,0:T(8,128)S(1)}) custom-call(s32[2,128]{1,0:T(2,128)S(1)} %copy-done.4, f32[6,4,8,128]{3,2,1,0:T(8,128)S(1)} %get-tuple-element.36.part_ref, f32[4,8,128]{2,1,0:T(8,128)S(1)} %get-tuple-element.37.rec_ref, f32[6,4,8,128]{3,2,1,0:T(8,128)S(1)} %get-tuple-element.38.pack_ref, ...), custom_call_target="tpu_custom_call" | custom-call | tf_op jit(solution)/shard_map/cycle_update/pallas_call | solution.py:538
  43.5 20.1 %all_to_all.10 = f32[128,1,384]{2,1,0:T(1,128)S(1)} all-to-all(f32[128,1,384]{2,1,0:T(1,128)S(1)} %bitcast.18), channel_id=1, replica_groups=mesh['row'=2,'span'=32,'pitch'=4] {'span','pitch'}, dimensions={0} | all-to-all | bytes 393216 | tf_op jit(solution)/shard_map/all_to_all | solution.py:549
  63.5 0.2 reduce_sum.9
  63.7 0.6 reshape.19
  (20 shorter events, 0.1 us)
Async XLA Ops:
  0.6 12.7 %copy-start.3 = (f32[1,6,4,8,128]{4,3,2,1,0:T(8,128)S(1)}, f32[1,6,4,8,128]{4,3,2,1,0:T(8,128)}, u32[]{:S(2)}) copy-start(f32[1,6,4,8,128]{4,3,2,1,0:T(8,128)} %adj_ref.1) | copy-start | bytes 294916
  0.6 12.7 %copy-start = (bf16[1,7,6,6,4,8,128]{6,5,4,3,2,1,0:T(8,128)(2,1)S(1)}, bf16[1,7,6,6,4,8,128]{6,5,4,3,2,1,0:T(8,128)(2,1)}, u32[]{:S(2)}) copy-start(bf16[1,7,6,6,4,8,128]{6,5,4,3,2,1,0:T(8,128)(2,1)} %param.11) | copy-start | bytes 6193156
  0.7 12.7 %copy-start.2 = (f32[1,4,8,128]{3,2,1,0:T(8,128)S(1)}, f32[1,4,8,128]{3,2,1,0:T(8,128)}, u32[]{:S(2)}) copy-start(f32[1,4,8,128]{3,2,1,0:T(8,128)} %param.10) | copy-start | bytes 49156
  0.7 12.7 %copy-start.1 = (f32[1,6,4,8,128]{4,3,2,1,0:T(8,128)S(1)}, f32[1,6,4,8,128]{4,3,2,1,0:T(8,128)}, u32[]{:S(2)}) copy-start(f32[1,6,4,8,128]{4,3,2,1,0:T(8,128)} %param.9) | copy-start | bytes 294916
  1.6 14.9 %collective-permute-start = (f32[6,8,128]{2,1,0:T(8,128)S(1)}, f32[6,8,128]{2,1,0:T(8,128)S(1)}, u32[]{:S(2)}, u32[]{:S(2)}) collective-permute-start(f32[6,8,128]{2,1,0:T(8,128)S(1)} %get-tuple-element.26), channel_id=1, source_target_pairs={{0,4},{4,8},{8,12},{12,16},{16,20},{20,24},{24,28},{28,32},{32,36}... | collective-permute-start | bytes 73736 | tf_op jit(solution)/shard_map/ppermute | solution.py:463
  3.2 13.3 %collective-permute-start.1 = (f32[6,8,128]{2,1,0:T(8,128)S(1)}, f32[6,8,128]{2,1,0:T(8,128)S(1)}, u32[]{:S(2)}, u32[]{:S(2)}) collective-permute-start(f32[6,8,128]{2,1,0:T(8,128)S(1)} %get-tuple-element.27), channel_id=1, source_target_pairs={{0,124},{4,0},{8,4},{12,8},{16,12},{20,16},{24,20},{28,24},{32,28}... | collective-permute-start | bytes 73736 | tf_op jit(solution)/shard_map/ppermute | solution.py:463
  7.9 7.1 %collective-permute-start.2 = (f32[6,4,128]{2,1,0:T(4,128)S(1)}, f32[6,4,128]{2,1,0:T(4,128)S(1)}, u32[]{:S(2)}, u32[]{:S(2)}) collective-permute-start(f32[6,4,128]{2,1,0:T(4,128)S(1)} %get-tuple-element.28), channel_id=1, source_target_pairs={{0,1},{1,2},{2,3},{3,0},{4,5},{5,6},{6,7},{7,4},{8,9},{9,10},{10,1... | collective-permute-start | bytes 36872 | tf_op jit(solution)/shard_map/ppermute | solution.py:463
  11.2 5.3 %collective-permute-start.3 = (f32[6,4,128]{2,1,0:T(4,128)S(1)}, f32[6,4,128]{2,1,0:T(4,128)S(1)}, u32[]{:S(2)}, u32[]{:S(2)}) collective-permute-start(f32[6,4,128]{2,1,0:T(4,128)S(1)} %get-tuple-element.29), channel_id=1, source_target_pairs={{0,3},{1,0},{2,1},{3,2},{4,7},{5,4},{6,5},{7,6},{8,11},{9,8},{10,9... | collective-permute-start | bytes 36872 | tf_op jit(solution)/shard_map/ppermute | solution.py:463
  13.4 23.3 %copy-start.7 = (f32[1,1,1,18,128]{4,2,3,1,0:T(1,128)S(1)}, f32[1,1,1,18,128]{4,2,3,1,0:T(1,128)}, u32[]{:S(2)}) copy-start(f32[1,1,1,18,128]{4,2,3,1,0:T(1,128)} %param.15) | copy-start | bytes 27652
  13.4 23.3 %copy-start.4 = (s32[2,128]{1,0:T(2,128)S(1)}, s32[2,128]{1,0:T(2,128)}, u32[]{:S(2)}) copy-start(s32[2,128]{1,0:T(2,128)} %bands_ref.3) | copy-start | bytes 3076
  13.4 23.2 %copy-start.5 = (s32[1,1,1,128]{3,2,1,0:T(1,128)S(1)}, s32[1,1,1,128]{3,2,1,0:T(1,128)}, u32[]{:S(2)}) copy-start(s32[1,1,1,128]{3,2,1,0:T(1,128)} %cell_ref.3) | copy-start | bytes 1540
  13.4 23.2 %copy-start.6 = (s32[1,1,1,128]{3,2,1,0:T(1,128)S(1)}, s32[1,1,1,128]{3,2,1,0:T(1,128)}, u32[]{:S(2)}) copy-start(s32[1,1,1,128]{3,2,1,0:T(1,128)} %owner_ref.3) | copy-start | bytes 1540
  17.5 23.8 %all-to-all-start = ((f32[256,1,256]{2,1,0:T(1,128)}), f32[256,1,256]{2,1,0:T(1,128)S(1)}, u32[]{:S(2)}, u32[]{:S(2)}) async-start(f32[256,1,256]{2,1,0:T(1,128)} %bitcast.4), calls=%async_computation | async-start | bytes 524288 | tf_op jit(solution)/shard_map/all_to_all | solution.py:515
  26.0 14.1 %collective-permute-start.4 = (f32[7,8,128]{2,1,0:T(8,128)S(1)}, f32[7,8,128]{2,1,0:T(8,128)S(1)}, u32[]{:S(2)}, u32[]{:S(2)}) collective-permute-start(f32[7,8,128]{2,1,0:T(8,128)S(1)} %get-tuple-element.32), channel_id=1, source_target_pairs={{0,4},{4,8},{8,12},{12,16},{16,20},{20,24},{24,28},{28,32},{32,36}... | collective-permute-start | bytes 86024 | tf_op jit(solution)/shard_map/ppermute | solution.py:463
  27.6 12.6 %collective-permute-start.5 = (f32[7,8,128]{2,1,0:T(8,128)S(1)}, f32[7,8,128]{2,1,0:T(8,128)S(1)}, u32[]{:S(2)}, u32[]{:S(2)}) collective-permute-start(f32[7,8,128]{2,1,0:T(8,128)S(1)} %get-tuple-element.33), channel_id=1, source_target_pairs={{0,124},{4,0},{8,4},{12,8},{16,12},{20,16},{24,20},{28,24},{32,28}... | collective-permute-start | bytes 86024 | tf_op jit(solution)/shard_map/ppermute | solution.py:463
  32.3 6.0 %collective-permute-start.6 = (f32[7,4,128]{2,1,0:T(4,128)S(1)}, f32[7,4,128]{2,1,0:T(4,128)S(1)}, u32[]{:S(2)}, u32[]{:S(2)}) collective-permute-start(f32[7,4,128]{2,1,0:T(4,128)S(1)} %get-tuple-element.34), channel_id=1, source_target_pairs={{0,1},{1,2},{2,3},{3,0},{4,5},{5,6},{6,7},{7,4},{8,9},{9,10},{10,1... | collective-permute-start | bytes 43016 | tf_op jit(solution)/shard_map/ppermute | solution.py:463
  35.2 4.9 %collective-permute-start.7 = (f32[7,4,128]{2,1,0:T(4,128)S(1)}, f32[7,4,128]{2,1,0:T(4,128)S(1)}, u32[]{:S(2)}, u32[]{:S(2)}) collective-permute-start(f32[7,4,128]{2,1,0:T(4,128)S(1)} %get-tuple-element.35), channel_id=1, source_target_pairs={{0,3},{1,0},{2,1},{3,2},{4,7},{5,4},{6,5},{7,6},{8,11},{9,8},{10,9... | collective-permute-start | bytes 43016 | tf_op jit(solution)/shard_map/ppermute | solution.py:463
